TPU v7x, 32 devices: a whole 2x2x4 slice. The times are simulated.
32 devices in a mesh: fsdp: 8 (over y, x, core), seq: 4 (over z).
Axes of the slice: x: 2, y: 2, z: 4, core: 2. Of those that a mesh axis runs over, the one named last changes fastest.
Arguments:
- tokens: bfloat16 [8192, 2048], P(('fsdp', 'seq')), may hold values from -6 to 6
- seq_lengths: int32 [8], P('fsdp'), may hold values from 512 to 1024, as said below
- attn_gain: bfloat16 [2048], P('fsdp'), may hold values from 0.5 to 1.5
- query_proj: bfloat16 [2048, 2048], P('fsdp'), may hold values from -0.125 to 0.125
- key_proj: bfloat16 [2048, 2048], P('fsdp'), may hold values from -0.125 to 0.125
- value_proj: bfloat16 [2048, 2048], P('fsdp'), may hold values from -0.125 to 0.125
- decay_down: bfloat16 [2048, 16], P('fsdp'), may hold values from -0.125 to 0.125
- decay_up: bfloat16 [16, 256], P(None, 'fsdp'), may hold values from -1.5 to 1.5
- decay_bias: bfloat16 [256], P('fsdp'), may hold values from 1.5 to 6
- swish_proj: bfloat16 [2048, 2048], P('fsdp'), may hold values from -0.125 to 0.125
- slot_gain: bfloat16 [2048], P('fsdp'), may hold values from 0.5 to 1.5
- out_proj: bfloat16 [2048, 2048], P('fsdp'), may hold values from -0.25 to 0.25
- mlp_gain: bfloat16 [2048], P('fsdp'), may hold values from 0.5 to 1.5
- mlp_gate: bfloat16 [2048, 5632], P('fsdp'), may hold values from -0.125 to 0.125
- mlp_up: bfloat16 [2048, 5632], P('fsdp'), may hold values from -0.125 to 0.125
- mlp_down: bfloat16 [5632, 2048], P('fsdp'), may hold values from -0.078125 to 0.078125
- grad_out: bfloat16 [8192, 2048], P(('fsdp', 'seq')), may hold values from -6 to 6
Outputs:
- result: bfloat16 [8192, 2048], P(('fsdp', 'seq'))
- grad_tokens: bfloat16 [8192, 2048], P(('fsdp', 'seq'))
- attn_gain_grad: float32 [2048], P('fsdp')
- query_proj_grad: float32 [2048, 2048], P('fsdp')
- key_proj_grad: float32 [2048, 2048], P('fsdp')
- value_proj_grad: float32 [2048, 2048], P('fsdp')
- decay_down_grad: float32 [2048, 16], P('fsdp')
- decay_up_grad: float32 [16, 256], P(None, 'fsdp')
- decay_bias_grad: float32 [256], P('fsdp')
- swish_proj_grad: float32 [2048, 2048], P('fsdp')
- slot_gain_grad: float32 [2048], P('fsdp')
- out_proj_grad: float32 [2048, 2048], P('fsdp')
- mlp_gain_grad: float32 [2048], P('fsdp')
- mlp_gate_grad: float32 [2048, 5632], P('fsdp')
- mlp_up_grad: float32 [2048, 5632], P('fsdp')
- mlp_down_grad: float32 [5632, 2048], P('fsdp')
Inputs may be any that keep to these rules, and one draw needn't show every extreme that they name: `seq_lengths`: rows of a sequence from its valid length on are padding; in every draw one sequence fills all 1024 positions and another has 512.
All inputs are finite; a program needn't handle non-finite values.
Results may differ from a plain program's by a relative error of at most 0.02.
Values may be sent and summed in bfloat16 or wider, within the bound.
No kernel may reach another device: no remote copies, remote signals or barrier semaphores. Data moves between devices by JAX's collectives and lax.ppermute only.
A program may use at most 512 MiB of HBM per device.

v0:
```python
import jax
import jax.numpy as jnp
from jax import lax
from jax.sharding import PartitionSpec as P

D = 2048
HEADS = 4
HEAD = 512
SLOTS = 64
GROUP = 64


EPSILON = 1e-06
NORMALIZER = 8.0
HIGHEST = lax.Precision.HIGHEST


def carried_in(value, axis, combine, identity):
    peers, here = (lax.axis_size(axis), lax.axis_index(axis))
    everything = jax.tree.map(
        lambda part, kind: lax.all_gather(part.astype(kind), axis),
        value,
        (jnp.bfloat16, jnp.bfloat16, jnp.bfloat16),
    )
    start = jax.tree.map(
        lambda part, zero: jnp.broadcast_to(jnp.asarray(zero, part.dtype), part.shape),
        value,
        identity,
    )

    def hop(k, before):
        reached = k < here
        new = combine(
            before, jax.tree.map(lambda part, own: part[k].astype(own.dtype), everything, value)
        )
        return jax.tree.map(lambda a, b: jnp.where(reached, a, b), new, before)

    return lax.fori_loop(0, peers, hop, start)


def carried_in_2(value, axis, join, neutral):
    count = lax.axis_size(axis)
    place = lax.axis_index(axis)
    ahead = count - 1 - place
    gathered = jax.tree.map(
        lambda a, kind: lax.all_gather(a.astype(kind), axis),
        value,
        jax.tree.map(lambda a: jnp.bfloat16 if a.dtype == jnp.float32 else a.dtype, value),
    )
    state = jax.tree.map(lambda a, e: jnp.zeros_like(a) + jnp.asarray(e, a.dtype), value, neutral)

    def one(hop, state):
        source = count - 1 - hop
        return join(
            state,
            jax.tree.map(
                lambda a, own: lax.dynamic_index_in_dim(a, source, 0, False).astype(own.dtype),
                gathered,
                value,
            ),
        )

    return lax.fori_loop(0, ahead, one, state)


def inverse_rms(values):
    return lax.rsqrt(jnp.mean(values * values, axis=-1, keepdims=True) + EPSILON)


def bf_dot(left_mat, right_mat):
    return jnp.dot(left_mat, right_mat, preferred_element_type=jnp.float32)


def left_dot(left_mat, right_mat):
    return lax.dot_general(
        left_mat, right_mat, (((0,), (0,)), ((), ())), preferred_element_type=jnp.float32
    )


def right_dot(left_mat, right_mat):
    return lax.dot_general(
        left_mat, right_mat, (((1,), (1,)), ((), ())), preferred_element_type=jnp.float32
    )


def silu_slope(values):
    sigmoid_val = jax.nn.sigmoid(values)
    return sigmoid_val * (1.0 + values * (1.0 - sigmoid_val))


def norm_back(grad_hat, hat_rows, scale_rows):
    return scale_rows * (
        grad_hat - hat_rows * jnp.mean(grad_hat * hat_rows, axis=-1, keepdims=True)
    )


def decay_terms(forget, live_mask):
    log_sig = jax.nn.log_sigmoid(forget) / NORMALIZER
    mask_cube = live_mask[:, None, None]
    return (mask_cube * log_sig, mask_cube * -jnp.expm1(log_sig))


def to_blocks(array):
    return array.reshape((array.shape[0] // GROUP, GROUP) + array.shape[1:])


def block_dots(queries_low, keys_low):
    scale_dot = HEAD ** (-0.5)
    query_blocks = queries_low.reshape(-1, GROUP, HEADS, HEAD)
    key_blocks = keys_low.reshape(-1, GROUP, HEADS, HEAD)
    return (
        jnp.einsum("nthe,nshe->ntsh", query_blocks, key_blocks, preferred_element_type=jnp.float32)
        * scale_dot
    )


def advance_states(carried, block_pack):
    keys_now, values_now, log_now = carried
    block_keys, block_values, block_log, block_in = block_pack
    running = jnp.cumsum(block_log, axis=0)
    total_log = running[-1]
    weight = jnp.exp(total_log[None] - running) * block_in
    factor = jnp.exp(total_log)[..., None]
    keys_next = factor * keys_now + jnp.einsum(
        "shj,she->hje", weight, block_keys, precision=HIGHEST
    )
    values_next = factor * values_now + jnp.einsum(
        "shj,she->hje", weight, block_values, precision=HIGHEST
    )
    return ((keys_next, values_next, log_now + total_log), (keys_now, values_now, log_now))


def group_states(key_rows, value_rows, log_decay, inflow):
    zeros_state = jnp.zeros((key_rows.shape[1], log_decay.shape[2], key_rows.shape[2]), jnp.float32)
    start_carry = (zeros_state, zeros_state, jnp.zeros(log_decay.shape[1:], jnp.float32))
    final_state, starts = lax.scan(
        jax.checkpoint(advance_states),
        start_carry,
        (to_blocks(key_rows), to_blocks(value_rows), to_blocks(log_decay), to_blocks(inflow)),
    )
    return (starts, final_state)


def attend_block(queries, qk_dots, value_rows, log_decay, inflow, state_keys, state_values):
    positions = jnp.arange(queries.shape[0], dtype=jnp.int32)
    causal = (positions[:, None] >= positions[None, :]).astype(jnp.float32)
    running = jnp.cumsum(log_decay, axis=0)
    log_gap = running[:, None] - running[None, :]
    decay_tab = jnp.exp(jnp.minimum(log_gap, 0.0)) * causal[:, :, None, None]
    growth = jnp.exp(running)
    scale_dot = queries.shape[-1] ** (-0.5)
    within = jnp.einsum("tsh,tshj,shj->thj", qk_dots, decay_tab, inflow, precision=HIGHEST)
    across = jnp.einsum("hje,the->thj", state_keys, queries, precision=HIGHEST) * scale_dot * growth
    probs_slot = jax.nn.softmax(within + across, axis=-1)
    mix_weight = jnp.einsum("thj,tshj,shj->tsh", probs_slot, decay_tab, inflow, precision=HIGHEST)
    recent = jnp.einsum("tsh,she->the", mix_weight, value_rows, precision=HIGHEST)
    earlier_part = jnp.einsum("thj,hje->the", probs_slot * growth, state_values, precision=HIGHEST)
    return recent + earlier_part


def attend_pack(block_pack):
    return attend_block(*block_pack)


def attend_groups(
    queries,
    qk_blocks,
    value_rows,
    log_decay,
    inflow,
    start_keys,
    start_values,
    start_log,
    init_keys,
    init_values,
):
    factor = jnp.exp(start_log)[..., None]
    state_keys = factor * init_keys[None] + start_keys
    state_values = factor * init_values[None] + start_values
    outputs = lax.map(
        jax.checkpoint(attend_pack),
        (
            to_blocks(queries),
            qk_blocks,
            to_blocks(value_rows),
            to_blocks(log_decay),
            to_blocks(inflow),
            state_keys,
            state_values,
        ),
    )
    return outputs.reshape(queries.shape)


def local_mixer(
    queries, key_rows, value_rows, qk_blocks, forget, live_mask, init_keys, init_values
):
    log_decay, inflow = decay_terms(forget, live_mask)
    starts, final_state = group_states(key_rows, value_rows, log_decay, inflow)
    return attend_groups(
        queries,
        qk_blocks,
        value_rows,
        log_decay,
        inflow,
        starts[0],
        starts[1],
        starts[2],
        init_keys,
        init_values,
    )


def end_states(key_rows, value_rows, forget, live_mask, init_keys, init_values):
    log_decay, inflow = decay_terms(forget, live_mask)
    starts, final_state = group_states(key_rows, value_rows, log_decay, inflow)
    factor = jnp.exp(final_state[2])[..., None]
    return (factor * init_keys + final_state[0], factor * init_values + final_state[1])


def combine_states(earlier, later):
    factor = later[0][..., None]
    return (earlier[0] * later[0], factor * earlier[1] + later[1], factor * earlier[2] + later[2])


def body(
    tokens,
    seq_lengths,
    attn_gain,
    query_proj,
    key_proj,
    value_proj,
    decay_down,
    decay_up,
    decay_bias,
    swish_proj,
    slot_gain,
    out_proj,
    mlp_gain,
    mlp_gate,
    mlp_up,
    mlp_down,
    grad_out,
):
    row_count = tokens.shape[0]
    positions = lax.axis_index("seq") * row_count + jnp.arange(row_count, dtype=jnp.int32)
    live_mask = (positions < seq_lengths[0]).astype(jnp.float32)
    live_col = live_mask[:, None]
    gathered = (
        lax.all_gather(attn_gain, "fsdp", axis=0, tiled=True),
        lax.all_gather(query_proj, "fsdp", axis=0, tiled=True),
        lax.all_gather(key_proj, "fsdp", axis=0, tiled=True),
        lax.all_gather(value_proj, "fsdp", axis=0, tiled=True),
        lax.all_gather(decay_down, "fsdp", axis=0, tiled=True),
        lax.all_gather(decay_up, "fsdp", axis=1, tiled=True),
        lax.all_gather(decay_bias, "fsdp", axis=0, tiled=True),
        lax.all_gather(swish_proj, "fsdp", axis=0, tiled=True),
        lax.all_gather(slot_gain, "fsdp", axis=0, tiled=True),
        lax.all_gather(out_proj, "fsdp", axis=0, tiled=True),
        lax.all_gather(mlp_gain, "fsdp", axis=0, tiled=True),
        lax.all_gather(mlp_gate, "fsdp", axis=0, tiled=True),
        lax.all_gather(mlp_up, "fsdp", axis=0, tiled=True),
        lax.all_gather(mlp_down, "fsdp", axis=0, tiled=True),
    )
    (
        gain_one,
        proj_query,
        proj_key,
        proj_value,
        proj_down,
        proj_up,
        bias_full,
        proj_swish,
        gain_slot,
        proj_out,
        gain_two,
        proj_gate,
        proj_hidden,
        proj_back,
    ) = gathered
    tokens_f = tokens.astype(jnp.float32)
    scale_one = inverse_rms(tokens_f)
    hat_one = tokens_f * scale_one
    gain_one_f = gain_one.astype(jnp.float32)
    normed = (hat_one * gain_one_f).astype(jnp.bfloat16)
    queries = bf_dot(normed, proj_query).astype(jnp.bfloat16)
    key_rows = bf_dot(normed, proj_key).astype(jnp.bfloat16)
    value_rows = bf_dot(normed, proj_value).astype(jnp.bfloat16)
    gate_low = bf_dot(normed, proj_down)
    up_full = proj_up.astype(jnp.float32)
    forget = (
        jnp.dot(gate_low, up_full, precision=HIGHEST, preferred_element_type=jnp.float32)
        + bias_full.astype(jnp.float32)
    ).reshape(row_count, HEADS, SLOTS)
    swish_pre = bf_dot(normed, proj_swish)
    query3 = queries.astype(jnp.float32).reshape(row_count, HEADS, HEAD)
    key3 = key_rows.astype(jnp.float32).reshape(row_count, HEADS, HEAD)
    value3 = value_rows.astype(jnp.float32).reshape(row_count, HEADS, HEAD)
    qk_blocks = block_dots(queries, key_rows)
    log_decay, inflow = decay_terms(forget, live_mask)
    starts, final_state = group_states(key3, value3, log_decay, inflow)
    decay_total = jnp.exp(final_state[2])
    zeros_state = jnp.zeros((HEADS, SLOTS, HEAD), jnp.float32)
    identity = (jnp.ones((HEADS, SLOTS), jnp.float32), zeros_state, zeros_state)
    before = carried_in(
        (decay_total, final_state[0], final_state[1]), "seq", combine_states, identity
    )
    init_keys = before[1]
    init_values = before[2]
    mixer_out = attend_groups(
        query3,
        qk_blocks,
        value3,
        log_decay,
        inflow,
        starts[0],
        starts[1],
        starts[2],
        init_keys,
        init_values,
    )
    scale_out = inverse_rms(mixer_out)
    hat_cube = mixer_out * scale_out
    hat_out = hat_cube.reshape(row_count, HEADS * HEAD)
    gain_slot_f = gain_slot.astype(jnp.float32)
    swish_val = jax.nn.silu(swish_pre)
    gated_rows = (hat_out * gain_slot_f * swish_val).astype(jnp.bfloat16)
    attn_out = bf_dot(gated_rows, proj_out)
    residual = tokens_f + live_col * attn_out
    scale_two = inverse_rms(residual)
    hat_two = residual * scale_two
    gain_two_f = gain_two.astype(jnp.float32)
    normed_two = (hat_two * gain_two_f).astype(jnp.bfloat16)
    gate_pre = bf_dot(normed_two, proj_gate)
    up_pre = bf_dot(normed_two, proj_hidden)
    hidden_act = (jax.nn.silu(gate_pre) * up_pre).astype(jnp.bfloat16)
    mlp_out = bf_dot(hidden_act, proj_back)
    result = (residual + live_col * mlp_out).astype(jnp.bfloat16)
    back_full = (
        lax.all_gather(attn_gain, "fsdp", axis=0, tiled=True),
        lax.all_gather(query_proj, "fsdp", axis=0, tiled=True),
        lax.all_gather(key_proj, "fsdp", axis=0, tiled=True),
        lax.all_gather(value_proj, "fsdp", axis=0, tiled=True),
        lax.all_gather(decay_down, "fsdp", axis=0, tiled=True),
        lax.all_gather(decay_up, "fsdp", axis=1, tiled=True),
        lax.all_gather(decay_bias, "fsdp", axis=0, tiled=True),
        lax.all_gather(swish_proj, "fsdp", axis=0, tiled=True),
        lax.all_gather(slot_gain, "fsdp", axis=0, tiled=True),
        lax.all_gather(out_proj, "fsdp", axis=0, tiled=True),
        lax.all_gather(mlp_gain, "fsdp", axis=0, tiled=True),
        lax.all_gather(mlp_gate, "fsdp", axis=0, tiled=True),
        lax.all_gather(mlp_up, "fsdp", axis=0, tiled=True),
        lax.all_gather(mlp_down, "fsdp", axis=0, tiled=True),
    )
    (
        gain_one,
        proj_query,
        proj_key,
        proj_value,
        proj_down,
        proj_up,
        bias_full,
        proj_swish,
        gain_slot,
        proj_out,
        gain_two,
        proj_gate,
        proj_hidden,
        proj_back,
    ) = back_full
    grad_rows = grad_out.astype(jnp.float32)
    grad_mlp = (live_col * grad_rows).astype(jnp.bfloat16)
    down_grad = left_dot(hidden_act, grad_mlp)
    grad_act = right_dot(grad_mlp, proj_back)
    grad_gate = (grad_act * up_pre * silu_slope(gate_pre)).astype(jnp.bfloat16)
    grad_up = (grad_act * jax.nn.silu(gate_pre)).astype(jnp.bfloat16)
    gate_grad = left_dot(normed_two, grad_gate)
    up_grad = left_dot(normed_two, grad_up)
    grad_norm_two = right_dot(grad_gate, proj_gate) + right_dot(grad_up, proj_hidden)
    gain_two_grad = jnp.sum(grad_norm_two * hat_two, axis=0)
    grad_resid = grad_rows + norm_back(grad_norm_two * gain_two_f, hat_two, scale_two)
    mlp_shares = (
        lax.psum_scatter(
            gain_two_grad.astype(jnp.bfloat16), "fsdp", scatter_dimension=0, tiled=True
        ).astype(jnp.float32),
        lax.psum_scatter(
            gate_grad.astype(jnp.bfloat16), "fsdp", scatter_dimension=0, tiled=True
        ).astype(jnp.float32),
        lax.psum_scatter(
            up_grad.astype(jnp.bfloat16), "fsdp", scatter_dimension=0, tiled=True
        ).astype(jnp.float32),
        lax.psum_scatter(
            down_grad.astype(jnp.bfloat16), "fsdp", scatter_dimension=0, tiled=True
        ).astype(jnp.float32),
    )
    mlp_totals = (
        lax.psum(mlp_shares[0].astype(jnp.bfloat16), "seq").astype(jnp.float32),
        lax.psum(mlp_shares[1].astype(jnp.bfloat16), "seq").astype(jnp.float32),
        lax.psum(mlp_shares[2].astype(jnp.bfloat16), "seq").astype(jnp.float32),
        lax.psum(mlp_shares[3].astype(jnp.bfloat16), "seq").astype(jnp.float32),
    )
    grad_attn = (live_col * grad_resid).astype(jnp.bfloat16)
    out_grad = left_dot(gated_rows, grad_attn)
    grad_gated = right_dot(grad_attn, proj_out)
    grad_swish = (grad_gated * hat_out * gain_slot_f * silu_slope(swish_pre)).astype(jnp.bfloat16)
    slot_gain_grad = jnp.sum(grad_gated * hat_out * swish_val, axis=0)
    grad_hat_out = (grad_gated * gain_slot_f * swish_val).reshape(row_count, HEADS, HEAD)
    grad_mixer = norm_back(grad_hat_out, hat_cube, scale_out)

    def mixer_part(queries_in, keys_in, values_in, dots_in, forget_in, keys_init, values_init):
        return local_mixer(
            queries_in, keys_in, values_in, dots_in, forget_in, live_mask, keys_init, values_init
        )

    unused_out, mixer_pull = jax.vjp(
        mixer_part, query3, key3, value3, qk_blocks, forget, init_keys, init_values
    )
    grad_query3, grad_key3, grad_value3, grad_dots, grad_forget, from_keys, from_values = (
        mixer_pull(grad_mixer)
    )
    scale_dot = HEAD ** (-0.5)
    query_blocks = query3.reshape(-1, GROUP, HEADS, HEAD)
    key_blocks = key3.reshape(-1, GROUP, HEADS, HEAD)
    dots_to_query = (
        jnp.einsum("ntsh,nshe->nthe", grad_dots, key_blocks, precision=HIGHEST) * scale_dot
    )
    dots_to_key = (
        jnp.einsum("ntsh,nthe->nshe", grad_dots, query_blocks, precision=HIGHEST) * scale_dot
    )
    after = carried_in_2((decay_total, from_keys, from_values), "seq", combine_states, identity)

    def end_part(keys_in, values_in, forget_in):
        return end_states(keys_in, values_in, forget_in, live_mask, init_keys, init_values)

    unused_end, end_pull = jax.vjp(end_part, key3, value3, forget)
    extra_keys, extra_values, extra_forget = end_pull((after[1], after[2]))
    grad_queries = (
        (grad_query3 + dots_to_query.reshape(row_count, HEADS, HEAD))
        .reshape(row_count, D)
        .astype(jnp.bfloat16)
    )
    grad_keys = (
        (grad_key3 + dots_to_key.reshape(row_count, HEADS, HEAD) + extra_keys)
        .reshape(row_count, D)
        .astype(jnp.bfloat16)
    )
    grad_values = (grad_value3 + extra_values).reshape(row_count, D).astype(jnp.bfloat16)
    grad_decay = (grad_forget + extra_forget).reshape(row_count, HEADS * SLOTS)
    bias_grad = jnp.sum(grad_decay, axis=0)
    decay_up_grad = jnp.dot(
        gate_low.T, grad_decay, precision=HIGHEST, preferred_element_type=jnp.float32
    )
    up_back = proj_up.astype(jnp.float32)
    grad_low = jnp.dot(
        grad_decay, up_back.T, precision=HIGHEST, preferred_element_type=jnp.float32
    ).astype(jnp.bfloat16)
    decay_down_grad = left_dot(normed, grad_low)
    query_grad = left_dot(normed, grad_queries)
    key_grad = left_dot(normed, grad_keys)
    value_grad = left_dot(normed, grad_values)
    swish_grad = left_dot(normed, grad_swish)
    grad_norm_one = (
        right_dot(grad_queries, proj_query)
        + right_dot(grad_keys, proj_key)
        + right_dot(grad_values, proj_value)
        + right_dot(grad_low, proj_down)
        + right_dot(grad_swish, proj_swish)
    )
    gain_one_grad = jnp.sum(grad_norm_one * hat_one, axis=0)
    grad_tokens = (grad_resid + norm_back(grad_norm_one * gain_one_f, hat_one, scale_one)).astype(
        jnp.bfloat16
    )
    shares = (
        lax.psum_scatter(
            gain_one_grad.astype(jnp.bfloat16), "fsdp", scatter_dimension=0, tiled=True
        ).astype(jnp.float32),
        lax.psum_scatter(
            query_grad.astype(jnp.bfloat16), "fsdp", scatter_dimension=0, tiled=True
        ).astype(jnp.float32),
        lax.psum_scatter(
            key_grad.astype(jnp.bfloat16), "fsdp", scatter_dimension=0, tiled=True
        ).astype(jnp.float32),
        lax.psum_scatter(
            value_grad.astype(jnp.bfloat16), "fsdp", scatter_dimension=0, tiled=True
        ).astype(jnp.float32),
        lax.psum_scatter(
            decay_down_grad.astype(jnp.bfloat16), "fsdp", scatter_dimension=0, tiled=True
        ).astype(jnp.float32),
        lax.psum_scatter(
            decay_up_grad.astype(jnp.bfloat16), "fsdp", scatter_dimension=1, tiled=True
        ).astype(jnp.float32),
        lax.psum_scatter(
            bias_grad.astype(jnp.bfloat16), "fsdp", scatter_dimension=0, tiled=True
        ).astype(jnp.float32),
        lax.psum_scatter(
            swish_grad.astype(jnp.bfloat16), "fsdp", scatter_dimension=0, tiled=True
        ).astype(jnp.float32),
        lax.psum_scatter(
            slot_gain_grad.astype(jnp.bfloat16), "fsdp", scatter_dimension=0, tiled=True
        ).astype(jnp.float32),
        lax.psum_scatter(
            out_grad.astype(jnp.bfloat16), "fsdp", scatter_dimension=0, tiled=True
        ).astype(jnp.float32),
    )
    totals = (
        lax.psum(shares[0].astype(jnp.bfloat16), "seq").astype(jnp.float32),
        lax.psum(shares[1].astype(jnp.bfloat16), "seq").astype(jnp.float32),
        lax.psum(shares[2].astype(jnp.bfloat16), "seq").astype(jnp.float32),
        lax.psum(shares[3].astype(jnp.bfloat16), "seq").astype(jnp.float32),
        lax.psum(shares[4].astype(jnp.bfloat16), "seq").astype(jnp.float32),
        lax.psum(shares[5].astype(jnp.bfloat16), "seq").astype(jnp.float32),
        lax.psum(shares[6].astype(jnp.bfloat16), "seq").astype(jnp.float32),
        lax.psum(shares[7].astype(jnp.bfloat16), "seq").astype(jnp.float32),
        lax.psum(shares[8].astype(jnp.bfloat16), "seq").astype(jnp.float32),
        lax.psum(shares[9].astype(jnp.bfloat16), "seq").astype(jnp.float32),
    )
    return (
        result,
        grad_tokens,
        totals[0],
        totals[1],
        totals[2],
        totals[3],
        totals[4],
        totals[5],
        totals[6],
        totals[7],
        totals[8],
        totals[9],
        mlp_totals[0],
        mlp_totals[1],
        mlp_totals[2],
        mlp_totals[3],
    )


def solution(mesh):
    in_specs = (
        P(("fsdp", "seq"), None),
        P("fsdp"),
        P("fsdp"),
        P("fsdp", None),
        P("fsdp", None),
        P("fsdp", None),
        P("fsdp", None),
        P(None, "fsdp"),
        P("fsdp"),
        P("fsdp", None),
        P("fsdp"),
        P("fsdp", None),
        P("fsdp"),
        P("fsdp", None),
        P("fsdp", None),
        P("fsdp", None),
        P(("fsdp", "seq"), None),
    )
    out_specs = (
        P(("fsdp", "seq"), None),
        P(("fsdp", "seq"), None),
        P("fsdp"),
        P("fsdp", None),
        P("fsdp", None),
        P("fsdp", None),
        P("fsdp", None),
        P(None, "fsdp"),
        P("fsdp"),
        P("fsdp", None),
        P("fsdp"),
        P("fsdp", None),
        P("fsdp"),
        P("fsdp", None),
        P("fsdp", None),
        P("fsdp", None),
    )
    return jax.shard_map(body, mesh=mesh, in_specs=in_specs, out_specs=out_specs, check_vma=False)
```

profile of v0, /device:TPU:0, one launch (start us, length us, event | category | flops | bytes accessed | tf_op | source)
XLA Modules:
  0.0 2634.4 jit_solution(12028363917115052504)
XLA Ops:
  9.6 10.4 all-gather.5
  21.6 14.0 all-reduce.2
  35.7 9.0 all-gather.6
  78.0 45.5 %all-gather.25.cloned.1.call-done = bf16[2048,2048]{1,0:T(8,128)(2,1)} async-done(((bf16[256,2048]{1,0:T(8,128)(2,1)}), bf16[2048,2048]{1,0:T(8,128)(2,1)}) %all-gather.25.cloned.1.call-update) | async-done | bytes 8388624 | tf_op jit(solution)/shard_map/all_gather | solution.py:252
  139.5 37.3 %while.186 = (s32[]{:T(128)}, f32[4,64,512]{2,1,0:T(8,128)}, f32[4,64,512]{2,1,0:T(8,128)}, f32[4,64]{1,0:T(4,128)S(1)}, f32[4,4,64,512]{3,2,1,0:T(8,128)}, /*in...) while((s32[]{:T(128)}, f32[4,64,512]{2,1,0:T(8,128)}, ...), condition=%wide.region_3.4_spmd.clone, body=%wide.region_1.3_spmd.clone.sunk | while | flops 203440896 | bytes 5979283 | solution.py:136
  214.6 37.5 %while.188 = (s32[]{:T(128)}, f32[4,64,512]{2,1,0:T(8,128)}, f32[4,64,512]{2,1,0:T(8,128)}, f32[4,64]{1,0:T(4,128)S(1)}, f32[4,4,64,512]{3,2,1,0:T(8,128)}, /*in...) while((s32[]{:T(128)}, f32[4,64,512]{2,1,0:T(8,128)}, ...), condition=%wide.region_17.19_spmd.clone, body=%wide.region_15.18_spmd.clone.sunk | while | flops 203440896 | bytes 5979283 | solution.py:136
  262.9 11.0 all-gather.7
  278.4 10.0 while.187
  297.9 176.4 %while.182 = (s32[]{:T(128)}, f32[4,64,4,512]{3,1,2,0:T(8,128)}, f32[4,64,4,512]{3,1,2,0:T(8,128)S(1)}, f32[4,64,4,64]{3,2,1,0:T(4,128)}, f32[4,64,4,64]{3,2,1,0...) while((s32[]{:T(128)}, f32[4,64,4,512]{3,1,2,0:T(8,128)}, ...), condition=%wide.region_10.11_spmd, body=%wide.region_6.10_spmd.sunk | while | flops 332652608 | bytes 18454128 | solution.py:180
  308.4 10.0 fusion.446
  323.1 16.2 fusion.450
  352.6 10.0 fusion.446
  367.5 15.7 fusion.450
  396.6 10.0 fusion.446
  411.3 15.8 fusion.450
  440.5 10.0 fusion.446
  455.1 15.7 fusion.450
  489.3 9.7 multiply_convert_fusion.6
  506.8 14.5 fusion.232
  521.3 64.7 %all-gather.35.cloned.1.call-done = bf16[2048,5632]{1,0:T(8,128)(2,1)} async-done(((bf16[256,5632]{1,0:T(8,128)(2,1)}), bf16[2048,5632]{1,0:T(8,128)(2,1)}) %all-gather.35.cloned.1.call-update) | async-done | bytes 23068688 | tf_op jit(solution)/shard_map/all_gather | solution.py:262
  586.0 13.7 fusion.233
  599.6 104.4 %all-gather.37.cloned.1.call-done = bf16[5632,2048]{1,0:T(8,128)(2,1)} async-done(((bf16[704,2048]{1,0:T(8,128)(2,1)}), bf16[5632,2048]{1,0:T(8,128)(2,1)}) %all-gather.37.cloned.1.call-update) | async-done | bytes 23068688 | tf_op jit(solution)/shard_map/all_gather | solution.py:263
  704.0 17.4 multiply_convert_fusion
  721.5 13.1 fusion.234
  734.5 14.5 multiply_reduce_fusion.5
  752.5 9.2 multiply_reduce_fusion.6
  781.4 397.6 %while.183 = (s32[]{:T(128)}, f32[4,64,4,512]{3,1,2,0:T(8,128)}, f32[4,64,64,4]{1,2,3,0:T(8,128)}, f32[4,64,4,512]{3,1,2,0:T(8,128)}, f32[4,64,4,64]{3,2,1,0:T(4...) while((s32[]{:T(128)}, f32[4,64,4,512]{3,1,2,0:T(8,128)}, ...), condition=%wide.region_26.28_spmd, body=%wide.region_18.27_spmd.sunk | while | flops 789045248 | bytes 27920204 | solution.py:180
  863.2 14.6 fusion.485
  905.7 9.2 fusion.478
  961.6 14.6 fusion.485
  1060.3 14.6 fusion.485
  1102.9 9.2 fusion.478
  1158.8 14.6 fusion.485
  1194.7 22.5 while.190
  1240.8 67.0 %while.189 = (s32[]{:T(128)}, f32[4,64,512]{2,1,0:T(8,128)}, f32[4,64,512]{2,1,0:T(8,128)}, f32[4,64]{1,0:T(4,128)S(1)}, f32[4,64,4,512]{3,1,2,0:T(8,128)}, /*in...) while((s32[]{:T(128)}, f32[4,64,512]{2,1,0:T(8,128)}, ...), condition=%wide.region_35.37_spmd.clone, body=%wide.region_29.36_spmd.clone.sunk | while | flops 406242048 | bytes 26831204 | solution.py:136
  1320.4 57.8 %while.185 = (s32[]{:T(128)}, f32[4,64,512]{2,1,0:T(8,128)S(1)}, f32[4,64,512]{2,1,0:T(8,128)S(1)}, f32[4,64]{1,0:T(4,128)S(1)}, f32[4,64,4,512]{3,1,2,0:T(8,128...) while((s32[]{:T(128)}, f32[4,64,512]{2,1,0:T(8,128)S(1)}, ...), condition=%wide.region_51.53_spmd, body=%wide.region_45.52_spmd.sunk | while | flops 405700864 | bytes 13192393 | solution.py:136
  1402.5 13.2 convolution_convert_fusion.2
  1415.7 13.0 convolution_convert_fusion.1
  1430.0 13.1 convolution_convert_fusion
  1464.4 74.8 %reduce-scatter.17.cloned.1.call-done = bf16[256,2048]{1,0:T(8,128)(2,1)} async-done(((bf16[2048,2048]{1,0:T(8,128)(2,1)}), bf16[256,2048]{1,0:T(8,128)(2,1)}) %reduce-scatter.17.cloned.1.call-update) | async-done | bytes 1048592 | tf_op jit(solution)/shard_map/reduce_scatter | solution.py:483
  1539.3 74.8 %reduce-scatter.15.cloned.1.call-done = bf16[256,2048]{1,0:T(8,128)(2,1)} async-done(((bf16[2048,2048]{1,0:T(8,128)(2,1)}), bf16[256,2048]{1,0:T(8,128)(2,1)}) %reduce-scatter.15.cloned.1.call-update) | async-done | bytes 1048592 | tf_op jit(solution)/shard_map/reduce_scatter | solution.py:480
  1614.1 149.9 %reduce-scatter.25.cloned.1.call-done = bf16[256,5632]{1,0:T(8,128)(2,1)} async-done(((bf16[2048,5632]{1,0:T(8,128)(2,1)}), bf16[256,5632]{1,0:T(8,128)(2,1)}) %reduce-scatter.25.cloned.1.call-update) | async-done | bytes 2883600 | tf_op jit(solution)/shard_map/reduce_scatter | solution.py:386
  1764.0 150.0 %reduce-scatter.27.cloned.1.call-done = bf16[256,5632]{1,0:T(8,128)(2,1)} async-done(((bf16[2048,5632]{1,0:T(8,128)(2,1)}), bf16[256,5632]{1,0:T(8,128)(2,1)}) %reduce-scatter.27.cloned.1.call-update) | async-done | bytes 2883600 | tf_op jit(solution)/shard_map/reduce_scatter | solution.py:389
  1914.0 149.9 %reduce-scatter.29.cloned.1.call-done = bf16[704,2048]{1,0:T(8,128)(2,1)} async-done(((bf16[5632,2048]{1,0:T(8,128)(2,1)}), bf16[704,2048]{1,0:T(8,128)(2,1)}) %reduce-scatter.29.cloned.1.call-update) | async-done | bytes 2883600 | tf_op jit(solution)/shard_map/reduce_scatter | solution.py:392
  2079.8 12.2 fusion.171
  2106.6 22.9 all-reduce.7
  2136.0 19.3 all-reduce.8
  2158.8 449.3 %all-reduce.12.cloned.1.call-done = (bf16[256,2048]{1,0:T(8,128)(2,1)}, bf16[256,2048]{1,0:T(8,128)(2,1)}, bf16[256,2048]{1,0:T(8,128)(2,1)}, bf16[256,2048]{1,0...) async-done(((bf16[256,2048]{1,0:T(8,128)(2,1)}, bf16[256,2048]{1,0:T(8,128)(2,1)}, ...) | async-done | bytes 13893648 | tf_op jit(solution)/shard_map/psum | solution.py:507
  (1078 shorter events, 940.2 us)
Async XLA Ops:
  7.2 12.9 copy-start.85
  7.2 14.2 copy-start.87
  7.2 28.5 %copy-start.82 = (bf16[16,32]{1,0:T(8,128)(2,1)S(1)}, bf16[16,32]{1,0:T(8,128)(2,1)}, u32[]{:S(2)}) copy-start(bf16[16,32]{1,0:T(8,128)(2,1)} %param.43) | copy-start | bytes 3076
  7.2 37.6 %copy-start.80 = (bf16[256,16]{0,1:T(8,128)(2,1)S(1)}, bf16[256,16]{0,1:T(8,128)(2,1)}, u32[]{:S(2)}) copy-start(bf16[256,16]{0,1:T(8,128)(2,1)} %param.42) | copy-start | bytes 24580
  7.2 46.6 %copy-start.1 = (bf16[256,2048]{1,0:T(8,128)(2,1)S(1)}, bf16[256,2048]{1,0:T(8,128)(2,1)}, u32[]{:S(2)}) copy-start(bf16[256,2048]{1,0:T(8,128)(2,1)} %param.36) | copy-start | bytes 3145732
  7.2 60.0 %all-gather.23.cloned.1.call-start = ((), (), s32[]{:S(2)}) async-start(), calls=%async_computation.10 | async-start | bytes 9437184 | tf_op jit(solution)/shard_map/all_gather | solution.py:253
  8.0 115.5 %all-gather.25.cloned.1.call-start = ((), (), s32[]{:S(2)}) async-start(), calls=%async_computation.11 | async-start | bytes 9437184 | tf_op jit(solution)/shard_map/all_gather | solution.py:252
  8.7 244.7 %all-gather.27.cloned.1.call-start = ((), (), s32[]{:S(2)}) async-start(), calls=%async_computation.12 | async-start | bytes 9437184 | tf_op jit(solution)/shard_map/all_gather | solution.py:251
  9.5 268.9 %all-gather.39.cloned.1.call-start = ((), (), s32[]{:S(2)}) async-start(), calls=%async_computation.27 | async-start | bytes 1310720 | tf_op jit(solution)/shard_map/all_gather | solution.py:21
  20.0 469.2 %copy-start.50 = (f32[8,1,256]{2,1,0:T(1,128)}, f32[8,1,256]{2,1,0:T(1,128)S(1)}, u32[]{:S(2)}) copy-start(f32[8,1,256]{2,1,0:T(1,128)S(1)} %convert_element_type.413) | copy-start | bytes 24580
  54.1 69.3 %copy-start.64 = (f32[256]{0:T(256)}, f32[256]{0:T(256)S(1)}, u32[]{:S(2)}) copy-start(f32[256]{0:T(256)S(1)} %add_rsqrt_fusion.2) | copy-start | bytes 3076
  54.9 18.1 copy-start.72
  178.7 99.7 %all-gather.41.cloned.1.call-start = ((), (), s32[]{:S(2)}) async-start(), calls=%async_computation.28 | async-start | bytes 1310720 | tf_op jit(solution)/shard_map/all_gather | solution.py:21
  180.5 308.7 %all-gather.29.cloned.1.call-start = ((), (), s32[]{:S(2)}) async-start(), calls=%async_computation.13 | async-start | bytes 9437184 | tf_op jit(solution)/shard_map/all_gather | solution.py:257
  181.1 317.9 %all-gather.31.cloned.1.call-start = ((), (), s32[]{:S(2)}) async-start(), calls=%async_computation.14 | async-start | bytes 9437184 | tf_op jit(solution)/shard_map/all_gather | solution.py:259
  181.8 325.0 %all-gather.33.cloned.1.call-start = ((), (), s32[]{:S(2)}) async-start(), calls=%async_computation.15 | async-start | bytes 25952256 | tf_op jit(solution)/shard_map/all_gather | solution.py:261
  182.6 403.4 %all-gather.35.cloned.1.call-start = ((), (), s32[]{:S(2)}) async-start(), calls=%async_computation.16 | async-start | bytes 25952256 | tf_op jit(solution)/shard_map/all_gather | solution.py:262
  183.3 520.7 %all-gather.37.cloned.1.call-start = ((), (), s32[]{:S(2)}) async-start(), calls=%async_computation.17 | async-start | bytes 25952256 | tf_op jit(solution)/shard_map/all_gather | solution.py:263
  183.9 1124.0 %all-gather.43.cloned.1.call-start = ((), (), s32[]{:S(2)}) async-start(), calls=%async_computation.29 | async-start | bytes 1310720 | tf_op jit(solution)/shard_map/all_gather | solution.py:46
  184.3 17.8 copy-start.89
  252.8 35.7 %copy-start.67 = (f32[4,4,64]{2,1,0:T(4,128)}, f32[4,4,64]{2,1,0:T(4,128)S(1)}, u32[]{:S(2)}) copy-start(f32[4,4,64]{2,1,0:T(4,128)S(1)} %exp.182) | copy-start | bytes 12292
  262.9 13.9 copy-start.19
  506.8 79.2 %copy-start.17 = (bf16[256,2048]{1,0:T(8,128)(2,1)}, bf16[256,2048]{1,0:T(8,128)(2,1)S(1)}, u32[]{:S(2)}) copy-start(bf16[256,2048]{1,0:T(8,128)(2,1)S(1)} %multiply_convert_fusion.5) | copy-start | bytes 3145732
  721.4 13.1 copy-start.44
  734.5 14.5 copy-start.26
  788.8 12.1 copy-start.15
  790.8 16.0 copy-start.11
  826.4 18.5 copy-start.9
  887.1 12.1 copy-start.15
  889.1 16.0 copy-start.11
  924.9 18.5 copy-start.9
  987.7 16.0 copy-start.11
  1023.3 18.5 copy-start.9
  1084.3 12.1 copy-start.15
  1086.3 16.0 copy-start.11
  1122.1 18.5 copy-start.9
  1183.4 124.5 %all-gather.45.cloned.1.call-start = ((), (), s32[]{:S(2)}) async-start(), calls=%async_computation.30 | async-start | bytes 1310720 | tf_op jit(solution)/shard_map/all_gather | solution.py:46
  1184.0 275.4 %reduce-scatter.23.cloned.1.call-start = ((), (), s32[]{:S(2)}) async-start(), calls=%async_computation.23 | async-start | bytes 9437184 | tf_op jit(solution)/shard_map/reduce_scatter | solution.py:501
  1191.4 268.1 %reduce-scatter.13.cloned.1.call-start = ((), (), s32[]{:S(2)}) async-start(), calls=%async_computation.18 | async-start | bytes 9437184 | tf_op jit(solution)/shard_map/reduce_scatter | solution.py:477
  1235.3 229.1 %reduce-scatter.21.cloned.1.call-start = ((), (), s32[]{:S(2)}) async-start(), calls=%async_computation.22 | async-start | bytes 9437184 | tf_op jit(solution)/shard_map/reduce_scatter | solution.py:495
  1307.9 231.4 %reduce-scatter.17.cloned.1.call-start = ((), (), s32[]{:S(2)}) async-start(), calls=%async_computation.20 | async-start | bytes 9437184 | tf_op jit(solution)/shard_map/reduce_scatter | solution.py:483
  1388.7 225.4 %reduce-scatter.15.cloned.1.call-start = ((), (), s32[]{:S(2)}) async-start(), calls=%async_computation.19 | async-start | bytes 9437184 | tf_op jit(solution)/shard_map/reduce_scatter | solution.py:480
  1401.0 362.9 %reduce-scatter.25.cloned.1.call-start = ((), (), s32[]{:S(2)}) async-start(), calls=%async_computation.24 | async-start | bytes 25952256 | tf_op jit(solution)/shard_map/reduce_scatter | solution.py:386
  1415.7 498.3 %reduce-scatter.27.cloned.1.call-start = ((), (), s32[]{:S(2)}) async-start(), calls=%async_computation.25 | async-start | bytes 25952256 | tf_op jit(solution)/shard_map/reduce_scatter | solution.py:389
  1428.8 635.1 %reduce-scatter.29.cloned.1.call-start = ((), (), s32[]{:S(2)}) async-start(), calls=%async_computation.26 | async-start | bytes 25952256 | tf_op jit(solution)/shard_map/reduce_scatter | solution.py:392
  1443.2 690.5 %reduce-scatter.31.cloned.1.call-start = ((), (), s32[]{:S(2)}) async-start(), calls=%async_computation.31 | async-start | bytes 73728
  1458.3 677.8 %reduce-scatter.19.cloned.1.call-start = ((), (), s32[]{:S(2)}) async-start(), calls=%async_computation.21 | async-start | bytes 73728 | tf_op jit(solution)/shard_map/reduce_scatter | solution.py:486
  1459.4 1148.7 %all-reduce.12.cloned.1.call-start = ((), (), s32[]{:S(2)}) async-start(), calls=%async_computation.32 | async-start | bytes 27787264 | tf_op jit(solution)/shard_map/psum | solution.py:507
  (145 other events, 624.9 us)
Sparse Core Ops, SparseCore 0:
  9.9 57.2 all-gather.22
  69.1 54.2 all-gather.24
  125.3 54.2 all-gather.26
  181.0 27.9 all-gather.38
  210.5 27.3 all-gather.40
  239.6 53.6 all-gather.28
  295.2 54.2 all-gather.30
  351.3 116.3 all-gather.32
  469.6 116.3 all-gather.34
  587.7 116.3 all-gather.36
  1183.6 27.9 all-gather.42
  1213.0 27.3 all-gather.44
  1243.8 70.8 reduce-scatter.22
  1318.1 71.4 reduce-scatter.12
  1392.9 71.4 reduce-scatter.20
  1467.7 71.4 reduce-scatter.16
  1542.6 71.4 reduce-scatter.14
  1617.6 146.3 reduce-scatter.24
  1767.6 146.3 reduce-scatter.26
  1917.5 146.3 reduce-scatter.28
  2067.4 33.5 reduce-scatter.30
  2104.6 31.3 reduce-scatter.18
  2139.5 468.5 all-reduce.11
where the time goes:
time: 2650 us; the launch traced here: 2630 us
  waiting for transfers between devices  1280 us (48%)
  matrix products  625 us (24%)
  other arithmetic  300 us (11%)
  local copies, waits for them, and re-layouts  284 us (11%)
  blocking collectives  113 us (4%)
    psum x1, waiting for transfers between devices, body(): lax.psum(shares[1].astype(jnp.bfloat16), 'seq').astype(jnp.float32)  449 us
    reduce_scatter x1, waiting for transfers between devices, body(): lax.psum_scatter(up_grad.astype(jnp.bfloat16), 'fsdp', scatter_dimension=...  150 us
    reduce_scatter x1, waiting for transfers between devices, body(): lax.psum_scatter(gate_grad.astype(jnp.bfloat16), 'fsdp', scatter_dimensio...  150 us
    reduce_scatter x1, waiting for transfers between devices, body(): lax.psum_scatter(down_grad.astype(jnp.bfloat16), 'fsdp', scatter_dimensio...  150 us
    dot_general x12, matrix products, attend_block(): jnp.einsum('tsh,tshj,shj->thj', qk_dots, decay_tab, inflow, precision=HIG...  134 us
    all_gather x1, waiting for transfers between devices, body(): lax.all_gather(mlp_down, 'fsdp', axis=0, tiled=True)  104 us
    dot_general x8, matrix products, attend_block(): jnp.einsum('thj,tshj,shj->tsh', probs_slot, decay_tab, inflow, precision=...  100 us
    dot_general x9, matrix products, right_dot(): lax.dot_general(left_mat, right_mat, (((1,), (1,)), ((), ())), preferred_...  83.1 us
  transfers between devices with their start and end apart: 23, of which 12 were waited for; matrix products, arithmetic and copies ran while one was open for 27% of the time, Pallas kernels for 0%

commit v1 on v0

v1 whole, which is shorter than its diff:
```python
import functools
import jax
import jax.numpy as jnp
from jax import lax
from jax.experimental import pallas as pl
from jax.experimental.pallas import tpu as pltpu
from jax.sharding import Mesh, PartitionSpec as P

HEAD = 512
SLOTS = 64
SCALE = HEAD ** (-0.5)
EPSILON = 1e-06
HIGHEST = lax.Precision.HIGHEST
BF = jnp.bfloat16
F32 = jnp.float32


def mm(a, b):
    return lax.dot_general(a, b, (((1,), (0,)), ((), ())), preferred_element_type=F32)


def mm_nt(a, b):
    return lax.dot_general(a, b, (((1,), (1,)), ((), ())), preferred_element_type=F32)


def mm_tn(a, b):
    return lax.dot_general(a, b, (((0,), (0,)), ((), ())), preferred_element_type=F32)


def exact(a, b):
    return lax.dot_general(
        a, b, (((1,), (0,)), ((), ())), precision=HIGHEST, preferred_element_type=F32
    )


def row_bit(rows, level):
    t = lax.broadcasted_iota(jnp.int32, (rows, SLOTS), 0)
    return ((t >> level) & 1) == 1


def prefix_levels(log_decay):
    rows = log_decay.shape[0]
    levels = rows.bit_length() - 1
    f, g = log_decay, jnp.zeros_like(log_decay)
    out = []
    for level in range(levels):
        out.append((f, g))
        total = f + g
        step = 1 << level
        bit = row_bit(rows, level)
        f = f + jnp.where(bit, pltpu.roll(total, step, 0), 0.0)
        g = g + jnp.where(bit, 0.0, pltpu.roll(total, rows - step, 0))
    return out, f, g


def same_block(rows, level):
    t = lax.broadcasted_iota(jnp.int32, (rows, rows), 0)
    s = lax.broadcasted_iota(jnp.int32, (rows, rows), 1)
    return (t >> (level + 1)) == (s >> (level + 1))


def level_mask(table, level, levels):
    if level == levels - 1:
        return table
    return jnp.where(same_block(table.shape[0], level), table, jnp.zeros_like(table))


def factors(pair, level, inflow):
    f, g = pair
    bit = row_bit(f.shape[0], level)
    left = jnp.where(bit, jnp.exp(f), 0.0)
    right = jnp.where(bit, 0.0, jnp.exp(g))
    return left, right, right * inflow


def diagonal(rows):
    t = lax.broadcasted_iota(jnp.int32, (rows, rows), 0)
    s = lax.broadcasted_iota(jnp.int32, (rows, rows), 1)
    return t == s


def slot_table(weights, pairs, inflow):
    rows = weights.shape[0]
    levels = len(pairs)
    table = jnp.where(diagonal(rows), jnp.sum(weights * inflow, axis=1, keepdims=True), 0.0)
    for level in range(levels):
        left, _, gain = factors(pairs[level], level, inflow)
        block = mm_nt((weights * left).astype(BF), gain.astype(BF))
        table = table + level_mask(block, level, levels)
    return table


def slot_sums(table, pairs, inflow):
    rows = table.shape[0]
    levels = len(pairs)
    own = jnp.sum(jnp.where(diagonal(rows), table, 0.0), axis=1, keepdims=True)
    low = table.astype(BF)
    total = own * inflow
    for level in range(levels):
        left, _, gain = factors(pairs[level], level, inflow)
        total = total + left * mm(level_mask(low, level, levels), gain.astype(BF))
    return total


def states_kernel(kv_ref, li_ref, state_ref, decay_ref):
    kv = kv_ref[0]
    log_decay = li_ref[0, :, :SLOTS]
    inflow = li_ref[0, :, SLOTS:]
    rows = kv.shape[0]
    t = lax.broadcasted_iota(jnp.int32, (rows, rows), 0)
    s = lax.broadcasted_iota(jnp.int32, (rows, rows), 1)
    after = exact((s > t).astype(F32), log_decay)
    weight = jnp.exp(after) * inflow
    state_ref[0] = mm_tn(weight.astype(BF), kv)
    total = lax.dot_general(
        log_decay, jnp.ones((rows, 128), F32), (((0,), (0,)), ((), ())),
        precision=HIGHEST, preferred_element_type=F32,
    )
    decay_ref[0] = jnp.exp(total)


def forward_kernel(qs_ref, kv_ref, li_ref, init_ref, gain_ref, gated_ref, out_ref, prob_ref, mix_ref):
    queries = qs_ref[0, :, :HEAD].astype(BF)
    swish = qs_ref[0, :, HEAD:]
    keys = kv_ref[0, :, :HEAD]
    values = kv_ref[0, :, HEAD:]
    log_decay = li_ref[0, :, :SLOTS]
    inflow = li_ref[0, :, SLOTS:]
    init = init_ref[0].astype(BF)
    pairs, running, _ = prefix_levels(log_decay)
    growth = jnp.exp(running)
    scores = mm_nt(queries, keys) * SCALE
    slots = slot_sums(scores, pairs, inflow) + mm_nt(queries, init[:, :HEAD]) * SCALE * growth
    top = jnp.max(slots, axis=1, keepdims=True)
    weights = jnp.exp(slots - top)
    probs = weights / jnp.sum(weights, axis=1, keepdims=True)
    mix = slot_table(probs, pairs, inflow).astype(BF)
    out = mm(mix, values) + mm((probs * growth).astype(BF), init[:, HEAD:])
    hat = out * lax.rsqrt(jnp.mean(out * out, axis=1, keepdims=True) + EPSILON)
    gated_ref[0] = (hat * gain_ref[0:1] * (swish * jax.nn.sigmoid(swish))).astype(BF)
    out_ref[0] = out
    prob_ref[0] = probs
    mix_ref[0] = mix


def backward_kernel(
    qs_ref, kv_ref, li_ref, init_ref, gain_ref, out_ref, prob_ref, mix_ref, gg_ref,
    dqs_ref, dkv_ref, ddi_ref, adj_ref, sg_ref,
):
    queries = qs_ref[0, :, :HEAD].astype(BF)
    swish = qs_ref[0, :, HEAD:]
    keys = kv_ref[0, :, :HEAD]
    values = kv_ref[0, :, HEAD:]
    log_decay = li_ref[0, :, :SLOTS]
    inflow = li_ref[0, :, SLOTS:]
    init = init_ref[0].astype(BF)
    out = out_ref[0]
    probs = prob_ref[0]
    gain = gain_ref[0:1]
    rows = out.shape[0]
    scale_out = lax.rsqrt(jnp.mean(out * out, axis=1, keepdims=True) + EPSILON)
    hat = out * scale_out
    sig = jax.nn.sigmoid(swish)
    silu = swish * sig
    gg = gg_ref[0].astype(F32)
    gg_hat = gg * hat
    dqs_ref[0, :, HEAD:] = (gg_hat * gain * (sig * (1.0 + swish * (1.0 - sig)))).astype(BF)
    part = jnp.broadcast_to(jnp.sum(gg_hat * silu, axis=0, keepdims=True), (8, HEAD))

    @pl.when(pl.program_id(0) == 0)
    def _():
        sg_ref[...] = part

    @pl.when(pl.program_id(0) > 0)
    def _():
        sg_ref[...] = sg_ref[...] + part

    grad_hat = gg * gain * silu
    dout = scale_out * (grad_hat - hat * jnp.mean(grad_hat * hat, axis=1, keepdims=True))
    dout = dout.astype(BF)
    pairs, running, _ = prefix_levels(log_decay)
    levels = len(pairs)
    growth = jnp.exp(running)
    scores = mm_nt(queries, keys) * SCALE
    grads = mm_nt(dout, values)
    key_part = mm_nt(queries, init[:, :HEAD]) * SCALE * growth
    value_part = mm_nt(dout, init[:, HEAD:]) * growth
    dprob = slot_sums(grads, pairs, inflow) + value_part
    dslot = probs * (dprob - jnp.sum(probs * dprob, axis=1, keepdims=True))
    back = slot_table(dslot, pairs, inflow).astype(BF)
    dslot_g = (dslot * growth).astype(BF)
    prob_g = (probs * growth).astype(BF)
    dqs_ref[0, :, :HEAD] = (SCALE * (mm(back, keys) + mm(dslot_g, init[:, :HEAD]))).astype(BF)
    dkv_ref[0, :, :HEAD] = SCALE * mm_tn(back, queries)
    dkv_ref[0, :, HEAD:] = mm_tn(mix_ref[0], dout)
    adj_ref[0, :, :HEAD] = SCALE * mm_tn(dslot_g, queries)
    adj_ref[0, :, HEAD:] = mm_tn(prob_g, dout)
    diag = diagonal(rows)
    own_a = jnp.sum(jnp.where(diag, scores, 0.0), axis=1, keepdims=True)
    own_b = jnp.sum(jnp.where(diag, grads, 0.0), axis=1, keepdims=True)
    dinflow = dslot * own_a + probs * own_b
    scores_low = scores.astype(BF)
    grads_low = grads.astype(BF)
    fbar = dslot * key_part + probs * value_part
    gbar = jnp.zeros_like(fbar)
    for level in range(levels - 1, -1, -1):
        left, right, amount = factors(pairs[level], level, inflow)
        table_a = level_mask(scores_low, level, levels)
        table_b = level_mask(grads_low, level, levels)
        amount_low = amount.astype(BF)
        dleft = dslot * left
        pleft = probs * left
        grow = dleft * mm(table_a, amount_low) + pleft * mm(table_b, amount_low)
        back_in = mm_tn(table_a, dleft.astype(BF)) + mm_tn(table_b, pleft.astype(BF))
        dinflow = dinflow + right * back_in
        step = 1 << level
        bit = row_bit(rows, level)
        total = pltpu.roll(jnp.where(bit, fbar, 0.0), rows - step, 0) + pltpu.roll(
            jnp.where(bit, 0.0, gbar), step, 0
        )
        fbar = fbar + grow + total
        gbar = gbar + amount * back_in + total
    ddi_ref[0, :, :SLOTS] = fbar
    ddi_ref[0, :, SLOTS:] = dinflow


def finish_kernel(kv_ref, li_ref, init_ref, end_ref, dkv_ref, ddi_ref, okv_ref, oddi_ref):
    kv = kv_ref[0]
    log_decay = li_ref[0, :, :SLOTS]
    inflow = li_ref[0, :, SLOTS:]
    end = end_ref[0]
    rows = kv.shape[0]
    t = lax.broadcasted_iota(jnp.int32, (rows, rows), 0)
    s = lax.broadcasted_iota(jnp.int32, (rows, rows), 1)
    earlier = (s < t).astype(F32)
    after = exact((s > t).astype(F32), log_decay)
    fade = jnp.exp(after)
    weight = fade * inflow
    end_low = end.astype(BF)
    okv_ref[0] = (dkv_ref[0] + mm(weight.astype(BF), end_low)).astype(BF)
    reach = mm_nt(kv, end_low)
    whole = jnp.exp(jnp.sum(log_decay, axis=0, keepdims=True))
    carry = lax.dot_general(
        jnp.ones((8, 2 * HEAD), F32), end * init_ref[0], (((1,), (1,)), ((), ())),
        precision=HIGHEST, preferred_element_type=F32,
    )[0:1]
    oddi_ref[0, :, :SLOTS] = (
        ddi_ref[0, :, :SLOTS] + exact(earlier, weight * reach) + whole * carry
    )
    oddi_ref[0, :, SLOTS:] = ddi_ref[0, :, SLOTS:] + fade * reach


def blocked(shape):
    return pl.BlockSpec((1,) + shape, lambda i: (i, 0, 0))


def run(kernel, args, specs, outs, out_specs, flops, moved):
    return pl.pallas_call(
        kernel,
        grid=(args[0].shape[0],),
        in_specs=specs,
        out_specs=out_specs,
        out_shape=outs,
        cost_estimate=pl.CostEstimate(flops=flops, bytes_accessed=moved, transcendentals=0),
        compiler_params=pltpu.CompilerParams(vmem_limit_bytes=56 << 20),
    )(*args)


def sds(shape, dtype=F32):
    return jax.ShapeDtypeStruct(shape, dtype)


def chunk_states(kv, li):
    n, rows, _ = kv.shape
    return run(
        states_kernel, (kv, li),
        [blocked((rows, 2 * HEAD)), blocked((rows, 2 * SLOTS))],
        (sds((n, SLOTS, 2 * HEAD)), sds((n, SLOTS, 128))),
        (blocked((SLOTS, 2 * HEAD)), blocked((SLOTS, 128))),
        n * 10**9, n * 10**6,
    )


def mixer_forward(qs, kv, li, init, gain):
    n, rows, _ = kv.shape
    return run(
        forward_kernel, (qs, kv, li, init, gain),
        [blocked((rows, 2 * HEAD)), blocked((rows, 2 * HEAD)), blocked((rows, 2 * SLOTS)),
         blocked((SLOTS, 2 * HEAD)), pl.BlockSpec((8, HEAD), lambda i: (0, 0))],
        (sds((n, rows, HEAD), BF), sds((n, rows, HEAD)), sds((n, rows, SLOTS)), sds((n, rows, rows), BF)),
        (blocked((rows, HEAD)), blocked((rows, HEAD)), blocked((rows, SLOTS)), blocked((rows, rows))),
        n * 3 * 10**9, n * 4 * 10**6,
    )


def mixer_backward(qs, kv, li, init, gain, out, probs, mix, gg):
    n, rows, _ = kv.shape
    return run(
        backward_kernel, (qs, kv, li, init, gain, out, probs, mix, gg),
        [blocked((rows, 2 * HEAD)), blocked((rows, 2 * HEAD)), blocked((rows, 2 * SLOTS)),
         blocked((SLOTS, 2 * HEAD)), pl.BlockSpec((8, HEAD), lambda i: (0, 0)),
         blocked((rows, HEAD)), blocked((rows, SLOTS)), blocked((rows, rows)), blocked((rows, HEAD))],
        (sds((n, rows, 2 * HEAD), BF), sds((n, rows, 2 * HEAD)), sds((n, rows, 2 * SLOTS)),
         sds((n, SLOTS, 2 * HEAD)), sds((8, HEAD))),
        (blocked((rows, 2 * HEAD)), blocked((rows, 2 * HEAD)), blocked((rows, 2 * SLOTS)),
         blocked((SLOTS, 2 * HEAD)), pl.BlockSpec((8, HEAD), lambda i: (0, 0))),
        n * 6 * 10**9, n * 5 * 10**6,
    )


def mixer_finish(kv, li, init, end, dkv, ddi):
    n, rows, _ = kv.shape
    return run(
        finish_kernel, (kv, li, init, end, dkv, ddi),
        [blocked((rows, 2 * HEAD)), blocked((rows, 2 * SLOTS)), blocked((SLOTS, 2 * HEAD)),
         blocked((SLOTS, 2 * HEAD)), blocked((rows, 2 * HEAD)), blocked((rows, 2 * SLOTS))],
        (sds((n, rows, 2 * HEAD), BF), sds((n, rows, 2 * SLOTS))),
        (blocked((rows, 2 * HEAD)), blocked((rows, 2 * SLOTS))),
        n * 10**9, n * 3 * 10**6,
    )


D = 2048
HEADS = 4
RANK = 16
NORMALIZER = 8.0


def inverse_rms(values):
    return lax.rsqrt(jnp.mean(values * values, axis=-1, keepdims=True) + EPSILON)


def silu_slope(values):
    sigmoid_val = jax.nn.sigmoid(values)
    return sigmoid_val * (1.0 + values * (1.0 - sigmoid_val))


def norm_back(grad_hat, hat_rows, scale_rows):
    return scale_rows * (
        grad_hat - hat_rows * jnp.mean(grad_hat * hat_rows, axis=-1, keepdims=True)
    )


def swap(value, axis, step):
    count = lax.axis_size(axis)
    return lax.ppermute(value, axis, [(i, i ^ step) for i in range(count)])


def gather_heads(block):
    return [block] + [swap(block, "p", k) for k in range(1, HEADS)]


def scatter_heads(parts):
    total = parts[0].astype(F32)
    for k in range(1, HEADS):
        total = total + swap(parts[k], "p", k).astype(F32)
    return total


def after(value, *others):
    return lax.optimization_barrier((value,) + others)[0]


def head_columns(shards, here):
    width = [shard.shape[1] // HEADS for shard in shards]
    rows = shards[0].shape[0]
    copies = lax.axis_size("r")
    turn = lax.axis_index("r")
    pieces = []
    for k in range(HEADS):
        cut = jnp.concatenate(
            [
                lax.dynamic_slice_in_dim(shard, (here ^ k) * w, w, 1)
                for shard, w in zip(shards, width)
            ],
            axis=1,
        )
        pieces.append(cut if k == 0 else swap(cut, "p", k))
    whole = jnp.zeros((HEADS * copies * rows, sum(width)), BF)
    for k in range(HEADS):
        for m in range(copies):
            piece = pieces[k] if m == 0 else swap(pieces[k], "r", m)
            start = ((here ^ k) * copies + (turn ^ m)) * rows
            whole = lax.dynamic_update_slice_in_dim(whole, piece, start, 0)
    return whole, pieces


def chain(state, decay, forward):
    count = lax.axis_size("seq")
    total = jnp.zeros_like(state)
    for hop in range(count - 1):
        pair = (hop, hop + 1) if forward else (count - 1 - hop, count - 2 - hop)
        sent = (decay * total + state).astype(BF)
        total = total + lax.ppermute(sent, "seq", [pair]).astype(F32)
    return total


def chain_pair(both, decay, forward):
    return jnp.concatenate(
        [chain(both[..., :HEAD], decay, forward), chain(both[..., HEAD:], decay, forward)], axis=-1
    )


def split_rows(left, here, step):
    return lax.dynamic_index_in_dim(left, here ^ step, 2, False).reshape(left.shape[0], -1)


def reduce_copies(parts):
    total = parts[0]
    for m in range(1, len(parts)):
        total = total + swap(parts[m].astype(BF), "r", m).astype(F32)
    return total


def reduce_seq(value):
    count = lax.axis_size("seq")
    place = lax.axis_index("seq")
    step = 1
    while step < count:
        half = value.shape[1] // 2
        bit = (place // step) % 2
        away = lax.dynamic_slice_in_dim(value, (1 - bit) * half, half, 1)
        kept = lax.dynamic_slice_in_dim(value, bit * half, half, 1)
        value = kept.astype(F32) + swap(away.astype(BF), "seq", step).astype(F32)
        step *= 2
    return value.astype(BF)


def gather_seq(value):
    count = lax.axis_size("seq")
    found = {0: value}
    step = count // 2
    while step >= 1:
        for j in list(found):
            found[j ^ step] = swap(found[j], "seq", step)
        step //= 2
    return [found[j] for j in range(count)]


def row_starts(rows):
    count = lax.axis_size("seq")
    place = lax.axis_index("seq")
    starts = []
    for j in range(count):
        other = place ^ j
        start, half, step = 0, rows // 2, 1
        while step < count:
            start = start + ((other // step) % 2) * half
            half //= 2
            step *= 2
        starts.append(start)
    return starts


def assemble_kernel(counts, spot_ref, *refs):
    n_in, n_out, part = counts
    ins, outs = refs[:n_in], refs[n_in:]
    width = outs[0].shape[1]
    for j in range(n_in):
        start = pl.multiple_of(spot_ref[j] * part, part)
        for o in range(n_out):
            outs[o][pl.ds(start, part), :] = ins[j][0, :, o * width : (o + 1) * width].astype(F32)


def assemble(parts, columns, n_out, starts):
    blocks, part, width = parts[0].shape
    width //= n_out
    rows = part * len(parts)
    if part % 16:
        outs = []
        for o in range(n_out):
            whole = jnp.zeros((rows, blocks * width), F32)
            for j, value in enumerate(parts):
                for i in range(blocks):
                    cut = value[i, :, o * width : (o + 1) * width].astype(F32)
                    whole = lax.dynamic_update_slice(whole, cut, (starts[j], columns[i] * width))
            outs.append(whole)
        return outs
    spots = jnp.stack(
        [jnp.asarray(s // part, jnp.int32) for s in starts]
        + [jnp.asarray(c, jnp.int32) for c in columns]
    )
    n_in = len(parts)
    return pl.pallas_call(
        functools.partial(assemble_kernel, (n_in, n_out, part)),
        grid_spec=pltpu.PrefetchScalarGridSpec(
            num_scalar_prefetch=1,
            grid=(blocks,),
            in_specs=[pl.BlockSpec((1, part, n_out * width), lambda i, s: (i, 0, 0))] * n_in,
            out_specs=[pl.BlockSpec((rows, width), lambda i, s: (0, s[n_in + i]))] * n_out,
        ),
        out_shape=[jax.ShapeDtypeStruct((rows, blocks * width), F32)] * n_out,
        cost_estimate=pl.CostEstimate(
            flops=0, bytes_accessed=6 * n_out * rows * blocks * width, transcendentals=0
        ),
        compiler_params=pltpu.CompilerParams(vmem_limit_bytes=56 << 20),
    )(spots, *parts)


def finish_columns(total, here, n_out):
    rows = total.shape[1]
    part = reduce_seq(total)
    mine = [lax.dynamic_index_in_dim(part, here ^ k, 0, False) for k in range(HEADS)]
    got = jnp.stack([mine[0]] + [swap(mine[k], "p", k) for k in range(1, HEADS)])
    return assemble(gather_seq(got), [here ^ k for k in range(HEADS)], n_out, row_starts(rows))


def finish_rows(total):
    rows = total.shape[0]
    parts = [value for value in gather_seq(reduce_seq(total[None]))]
    return assemble(parts, [0], 1, row_starts(rows))[0]


def body(
    tokens,
    seq_lengths,
    attn_gain,
    query_proj,
    key_proj,
    value_proj,
    decay_down,
    decay_up,
    decay_bias,
    swish_proj,
    slot_gain,
    out_proj,
    mlp_gain,
    mlp_gate,
    mlp_up,
    mlp_down,
    grad_out,
):
    rows = tokens.shape[0]
    copies = lax.axis_size("r")
    owners = HEADS * copies
    shard = D // owners
    here, turn, place = lax.axis_index("p"), lax.axis_index("r"), lax.axis_index("seq")
    group = HEADS * rows

    small = [attn_gain, decay_down, decay_up, decay_bias, slot_gain, mlp_gain, seq_lengths]
    packed = jnp.concatenate([a.astype(F32).reshape(-1) for a in small])
    packed = lax.all_gather(packed, ("p", "r"), axis=0)
    fields, offset = [], 0
    for a in small:
        fields.append(packed[:, offset : offset + a.size])
        offset += a.size
    gain_one = fields[0].reshape(D)
    down_full = fields[1].reshape(D, RANK).astype(BF)
    up_full = fields[2].reshape(owners, RANK, -1).transpose(1, 0, 2).reshape(RANK, HEADS * SLOTS)
    up_head = lax.dynamic_slice_in_dim(up_full, here * SLOTS, SLOTS, 1)
    bias_head = lax.dynamic_slice_in_dim(fields[3].reshape(HEADS * SLOTS), here * SLOTS, SLOTS, 0)
    gain_head = lax.dynamic_slice_in_dim(fields[4].reshape(D), here * HEAD, HEAD, 0)
    gain_head8 = jnp.broadcast_to(gain_head[None], (8, HEAD))
    gain_two = fields[5].reshape(D)
    lengths = fields[6].reshape(HEADS, copies)
    positions = (place * rows + jnp.arange(rows, dtype=jnp.int32)).astype(F32)
    masks = [
        (positions < lax.dynamic_index_in_dim(lengths, here ^ k, 0, False)[turn]).astype(F32)
        for k in range(HEADS)
    ]
    mask_all = jnp.concatenate(masks)[:, None]
    mask_own = masks[0][:, None]

    token_blocks = gather_heads(tokens)
    weight_kv, kv_pieces = head_columns([key_proj, value_proj], here)
    query_late = after(query_proj, *kv_pieces[1:])
    weight_qs, qs_pieces = head_columns([query_late, swish_proj], here)
    gate_late = after(mlp_gate, *qs_pieces[1:])
    weight_gu, _ = head_columns([gate_late, mlp_up], here)
    weight_out = lax.all_gather(out_proj, "r", axis=0, tiled=True)
    weight_down = lax.all_gather(mlp_down, "r", axis=0, tiled=True)

    tokens_all = jnp.concatenate(token_blocks).astype(F32)
    normed = (tokens_all * inverse_rms(tokens_all) * gain_one).astype(BF)
    kv = mm(normed, weight_kv).astype(BF).reshape(HEADS, rows, 2 * HEAD)
    gate_low = mm(normed, down_full)
    forget = exact(gate_low, up_head) + bias_head
    log_sig = jax.nn.log_sigmoid(forget) / NORMALIZER
    li = jnp.concatenate([mask_all * log_sig, mask_all * -jnp.expm1(log_sig)], axis=1)
    li = li.reshape(HEADS, rows, 2 * SLOTS)
    state, decay = chunk_states(kv, li)
    decay = decay[:, :, :1]
    init = chain_pair(state, decay, True)
    qs = mm(normed, weight_qs).reshape(HEADS, rows, 2 * HEAD)
    gated, mixer_out, probs, mix = mixer_forward(qs, kv, li, init, gain_head8)
    gated = gated.reshape(group, HEAD)
    attn_part = mm(gated, weight_out).astype(BF).reshape(HEADS, rows, D)
    attn_out = scatter_heads([attn_part[k] for k in range(HEADS)])

    tokens_f = tokens.astype(F32)
    residual = tokens_f + mask_own * attn_out
    scale_two = inverse_rms(residual)
    hat_two = residual * scale_two
    normed_two_own = (hat_two * gain_two).astype(BF)
    two_blocks = gather_heads(normed_two_own)
    normed_two = jnp.concatenate(two_blocks)
    grad_blocks = gather_heads(after(grad_out, *two_blocks[1:]))
    grad_mlp = (mask_all * jnp.concatenate(grad_blocks).astype(F32)).astype(BF)

    hidden_width = weight_down.shape[0]
    gate_up = mm(normed_two, weight_gu)
    gate_pre, up_pre = gate_up[:, :hidden_width], gate_up[:, hidden_width:]
    hidden = (jax.nn.silu(gate_pre) * up_pre).astype(BF)
    mlp_part = mm(hidden, weight_down).astype(BF).reshape(HEADS, rows, D)

    grad_act = mm_nt(grad_mlp, weight_down)
    grad_gate = (grad_act * up_pre * silu_slope(gate_pre)).astype(BF)
    grad_up = (grad_act * jax.nn.silu(gate_pre)).astype(BF)
    grad_gu = jnp.concatenate([grad_gate, grad_up], axis=1)
    two_part = mm_nt(grad_gu, weight_gu).astype(BF).reshape(HEADS, rows, D)
    grad_norm_two = scatter_heads([two_part[k] for k in range(HEADS)])
    gain_two_grad = jnp.sum(grad_norm_two * hat_two, axis=0)
    grad_rows = grad_out.astype(F32)
    grad_resid = grad_rows + norm_back(grad_norm_two * gain_two, hat_two, scale_two)
    grad_attn_own = (mask_own * grad_resid).astype(BF)
    attn_blocks = gather_heads(grad_attn_own)
    grad_attn = jnp.concatenate(attn_blocks)

    mlp_out = scatter_heads([mlp_part[k] for k in range(HEADS)])
    result = (residual + mask_own * mlp_out).astype(BF)

    two_view = normed_two.reshape(group, HEADS, copies, shard)
    gu_parts = [mm_tn(split_rows(two_view, turn, m), grad_gu) for m in range(copies)]
    gu_total = reduce_copies(gu_parts).reshape(HEADS, shard, 2 * hidden_width)
    down_part = mm_tn(hidden, grad_mlp)
    down_rows = mlp_down.shape[0]
    down_total = reduce_copies(
        [
            lax.dynamic_slice_in_dim(down_part, (turn ^ m) * down_rows, down_rows, 0)
            for m in range(copies)
        ]
    )
    gate_grad, up_grad = finish_columns(gu_total, here, 2)
    down_grad = finish_rows(down_total)

    grad_gated = mm_nt(grad_attn, weight_out).reshape(HEADS, rows, HEAD)
    grad_qs, grad_kv, grad_li, adjoint, slot_part = mixer_backward(
        qs, kv, li, init, gain_head8, mixer_out, probs, mix, grad_gated
    )
    ends = chain_pair(adjoint, decay, False)
    grad_kv, grad_li = mixer_finish(kv, li, init, ends, grad_kv, grad_li)
    grad_qs = grad_qs.reshape(group, 2 * HEAD)
    grad_kv = grad_kv.reshape(group, 2 * HEAD)
    grad_li = grad_li.reshape(group, 2 * SLOTS)
    grad_decay = (
        mask_all
        * (grad_li[:, :SLOTS] - grad_li[:, SLOTS:] * jnp.exp(log_sig))
        / NORMALIZER
        * jax.nn.sigmoid(-forget)
    )
    bias_part = jnp.sum(grad_decay, axis=0)
    up_part = lax.dot_general(
        gate_low, grad_decay, (((0,), (0,)), ((), ())), precision=HIGHEST, preferred_element_type=F32
    )
    grad_low = lax.dot_general(
        grad_decay, up_head, (((1,), (1,)), ((), ())), precision=HIGHEST, preferred_element_type=F32
    ).astype(BF)
    down_low_part = mm_tn(normed, grad_low)

    one_part = (
        (mm_nt(grad_qs, weight_qs) + mm_nt(grad_kv, weight_kv) + mm_nt(grad_low, down_full))
        .astype(BF)
        .reshape(HEADS, rows, D)
    )
    grad_norm_one = scatter_heads([one_part[k] for k in range(HEADS)])
    scale_one = inverse_rms(tokens_f)
    hat_one = tokens_f * scale_one
    gain_one_grad = jnp.sum(grad_norm_one * hat_one, axis=0)
    grad_tokens = (grad_resid + norm_back(grad_norm_one * gain_one, hat_one, scale_one)).astype(BF)

    one_view = normed.reshape(group, HEADS, copies, shard)
    one_views = [split_rows(one_view, turn, m) for m in range(copies)]
    qs_total = reduce_copies([mm_tn(v, grad_qs) for v in one_views])
    kv_total = reduce_copies([mm_tn(v, grad_kv) for v in one_views])
    out_view = gated.reshape(group, 1, copies, shard)
    out_total = reduce_copies([mm_tn(split_rows(out_view, turn, m), grad_attn) for m in range(copies)])
    query_grad, swish_grad = finish_columns(qs_total.reshape(HEADS, shard, 2 * HEAD), here, 2)
    key_grad, value_grad = finish_columns(kv_total.reshape(HEADS, shard, 2 * HEAD), here, 2)
    out_grad = finish_rows(out_total)

    def placed(part, width):
        whole = jnp.zeros(part.shape[:-1] + (HEADS * width,), F32)
        return lax.dynamic_update_slice_in_dim(whole, part, here * width, part.ndim - 1)

    sums = [
        gain_one_grad,
        down_low_part,
        placed(up_part, SLOTS),
        placed(bias_part, SLOTS),
        placed(slot_part[0], HEAD),
        gain_two_grad,
    ]
    flat = jnp.concatenate([a.reshape(-1) for a in sums]).astype(BF)
    flat = lax.psum(flat, ("p", "r", "seq")).astype(F32)
    totals, offset = [], 0
    for a in sums:
        totals.append(flat[offset : offset + a.size].reshape(a.shape))
        offset += a.size
    owner = here * copies + turn

    def own(whole, axis):
        size = whole.shape[axis] // owners
        return lax.dynamic_slice_in_dim(whole, owner * size, size, axis)

    return (
        result,
        grad_tokens,
        own(totals[0], 0),
        query_grad,
        key_grad,
        value_grad,
        own(totals[1], 0),
        own(totals[2], 1),
        own(totals[3], 0),
        swish_grad,
        own(totals[4], 0),
        out_grad,
        own(totals[5], 0),
        gate_grad,
        up_grad,
        down_grad,
    )


def solution(mesh):
    count, span = mesh.devices.shape
    split = Mesh(mesh.devices.reshape(HEADS, count // HEADS, span), ("p", "r", "seq"))
    rows = P(("p", "r", "seq"), None)
    matrix, vector, last = P(("p", "r"), None), P(("p", "r")), P(None, ("p", "r"))
    in_specs = (
        rows, vector, vector, matrix, matrix, matrix, matrix, last, vector, matrix, vector, matrix,
        vector, matrix, matrix, matrix, rows,
    )
    out_specs = (
        rows, rows, vector, matrix, matrix, matrix, matrix, last, vector, matrix, vector, matrix,
        vector, matrix, matrix, matrix,
    )
    return jax.shard_map(body, mesh=split, in_specs=in_specs, out_specs=out_specs, check_vma=False)
```

time: 2650 us -> 1300 us (0.49)
  waiting for transfers between devices: 1280 us -> 709 us
  matrix products: 625 us -> 160 us
  other arithmetic: 300 us -> 69.2 us
  local copies, waits for them, and re-layouts: 284 us -> 161 us
  blocking collectives: 113 us -> 0 us
  starting transfers between devices: 1.73 us -> 90.1 us
  Pallas kernels: 0 us -> 76.2 us
    reduce_scatter x9 -> x0, waiting for transfers between devices: 606 us -> none  [the longest x1 150 us: body(): lax.psum_scatter(up_grad.astype(jnp.bfloat16), 'fsdp', scatter_dimension=...]
    ppermute x0 -> x96, waiting for transfers between devices: none -> 551 us  [the longest x84 538 us: swap(): return lax.ppermute(value, axis, [(i, i ^ step) for i in range(count)])]
    dot_general x149 -> x25, matrix products: 625 us -> 160 us  [the longest x6 62.7 us: mm_nt(): lax.dot_general(a, b, (((1,), (1,)), ((), ())), preferred_element_type=F32)]
    psum x1, waiting for transfers between devices: 449 us -> 101 us  [body(): flat = lax.psum(flat, ('p', 'r', 'seq')).astype(F32)]
    all_gather x12 -> x2, waiting for transfers between devices: 223 us -> 0.02 us  [the longest x1 0.02 us: body(): weight_out = lax.all_gather(out_proj, 'r', axis=0, tiled=True)]
    ppermute x0 -> x96, starting transfers between devices: none -> 89.9 us  [the longest x84 77 us: swap(): return lax.ppermute(value, axis, [(i, i ^ step) for i in range(count)])]
    squeeze x84 -> x0, local copies, waits for them, and re-layouts: 83 us -> none  [the longest x48 50.6 us: group_states(): lax.scan(jax.checkpoint(advance_states), start_carry, (to_blocks(key_rows...]
    pallas_call x0 -> x9, Pallas kernels: none -> 76.2 us  [the longest x4 49.9 us: run(): pl.pallas_call(kernel, grid=(args[0].shape[0],), in_specs=specs, out_spec...]
  transfers between devices with their start and end apart: 23 -> 100, of which waited for: 12 -> 32; matrix products, arithmetic and copies ran while one was open for 27% -> 26% of each run, Pallas kernels for 0% -> 5%
where the time goes in v1:
time: 1300 us; the launch traced here: 1280 us
  waiting for transfers between devices  709 us (55%)
  local copies, waits for them, and re-layouts  161 us (12%)
  matrix products  160 us (12%)
  starting transfers between devices  90.1 us (7%)
  Pallas kernels  76.2 us (6%)
  other arithmetic  69.2 us (5%)
  between operations  19.5 us (2%)
    ppermute x84, waiting for transfers between devices, swap(): return lax.ppermute(value, axis, [(i, i ^ step) for i in range(count)])  538 us
    psum x1, waiting for transfers between devices, body(): flat = lax.psum(flat, ('p', 'r', 'seq')).astype(F32)  101 us
    ppermute x84, starting transfers between devices, swap(): return lax.ppermute(value, axis, [(i, i ^ step) for i in range(count)])  77 us
    dot_general x6, matrix products, mm_nt(): lax.dot_general(a, b, (((1,), (1,)), ((), ())), preferred_element_type=F32)  62.7 us
    unnamed x5, waiting for transfers between devices  57.6 us
    pallas_call x4, Pallas kernels, run(): pl.pallas_call(kernel, grid=(args[0].shape[0],), in_specs=specs, out_spec...  49.9 us
    dot_general x10, matrix products, mm_tn(): lax.dot_general(a, b, (((0,), (0,)), ((), ())), preferred_element_type=F32)  49.6 us
    dot_general x6, matrix products, mm(): lax.dot_general(a, b, (((1,), (0,)), ((), ())), preferred_element_type=F32)  45.6 us
  transfers between devices with their start and end apart: 100, of which 32 were waited for; matrix products, arithmetic and copies ran while one was open for 26% of the time, Pallas kernels for 5%

profile of v1, /device:TPU:0, one launch (start us, length us, event | category | flops | bytes accessed | tf_op | source)
XLA Modules:
  0.0 1284.8 jit_solution(17115448450254018473)
XLA Ops:
  43.3 57.0 %all-reduce.6.cloned.1.call-done = f32[43272]{0:T(1024)} async-done(((f32[43272]{0:T(1024)}), f32[43272]{0:T(1024)}) %all-reduce.6.cloned.1.call-update) | async-done | bytes 173104
  134.7 7.3 collective-permute-done
  149.6 8.7 convolution_convert_fusion.8
  203.2 6.1 fusion.42
  212.6 15.0 %shard_map.289 = (bf16[4,256,512]{2,1,0:T(8,128)(2,1)}, f32[4,256,512]{2,1,0:T(8,128)}, f32[4,256,64]{2,1,0:T(8,128)}, bf16[4,256,256]{2,1,0:T(8,128)(2,1)}) custom-call(f32[4,256,1024]{2,1,0:T(8,128)} %bitcast.175, bf16[4,256,1024]{2,1,0:T(8,128)(2,1)} %bitcast.178, f32[4,256,128]{2,1,0:T(8,128)} %bitcast.152, f32[4,64,1024]{2,1,0:T(8,128)} %pad_maximum_fusion.14.init_ref, ...), custom_call_target="tpu_custom_call" | custom-call | flops 12000000000 | bytes 16000000 | tf_op jit(solution)/shard_map/pallas_call | solution.py:258
  248.4 37.1 %collective-permute-done.32 = bf16[256,2816]{1,0:T(8,128)(2,1)} collective-permute-done((bf16[256,2816]{1,0:T(8,128)(2,1)}, bf16[256,2816]{1,0:T(8,128)(2,1)}, u32[]{:S(2)}, u32[]{:S(2)}) %collective-permute-start.32) | collective-permute-done | bytes 1441824 | tf_op jit(solution)/shard_map/ppermute | solution.py:346
  288.7 19.7 %collective-permute-done.24 = bf16[256,2048]{1,0:T(8,128)(2,1)} collective-permute-done((bf16[256,2048]{1,0:T(8,128)(2,1)}, bf16[256,2048]{1,0:T(8,128)(2,1)}, u32[]{:S(2)}, u32[]{:S(2)}) %collective-permute-start.24) | collective-permute-done | bytes 1048608 | tf_op jit(solution)/shard_map/ppermute | solution.py:346
  324.9 14.0 %collective-permute-done.28 = bf16[256,2048]{1,0:T(8,128)(2,1)S(1)} collective-permute-done((bf16[256,2048]{1,0:T(8,128)(2,1)S(1)}, bf16[256,2048]{1,0:T(8,128)(2,1)S(1)}, u32[]{:S(2)}, u32[]{:S(2)}) %collective-permute-start.28) | collective-permute-done | bytes 1048608 | tf_op jit(solution)/shard_map/ppermute | solution.py:346
  338.9 21.4 %collective-permute-done.27 = bf16[256,2048]{1,0:T(8,128)(2,1)S(1)} collective-permute-done((bf16[256,2048]{1,0:T(8,128)(2,1)S(1)}, bf16[256,2048]{1,0:T(8,128)(2,1)S(1)}, u32[]{:S(2)}, u32[]{:S(2)}) %collective-permute-start.27) | collective-permute-done | bytes 1048608 | tf_op jit(solution)/shard_map/ppermute | solution.py:346
  363.8 17.4 %fusion.32 = f32[1024,2816]{1,0:T(8,128)} fusion(bf16[2048,2816]{1,0:T(8,128)(2,1)} %constant_dynamic-update-slice_fusion, bf16[256,2048]{1,0:T(8,128)(2,1)S(1)} %collective-permute-done.28, bf16[256,2048]{1,0:T(8,128)(2,1)S(1)} %collective-permute-done.27, bf16[256,2048]{1,0:T(8,128)(2,1)S(1)} %collective-permute-done.26, ...), kind=kOutput, calls=%fused_computation.231 | convolution fusion | flops 11827937280 | bytes 27262976 | tf_op jit(solution)/shard_map/dot_general | solution.py:19
  383.6 7.8 reshape.281
  391.4 17.8 %collective-permute-done.40 = bf16[256,2048]{1,0:T(8,128)(2,1)} collective-permute-done((bf16[256,2048]{1,0:T(8,128)(2,1)}, bf16[256,2048]{1,0:T(8,128)(2,1)}, u32[]{:S(2)}, u32[]{:S(2)}) %collective-permute-start.40) | collective-permute-done | bytes 1048608 | tf_op jit(solution)/shard_map/ppermute | solution.py:346
  409.1 17.5 %multiply_convert_fusion.3 = (bf16[1024,1408]{1,0:T(8,128)(2,1)}, bf16[1024,1408]{1,0:T(8,128)(2,1)}, bf16[1024,1408]{1,0:T(8,128)(2,1)}) fusion(f32[1024,2816]{1,0:T(8,128)} %fusion.32, bf16[1408,2048]{1,0:T(8,128)(2,1)} %all-gather.6.cloned.1.call-done, bf16[256,2048]{1,0:T(8,128)(2,1)} %collective-permute-done.41, ...), kind=kOutput, calls=%fused_computation.15 | convolution fusion | flops 5948178432 | bytes 30150656 | tf_op jit(solution)/shard_map/dot_general | solution.py:23
  426.6 16.7 %convolution_convert_fusion.1 = bf16[1024,2048]{1,0:T(8,128)(2,1)S(1)} fusion(bf16[2048,2816]{1,0:T(8,128)(2,1)} %constant_dynamic-update-slice_fusion, bf16[1024,1408]{1,0:T(8,128)(2,1)} %get-tuple-element.103, bf16[1024,1408]{1,0:T(8,128)(2,1)} %get-tuple-element.102), kind=kOutput, calls=%fused_computation.25 | convolution fusion | flops 11824791552 | bytes 21495808 | tf_op jit(solution)/shard_map/dot_general | solution.py:23
  448.4 8.4 convolution_convert_fusion.2
  460.6 11.3 collective-permute-done.44
  472.4 10.0 constant_dynamic-slice_fusion.2
  482.4 10.6 copy.70
  493.1 10.5 copy.69
  507.0 9.9 collective-permute-done.38
  516.9 21.4 %collective-permute-done.37 = bf16[256,2048]{1,0:T(8,128)(2,1)} collective-permute-done((bf16[256,2048]{1,0:T(8,128)(2,1)}, bf16[256,2048]{1,0:T(8,128)(2,1)}, u32[]{:S(2)}, u32[]{:S(2)}) %collective-permute-start.37) | collective-permute-done | bytes 1048608 | tf_op jit(solution)/shard_map/ppermute | solution.py:346
  538.4 5.8 multiply_convert_fusion.5
  547.7 8.3 fusion.29
  558.1 13.1 %collective-permute-done.47 = bf16[256,2048]{1,0:T(8,128)(2,1)S(1)} collective-permute-done((bf16[256,2048]{1,0:T(8,128)(2,1)S(1)}, bf16[256,2048]{1,0:T(8,128)(2,1)S(1)}, u32[]{:S(2)}, u32[]{:S(2)}) %collective-permute-start.47) | collective-permute-done | bytes 1048608 | tf_op jit(solution)/shard_map/ppermute | solution.py:346
  571.2 21.5 %collective-permute-done.46 = bf16[256,2048]{1,0:T(8,128)(2,1)S(1)} collective-permute-done((bf16[256,2048]{1,0:T(8,128)(2,1)S(1)}, bf16[256,2048]{1,0:T(8,128)(2,1)S(1)}, u32[]{:S(2)}, u32[]{:S(2)}) %collective-permute-start.46) | collective-permute-done | bytes 1048608 | tf_op jit(solution)/shard_map/ppermute | solution.py:346
  592.7 6.2 fusion.31
  598.9 20.2 %shard_map.290 = (bf16[4,256,1024]{2,1,0:T(8,128)(2,1)}, f32[4,256,1024]{2,1,0:T(8,128)}, f32[4,256,128]{2,1,0:T(8,128)}, f32[4,64,1024]{2,1,0:T(8,128)}, f32[8,512]{1,0:T(8,128)}) custom-call(f32[4,256,1024]{2,1,0:T(8,128)} %bitcast.176, bf16[4,256,1024]{2,1,0:T(8,128)(2,1)} %bitcast.179, f32[4,256,128]{2,1,0:T(8,128)} %bitcast.153, ...), custom_call_target="tpu_custom_call" | custom-call | flops 24000000000 | bytes 20000000 | tf_op jit(solution)/shard_map/pallas_call | solution.py:258
  621.2 10.8 convolution_convert_fusion
  650.9 12.3 collective-permute-done.50
  671.2 9.1 shard_map.291
  684.4 9.0 fusion.44
  693.4 12.1 add_convert_fusion
  713.0 9.3 convert_add_fusion
  733.5 57.7 %collective-permute-done.77 = bf16[1,64,2048]{2,1,0:T(8,128)(2,1)} collective-permute-done((bf16[1,64,2048]{2,1,0:T(8,128)(2,1)}, bf16[1,64,2048]{2,1,0:T(8,128)(2,1)}, u32[]{:S(2)}, u32[]{:S(2)}) %collective-permute-start.77) | collective-permute-done | bytes 262176 | tf_op jit(solution)/shard_map/ppermute | solution.py:346
  809.4 29.2 %collective-permute-done.92 = bf16[1,176,2048]{2,1,0:T(8,128)(2,1)S(1)} collective-permute-done((bf16[1,176,2048]{2,1,0:T(8,128)(2,1)S(1)}, bf16[1,176,2048]{2,1,0:T(8,128)(2,1)S(1)}, u32[]{:S(2)}, u32[]{:S(2)}) %collective-permute-start.92) | collective-permute-done | bytes 720928 | tf_op jit(solution)/shard_map/ppermute | solution.py:346
  845.4 71.3 %collective-permute-done.83 = bf16[4,64,2816]{2,1,0:T(8,128)(2,1)S(1)} collective-permute-done((bf16[4,64,2816]{2,1,0:T(8,128)(2,1)S(1)}, bf16[4,64,2816]{2,1,0:T(8,128)(2,1)S(1)}, u32[]{:S(2)}, u32[]{:S(2)}) %collective-permute-start.83) | collective-permute-done | bytes 1441824 | tf_op jit(solution)/shard_map/ppermute | solution.py:346
  917.2 10.8 collective-permute-done.59
  929.3 21.0 %collective-permute-done.67 = bf16[4,128,1024]{2,1,0:T(8,128)(2,1)S(1)} collective-permute-done((bf16[4,128,1024]{2,1,0:T(8,128)(2,1)S(1)}, bf16[4,128,1024]{2,1,0:T(8,128)(2,1)S(1)}, u32[]{:S(2)}, u32[]{:S(2)}) %collective-permute-start.67) | collective-permute-done | bytes 1048608 | tf_op jit(solution)/shard_map/ppermute | solution.py:346
  951.6 9.1 collective-permute-done.85
  961.1 9.1 collective-permute-done.84
  976.4 6.7 collective-permute-done.78.refs_1_
  984.1 34.9 %collective-permute-done.79.refs_2_ = bf16[1,64,2048]{2,1,0:T(8,128)(2,1)S(1)} collective-permute-done((bf16[1,64,2048]{2,1,0:T(8,128)(2,1)S(1)}, bf16[1,64,2048]{2,1,0:T(8,128)(2,1)S(1)}, u32[]{:S(2)}, u32[]{:S(2)}) %collective-permute-start.79) | collective-permute-done | bytes 262176 | tf_op jit(solution)/shard_map/ppermute | solution.py:346
  1036.2 44.6 %collective-permute-done.94.refs_2_ = bf16[1,176,2048]{2,1,0:T(8,128)(2,1)} collective-permute-done((bf16[1,176,2048]{2,1,0:T(8,128)(2,1)S(1)}, bf16[1,176,2048]{2,1,0:T(8,128)(2,1)}, u32[]{:S(2)}, u32[]{:S(2)}) %collective-permute-start.94) | collective-permute-done | bytes 720928 | tf_op jit(solution)/shard_map/ppermute | solution.py:346
  1090.8 16.0 %collective-permute-done.63.refs_1_ = bf16[4,64,1024]{2,1,0:T(8,128)(2,1)} collective-permute-done((bf16[4,64,1024]{2,1,0:T(8,128)(2,1)}, bf16[4,64,1024]{2,1,0:T(8,128)(2,1)}, u32[]{:S(2)}, u32[]{:S(2)}) %collective-permute-start.63) | collective-permute-done | bytes 524320 | tf_op jit(solution)/shard_map/ppermute | solution.py:346
  1113.9 11.1 collective-permute-done.64.refs_2_
  1125.0 10.9 collective-permute-done.95.refs_3_
  1142.5 100.9 %all-reduce.4.cloned.1.call-done = bf16[43264]{0:T(1024)(128)(2,1)} async-done(((bf16[43264]{0:T(1024)(128)(2,1)}), bf16[43264]{0:T(1024)(128)(2,1)}) %all-reduce.4.cloned.1.call-update) | async-done | bytes 86544 | tf_op jit(solution)/shard_map/psum | solution.py:694
  1269.0 7.9 shard_map.295
  (546 shorter events, 340.9 us)
Async XLA Ops:
  8.0 92.4 %all-reduce.6.cloned.1.call-start = ((), (), s32[]{:S(2)}) async-start(), calls=%async_computation.3 | async-start | bytes 352256
  16.3 211.4 %all-gather.4.cloned.1.call-start = ((), (), s32[]{:S(2)}) async-start(), calls=%async_computation | async-start | bytes 3145728 | tf_op jit(solution)/shard_map/all_gather | solution.py:570
  16.8 392.3 %all-gather.6.cloned.1.call-start = ((), (), s32[]{:S(2)}) async-start(), calls=%async_computation.1 | async-start | bytes 8650752 | tf_op jit(solution)/shard_map/all_gather | solution.py:571
  18.4 113.3 %collective-permute-start.2 = (bf16[256,2048]{0,1:T(8,128)(2,1)S(1)}, bf16[256,2048]{0,1:T(8,128)(2,1)S(1)}, u32[]{:S(2)}, u32[]{:S(2)}) collective-permute-start(bf16[256,2048]{0,1:T(8,128)(2,1)S(1)} %copy.53), channel_id=1, source_target_pairs={{0,24},{8,16},{16,8},{24,0},{1,25},{9,17},{17,9},{25,1},{2,26},{10... | collective-permute-start | bytes 3145736 | tf_op jit(solution)/shard_map/ppermute | solution.py:346
  22.4 110.9 %collective-permute-start.1 = (bf16[256,2048]{0,1:T(8,128)(2,1)S(1)}, bf16[256,2048]{0,1:T(8,128)(2,1)S(1)}, u32[]{:S(2)}, u32[]{:S(2)}) collective-permute-start(bf16[256,2048]{0,1:T(8,128)(2,1)S(1)} %copy.53), channel_id=1, source_target_pairs={{0,16},{8,24},{16,0},{24,8},{1,17},{9,25},{17,1},{25,9},{2,18},{10... | collective-permute-start | bytes 3145736 | tf_op jit(solution)/shard_map/ppermute | solution.py:346
  26.2 89.7 %collective-permute-start.3 = (bf16[256,1024]{1,0:T(8,128)(2,1)}, bf16[256,1024]{1,0:T(8,128)(2,1)}, u32[]{:S(2)}, u32[]{:S(2)}) collective-permute-start(bf16[256,1024]{1,0:T(8,128)(2,1)} %pad_maximum_fusion.16), channel_id=1, source_target_pairs={{0,8},{8,0},{16,24},{24,16},{1,9},{9,1},{17,25},{25,17},{2,10},{10... | collective-permute-start | bytes 1572872 | tf_op jit(solution)/shard_map/ppermute | solution.py:346
  27.2 90.3 %collective-permute-start.4 = (bf16[256,1024]{1,0:T(8,128)(2,1)}, bf16[256,1024]{1,0:T(8,128)(2,1)}, u32[]{:S(2)}, u32[]{:S(2)}) collective-permute-start(bf16[256,1024]{1,0:T(8,128)(2,1)} %pad_maximum_fusion.17), channel_id=1, source_target_pairs={{0,16},{8,24},{16,0},{24,8},{1,17},{9,25},{17,1},{25,9},{2,18},{10... | collective-permute-start | bytes 1572872 | tf_op jit(solution)/shard_map/ppermute | solution.py:346
  29.9 87.5 %collective-permute-start.5 = (bf16[256,1024]{1,0:T(8,128)(2,1)}, bf16[256,1024]{1,0:T(8,128)(2,1)}, u32[]{:S(2)}, u32[]{:S(2)}) collective-permute-start(bf16[256,1024]{1,0:T(8,128)(2,1)} %pad_maximum_fusion.18), channel_id=1, source_target_pairs={{0,24},{8,16},{16,8},{24,0},{1,25},{9,17},{17,9},{25,1},{2,26},{10... | collective-permute-start | bytes 1572872 | tf_op jit(solution)/shard_map/ppermute | solution.py:346
  31.4 1212.0 %all-reduce.4.cloned.1.call-start = ((), (), s32[]{:S(2)}) async-start(), calls=%async_computation.2 | async-start | bytes 176128 | tf_op jit(solution)/shard_map/psum | solution.py:694
  125.3 67.0 %collective-permute-start.6 = (bf16[256,1024]{1,0:T(8,128)(2,1)}, bf16[256,1024]{1,0:T(8,128)(2,1)}, u32[]{:S(2)}, u32[]{:S(2)}) collective-permute-start(bf16[256,1024]{1,0:T(8,128)(2,1)} %get-tuple-element.175), channel_id=1, source_target_pairs={{0,4},{4,0},{1,5},{5,1},{2,6},{6,2},{3,7},{7,3},{8,12},{12,8},{9,1... | collective-permute-start | bytes 1572872 | tf_op jit(solution)/shard_map/ppermute | solution.py:346
  128.5 47.6 %collective-permute-start.7 = (bf16[256,1024]{1,0:T(8,128)(2,1)}, bf16[256,1024]{1,0:T(8,128)(2,1)}, u32[]{:S(2)}, u32[]{:S(2)}) collective-permute-start(bf16[256,1024]{1,0:T(8,128)(2,1)} %pad_maximum_fusion.20), channel_id=1, source_target_pairs={{0,8},{8,0},{16,24},{24,16},{1,9},{9,1},{17,25},{25,17},{2,10},{10... | collective-permute-start | bytes 1572872 | tf_op jit(solution)/shard_map/ppermute | solution.py:346
  185.6 51.6 %collective-permute-start.29 = (bf16[256,2816]{1,0:T(8,128)(2,1)}, bf16[256,2816]{1,0:T(8,128)(2,1)}, u32[]{:S(2)}, u32[]{:S(2)}) collective-permute-start(bf16[256,2816]{1,0:T(8,128)(2,1)} %get-tuple-element.134), channel_id=1, source_target_pairs={{0,4},{4,0},{1,5},{5,1},{2,6},{6,2},{3,7},{7,3},{8,12},{12,8},{9,1... | collective-permute-start | bytes 4325384 | tf_op jit(solution)/shard_map/ppermute | solution.py:346
  199.0 86.5 %collective-permute-start.32 = (bf16[256,2816]{1,0:T(8,128)(2,1)}, bf16[256,2816]{1,0:T(8,128)(2,1)}, u32[]{:S(2)}, u32[]{:S(2)}) collective-permute-start(bf16[256,2816]{1,0:T(8,128)(2,1)} %pad_maximum_fusion.11), channel_id=1, source_target_pairs={{0,16},{8,24},{16,0},{24,8},{1,17},{9,25},{17,1},{25,9},{2,18},{10... | collective-permute-start | bytes 4325384 | tf_op jit(solution)/shard_map/ppermute | solution.py:346
  209.3 78.8 %collective-permute-start.34 = (bf16[256,2816]{1,0:T(8,128)(2,1)}, bf16[256,2816]{1,0:T(8,128)(2,1)}, u32[]{:S(2)}, u32[]{:S(2)}) collective-permute-start(bf16[256,2816]{1,0:T(8,128)(2,1)} %pad_maximum_fusion.12), channel_id=1, source_target_pairs={{0,24},{8,16},{16,8},{24,0},{1,25},{9,17},{17,9},{25,1},{2,26},{10... | collective-permute-start | bytes 4325384 | tf_op jit(solution)/shard_map/ppermute | solution.py:346
  235.7 52.9 %collective-permute-start.25 = (bf16[256,2048]{1,0:T(8,128)(2,1)}, bf16[256,2048]{1,0:T(8,128)(2,1)S(1)}, u32[]{:S(2)}, u32[]{:S(2)}) collective-permute-start(bf16[256,2048]{1,0:T(8,128)(2,1)} %get-tuple-element.119), channel_id=1, source_target_pairs={{0,24},{8,16},{16,8},{24,0},{1,25},{9,17},{17,9},{25,1},{2,26},{10... | collective-permute-start | bytes 3145736 | tf_op jit(solution)/shard_map/ppermute | solution.py:346
  237.2 71.2 %collective-permute-start.24 = (bf16[256,2048]{1,0:T(8,128)(2,1)}, bf16[256,2048]{1,0:T(8,128)(2,1)}, u32[]{:S(2)}, u32[]{:S(2)}) collective-permute-start(bf16[256,2048]{1,0:T(8,128)(2,1)} %get-tuple-element.120), channel_id=1, source_target_pairs={{0,16},{8,24},{16,0},{24,8},{1,17},{9,25},{17,1},{25,9},{2,18},{10... | collective-permute-start | bytes 3145736 | tf_op jit(solution)/shard_map/ppermute | solution.py:346
  238.7 69.7 %collective-permute-start.23 = (bf16[256,2048]{1,0:T(8,128)(2,1)}, bf16[256,2048]{1,0:T(8,128)(2,1)}, u32[]{:S(2)}, u32[]{:S(2)}) collective-permute-start(bf16[256,2048]{1,0:T(8,128)(2,1)} %get-tuple-element.118), channel_id=1, source_target_pairs={{0,8},{8,0},{16,24},{24,16},{1,9},{9,1},{17,25},{25,17},{2,10},{10... | collective-permute-start | bytes 3145736 | tf_op jit(solution)/shard_map/ppermute | solution.py:346
  446.3 57.3 %collective-permute-start.43 = (bf16[256,2048]{1,0:T(8,128)(2,1)}, bf16[256,2048]{1,0:T(8,128)(2,1)}, u32[]{:S(2)}, u32[]{:S(2)}) collective-permute-start(bf16[256,2048]{1,0:T(8,128)(2,1)} %get-tuple-element.114), channel_id=1, source_target_pairs={{0,16},{8,24},{16,0},{24,8},{1,17},{9,25},{17,1},{25,9},{2,18},{10... | collective-permute-start | bytes 3145736 | tf_op jit(solution)/shard_map/ppermute | solution.py:346
  446.9 56.7 %collective-permute-start.42 = (bf16[256,2048]{1,0:T(8,128)(2,1)}, bf16[256,2048]{1,0:T(8,128)(2,1)}, u32[]{:S(2)}, u32[]{:S(2)}) collective-permute-start(bf16[256,2048]{1,0:T(8,128)(2,1)} %get-tuple-element.112), channel_id=1, source_target_pairs={{0,8},{8,0},{16,24},{24,16},{1,9},{9,1},{17,25},{25,17},{2,10},{10... | collective-permute-start | bytes 3145736 | tf_op jit(solution)/shard_map/ppermute | solution.py:346
  458.5 58.4 %collective-permute-start.38 = (bf16[256,2048]{1,0:T(8,128)(2,1)}, bf16[256,2048]{1,0:T(8,128)(2,1)}, u32[]{:S(2)}, u32[]{:S(2)}) collective-permute-start(bf16[256,2048]{1,0:T(8,128)(2,1)} %get-tuple-element.116), channel_id=1, source_target_pairs={{0,24},{8,16},{16,8},{24,0},{1,25},{9,17},{17,9},{25,1},{2,26},{10... | collective-permute-start | bytes 3145736 | tf_op jit(solution)/shard_map/ppermute | solution.py:346
  459.9 78.4 %collective-permute-start.37 = (bf16[256,2048]{1,0:T(8,128)(2,1)}, bf16[256,2048]{1,0:T(8,128)(2,1)}, u32[]{:S(2)}, u32[]{:S(2)}) collective-permute-start(bf16[256,2048]{1,0:T(8,128)(2,1)} %get-tuple-element.117), channel_id=1, source_target_pairs={{0,16},{8,24},{16,0},{24,8},{1,17},{9,25},{17,1},{25,9},{2,18},{10... | collective-permute-start | bytes 3145736 | tf_op jit(solution)/shard_map/ppermute | solution.py:346
  471.8 66.5 %collective-permute-start.36 = (bf16[256,2048]{1,0:T(8,128)(2,1)}, bf16[256,2048]{1,0:T(8,128)(2,1)}, u32[]{:S(2)}, u32[]{:S(2)}) collective-permute-start(bf16[256,2048]{1,0:T(8,128)(2,1)} %get-tuple-element.115), channel_id=1, source_target_pairs={{0,8},{8,0},{16,24},{24,16},{1,9},{9,1},{17,25},{25,17},{2,10},{10... | collective-permute-start | bytes 3145736 | tf_op jit(solution)/shard_map/ppermute | solution.py:346
  558.1 85.2 %collective-permute-start.90 = (bf16[704,2048]{1,0:T(8,128)(2,1)}, bf16[704,2048]{1,0:T(8,128)(2,1)}, u32[]{:S(2)}, u32[]{:S(2)}) collective-permute-start(bf16[704,2048]{1,0:T(8,128)(2,1)} %dynamic-slice_convert_fusion), channel_id=1, source_target_pairs={{0,4},{4,0},{1,5},{5,1},{2,6},{6,2},{3,7},{7,3},{8,12},{12,8},{9,1... | collective-permute-start | bytes 8650760 | tf_op jit(solution)/shard_map/ppermute | solution.py:346
  632.0 81.0 %collective-permute-start.81 = (bf16[1024,2816]{1,0:T(8,128)(2,1)}, bf16[1024,2816]{1,0:T(8,128)(2,1)}, u32[]{:S(2)}, u32[]{:S(2)}) collective-permute-start(bf16[1024,2816]{1,0:T(8,128)(2,1)} %convolution_convert_fusion), channel_id=1, source_target_pairs={{0,4},{4,0},{1,5},{5,1},{2,6},{6,2},{3,7},{7,3},{8,12},{12,8},{9,1... | collective-permute-start | bytes 17301512 | tf_op jit(solution)/shard_map/ppermute | solution.py:346
  637.9 156.2 %collective-permute-start.57 = (bf16[1024,1024]{1,0:T(8,128)(2,1)}, bf16[1024,1024]{1,0:T(8,128)(2,1)}, u32[]{:S(2)}, u32[]{:S(2)}) collective-permute-start(bf16[1024,1024]{1,0:T(8,128)(2,1)} %convolution_convert_fusion.7), channel_id=1, source_target_pairs={{0,4},{4,0},{1,5},{5,1},{2,6},{6,2},{3,7},{7,3},{8,12},{12,8},{9,1... | collective-permute-start | bytes 6291464 | tf_op jit(solution)/shard_map/ppermute | solution.py:346
  663.2 136.6 %collective-permute-start.91 = (bf16[1,352,2048]{2,1,0:T(8,128)(2,1)}, bf16[1,352,2048]{2,1,0:T(8,128)(2,1)}, u32[]{:S(2)}, u32[]{:S(2)}) collective-permute-start(bf16[1,352,2048]{2,1,0:T(8,128)(2,1)} %fusion.15), channel_id=1, source_target_pairs={{0,1},{1,0},{2,3},{3,2},{4,5},{5,4},{6,7},{7,6},{8,9},{9,8},{10,11... | collective-permute-start | bytes 4325384 | tf_op jit(solution)/shard_map/ppermute | solution.py:346
  666.8 57.8 %collective-permute-start.76 = (bf16[1,128,2048]{2,1,0:T(8,128)(2,1)S(1)}, bf16[1,128,2048]{2,1,0:T(8,128)(2,1)S(1)}, u32[]{:S(2)}, u32[]{:S(2)}) collective-permute-start(bf16[1,128,2048]{2,1,0:T(8,128)(2,1)S(1)} %fusion.24), channel_id=1, source_target_pairs={{0,1},{1,0},{2,3},{3,2},{4,5},{5,4},{6,7},{7,6},{8,9},{9,8},{10,11... | collective-permute-start | bytes 1572872 | tf_op jit(solution)/shard_map/ppermute | solution.py:346
  724.2 77.6 %collective-permute-start.82 = (bf16[4,128,2816]{2,1,0:T(8,128)(2,1)}, bf16[4,128,2816]{2,1,0:T(8,128)(2,1)}, u32[]{:S(2)}, u32[]{:S(2)}) collective-permute-start(bf16[4,128,2816]{2,1,0:T(8,128)(2,1)} %dynamic-slice_convert_fusion.1), channel_id=1, source_target_pairs={{0,1},{1,0},{2,3},{3,2},{4,5},{5,4},{6,7},{7,6},{8,9},{9,8},{10,11... | collective-permute-start | bytes 8650760 | tf_op jit(solution)/shard_map/ppermute | solution.py:346
  726.3 65.0 %collective-permute-start.77 = (bf16[1,64,2048]{2,1,0:T(8,128)(2,1)}, bf16[1,64,2048]{2,1,0:T(8,128)(2,1)}, u32[]{:S(2)}, u32[]{:S(2)}) collective-permute-start(bf16[1,64,2048]{2,1,0:T(8,128)(2,1)} %dynamic-slice_convert_fusion.10), channel_id=1, source_target_pairs={{0,2},{1,3},{2,0},{3,1},{4,6},{5,7},{6,4},{7,5},{8,10},{9,11},{10,... | collective-permute-start | bytes 786440 | tf_op jit(solution)/shard_map/ppermute | solution.py:346
  730.8 240.6 %collective-permute-start.56 = (bf16[256,2048]{1,0:T(8,128)(2,1)}, bf16[256,2048]{1,0:T(8,128)(2,1)}, u32[]{:S(2)}, u32[]{:S(2)}) collective-permute-start(bf16[256,2048]{1,0:T(8,128)(2,1)} %get-tuple-element.110), channel_id=1, source_target_pairs={{0,24},{8,16},{16,8},{24,0},{1,25},{9,17},{17,9},{25,1},{2,26},{10... | collective-permute-start | bytes 3145736 | tf_op jit(solution)/shard_map/ppermute | solution.py:346
  791.3 183.2 %collective-permute-start.55 = (bf16[256,2048]{1,0:T(8,128)(2,1)}, bf16[256,2048]{1,0:T(8,128)(2,1)S(1)}, u32[]{:S(2)}, u32[]{:S(2)}) collective-permute-start(bf16[256,2048]{1,0:T(8,128)(2,1)} %get-tuple-element.111), channel_id=1, source_target_pairs={{0,16},{8,24},{16,0},{24,8},{1,17},{9,25},{17,1},{25,9},{2,18},{10... | collective-permute-start | bytes 3145736 | tf_op jit(solution)/shard_map/ppermute | solution.py:346
  794.1 48.6 %collective-permute-start.66 = (bf16[1024,1024]{1,0:T(8,128)(2,1)}, bf16[1024,1024]{1,0:T(8,128)(2,1)S(1)}, u32[]{:S(2)}, u32[]{:S(2)}) collective-permute-start(bf16[1024,1024]{1,0:T(8,128)(2,1)} %convolution_convert_fusion.6), channel_id=1, source_target_pairs={{0,4},{4,0},{1,5},{5,1},{2,6},{6,2},{3,7},{7,3},{8,12},{12,8},{9,1... | collective-permute-start | bytes 6291464 | tf_op jit(solution)/shard_map/ppermute | solution.py:346
  838.6 78.1 %collective-permute-start.83 = (bf16[4,64,2816]{2,1,0:T(8,128)(2,1)S(1)}, bf16[4,64,2816]{2,1,0:T(8,128)(2,1)S(1)}, u32[]{:S(2)}, u32[]{:S(2)}) collective-permute-start(bf16[4,64,2816]{2,1,0:T(8,128)(2,1)S(1)} %dynamic-slice_convert_fusion.3), channel_id=1, source_target_pairs={{0,2},{1,3},{2,0},{3,1},{4,6},{5,7},{6,4},{7,5},{8,10},{9,11},{10,... | collective-permute-start | bytes 4325384 | tf_op jit(solution)/shard_map/ppermute | solution.py:346
  842.2 133.7 %collective-permute-start.54 = (bf16[256,2048]{1,0:T(8,128)(2,1)S(1)}, bf16[256,2048]{1,0:T(8,128)(2,1)S(1)}, u32[]{:S(2)}, u32[]{:S(2)}) collective-permute-start(bf16[256,2048]{1,0:T(8,128)(2,1)S(1)} %copy-done.43), channel_id=1, source_target_pairs={{0,8},{8,0},{16,24},{24,16},{1,9},{9,1},{17,25},{25,17},{2,10},{10... | collective-permute-start | bytes 3145736 | tf_op jit(solution)/shard_map/ppermute | solution.py:346
  842.8 85.2 %collective-permute-start.59 = (bf16[4,64,1024]{2,1,0:T(8,128)(2,1)S(1)}, bf16[4,64,1024]{2,1,0:T(8,128)(2,1)S(1)}, u32[]{:S(2)}, u32[]{:S(2)}) collective-permute-start(bf16[4,64,1024]{2,1,0:T(8,128)(2,1)S(1)} %dynamic-slice_convert_fusion.9), channel_id=1, source_target_pairs={{0,2},{1,3},{2,0},{3,1},{4,6},{5,7},{6,4},{7,5},{8,10},{9,11},{10,... | collective-permute-start | bytes 1572872 | tf_op jit(solution)/shard_map/ppermute | solution.py:346
  971.5 47.5 %collective-permute-start.79 = (bf16[1,64,2048]{2,1,0:T(8,128)(2,1)S(1)}, bf16[1,64,2048]{2,1,0:T(8,128)(2,1)S(1)}, u32[]{:S(2)}, u32[]{:S(2)}) collective-permute-start(bf16[1,64,2048]{2,1,0:T(8,128)(2,1)S(1)} %add_convert_fusion.6.refs_0_), channel_id=1, source_target_pairs={{0,2},{1,3},{2,0},{3,1},{4,6},{5,7},{6,4},{7,5},{8,10},{9,11},{10,... | collective-permute-start | bytes 786440 | tf_op jit(solution)/shard_map/ppermute | solution.py:346
  983.8 122.9 %collective-permute-start.88 = (bf16[4,64,2816]{2,1,0:T(8,128)(2,1)}, bf16[4,64,2816]{2,1,0:T(8,128)(2,1)}, u32[]{:S(2)}, u32[]{:S(2)}) collective-permute-start(bf16[4,64,2816]{2,1,0:T(8,128)(2,1)} %pad_maximum_fusion.13.refs_0_), channel_id=1, source_target_pairs={{0,2},{1,3},{2,0},{3,1},{4,6},{5,7},{6,4},{7,5},{8,10},{9,11},{10,... | collective-permute-start | bytes 4325384 | tf_op jit(solution)/shard_map/ppermute | solution.py:346
  1018.9 67.4 %collective-permute-start.93 = (bf16[1,176,2048]{2,1,0:T(8,128)(2,1)S(1)}, bf16[1,176,2048]{2,1,0:T(8,128)(2,1)S(1)}, u32[]{:S(2)}, u32[]{:S(2)}) collective-permute-start(bf16[1,176,2048]{2,1,0:T(8,128)(2,1)S(1)} %add_convert_fusion.3.refs_0_), channel_id=1, source_target_pairs={{0,1},{1,0},{2,3},{3,2},{4,5},{5,4},{6,7},{7,6},{8,9},{9,8},{10,11... | collective-permute-start | bytes 2162696 | tf_op jit(solution)/shard_map/ppermute | solution.py:346
  1019.0 61.9 %collective-permute-start.94 = (bf16[1,176,2048]{2,1,0:T(8,128)(2,1)S(1)}, bf16[1,176,2048]{2,1,0:T(8,128)(2,1)}, u32[]{:S(2)}, u32[]{:S(2)}) collective-permute-start(bf16[1,176,2048]{2,1,0:T(8,128)(2,1)S(1)} %add_convert_fusion.3.refs_0_), channel_id=1, source_target_pairs={{0,2},{1,3},{2,0},{3,1},{4,6},{5,7},{6,4},{7,5},{8,10},{9,11},{10,... | collective-permute-start | bytes 2162696 | tf_op jit(solution)/shard_map/ppermute | solution.py:346
  1027.0 59.3 %collective-permute-start.80 = (bf16[1,64,2048]{2,1,0:T(8,128)(2,1)S(1)}, bf16[1,64,2048]{2,1,0:T(8,128)(2,1)S(1)}, u32[]{:S(2)}, u32[]{:S(2)}) collective-permute-start(bf16[1,64,2048]{2,1,0:T(8,128)(2,1)S(1)} %collective-permute-done.79.refs_2_), channel_id=1, source_target_pairs={{0,1},{1,0},{2,3},{3,2},{4,5},{5,4},{6,7},{7,6},{8,9},{9,8},{10,11... | collective-permute-start | bytes 786440 | tf_op jit(solution)/shard_map/ppermute | solution.py:346
  1035.0 71.7 %collective-permute-start.63 = (bf16[4,64,1024]{2,1,0:T(8,128)(2,1)}, bf16[4,64,1024]{2,1,0:T(8,128)(2,1)}, u32[]{:S(2)}, u32[]{:S(2)}) collective-permute-start(bf16[4,64,1024]{2,1,0:T(8,128)(2,1)} %pad_maximum_fusion.25.refs_0_), channel_id=1, source_target_pairs={{0,1},{1,0},{2,3},{3,2},{4,5},{5,4},{6,7},{7,6},{8,9},{9,8},{10,11... | collective-permute-start | bytes 1572872 | tf_op jit(solution)/shard_map/ppermute | solution.py:346
  1080.9 55.0 %collective-permute-start.95 = (bf16[1,176,2048]{2,1,0:T(8,128)(2,1)}, bf16[1,176,2048]{2,1,0:T(8,128)(2,1)}, u32[]{:S(2)}, u32[]{:S(2)}) collective-permute-start(bf16[1,176,2048]{2,1,0:T(8,128)(2,1)} %collective-permute-done.94.refs_2_), channel_id=1, source_target_pairs={{0,1},{1,0},{2,3},{3,2},{4,5},{5,4},{6,7},{7,6},{8,9},{9,8},{10,11... | collective-permute-start | bytes 2162696 | tf_op jit(solution)/shard_map/ppermute | solution.py:346
  1087.3 48.7 %collective-permute-start.73 = (bf16[4,64,1024]{2,1,0:T(8,128)(2,1)}, bf16[4,64,1024]{2,1,0:T(8,128)(2,1)}, u32[]{:S(2)}, u32[]{:S(2)}) collective-permute-start(bf16[4,64,1024]{2,1,0:T(8,128)(2,1)} %pad_maximum_fusion.26.refs_0_), channel_id=1, source_target_pairs={{0,2},{1,3},{2,0},{3,1},{4,6},{5,7},{6,4},{7,5},{8,10},{9,11},{10,... | collective-permute-start | bytes 1572872 | tf_op jit(solution)/shard_map/ppermute | solution.py:346
  1106.7 162.3 %collective-permute-start.87 = (bf16[4,64,2816]{2,1,0:T(8,128)(2,1)}, bf16[4,64,2816]{2,1,0:T(8,128)(2,1)}, u32[]{:S(2)}, u32[]{:S(2)}) collective-permute-start(bf16[4,64,2816]{2,1,0:T(8,128)(2,1)} %pad_maximum_fusion.13.refs_0_), channel_id=1, source_target_pairs={{0,1},{1,0},{2,3},{3,2},{4,5},{5,4},{6,7},{7,6},{8,9},{9,8},{10,11... | collective-permute-start | bytes 4325384 | tf_op jit(solution)/shard_map/ppermute | solution.py:346
  1106.8 162.3 %collective-permute-start.89 = (bf16[4,64,2816]{2,1,0:T(8,128)(2,1)}, bf16[4,64,2816]{2,1,0:T(8,128)(2,1)}, u32[]{:S(2)}, u32[]{:S(2)}) collective-permute-start(bf16[4,64,2816]{2,1,0:T(8,128)(2,1)} %collective-permute-done.88.refs_2_), channel_id=1, source_target_pairs={{0,1},{1,0},{2,3},{3,2},{4,5},{5,4},{6,7},{7,6},{8,9},{9,8},{10,11... | collective-permute-start | bytes 4325384 | tf_op jit(solution)/shard_map/ppermute | solution.py:346
  1125.0 134.2 %collective-permute-start.65 = (bf16[4,64,1024]{2,1,0:T(8,128)(2,1)}, bf16[4,64,1024]{2,1,0:T(8,128)(2,1)}, u32[]{:S(2)}, u32[]{:S(2)}) collective-permute-start(bf16[4,64,1024]{2,1,0:T(8,128)(2,1)} %collective-permute-done.64.refs_2_), channel_id=1, source_target_pairs={{0,1},{1,0},{2,3},{3,2},{4,5},{5,4},{6,7},{7,6},{8,9},{9,8},{10,11... | collective-permute-start | bytes 1572872 | tf_op jit(solution)/shard_map/ppermute | solution.py:346
  1135.9 128.2 %collective-permute-start.72 = (bf16[4,64,1024]{2,1,0:T(8,128)(2,1)}, bf16[4,64,1024]{2,1,0:T(8,128)(2,1)}, u32[]{:S(2)}, u32[]{:S(2)}) collective-permute-start(bf16[4,64,1024]{2,1,0:T(8,128)(2,1)} %pad_maximum_fusion.26.refs_0_), channel_id=1, source_target_pairs={{0,1},{1,0},{2,3},{3,2},{4,5},{5,4},{6,7},{7,6},{8,9},{9,8},{10,11... | collective-permute-start | bytes 1572872 | tf_op jit(solution)/shard_map/ppermute | solution.py:346
  1135.9 128.2 %collective-permute-start.74 = (bf16[4,64,1024]{2,1,0:T(8,128)(2,1)}, bf16[4,64,1024]{2,1,0:T(8,128)(2,1)}, u32[]{:S(2)}, u32[]{:S(2)}) collective-permute-start(bf16[4,64,1024]{2,1,0:T(8,128)(2,1)} %collective-permute-done.73.refs_2_), channel_id=1, source_target_pairs={{0,1},{1,0},{2,3},{3,2},{4,5},{5,4},{6,7},{7,6},{8,9},{9,8},{10,11... | collective-permute-start | bytes 1572872 | tf_op jit(solution)/shard_map/ppermute | solution.py:346
  (139 other events, 3512.3 us)
Sparse Core Ops, SparseCore 0:
  16.4 83.9 all-reduce.5
  1114.1 129.2 all-reduce.3
Sparse Core Ops, SparseCore 1:
  18.3 13.2 all-gather.3
  32.9 17.0 all-gather.5

commit v2 on v1

--- a/solution.py
+++ b/solution.py
@@ -350,39 +350,110 @@
     return [block] + [swap(block, "p", k) for k in range(1, HEADS)]
 
 
-def scatter_heads(parts):
+def scatter_heads(parts, *fillers):
+    got = [swap(parts[k], "p", k) for k in range(1, HEADS)]
+    if fillers:
+        held = lax.optimization_barrier(tuple(got) + fillers)
+        got, fillers = held[: HEADS - 1], held[HEADS - 1 :]
     total = parts[0].astype(F32)
-    for k in range(1, HEADS):
-        total = total + swap(parts[k], "p", k).astype(F32)
-    return total
+    for part in got:
+        total = total + part.astype(F32)
+    return (total,) + tuple(fillers) if fillers else total
 
 
 def after(value, *others):
     return lax.optimization_barrier((value,) + others)[0]
 
 
+def place_kernel(blocks, spot_ref, *refs):
+    ins, out = refs[:-1], refs[-1]
+    part = ins[0].shape[1]
+    for i, ref in enumerate(ins):
+        for k in range(blocks):
+            start = pl.multiple_of(spot_ref[i * blocks + k] * part, part)
+            out[pl.ds(start, part), :] = ref[k]
+
+
+def place(parts, spots):
+    blocks, part, width = parts[0].shape
+    chunk = 256
+    table = jnp.stack([jnp.asarray(x, jnp.int32) for row in spots for x in row])
+    rows = len(parts) * blocks * part
+    return pl.pallas_call(
+        functools.partial(place_kernel, blocks),
+        grid_spec=pltpu.PrefetchScalarGridSpec(
+            num_scalar_prefetch=1,
+            grid=(width // chunk,),
+            in_specs=[pl.BlockSpec((blocks, part, chunk), lambda i, s: (0, 0, i))] * len(parts),
+            out_specs=pl.BlockSpec((rows, chunk), lambda i, s: (0, i)),
+        ),
+        out_shape=jax.ShapeDtypeStruct((rows, width), BF),
+        cost_estimate=pl.CostEstimate(flops=0, bytes_accessed=4 * rows * width, transcendentals=0),
+        compiler_params=pltpu.CompilerParams(vmem_limit_bytes=56 << 20),
+    )(table, *parts)
+
+
+def column_cuts(shards, here, k):
+    cuts = []
+    for shard in shards:
+        width = shard.shape[1] // HEADS
+        cuts.append(lax.dynamic_slice_in_dim(shard, (here ^ k) * width, width, 1))
+    return jnp.concatenate(cuts, axis=1)
+
+
 def head_columns(shards, here):
-    width = [shard.shape[1] // HEADS for shard in shards]
-    rows = shards[0].shape[0]
     copies = lax.axis_size("r")
     turn = lax.axis_index("r")
-    pieces = []
-    for k in range(HEADS):
-        cut = jnp.concatenate(
-            [
-                lax.dynamic_slice_in_dim(shard, (here ^ k) * w, w, 1)
-                for shard, w in zip(shards, width)
-            ],
-            axis=1,
-        )
-        pieces.append(cut if k == 0 else swap(cut, "p", k))
-    whole = jnp.zeros((HEADS * copies * rows, sum(width)), BF)
+    own = column_cuts(shards, here, 0)
+    pieces = [own] + [swap(column_cuts(shards, here, k), "p", k) for k in range(1, HEADS)]
+    parts, spots = [], []
     for k in range(HEADS):
         for m in range(copies):
             piece = pieces[k] if m == 0 else swap(pieces[k], "r", m)
-            start = ((here ^ k) * copies + (turn ^ m)) * rows
-            whole = lax.dynamic_update_slice_in_dim(whole, piece, start, 0)
-    return whole, pieces
+            parts.append(piece[None])
+            spots.append([(here ^ k) * copies + (turn ^ m)])
+    return place(parts, spots), pieces[1:]
+
+
+def head_columns_seq(shards, here):
+    copies, count = lax.axis_size("r"), lax.axis_size("seq")
+    turn, spot = lax.axis_index("r"), lax.axis_index("seq")
+    rows = shards[0].shape[0] // count
+    shards = [lax.dynamic_slice_in_dim(shard, spot * rows, rows, 0) for shard in shards]
+    own = column_cuts(shards, here, 0)
+    pieces = [own] + [swap(column_cuts(shards, here, k), "p", k) for k in range(1, HEADS)]
+    parts, spots = [], []
+    for j, part in enumerate(gather_seq(jnp.stack(pieces))):
+        for m in range(copies):
+            parts.append(part if m == 0 else swap(part, "r", m))
+            spots.append(
+                [(((here ^ k) * copies + (turn ^ m)) * count + (spot ^ j)) for k in range(HEADS)]
+            )
+    return place(parts, spots), pieces[1:]
+
+
+def gather_small(packed, here, turn):
+    copies = lax.axis_size("r")
+    near = jnp.concatenate([packed] + [swap(packed, "r", m) for m in range(1, copies)])
+    both = jnp.concatenate(gather_heads(near))
+    heads = jnp.arange(HEADS, dtype=jnp.int32) ^ here
+    turns = jnp.arange(copies, dtype=jnp.int32) ^ turn
+    order = (heads[:, None] * copies + turns[None, :]).reshape(-1)
+    return jnp.take(both, order, axis=0)
+
+
+def sum_small(value, here, turn):
+    mine = [lax.dynamic_index_in_dim(value, here ^ k, 0, False) for k in range(HEADS)]
+    total = scatter_heads(mine)
+    copies = lax.axis_size("r")
+    kept = lax.dynamic_index_in_dim(total, turn, 0, True)
+    for m in range(1, copies):
+        kept = kept + swap(lax.dynamic_index_in_dim(total, turn ^ m, 0, True), "r", m)
+    step = 1
+    while step < lax.axis_size("seq"):
+        kept = kept + swap(kept, "seq", step)
+        step *= 2
+    return kept[0]
 
 
 def chain(state, decay, forward):
@@ -401,8 +472,14 @@
     )
 
 
-def split_rows(left, here, step):
-    return lax.dynamic_index_in_dim(left, here ^ step, 2, False).reshape(left.shape[0], -1)
+def split_rows(left, turn, step, groups):
+    copies, width = left.shape[2:]
+    flat = left.reshape(left.shape[0], -1)
+    cuts = [
+        lax.dynamic_slice_in_dim(flat, (g * copies + (turn ^ step)) * width, width, 1)
+        for g in groups
+    ]
+    return jnp.concatenate(cuts, axis=1)
 
 
 def reduce_copies(parts):
@@ -410,20 +487,6 @@
     for m in range(1, len(parts)):
         total = total + swap(parts[m].astype(BF), "r", m).astype(F32)
     return total
-
-
-def reduce_seq(value):
-    count = lax.axis_size("seq")
-    place = lax.axis_index("seq")
-    step = 1
-    while step < count:
-        half = value.shape[1] // 2
-        bit = (place // step) % 2
-        away = lax.dynamic_slice_in_dim(value, (1 - bit) * half, half, 1)
-        kept = lax.dynamic_slice_in_dim(value, bit * half, half, 1)
-        value = kept.astype(F32) + swap(away.astype(BF), "seq", step).astype(F32)
-        step *= 2
-    return value.astype(BF)
 
 
 def gather_seq(value):
@@ -437,78 +500,77 @@
     return [found[j] for j in range(count)]
 
 
-def row_starts(rows):
-    count = lax.axis_size("seq")
-    place = lax.axis_index("seq")
-    starts = []
-    for j in range(count):
-        other = place ^ j
-        start, half, step = 0, rows // 2, 1
-        while step < count:
-            start = start + ((other // step) % 2) * half
-            half //= 2
-            step *= 2
-        starts.append(start)
-    return starts
-
-
 def assemble_kernel(counts, spot_ref, *refs):
     n_in, n_out, part = counts
     ins, outs = refs[:n_in], refs[n_in:]
     width = outs[0].shape[1]
     for j in range(n_in):
-        start = pl.multiple_of(spot_ref[j] * part, part)
         for o in range(n_out):
-            outs[o][pl.ds(start, part), :] = ins[j][0, :, o * width : (o + 1) * width].astype(F32)
-
-
-def assemble(parts, columns, n_out, starts):
-    blocks, part, width = parts[0].shape
+            cut = ins[j][0, :, o * width : (o + 1) * width]
+            outs[o][j * part : (j + 1) * part, :] = cut.astype(F32)
+
+
+def assemble(parts, columns, n_out):
+    spans, blocks, part, width = parts.shape
     width //= n_out
-    rows = part * len(parts)
-    if part % 16:
-        outs = []
-        for o in range(n_out):
-            whole = jnp.zeros((rows, blocks * width), F32)
-            for j, value in enumerate(parts):
-                for i in range(blocks):
-                    cut = value[i, :, o * width : (o + 1) * width].astype(F32)
-                    whole = lax.dynamic_update_slice(whole, cut, (starts[j], columns[i] * width))
-            outs.append(whole)
-        return outs
-    spots = jnp.stack(
-        [jnp.asarray(s // part, jnp.int32) for s in starts]
-        + [jnp.asarray(c, jnp.int32) for c in columns]
-    )
-    n_in = len(parts)
+    rows = part * spans
+    spots = jnp.stack([jnp.asarray(c, jnp.int32) for c in columns])
     return pl.pallas_call(
-        functools.partial(assemble_kernel, (n_in, n_out, part)),
+        functools.partial(assemble_kernel, (spans, n_out, part)),
         grid_spec=pltpu.PrefetchScalarGridSpec(
             num_scalar_prefetch=1,
             grid=(blocks,),
-            in_specs=[pl.BlockSpec((1, part, n_out * width), lambda i, s: (i, 0, 0))] * n_in,
-            out_specs=[pl.BlockSpec((rows, width), lambda i, s: (0, s[n_in + i]))] * n_out,
+            in_specs=[
+                pl.BlockSpec((None, 1, part, n_out * width), lambda i, s, j=j: (j, i, 0, 0))
+                for j in range(spans)
+            ],
+            out_specs=[pl.BlockSpec((rows, width), lambda i, s: (0, s[i]))] * n_out,
         ),
         out_shape=[jax.ShapeDtypeStruct((rows, blocks * width), F32)] * n_out,
         cost_estimate=pl.CostEstimate(
             flops=0, bytes_accessed=6 * n_out * rows * blocks * width, transcendentals=0
         ),
         compiler_params=pltpu.CompilerParams(vmem_limit_bytes=56 << 20),
-    )(spots, *parts)
-
-
-def finish_columns(total, here, n_out):
-    rows = total.shape[1]
-    part = reduce_seq(total)
-    mine = [lax.dynamic_index_in_dim(part, here ^ k, 0, False) for k in range(HEADS)]
-    got = jnp.stack([mine[0]] + [swap(mine[k], "p", k) for k in range(1, HEADS)])
-    return assemble(gather_seq(got), [here ^ k for k in range(HEADS)], n_out, row_starts(rows))
-
-
-def finish_rows(total):
-    rows = total.shape[0]
-    parts = [value for value in gather_seq(reduce_seq(total[None]))]
-    return assemble(parts, [0], 1, row_starts(rows))[0]
+    )(spots, *([parts] * spans))
+
+
+def finish_wide(total, here, n_out):
+    heads, rows, width = total.shape
+    count = lax.axis_size("seq")
+    spans = total.astype(BF).reshape(heads, count, rows // count, width).transpose(1, 0, 2, 3)
+    part = lax.psum_scatter(spans, "seq", scatter_dimension=0, tiled=False)
+    got = jnp.stack([part[0]] + [swap(part[k], "p", k) for k in range(1, HEADS)])
+    whole = lax.all_gather(got, "seq", axis=0, tiled=False)
+    return assemble(whole, [here ^ k for k in range(HEADS)], n_out)
+
+
+def line_sum(chunks):
+    count = lax.axis_size("seq")
+    half, spot = count // 2, lax.axis_index("seq")
+    totals, last = [], None
+    for chunk in chunks:
+        value = chunk.astype(BF)
+        if last is not None:
+            value = after(value, last)
+        sent = value
+        for i in range(half - 1):
+            got = lax.ppermute(sent, "seq", [(i, i + 1), (count - 1 - i, count - 2 - i)])
+            last = got if i == 0 else last
+            inner = (spot == i + 1) | (spot == count - 2 - i)
+            sent = jnp.where(inner, value + got, sent)
+        total = sent + lax.ppermute(sent, "seq", [(half - 1, half), (half, half - 1)])
+        for i in range(half - 2, -1, -1):
+            got = lax.ppermute(total, "seq", [(i + 1, i), (count - 2 - i, count - 1 - i)])
+            outer = (spot == i) | (spot == count - 1 - i)
+            total = jnp.where(outer, got, total)
+        totals.append(total)
+    return totals
+
+
+def finish_line(total, here, n_out):
+    near, far = line_sum([total[1::2], total[0::2]])
+    got = [far[0], swap(near[0], "p", 1), swap(far[1], "p", 2), swap(near[1], "p", 3)]
+    return assemble(jnp.stack(got)[None], [here ^ k for k in range(HEADS)], n_out)
 
 
 def body(
@@ -539,7 +601,7 @@
 
     small = [attn_gain, decay_down, decay_up, decay_bias, slot_gain, mlp_gain, seq_lengths]
     packed = jnp.concatenate([a.astype(F32).reshape(-1) for a in small])
-    packed = lax.all_gather(packed, ("p", "r"), axis=0)
+    packed = gather_small(packed[None], here, turn)
     fields, offset = [], 0
     for a in small:
         fields.append(packed[:, offset : offset + a.size])
@@ -563,10 +625,10 @@
 
     token_blocks = gather_heads(tokens)
     weight_kv, kv_pieces = head_columns([key_proj, value_proj], here)
-    query_late = after(query_proj, *kv_pieces[1:])
-    weight_qs, qs_pieces = head_columns([query_late, swish_proj], here)
-    gate_late = after(mlp_gate, *qs_pieces[1:])
-    weight_gu, _ = head_columns([gate_late, mlp_up], here)
+    late = lax.optimization_barrier((query_proj, swish_proj, mlp_gate, mlp_up) + tuple(kv_pieces))
+    weight_qs, qs_pieces = head_columns(late[:2], here)
+    weight_gu, gu_pieces = head_columns_seq(late[2:4], here)
+    grad_blocks = gather_heads(after(grad_out, *qs_pieces))
     weight_out = lax.all_gather(out_proj, "r", axis=0, tiled=True)
     weight_down = lax.all_gather(mlp_down, "r", axis=0, tiled=True)
 
@@ -585,7 +647,10 @@
     gated, mixer_out, probs, mix = mixer_forward(qs, kv, li, init, gain_head8)
     gated = gated.reshape(group, HEAD)
     attn_part = mm(gated, weight_out).astype(BF).reshape(HEADS, rows, D)
-    attn_out = scatter_heads([attn_part[k] for k in range(HEADS)])
+    grad_mlp = (mask_all * jnp.concatenate(grad_blocks).astype(F32)).astype(BF)
+    attn_out, grad_act = scatter_heads(
+        [attn_part[k] for k in range(HEADS)], mm_nt(grad_mlp, weight_down)
+    )
 
     tokens_f = tokens.astype(F32)
     residual = tokens_f + mask_own * attn_out
@@ -594,35 +659,36 @@
     normed_two_own = (hat_two * gain_two).astype(BF)
     two_blocks = gather_heads(normed_two_own)
     normed_two = jnp.concatenate(two_blocks)
-    grad_blocks = gather_heads(after(grad_out, *two_blocks[1:]))
-    grad_mlp = (mask_all * jnp.concatenate(grad_blocks).astype(F32)).astype(BF)
 
     hidden_width = weight_down.shape[0]
     gate_up = mm(normed_two, weight_gu)
     gate_pre, up_pre = gate_up[:, :hidden_width], gate_up[:, hidden_width:]
     hidden = (jax.nn.silu(gate_pre) * up_pre).astype(BF)
-    mlp_part = mm(hidden, weight_down).astype(BF).reshape(HEADS, rows, D)
-
-    grad_act = mm_nt(grad_mlp, weight_down)
     grad_gate = (grad_act * up_pre * silu_slope(gate_pre)).astype(BF)
     grad_up = (grad_act * jax.nn.silu(gate_pre)).astype(BF)
     grad_gu = jnp.concatenate([grad_gate, grad_up], axis=1)
     two_part = mm_nt(grad_gu, weight_gu).astype(BF).reshape(HEADS, rows, D)
-    grad_norm_two = scatter_heads([two_part[k] for k in range(HEADS)])
+    two_view = normed_two.reshape(group, HEADS, copies, shard)
+    order = [here ^ k for k in range(HEADS)]
+    gu_parts = [mm_tn(split_rows(two_view, turn, m, order), grad_gu) for m in range(copies)]
+    gu_parts = [gu_parts[0]] + [part.astype(BF) for part in gu_parts[1:]]
+    down_part = mm_tn(hidden, grad_mlp)
+    grad_norm_two, down_part, *gu_parts = scatter_heads(
+        [two_part[k] for k in range(HEADS)], down_part, *gu_parts
+    )
     gain_two_grad = jnp.sum(grad_norm_two * hat_two, axis=0)
     grad_rows = grad_out.astype(F32)
     grad_resid = grad_rows + norm_back(grad_norm_two * gain_two, hat_two, scale_two)
     grad_attn_own = (mask_own * grad_resid).astype(BF)
     attn_blocks = gather_heads(grad_attn_own)
+    mlp_part = mm(hidden, weight_down).astype(BF)
+    mlp_part, *attn_blocks = lax.optimization_barrier((mlp_part,) + tuple(attn_blocks))
     grad_attn = jnp.concatenate(attn_blocks)
-
+    mlp_part = mlp_part.reshape(HEADS, rows, D)
     mlp_out = scatter_heads([mlp_part[k] for k in range(HEADS)])
     result = (residual + mask_own * mlp_out).astype(BF)
 
-    two_view = normed_two.reshape(group, HEADS, copies, shard)
-    gu_parts = [mm_tn(split_rows(two_view, turn, m), grad_gu) for m in range(copies)]
     gu_total = reduce_copies(gu_parts).reshape(HEADS, shard, 2 * hidden_width)
-    down_part = mm_tn(hidden, grad_mlp)
     down_rows = mlp_down.shape[0]
     down_total = reduce_copies(
         [
@@ -630,8 +696,8 @@
             for m in range(copies)
         ]
     )
-    gate_grad, up_grad = finish_columns(gu_total, here, 2)
-    down_grad = finish_rows(down_total)
+    gate_grad, up_grad = finish_wide(gu_total, here, 2)
+    down_grad = lax.psum(down_total.astype(BF), "seq")
 
     grad_gated = mm_nt(grad_attn, weight_out).reshape(HEADS, rows, HEAD)
     grad_qs, grad_kv, grad_li, adjoint, slot_part = mixer_backward(
@@ -669,56 +735,55 @@
     grad_tokens = (grad_resid + norm_back(grad_norm_one * gain_one, hat_one, scale_one)).astype(BF)
 
     one_view = normed.reshape(group, HEADS, copies, shard)
-    one_views = [split_rows(one_view, turn, m) for m in range(copies)]
+    one_views = [split_rows(one_view, turn, m, order) for m in range(copies)]
     qs_total = reduce_copies([mm_tn(v, grad_qs) for v in one_views])
     kv_total = reduce_copies([mm_tn(v, grad_kv) for v in one_views])
     out_view = gated.reshape(group, 1, copies, shard)
-    out_total = reduce_copies([mm_tn(split_rows(out_view, turn, m), grad_attn) for m in range(copies)])
-    query_grad, swish_grad = finish_columns(qs_total.reshape(HEADS, shard, 2 * HEAD), here, 2)
-    key_grad, value_grad = finish_columns(kv_total.reshape(HEADS, shard, 2 * HEAD), here, 2)
-    out_grad = finish_rows(out_total)
+    out_total = reduce_copies(
+        [mm_tn(split_rows(out_view, turn, m, [0]), grad_attn) for m in range(copies)]
+    )
+    query_grad, swish_grad = finish_line(qs_total.reshape(HEADS, shard, 2 * HEAD), here, 2)
+    key_grad, value_grad = finish_line(kv_total.reshape(HEADS, shard, 2 * HEAD), here, 2)
+    out_grad = lax.psum(after(out_total.astype(BF), down_grad), "seq").astype(F32)
 
     def placed(part, width):
         whole = jnp.zeros(part.shape[:-1] + (HEADS * width,), F32)
         return lax.dynamic_update_slice_in_dim(whole, part, here * width, part.ndim - 1)
 
+    up_sum = placed(up_part, SLOTS).reshape(RANK, HEADS, copies, -1).transpose(1, 2, 0, 3)
     sums = [
         gain_one_grad,
         down_low_part,
-        placed(up_part, SLOTS),
+        up_sum,
         placed(bias_part, SLOTS),
         placed(slot_part[0], HEAD),
         gain_two_grad,
     ]
-    flat = jnp.concatenate([a.reshape(-1) for a in sums]).astype(BF)
-    flat = lax.psum(flat, ("p", "r", "seq")).astype(F32)
+    flat = jnp.concatenate([a.reshape(HEADS, copies, -1) for a in sums], axis=2)
+    flat = sum_small(flat, here, turn)
     totals, offset = [], 0
     for a in sums:
-        totals.append(flat[offset : offset + a.size].reshape(a.shape))
-        offset += a.size
-    owner = here * copies + turn
-
-    def own(whole, axis):
-        size = whole.shape[axis] // owners
-        return lax.dynamic_slice_in_dim(whole, owner * size, size, axis)
+        size = a.size // owners
+        totals.append(flat[offset : offset + size])
+        offset += size
 
     return (
         result,
         grad_tokens,
-        own(totals[0], 0),
+        totals[0],
         query_grad,
         key_grad,
         value_grad,
-        own(totals[1], 0),
-        own(totals[2], 1),
-        own(totals[3], 0),
+        totals[1].reshape(shard, RANK),
+        totals[2].reshape(RANK, -1),
+        totals[3],
         swish_grad,
-        own(totals[4], 0),
+        totals[4],
         out_grad,
-        own(totals[5], 0),
+        totals[5],
         gate_grad,
         up_grad,
-        down_grad,
+        down_grad.astype(F32),
     )
 
 

time: 1300 us -> 1100 us (0.85)
  waiting for transfers between devices: 709 us -> 527 us
  local copies, waits for them, and re-layouts: 161 us -> 66.8 us
  other arithmetic: 69.2 us -> 112 us
  starting transfers between devices: 90.1 us -> 114 us
  Pallas kernels: 76.2 us -> 93 us
    ppermute x84 -> x72, waiting for transfers between devices: 538 us -> 249 us  [swap(): return lax.ppermute(value, axis, [(i, i ^ step) for i in range(count)])]
    ppermute x0 -> x12, waiting for transfers between devices: none -> 149 us  [the longest x4 92.8 us: line_sum(): lax.ppermute(total, 'seq', [(i + 1, i), (count - 2 - i, count - 1 - i)])]
    psum x1 -> x2, waiting for transfers between devices: 101 us -> 0.02 us  [the longest x1 0.02 us: body(): down_grad = lax.psum(down_total.astype(BF), 'seq')]
    ppermute x12, waiting for transfers between devices: 12.3 us -> 99.5 us  [chain(): total = total + lax.ppermute(sent, 'seq', [pair]).astype(F32)]
    unnamed x5 -> x6, waiting for transfers between devices: 57.6 us -> 0.76 us
    convert_element_type x5 -> x6, other arithmetic: 1.8 us -> 33.3 us  [the longest x1 9.65 us: finish_wide(): total.astype(BF).reshape(heads, count, rows // count, width)]
    unnamed x192 -> x162, local copies, waits for them, and re-layouts: 40.5 us -> 10.8 us
    reduce_scatter x0 -> x1, waiting for transfers between devices: none -> 28.6 us  [finish_wide(): part = lax.psum_scatter(spans, 'seq', scatter_dimension=0, tiled=False)]
  transfers between devices with their start and end apart: 100 -> 102, of which waited for: 32 -> 32; matrix products, arithmetic and copies ran while one was open for 26% -> 27% of each run, Pallas kernels for 5% -> 8%
where the time goes in v2:
time: 1100 us; the launch traced here: 1090 us
  waiting for transfers between devices  527 us (48%)
  matrix products  163 us (15%)
  starting transfers between devices  114 us (10%)
  other arithmetic  112 us (10%)
  Pallas kernels  93 us (8%)
  local copies, waits for them, and re-layouts  66.8 us (6%)
  between operations  16.8 us (2%)
    ppermute x72, waiting for transfers between devices, swap(): return lax.ppermute(value, axis, [(i, i ^ step) for i in range(count)])  249 us
    ppermute x12, waiting for transfers between devices, chain(): total = total + lax.ppermute(sent, 'seq', [pair]).astype(F32)  99.5 us
    ppermute x4, waiting for transfers between devices, line_sum(): lax.ppermute(total, 'seq', [(i + 1, i), (count - 2 - i, count - 1 - i)])  92.8 us
    ppermute x72, starting transfers between devices, swap(): return lax.ppermute(value, axis, [(i, i ^ step) for i in range(count)])  76.9 us
    dot_general x10, matrix products, mm_tn(): lax.dot_general(a, b, (((0,), (0,)), ((), ())), preferred_element_type=F32)  60.4 us
    ppermute x4, waiting for transfers between devices, line_sum(): lax.ppermute(sent, 'seq', [(i, i + 1), (count - 1 - i, count - 2 - i)])  56.5 us
    dot_general x6, matrix products, mm_nt(): lax.dot_general(a, b, (((1,), (1,)), ((), ())), preferred_element_type=F32)  54.6 us
    pallas_call x4, Pallas kernels, run(): pl.pallas_call(kernel, grid=(args[0].shape[0],), in_specs=specs, out_spec...  50.2 us
  transfers between devices with their start and end apart: 102, of which 32 were waited for; matrix products, arithmetic and copies ran while one was open for 27% of the time, Pallas kernels for 8%

profile of v2, /device:TPU:0, one launch (start us, length us, event | category | flops | bytes accessed | tf_op | source)
XLA Modules:
  0.0 1092.8 jit_solution(2576268791888165876)
XLA Ops:
  27.4 9.6 collective-permute-done.1
  38.5 21.2 %collective-permute-done.2 = f32[2,5409]{1,0:T(2,128)S(1)} collective-permute-done((f32[2,5409]{1,0:T(2,128)S(1)}, f32[2,5409]{1,0:T(2,128)S(1)}, u32[]{:S(2)}, u32[]{:S(2)}) %collective-permute-start.2) | collective-permute-done | bytes 43304 | tf_op jit(solution)/shard_map/ppermute | solution.py:346
  68.7 16.4 %collective-permute-done.8 = bf16[256,1024]{1,0:T(8,128)(2,1)} collective-permute-done((bf16[256,1024]{1,0:T(8,128)(2,1)}, bf16[256,1024]{1,0:T(8,128)(2,1)}, u32[]{:S(2)}, u32[]{:S(2)}) %collective-permute-start.8) | collective-permute-done | bytes 524320 | tf_op jit(solution)/shard_map/ppermute | solution.py:346
  106.5 5.6 shard_map.289
  112.1 6.8 fusion.2
  118.9 5.7 convolution_convert_fusion.7
  128.3 5.5 shard_map.290
  155.2 5.7 collective-permute-done.15
  174.8 6.1 shard_map.288
  182.4 8.4 fusion.74
  194.8 14.9 %shard_map.291 = (bf16[4,256,512]{2,1,0:T(8,128)(2,1)}, f32[4,256,512]{2,1,0:T(8,128)}, f32[4,256,64]{2,1,0:T(8,128)}, bf16[4,256,256]{2,1,0:T(8,128)(2,1)}) custom-call(f32[4,256,1024]{2,1,0:T(8,128)} %bitcast.233, bf16[4,256,1024]{2,1,0:T(8,128)(2,1)} %bitcast.236, f32[4,256,128]{2,1,0:T(8,128)} %bitcast.210, f32[4,64,1024]{2,1,0:T(8,128)} %pad_maximum_fusion.10.init_ref, ...), custom_call_target="tpu_custom_call" | custom-call | flops 12000000000 | bytes 16000000 | tf_op jit(solution)/shard_map/pallas_call | solution.py:258
  227.8 7.9 collective-permute-done.42.refs_4_
  235.8 7.5 collective-permute-done.27
  243.6 13.7 %fusion.58 = f32[1024,1408]{1,0:T(8,128)} fusion(bf16[1408,2048]{1,0:T(8,128)(2,1)} %all-gather.7.cloned.1.call-done, bf16[256,2048]{1,0:T(8,128)(2,1)} %collective-permute-done.32, bf16[256,2048]{1,0:T(8,128)(2,1)} %collective-permute-done.31, bf16[256,2048]{1,0:T(8,128)(2,1)} %collective-permute-done.30, bf16[256,2048]{1,0:T(8,128)(2,1)} %param.33, ...), kind=kOutput, calls=%fused_computation.238 | convolution fusion | flops 5926551552 | bytes 15732736 | tf_op jit(solution)/shard_map/dot_general | solution.py:23
  257.3 9.8 collective-permute-done.28
  284.9 13.6 %shard_map.292 = bf16[2048,2816]{1,0:T(8,128)(2,1)} custom-call(s32[32]{0:T(128)} %stack.252.spot_ref, bf16[4,64,2816]{2,1,0:T(8,128)(2,1)} %pad_maximum_fusion.8.refs_0_, bf16[4,64,2816]{2,1,0:T(8,128)(2,1)} %collective-permute-done.39.refs_1_, bf16[4,64,2816]{2,1,0:T(8,128)(2,1)} %collective-permute-done.40.refs_2_, ...), custom_call_target="tpu_custom_call" | custom-call | bytes 23068672 | tf_op jit(solution)/shard_map/pallas_call | solution.py:382
  303.0 21.8 %collective-permute-done.34 = bf16[256,2048]{1,0:T(8,128)(2,1)} collective-permute-done((bf16[256,2048]{1,0:T(8,128)(2,1)S(1)}, bf16[256,2048]{1,0:T(8,128)(2,1)}, u32[]{:S(2)}, u32[]{:S(2)}) %collective-permute-start.34) | collective-permute-done | bytes 1048608 | tf_op jit(solution)/shard_map/ppermute | solution.py:346
  324.8 18.6 %fusion.59 = f32[1024,2816]{1,0:T(8,128)S(1)} fusion(bf16[2048,2816]{1,0:T(8,128)(2,1)} %shard_map.292, bf16[256,2048]{1,0:T(8,128)(2,1)} %collective-permute-done.35, bf16[256,2048]{1,0:T(8,128)(2,1)} %collective-permute-done.34, bf16[256,2048]{1,0:T(8,128)(2,1)} %collective-permute-done.33, bf16[256,2048]{1,0:T(8,128)(2,1)S(1)} %multiply_convert_fusion.5), kind=kOutput, calls=%fused_computation.239 | convolution fusion | flops 11827937280 | bytes 27262976 | tf_op jit(solution)/shard_map/dot_general | solution.py:19
  343.3 7.2 multiply_convert_fusion.2
  350.6 16.8 %convolution_convert_fusion.1 = bf16[1024,2048]{1,0:T(8,128)(2,1)S(1)} fusion(bf16[2048,2816]{1,0:T(8,128)(2,1)} %shard_map.292, bf16[1024,1408]{1,0:T(8,128)(2,1)} %get-tuple-element.143, bf16[1024,1408]{1,0:T(8,128)(2,1)} %get-tuple-element.142), kind=kOutput, calls=%fused_computation.23 | convolution fusion | flops 11824791552 | bytes 21495808 | tf_op jit(solution)/shard_map/dot_general | solution.py:23
  376.6 10.3 convolution_convert_fusion
  386.9 9.3 fusion.57
  396.2 16.2 %fusion.15 = f32[1024,2816]{1,0:T(8,128)} fusion(bf16[1024,256]{1,0:T(8,128)(2,1)S(1)} %get-tuple-element.162, bf16[1024,256]{1,0:T(8,128)(2,1)S(1)} %get-tuple-element.163, bf16[1024,256]{1,0:T(8,128)(2,1)S(1)} %get-tuple-element.164, bf16[1024,256]{1,0:T(8,128)(2,1)} %get-tuple-element.165, bf16[1024,1408]{1,0:T(8,128)(2,1)} %get-tuple-element.143, ...), kind=kOutput, calls=%fused_computation.42 | convolution fusion | flops 5925502976 | bytes 19398656 | tf_op jit(solution)/shard_map/dot_general | solution.py:27
  428.1 8.2 convolution_convert_fusion.2
  436.3 14.4 %collective-permute-done.49 = bf16[256,2048]{1,0:T(8,128)(2,1)} collective-permute-done((bf16[256,2048]{1,0:T(8,128)(2,1)S(1)}, bf16[256,2048]{1,0:T(8,128)(2,1)}, u32[]{:S(2)}, u32[]{:S(2)}) %collective-permute-start.49) | collective-permute-done | bytes 1048608 | tf_op jit(solution)/shard_map/ppermute | solution.py:346
  450.7 22.6 %collective-permute-done.50 = bf16[256,2048]{1,0:T(8,128)(2,1)} collective-permute-done((bf16[256,2048]{1,0:T(8,128)(2,1)S(1)}, bf16[256,2048]{1,0:T(8,128)(2,1)}, u32[]{:S(2)}, u32[]{:S(2)}) %collective-permute-start.50) | collective-permute-done | bytes 1048608 | tf_op jit(solution)/shard_map/ppermute | solution.py:346
  473.3 6.2 add_convert_fusion.2
  487.8 9.7 add_convert_fusion
  497.5 5.7 copy.63
  503.3 19.8 %shard_map.293 = (bf16[4,256,1024]{2,1,0:T(8,128)(2,1)}, f32[4,256,1024]{2,1,0:T(8,128)}, f32[4,256,128]{2,1,0:T(8,128)}, f32[4,64,1024]{2,1,0:T(8,128)}, f32[8,512]{1,0:T(8,128)}) custom-call(f32[4,256,1024]{2,1,0:T(8,128)} %bitcast.234, bf16[4,256,1024]{2,1,0:T(8,128)(2,1)} %bitcast.237, f32[4,256,128]{2,1,0:T(8,128)} %bitcast.211, ...), custom_call_target="tpu_custom_call" | custom-call | flops 24000000000 | bytes 20000000 | tf_op jit(solution)/shard_map/pallas_call | solution.py:258
  543.0 68.7 %collective-permute-done.57 = bf16[4,64,512]{2,1,0:T(8,128)(2,1)} collective-permute-done((bf16[4,64,512]{2,1,0:T(8,128)(2,1)}, bf16[4,64,512]{2,1,0:T(8,128)(2,1)}, u32[]{:S(2)}, u32[]{:S(2)}) %collective-permute-start.57) | collective-permute-done | bytes 262176 | tf_op jit(solution)/shard_map/ppermute | solution.py:465
  624.1 25.5 %collective-permute-done.60 = bf16[4,64,512]{2,1,0:T(8,128)(2,1)} collective-permute-done((bf16[4,64,512]{2,1,0:T(8,128)(2,1)}, bf16[4,64,512]{2,1,0:T(8,128)(2,1)}, u32[]{:S(2)}, u32[]{:S(2)}) %collective-permute-start.60) | collective-permute-done | bytes 262176 | tf_op jit(solution)/shard_map/ppermute | solution.py:465
  651.8 9.9 shard_map.294
  667.2 6.8 fusion.77
  673.9 12.3 %add_convert_fusion.1 = bf16[1024,2048]{1,0:T(8,128)(2,1)} fusion(f32[1024,2048]{1,0:T(8,128)S(1)} %fusion.78, f32[1024,2048]{1,0:T(8,128)} %fusion.77, bf16[1024,1024]{1,0:T(8,128)(2,1)} %bitcast.239, bf16[2048,1024]{1,0:T(8,128)(2,1)} %shard_map.288), kind=kOutput, calls=%fused_computation.7 | convolution fusion | flops 4301258752 | bytes 27262976 | tf_op jit(solution)/shard_map/dot_general | solution.py:23
  696.9 5.6 convolution_convert_fusion.5
  706.7 10.7 collective-permute-done.63
  717.4 21.6 %collective-permute-done.62 = bf16[256,2048]{1,0:T(8,128)(2,1)} collective-permute-done((bf16[256,2048]{1,0:T(8,128)(2,1)}, bf16[256,2048]{1,0:T(8,128)(2,1)}, u32[]{:S(2)}, u32[]{:S(2)}) %collective-permute-start.62) | collective-permute-done | bytes 1048608 | tf_op jit(solution)/shard_map/ppermute | solution.py:346
  746.4 28.6 %reduce-scatter.2.cloned.1.call-done = bf16[1,4,64,2816]{3,2,1,0:T(8,128)(2,1)} async-done(((bf16[4,4,64,2816]{3,2,1,0:T(8,128)(2,1)}), bf16[1,4,64,2816]{3,2,1,0:T(8,128)(2,1)}) %reduce-scatter.2.cloned.1.call-update) | async-done | bytes 1441808 | tf_op jit(solution)/shard_map/reduce_scatter | solution.py:541
  799.5 5.4 add_convert_fusion.3
  807.3 27.8 %collective-permute-done.72 = bf16[2,256,1024]{2,1,0:T(8,128)(2,1)S(1)} collective-permute-done((bf16[2,256,1024]{2,1,0:T(8,128)(2,1)}, bf16[2,256,1024]{2,1,0:T(8,128)(2,1)S(1)}, u32[]{:S(2)}, u32[]{:S(2)}) %collective-permute-start.72) | collective-permute-done | bytes 1048608 | tf_op jit(solution)/shard_map/ppermute | solution.py:557
  837.2 28.6 %collective-permute-done.81 = bf16[2,256,1024]{2,1,0:T(8,128)(2,1)S(1)} collective-permute-done((bf16[2,256,1024]{2,1,0:T(8,128)(2,1)S(1)}, bf16[2,256,1024]{2,1,0:T(8,128)(2,1)S(1)}, u32[]{:S(2)}, u32[]{:S(2)}) %collective-permute-start.81) | collective-permute-done | bytes 1048608 | tf_op jit(solution)/shard_map/ppermute | solution.py:557
  871.6 46.3 %collective-permute-done.68 = f32[1,5408]{1,0:T(1,128)S(1)} collective-permute-done((f32[1,5408]{1,0:T(1,128)S(1)}, f32[1,5408]{1,0:T(1,128)S(1)}, u32[]{:S(2)}, u32[]{:S(2)}) %collective-permute-start.68) | collective-permute-done | bytes 21664 | tf_op jit(solution)/shard_map/ppermute | solution.py:346
  940.3 38.3 %collective-permute-done.76 = bf16[2,256,1024]{2,1,0:T(8,128)(2,1)} collective-permute-done((bf16[2,256,1024]{2,1,0:T(8,128)(2,1)S(1)}, bf16[2,256,1024]{2,1,0:T(8,128)(2,1)}, u32[]{:S(2)}, u32[]{:S(2)}) %collective-permute-start.76) | collective-permute-done | bytes 1048608 | tf_op jit(solution)/shard_map/ppermute | solution.py:563
  986.7 18.4 %collective-permute-done.74 = bf16[2,256,1024]{2,1,0:T(8,128)(2,1)} collective-permute-done((bf16[2,256,1024]{2,1,0:T(8,128)(2,1)S(1)}, bf16[2,256,1024]{2,1,0:T(8,128)(2,1)}, u32[]{:S(2)}, u32[]{:S(2)}) %collective-permute-start.74) | collective-permute-done | bytes 1048608 | tf_op jit(solution)/shard_map/ppermute | solution.py:563
  1008.6 18.9 %collective-permute-done.86 = bf16[2,256,1024]{2,1,0:T(8,128)(2,1)S(1)} collective-permute-done((bf16[2,256,1024]{2,1,0:T(8,128)(2,1)S(1)}, bf16[2,256,1024]{2,1,0:T(8,128)(2,1)S(1)}, u32[]{:S(2)}, u32[]{:S(2)}) %collective-permute-start.86) | collective-permute-done | bytes 1048608 | tf_op jit(solution)/shard_map/ppermute | solution.py:563
  1031.0 17.1 %collective-permute-done.84 = bf16[2,256,1024]{2,1,0:T(8,128)(2,1)S(1)} collective-permute-done((bf16[2,256,1024]{2,1,0:T(8,128)(2,1)S(1)}, bf16[2,256,1024]{2,1,0:T(8,128)(2,1)S(1)}, u32[]{:S(2)}, u32[]{:S(2)}) %collective-permute-start.84) | collective-permute-done | bytes 1048608 | tf_op jit(solution)/shard_map/ppermute | solution.py:563
  1077.8 7.9 shard_map.297
  (515 shorter events, 332.4 us)
Async XLA Ops:
  7.2 202.5 %all-gather.5.cloned.1.call-start = ((), (), s32[]{:S(2)}) async-start(), calls=%async_computation.1 | async-start | bytes 3145728 | tf_op jit(solution)/shard_map/all_gather | solution.py:632
  7.9 235.7 %all-gather.7.cloned.1.call-start = ((), (), s32[]{:S(2)}) async-start(), calls=%async_computation.2 | async-start | bytes 8650752 | tf_op jit(solution)/shard_map/all_gather | solution.py:633
  8.0 90.2 %collective-permute-start.6 = (bf16[256,2048]{1,0:T(8,128)(2,1)}, bf16[256,2048]{1,0:T(8,128)(2,1)S(1)}, u32[]{:S(2)}, u32[]{:S(2)}) collective-permute-start(bf16[256,2048]{1,0:T(8,128)(2,1)} %param.17), channel_id=1, source_target_pairs={{0,24},{8,16},{16,8},{24,0},{1,25},{9,17},{17,9},{25,1},{2,26},{10... | collective-permute-start | bytes 3145736 | tf_op jit(solution)/shard_map/ppermute | solution.py:346
  12.0 86.4 %collective-permute-start.5 = (bf16[256,2048]{1,0:T(8,128)(2,1)}, bf16[256,2048]{1,0:T(8,128)(2,1)}, u32[]{:S(2)}, u32[]{:S(2)}) collective-permute-start(bf16[256,2048]{1,0:T(8,128)(2,1)} %param.17), channel_id=1, source_target_pairs={{0,16},{8,24},{16,0},{24,8},{1,17},{9,25},{17,1},{25,9},{2,18},{10... | collective-permute-start | bytes 3145736 | tf_op jit(solution)/shard_map/ppermute | solution.py:346
  17.7 728.7 %all-reduce.3.cloned.1.call-start = ((), (), s32[]{:S(2)}) async-start(), calls=%async_computation.3 | async-start | bytes 5767168 | tf_op jit(solution)/shard_map/psum | solution.py:700
  89.3 63.5 %collective-permute-start.11 = (bf16[256,1024]{1,0:T(8,128)(2,1)}, bf16[256,1024]{1,0:T(8,128)(2,1)}, u32[]{:S(2)}, u32[]{:S(2)}) collective-permute-start(bf16[256,1024]{1,0:T(8,128)(2,1)} %pad_maximum_fusion.16), channel_id=1, source_target_pairs={{0,8},{8,0},{16,24},{24,16},{1,9},{9,1},{17,25},{25,17},{2,10},{10... | collective-permute-start | bytes 1572872 | tf_op jit(solution)/shard_map/ppermute | solution.py:346
  102.1 53.1 %collective-permute-start.13 = (bf16[256,1024]{1,0:T(8,128)(2,1)}, bf16[256,1024]{1,0:T(8,128)(2,1)}, u32[]{:S(2)}, u32[]{:S(2)}) collective-permute-start(bf16[256,1024]{1,0:T(8,128)(2,1)} %pad_maximum_fusion.17), channel_id=1, source_target_pairs={{0,16},{8,24},{16,0},{24,8},{1,17},{9,25},{17,1},{25,9},{2,18},{10... | collective-permute-start | bytes 1572872 | tf_op jit(solution)/shard_map/ppermute | solution.py:346
  103.6 44.0 %collective-permute-start.38 = (bf16[64,2816]{1,0:T(8,128)(2,1)}, bf16[64,2816]{1,0:T(8,128)(2,1)}, u32[]{:S(2)}, u32[]{:S(2)}) collective-permute-start(bf16[64,2816]{1,0:T(8,128)(2,1)} %pad_maximum_fusion.23), channel_id=1, source_target_pairs={{0,24},{8,16},{16,8},{24,0},{1,25},{9,17},{17,9},{25,1},{2,26},{10... | collective-permute-start | bytes 1081352 | tf_op jit(solution)/shard_map/ppermute | solution.py:346
  105.0 47.0 %collective-permute-start.37 = (bf16[64,2816]{1,0:T(8,128)(2,1)}, bf16[64,2816]{1,0:T(8,128)(2,1)}, u32[]{:S(2)}, u32[]{:S(2)}) collective-permute-start(bf16[64,2816]{1,0:T(8,128)(2,1)} %pad_maximum_fusion.22), channel_id=1, source_target_pairs={{0,16},{8,24},{16,0},{24,8},{1,17},{9,25},{17,1},{25,9},{2,18},{10... | collective-permute-start | bytes 1081352 | tf_op jit(solution)/shard_map/ppermute | solution.py:346
  169.3 56.7 %collective-permute-start.40 = (bf16[4,64,2816]{2,1,0:T(8,128)(2,1)}, bf16[4,64,2816]{2,1,0:T(8,128)(2,1)}, u32[]{:S(2)}, u32[]{:S(2)}) collective-permute-start(bf16[4,64,2816]{2,1,0:T(8,128)(2,1)} %pad_maximum_fusion.8.refs_0_), channel_id=1, source_target_pairs={{0,1},{1,0},{2,3},{3,2},{4,5},{5,4},{6,7},{7,6},{8,9},{9,8},{10,11... | collective-permute-start | bytes 4325384 | tf_op jit(solution)/shard_map/ppermute | solution.py:346
  172.4 63.3 %collective-permute-start.42 = (bf16[4,64,2816]{2,1,0:T(8,128)(2,1)}, bf16[4,64,2816]{2,1,0:T(8,128)(2,1)}, u32[]{:S(2)}, u32[]{:S(2)}) collective-permute-start(bf16[4,64,2816]{2,1,0:T(8,128)(2,1)} %pad_maximum_fusion.8.refs_0_), channel_id=1, source_target_pairs={{0,2},{1,3},{2,0},{3,1},{4,6},{5,7},{6,4},{7,5},{8,10},{9,11},{10,... | collective-permute-start | bytes 4325384 | tf_op jit(solution)/shard_map/ppermute | solution.py:346
  218.9 58.0 %collective-permute-start.39 = (bf16[4,64,2816]{2,1,0:T(8,128)(2,1)}, bf16[4,64,2816]{2,1,0:T(8,128)(2,1)}, u32[]{:S(2)}, u32[]{:S(2)}) collective-permute-start(bf16[4,64,2816]{2,1,0:T(8,128)(2,1)} %pad_maximum_fusion.8.refs_0_), channel_id=1, source_target_pairs={{0,4},{4,0},{1,5},{5,1},{2,6},{6,2},{3,7},{7,3},{8,12},{12,8},{9,1... | collective-permute-start | bytes 4325384 | tf_op jit(solution)/shard_map/ppermute | solution.py:346
  220.7 46.4 %collective-permute-start.28 = (bf16[256,2048]{1,0:T(8,128)(2,1)S(1)}, bf16[256,2048]{1,0:T(8,128)(2,1)}, u32[]{:S(2)}, u32[]{:S(2)}) collective-permute-start(bf16[256,2048]{1,0:T(8,128)(2,1)S(1)} %get-tuple-element.171), channel_id=1, source_target_pairs={{0,16},{8,24},{16,0},{24,8},{1,17},{9,25},{17,1},{25,9},{2,18},{10... | collective-permute-start | bytes 3145736 | tf_op jit(solution)/shard_map/ppermute | solution.py:346
  226.0 46.3 %collective-permute-start.29 = (bf16[256,2048]{1,0:T(8,128)(2,1)S(1)}, bf16[256,2048]{1,0:T(8,128)(2,1)}, u32[]{:S(2)}, u32[]{:S(2)}) collective-permute-start(bf16[256,2048]{1,0:T(8,128)(2,1)S(1)} %get-tuple-element.170), channel_id=1, source_target_pairs={{0,24},{8,16},{16,8},{24,0},{1,25},{9,17},{17,9},{25,1},{2,26},{10... | collective-permute-start | bytes 3145736 | tf_op jit(solution)/shard_map/ppermute | solution.py:346
  276.9 47.9 %collective-permute-start.34 = (bf16[256,2048]{1,0:T(8,128)(2,1)S(1)}, bf16[256,2048]{1,0:T(8,128)(2,1)}, u32[]{:S(2)}, u32[]{:S(2)}) collective-permute-start(bf16[256,2048]{1,0:T(8,128)(2,1)S(1)} %multiply_convert_fusion.5), channel_id=1, source_target_pairs={{0,16},{8,24},{16,0},{24,8},{1,17},{9,25},{17,1},{25,9},{2,18},{10... | collective-permute-start | bytes 3145736 | tf_op jit(solution)/shard_map/ppermute | solution.py:346
  277.7 47.1 %collective-permute-start.33 = (bf16[256,2048]{1,0:T(8,128)(2,1)S(1)}, bf16[256,2048]{1,0:T(8,128)(2,1)}, u32[]{:S(2)}, u32[]{:S(2)}) collective-permute-start(bf16[256,2048]{1,0:T(8,128)(2,1)S(1)} %multiply_convert_fusion.5), channel_id=1, source_target_pairs={{0,8},{8,0},{16,24},{24,16},{1,9},{9,1},{17,25},{25,17},{2,10},{10... | collective-permute-start | bytes 3145736 | tf_op jit(solution)/shard_map/ppermute | solution.py:346
  369.5 47.5 %collective-permute-start.47 = (bf16[256,2048]{1,0:T(8,128)(2,1)}, bf16[256,2048]{1,0:T(8,128)(2,1)S(1)}, u32[]{:S(2)}, u32[]{:S(2)}) collective-permute-start(bf16[256,2048]{1,0:T(8,128)(2,1)} %get-tuple-element.168), channel_id=1, source_target_pairs={{0,16},{8,24},{16,0},{24,8},{1,17},{9,25},{17,1},{25,9},{2,18},{10... | collective-permute-start | bytes 3145736 | tf_op jit(solution)/shard_map/ppermute | solution.py:346
  370.7 46.3 %collective-permute-start.48 = (bf16[256,2048]{1,0:T(8,128)(2,1)S(1)}, bf16[256,2048]{1,0:T(8,128)(2,1)S(1)}, u32[]{:S(2)}, u32[]{:S(2)}) collective-permute-start(bf16[256,2048]{1,0:T(8,128)(2,1)S(1)} %get-tuple-element.167), channel_id=1, source_target_pairs={{0,24},{8,16},{16,8},{24,0},{1,25},{9,17},{17,9},{25,1},{2,26},{10... | collective-permute-start | bytes 3145736 | tf_op jit(solution)/shard_map/ppermute | solution.py:346
  417.0 70.8 %collective-permute-start.92 = (bf16[1024,2816]{1,0:T(8,128)(2,1)}, bf16[1024,2816]{1,0:T(8,128)(2,1)}, u32[]{:S(2)}, u32[]{:S(2)}) collective-permute-start(bf16[1024,2816]{1,0:T(8,128)(2,1)} %convolution_convert_fusion), channel_id=1, source_target_pairs={{0,4},{4,0},{1,5},{5,1},{2,6},{6,2},{3,7},{7,3},{8,12},{12,8},{9,1... | collective-permute-start | bytes 17301512 | tf_op jit(solution)/shard_map/ppermute | solution.py:346
  419.1 54.2 %collective-permute-start.91 = (bf16[704,2048]{1,0:T(8,128)(2,1)}, bf16[704,2048]{1,0:T(8,128)(2,1)}, u32[]{:S(2)}, u32[]{:S(2)}) collective-permute-start(bf16[704,2048]{1,0:T(8,128)(2,1)} %dynamic-slice_convert_fusion), channel_id=1, source_target_pairs={{0,4},{4,0},{1,5},{5,1},{2,6},{6,2},{3,7},{7,3},{8,12},{12,8},{9,1... | collective-permute-start | bytes 8650760 | tf_op jit(solution)/shard_map/ppermute | solution.py:346
  425.9 47.4 %collective-permute-start.50 = (bf16[256,2048]{1,0:T(8,128)(2,1)S(1)}, bf16[256,2048]{1,0:T(8,128)(2,1)}, u32[]{:S(2)}, u32[]{:S(2)}) collective-permute-start(bf16[256,2048]{1,0:T(8,128)(2,1)S(1)} %get-tuple-element.77), channel_id=1, source_target_pairs={{0,16},{8,24},{16,0},{24,8},{1,17},{9,25},{17,1},{25,9},{2,18},{10... | collective-permute-start | bytes 3145736 | tf_op jit(solution)/shard_map/ppermute | solution.py:346
  426.7 46.6 %collective-permute-start.51 = (bf16[256,2048]{1,0:T(8,128)(2,1)S(1)}, bf16[256,2048]{1,0:T(8,128)(2,1)}, u32[]{:S(2)}, u32[]{:S(2)}) collective-permute-start(bf16[256,2048]{1,0:T(8,128)(2,1)S(1)} %get-tuple-element.77), channel_id=1, source_target_pairs={{0,24},{8,16},{16,8},{24,0},{1,25},{9,17},{17,9},{25,1},{2,26},{10... | collective-permute-start | bytes 3145736 | tf_op jit(solution)/shard_map/ppermute | solution.py:346
  479.5 295.5 %reduce-scatter.2.cloned.1.call-start = ((), (), s32[]{:S(2)}) async-start(), calls=%async_computation.5 | async-start | bytes 7208960 | tf_op jit(solution)/shard_map/reduce_scatter | solution.py:541
  503.2 556.2 %all-reduce.5.cloned.1.call-start = ((), (), s32[]{:S(2)}) async-start(), calls=%async_computation.4 | async-start | bytes 2097152 | tf_op jit(solution)/shard_map/psum | solution.py:747
  527.3 89.1 %collective-permute-start.54 = (bf16[256,2048]{1,0:T(8,128)(2,1)}, bf16[256,2048]{1,0:T(8,128)(2,1)}, u32[]{:S(2)}, u32[]{:S(2)}) collective-permute-start(bf16[256,2048]{1,0:T(8,128)(2,1)} %get-tuple-element.157), channel_id=1, source_target_pairs={{0,24},{8,16},{16,8},{24,0},{1,25},{9,17},{17,9},{25,1},{2,26},{10... | collective-permute-start | bytes 3145736 | tf_op jit(solution)/shard_map/ppermute | solution.py:346
  528.6 89.1 %collective-permute-start.53 = (bf16[256,2048]{1,0:T(8,128)(2,1)}, bf16[256,2048]{1,0:T(8,128)(2,1)}, u32[]{:S(2)}, u32[]{:S(2)}) collective-permute-start(bf16[256,2048]{1,0:T(8,128)(2,1)} %get-tuple-element.158), channel_id=1, source_target_pairs={{0,16},{8,24},{16,0},{24,8},{1,17},{9,25},{17,1},{25,9},{2,18},{10... | collective-permute-start | bytes 3145736 | tf_op jit(solution)/shard_map/ppermute | solution.py:346
  529.4 88.3 %collective-permute-start.52 = (bf16[256,2048]{1,0:T(8,128)(2,1)}, bf16[256,2048]{1,0:T(8,128)(2,1)}, u32[]{:S(2)}, u32[]{:S(2)}) collective-permute-start(bf16[256,2048]{1,0:T(8,128)(2,1)} %get-tuple-element.156), channel_id=1, source_target_pairs={{0,8},{8,0},{16,24},{24,16},{1,9},{9,1},{17,25},{25,17},{2,10},{10... | collective-permute-start | bytes 3145736 | tf_op jit(solution)/shard_map/ppermute | solution.py:346
  537.1 76.7 %collective-permute-start.59 = (bf16[4,64,512]{2,1,0:T(8,128)(2,1)}, bf16[4,64,512]{2,1,0:T(8,128)(2,1)}, u32[]{:S(2)}, u32[]{:S(2)}) collective-permute-start(bf16[4,64,512]{2,1,0:T(8,128)(2,1)} %get-tuple-element.190), channel_id=1, source_target_pairs={{2,1},{6,5},{10,9},{14,13},{18,17},{22,21},{26,25},{30,29}} | collective-permute-start | bytes 786440 | tf_op jit(solution)/shard_map/ppermute | solution.py:465
  538.5 73.3 %collective-permute-start.57 = (bf16[4,64,512]{2,1,0:T(8,128)(2,1)}, bf16[4,64,512]{2,1,0:T(8,128)(2,1)}, u32[]{:S(2)}, u32[]{:S(2)}) collective-permute-start(bf16[4,64,512]{2,1,0:T(8,128)(2,1)} %get-tuple-element.189), channel_id=1, source_target_pairs={{1,0},{5,4},{9,8},{13,12},{17,16},{21,20},{25,24},{29,28}} | collective-permute-start | bytes 786440 | tf_op jit(solution)/shard_map/ppermute | solution.py:465
  613.8 88.8 %collective-permute-start.70 = (bf16[1024,1024]{1,0:T(8,128)(2,1)}, bf16[1024,1024]{1,0:T(8,128)(2,1)}, u32[]{:S(2)}, u32[]{:S(2)}) collective-permute-start(bf16[1024,1024]{1,0:T(8,128)(2,1)} %convolution_convert_fusion.6), channel_id=1, source_target_pairs={{0,4},{4,0},{1,5},{5,1},{2,6},{6,2},{3,7},{7,3},{8,12},{12,8},{9,1... | collective-permute-start | bytes 6291464 | tf_op jit(solution)/shard_map/ppermute | solution.py:346
  691.3 47.7 %collective-permute-start.62 = (bf16[256,2048]{1,0:T(8,128)(2,1)}, bf16[256,2048]{1,0:T(8,128)(2,1)}, u32[]{:S(2)}, u32[]{:S(2)}) collective-permute-start(bf16[256,2048]{1,0:T(8,128)(2,1)} %get-tuple-element.155), channel_id=1, source_target_pairs={{0,16},{8,24},{16,0},{24,8},{1,17},{9,25},{17,1},{25,9},{2,18},{10... | collective-permute-start | bytes 3145736 | tf_op jit(solution)/shard_map/ppermute | solution.py:346
  693.1 45.9 %collective-permute-start.61 = (bf16[256,2048]{1,0:T(8,128)(2,1)}, bf16[256,2048]{1,0:T(8,128)(2,1)}, u32[]{:S(2)}, u32[]{:S(2)}) collective-permute-start(bf16[256,2048]{1,0:T(8,128)(2,1)} %get-tuple-element.153), channel_id=1, source_target_pairs={{0,8},{8,0},{16,24},{24,16},{1,9},{9,1},{17,25},{25,17},{2,10},{10... | collective-permute-start | bytes 3145736 | tf_op jit(solution)/shard_map/ppermute | solution.py:346
  702.5 97.0 %collective-permute-start.80 = (bf16[1024,1024]{1,0:T(8,128)(2,1)}, bf16[1024,1024]{1,0:T(8,128)(2,1)}, u32[]{:S(2)}, u32[]{:S(2)}) collective-permute-start(bf16[1024,1024]{1,0:T(8,128)(2,1)} %convolution_convert_fusion.5), channel_id=1, source_target_pairs={{0,4},{4,0},{1,5},{5,1},{2,6},{6,2},{3,7},{7,3},{8,12},{12,8},{9,1... | collective-permute-start | bytes 6291464 | tf_op jit(solution)/shard_map/ppermute | solution.py:346
  746.4 331.4 %all-gather.9.cloned.1.call-start = ((), (), s32[]{:S(2)}) async-start(), calls=%async_computation.6 | async-start | bytes 7208960 | tf_op jit(solution)/shard_map/all_gather | solution.py:543
  805.0 60.9 %collective-permute-start.81 = (bf16[2,256,1024]{2,1,0:T(8,128)(2,1)S(1)}, bf16[2,256,1024]{2,1,0:T(8,128)(2,1)S(1)}, u32[]{:S(2)}, u32[]{:S(2)}) collective-permute-start(bf16[2,256,1024]{2,1,0:T(8,128)(2,1)S(1)} %slice.248), channel_id=1, source_target_pairs={{0,1},{3,2},{4,5},{7,6},{8,9},{11,10},{12,13},{15,14},{16,17},{19,... | collective-permute-start | bytes 3145736 | tf_op jit(solution)/shard_map/ppermute | solution.py:557
  806.5 65.0 %collective-permute-start.67 = (f32[1,5408]{1,0:T(1,128)S(1)}, f32[1,5408]{1,0:T(1,128)S(1)}, u32[]{:S(2)}, u32[]{:S(2)}) collective-permute-start(f32[1,5408]{1,0:T(1,128)S(1)} %constant_dynamic-slice_fusion.8), channel_id=1, source_target_pairs={{0,4},{4,0},{1,5},{5,1},{2,6},{6,2},{3,7},{7,3},{8,12},{12,8},{9,1... | collective-permute-start | bytes 64904 | tf_op jit(solution)/shard_map/ppermute | solution.py:346
  806.6 116.4 %collective-permute-start.75 = (bf16[2,256,1024]{2,1,0:T(8,128)(2,1)S(1)}, bf16[2,256,1024]{2,1,0:T(8,128)(2,1)S(1)}, u32[]{:S(2)}, u32[]{:S(2)}) collective-permute-start(bf16[2,256,1024]{2,1,0:T(8,128)(2,1)S(1)} %copy-done.15), channel_id=1, source_target_pairs={{1,2},{2,1},{5,6},{6,5},{9,10},{10,9},{13,14},{14,13},{17,18},{18,... | collective-permute-start | bytes 3145736 | tf_op jit(solution)/shard_map/ppermute | solution.py:561
  836.5 89.9 %collective-permute-start.73 = (bf16[2,256,1024]{2,1,0:T(8,128)(2,1)S(1)}, bf16[2,256,1024]{2,1,0:T(8,128)(2,1)S(1)}, u32[]{:S(2)}, u32[]{:S(2)}) collective-permute-start(bf16[2,256,1024]{2,1,0:T(8,128)(2,1)S(1)} %add_select_fusion.3), channel_id=1, source_target_pairs={{1,2},{2,1},{5,6},{6,5},{9,10},{10,9},{13,14},{14,13},{17,18},{18,... | collective-permute-start | bytes 3145736 | tf_op jit(solution)/shard_map/ppermute | solution.py:561
  867.0 61.0 %collective-permute-start.82 = (bf16[2,256,1024]{2,1,0:T(8,128)(2,1)S(1)}, bf16[2,256,1024]{2,1,0:T(8,128)(2,1)S(1)}, u32[]{:S(2)}, u32[]{:S(2)}) collective-permute-start(bf16[2,256,1024]{2,1,0:T(8,128)(2,1)S(1)} %get-tuple-element.90), channel_id=1, source_target_pairs={{0,1},{3,2},{4,5},{7,6},{8,9},{11,10},{12,13},{15,14},{16,17},{19,... | collective-permute-start | bytes 3145736 | tf_op jit(solution)/shard_map/ppermute | solution.py:557
  871.5 46.4 %collective-permute-start.68 = (f32[1,5408]{1,0:T(1,128)S(1)}, f32[1,5408]{1,0:T(1,128)S(1)}, u32[]{:S(2)}, u32[]{:S(2)}) collective-permute-start(f32[1,5408]{1,0:T(1,128)S(1)} %dynamic-slice_add_fusion), channel_id=1, source_target_pairs={{0,1},{1,0},{2,3},{3,2},{4,5},{5,4},{6,7},{7,6},{8,9},{9,8},{10,11... | collective-permute-start | bytes 64904 | tf_op jit(solution)/shard_map/ppermute | solution.py:346
  923.4 55.3 %collective-permute-start.76 = (bf16[2,256,1024]{2,1,0:T(8,128)(2,1)S(1)}, bf16[2,256,1024]{2,1,0:T(8,128)(2,1)}, u32[]{:S(2)}, u32[]{:S(2)}) collective-permute-start(bf16[2,256,1024]{2,1,0:T(8,128)(2,1)S(1)} %add.739), channel_id=1, source_target_pairs={{1,0},{2,3},{5,4},{6,7},{9,8},{10,11},{13,12},{14,15},{17,16},{18,... | collective-permute-start | bytes 3145736 | tf_op jit(solution)/shard_map/ppermute | solution.py:563
  926.7 78.4 %collective-permute-start.74 = (bf16[2,256,1024]{2,1,0:T(8,128)(2,1)S(1)}, bf16[2,256,1024]{2,1,0:T(8,128)(2,1)}, u32[]{:S(2)}, u32[]{:S(2)}) collective-permute-start(bf16[2,256,1024]{2,1,0:T(8,128)(2,1)S(1)} %add.737), channel_id=1, source_target_pairs={{1,0},{2,3},{5,4},{6,7},{9,8},{10,11},{13,12},{14,15},{17,16},{18,... | collective-permute-start | bytes 3145736 | tf_op jit(solution)/shard_map/ppermute | solution.py:563
  929.2 54.3 %collective-permute-start.83 = (bf16[2,256,1024]{2,1,0:T(8,128)(2,1)}, bf16[2,256,1024]{2,1,0:T(8,128)(2,1)}, u32[]{:S(2)}, u32[]{:S(2)}) collective-permute-start(bf16[2,256,1024]{2,1,0:T(8,128)(2,1)} %add_select_fusion.1), channel_id=1, source_target_pairs={{1,2},{2,1},{5,6},{6,5},{9,10},{10,9},{13,14},{14,13},{17,18},{18,... | collective-permute-start | bytes 3145736 | tf_op jit(solution)/shard_map/ppermute | solution.py:561
  939.0 88.5 %collective-permute-start.86 = (bf16[2,256,1024]{2,1,0:T(8,128)(2,1)S(1)}, bf16[2,256,1024]{2,1,0:T(8,128)(2,1)S(1)}, u32[]{:S(2)}, u32[]{:S(2)}) collective-permute-start(bf16[2,256,1024]{2,1,0:T(8,128)(2,1)S(1)} %add.744), channel_id=1, source_target_pairs={{1,0},{2,3},{5,4},{6,7},{9,8},{10,11},{13,12},{14,15},{17,16},{18,... | collective-permute-start | bytes 3145736 | tf_op jit(solution)/shard_map/ppermute | solution.py:563
  980.8 71.6 %collective-permute-start.79 = (bf16[256,1024]{1,0:T(8,128)(2,1)S(1)}, bf16[256,1024]{1,0:T(8,128)(2,1)S(1)}, u32[]{:S(2)}, u32[]{:S(2)}) collective-permute-start(bf16[256,1024]{1,0:T(8,128)(2,1)S(1)} %get-tuple-element.204), channel_id=1, source_target_pairs={{0,24},{8,16},{16,8},{24,0},{1,25},{9,17},{17,9},{25,1},{2,26},{10... | collective-permute-start | bytes 1572872 | tf_op jit(solution)/shard_map/ppermute | solution.py:346
  983.3 78.9 %collective-permute-start.77 = (bf16[256,1024]{1,0:T(8,128)(2,1)}, bf16[256,1024]{1,0:T(8,128)(2,1)}, u32[]{:S(2)}, u32[]{:S(2)}) collective-permute-start(bf16[256,1024]{1,0:T(8,128)(2,1)} %get-tuple-element.203), channel_id=1, source_target_pairs={{0,8},{8,0},{16,24},{24,16},{1,9},{9,1},{17,25},{25,17},{2,10},{10... | collective-permute-start | bytes 1572872 | tf_op jit(solution)/shard_map/ppermute | solution.py:346
  985.4 62.7 %collective-permute-start.84 = (bf16[2,256,1024]{2,1,0:T(8,128)(2,1)S(1)}, bf16[2,256,1024]{2,1,0:T(8,128)(2,1)S(1)}, u32[]{:S(2)}, u32[]{:S(2)}) collective-permute-start(bf16[2,256,1024]{2,1,0:T(8,128)(2,1)S(1)} %add.742), channel_id=1, source_target_pairs={{1,0},{2,3},{5,4},{6,7},{9,8},{10,11},{13,12},{14,15},{17,16},{18,... | collective-permute-start | bytes 3145736 | tf_op jit(solution)/shard_map/ppermute | solution.py:563
  1007.4 54.9 %collective-permute-start.78 = (bf16[256,1024]{1,0:T(8,128)(2,1)}, bf16[256,1024]{1,0:T(8,128)(2,1)}, u32[]{:S(2)}, u32[]{:S(2)}) collective-permute-start(bf16[256,1024]{1,0:T(8,128)(2,1)} %get-tuple-element.202), channel_id=1, source_target_pairs={{0,16},{8,24},{16,0},{24,8},{1,17},{9,25},{17,1},{25,9},{2,18},{10... | collective-permute-start | bytes 1572872 | tf_op jit(solution)/shard_map/ppermute | solution.py:346
  (130 other events, 2107.7 us)
Sparse Core Ops, SparseCore 0:
  9.5 13.2 all-gather.4
  24.4 17.1 all-gather.6
  479.6 170.9 all-reduce.2
  653.3 121.6 reduce-scatter.1
  777.2 68.9 all-reduce.4
  848.2 139.8 all-gather.8

commit v3 on v2

--- a/solution.py
+++ b/solution.py
@@ -482,11 +482,12 @@
     return jnp.concatenate(cuts, axis=1)
 
 
-def reduce_copies(parts):
-    total = parts[0]
-    for m in range(1, len(parts)):
-        total = total + swap(parts[m].astype(BF), "r", m).astype(F32)
-    return total
+def sum_copies(own, away):
+    got = [swap(part, "r", m + 1) for m, part in enumerate(away)]
+    total = own()
+    for part in got:
+        total = total + part.astype(F32)
+    return total.astype(BF)
 
 
 def gather_seq(value):
@@ -534,43 +535,35 @@
     )(spots, *([parts] * spans))
 
 
-def finish_wide(total, here, n_out):
-    heads, rows, width = total.shape
+def inward(value):
     count = lax.axis_size("seq")
-    spans = total.astype(BF).reshape(heads, count, rows // count, width).transpose(1, 0, 2, 3)
-    part = lax.psum_scatter(spans, "seq", scatter_dimension=0, tiled=False)
-    got = jnp.stack([part[0]] + [swap(part[k], "p", k) for k in range(1, HEADS)])
-    whole = lax.all_gather(got, "seq", axis=0, tiled=False)
-    return assemble(whole, [here ^ k for k in range(HEADS)], n_out)
-
-
-def line_sum(chunks):
-    count = lax.axis_size("seq")
-    half, spot = count // 2, lax.axis_index("seq")
-    totals, last = [], None
-    for chunk in chunks:
-        value = chunk.astype(BF)
-        if last is not None:
-            value = after(value, last)
-        sent = value
-        for i in range(half - 1):
-            got = lax.ppermute(sent, "seq", [(i, i + 1), (count - 1 - i, count - 2 - i)])
-            last = got if i == 0 else last
-            inner = (spot == i + 1) | (spot == count - 2 - i)
-            sent = jnp.where(inner, value + got, sent)
-        total = sent + lax.ppermute(sent, "seq", [(half - 1, half), (half, half - 1)])
-        for i in range(half - 2, -1, -1):
-            got = lax.ppermute(total, "seq", [(i + 1, i), (count - 2 - i, count - 1 - i)])
-            outer = (spot == i) | (spot == count - 1 - i)
-            total = jnp.where(outer, got, total)
-        totals.append(total)
-    return totals
-
-
-def finish_line(total, here, n_out):
-    near, far = line_sum([total[1::2], total[0::2]])
+    for i in range(count // 2 - 1):
+        value = value + lax.ppermute(value, "seq", [(i, i + 1), (count - 1 - i, count - 2 - i)])
+    return value
+
+
+def across(value):
+    half = lax.axis_size("seq") // 2
+    return value + lax.ppermute(value, "seq", [(half - 1, half), (half, half - 1)])
+
+
+def outward(total):
+    count, spot = lax.axis_size("seq"), lax.axis_index("seq")
+    for i in range(count // 2 - 2, -1, -1):
+        got = lax.ppermute(total, "seq", [(i + 1, i), (count - 2 - i, count - 1 - i)])
+        total = jnp.where((spot == i) | (spot == count - 1 - i), got, total)
+    return total
+
+
+def spread_line(near, far, here, n_out):
     got = [far[0], swap(near[0], "p", 1), swap(far[1], "p", 2), swap(near[1], "p", 3)]
     return assemble(jnp.stack(got)[None], [here ^ k for k in range(HEADS)], n_out)
+
+
+def swap_diagonal(part):
+    count = lax.axis_size("seq")
+    sends = [(p * count + z, (p ^ z) * count + z) for p in range(HEADS) for z in range(count)]
+    return lax.ppermute(part, ("p", "seq"), sends)
 
 
 def body(
@@ -624,7 +617,7 @@
     mask_own = masks[0][:, None]
 
     token_blocks = gather_heads(tokens)
-    weight_kv, kv_pieces = head_columns([key_proj, value_proj], here)
+    weight_kv, kv_pieces = head_columns_seq([key_proj, value_proj], here)
     late = lax.optimization_barrier((query_proj, swish_proj, mlp_gate, mlp_up) + tuple(kv_pieces))
     weight_qs, qs_pieces = head_columns(late[:2], here)
     weight_gu, gu_pieces = head_columns_seq(late[2:4], here)
@@ -667,45 +660,74 @@
     grad_gate = (grad_act * up_pre * silu_slope(gate_pre)).astype(BF)
     grad_up = (grad_act * jax.nn.silu(gate_pre)).astype(BF)
     grad_gu = jnp.concatenate([grad_gate, grad_up], axis=1)
+    order = [here ^ k for k in range(HEADS)]
+    hops = range(1, copies)
+    down_rows = mlp_down.shape[0]
+
+    def down_cut(m):
+        return lax.dynamic_slice_in_dim(hidden, (turn ^ m) * down_rows, down_rows, 1)
+
+    down_away = [mm_tn(down_cut(m), grad_mlp).astype(BF) for m in hops]
+    grad_gu, *down_away = lax.optimization_barrier((grad_gu,) + tuple(down_away))
+    two_view = normed_two.reshape(group, HEADS, copies, shard)
+    gu_away = [mm_tn(split_rows(two_view, turn, m, order), grad_gu).astype(BF) for m in hops]
+    down_total = sum_copies(lambda: mm_tn(down_cut(0), grad_mlp), down_away)
+    down_half = down_rows // 2
+    grad_gu, *gu_away, down_total = lax.optimization_barrier((grad_gu, *gu_away, down_total))
+    down_near, down_far = inward(down_total[:down_half]), inward(down_total[down_half:])
     two_part = mm_nt(grad_gu, weight_gu).astype(BF).reshape(HEADS, rows, D)
-    two_view = normed_two.reshape(group, HEADS, copies, shard)
-    order = [here ^ k for k in range(HEADS)]
-    gu_parts = [mm_tn(split_rows(two_view, turn, m, order), grad_gu) for m in range(copies)]
-    gu_parts = [gu_parts[0]] + [part.astype(BF) for part in gu_parts[1:]]
-    down_part = mm_tn(hidden, grad_mlp)
-    grad_norm_two, down_part, *gu_parts = scatter_heads(
-        [two_part[k] for k in range(HEADS)], down_part, *gu_parts
-    )
+    gu_total = sum_copies(
+        lambda: mm_tn(split_rows(two_view, turn, 0, order), after(grad_gu, two_part)), gu_away
+    )
+    grad_norm_two, gu_total, down_near = scatter_heads(
+        [two_part[k] for k in range(HEADS)], gu_total, down_near
+    )
+    gu_part = lax.psum_scatter(
+        gu_total.reshape(HEADS, shard, 2 * hidden_width), "seq", scatter_dimension=0, tiled=True
+    )
+    down_near = across(down_near)
     gain_two_grad = jnp.sum(grad_norm_two * hat_two, axis=0)
     grad_rows = grad_out.astype(F32)
     grad_resid = grad_rows + norm_back(grad_norm_two * gain_two, hat_two, scale_two)
     grad_attn_own = (mask_own * grad_resid).astype(BF)
     attn_blocks = gather_heads(grad_attn_own)
     mlp_part = mm(hidden, weight_down).astype(BF)
-    mlp_part, *attn_blocks = lax.optimization_barrier((mlp_part,) + tuple(attn_blocks))
+    mlp_part, down_near, down_far, *attn_blocks = lax.optimization_barrier(
+        (mlp_part, down_near, down_far) + tuple(attn_blocks)
+    )
+    down_grad = jnp.concatenate([outward(down_near), outward(across(down_far))])
     grad_attn = jnp.concatenate(attn_blocks)
     mlp_part = mlp_part.reshape(HEADS, rows, D)
     mlp_out = scatter_heads([mlp_part[k] for k in range(HEADS)])
     result = (residual + mask_own * mlp_out).astype(BF)
 
-    gu_total = reduce_copies(gu_parts).reshape(HEADS, shard, 2 * hidden_width)
-    down_rows = mlp_down.shape[0]
-    down_total = reduce_copies(
-        [
-            lax.dynamic_slice_in_dim(down_part, (turn ^ m) * down_rows, down_rows, 0)
-            for m in range(copies)
-        ]
-    )
-    gate_grad, up_grad = finish_wide(gu_total, here, 2)
-    down_grad = lax.psum(down_total.astype(BF), "seq")
-
     grad_gated = mm_nt(grad_attn, weight_out).reshape(HEADS, rows, HEAD)
     grad_qs, grad_kv, grad_li, adjoint, slot_part = mixer_backward(
         qs, kv, li, init, gain_head8, mixer_out, probs, mix, grad_gated
     )
+    adjoint, gu_part = lax.optimization_barrier((adjoint, gu_part))
+    gu_part = swap_diagonal(gu_part)
+    one_view = normed.reshape(group, HEADS, copies, shard)
+    one_views = [split_rows(one_view, turn, m, order) for m in range(copies)]
+    out_view = gated.reshape(group, 1, copies, shard)
+    out_views = [split_rows(out_view, turn, m, [0]) for m in range(copies)]
+
+    def weight_grad(views, right):
+        return sum_copies(
+            lambda: mm_tn(views[0], right), [mm_tn(views[m], right).astype(BF) for m in hops]
+        )
+
+    grad_qs = grad_qs.reshape(group, 2 * HEAD)
+    out_total = weight_grad(out_views, grad_attn)
+    qs_total = weight_grad(one_views, grad_qs)
     ends = chain_pair(adjoint, decay, False)
+    ends, gu_part, out_total, qs_total = lax.optimization_barrier(
+        (ends, gu_part, out_total, qs_total)
+    )
+    gu_whole = lax.all_gather(gu_part, "seq", axis=0, tiled=True)
+    qs_total = qs_total.reshape(HEADS, shard, 2 * HEAD)
+    out_total, qs_near, qs_far = inward(out_total), inward(qs_total[1::2]), inward(qs_total[0::2])
     grad_kv, grad_li = mixer_finish(kv, li, init, ends, grad_kv, grad_li)
-    grad_qs = grad_qs.reshape(group, 2 * HEAD)
     grad_kv = grad_kv.reshape(group, 2 * HEAD)
     grad_li = grad_li.reshape(group, 2 * SLOTS)
     grad_decay = (
@@ -728,23 +750,22 @@
         .astype(BF)
         .reshape(HEADS, rows, D)
     )
-    grad_norm_one = scatter_heads([one_part[k] for k in range(HEADS)])
+    kv_total = weight_grad(one_views, grad_kv)
+    grad_norm_one, kv_total, out_total, qs_near, qs_far = scatter_heads(
+        [one_part[k] for k in range(HEADS)], kv_total, out_total, qs_near, qs_far
+    )
+    kv_total = kv_total.reshape(HEADS, shard, 2 * HEAD)
+    kv_near, kv_far = inward(kv_total[1::2]), inward(kv_total[0::2])
+    out_grad = outward(across(out_total)).astype(F32)
+    qs_near, qs_far = outward(across(qs_near)), outward(across(qs_far))
+    kv_near, kv_far = outward(across(kv_near)), outward(across(kv_far))
+    gate_grad, up_grad = assemble(gu_whole[None], order, 2)
+    query_grad, swish_grad = spread_line(qs_near, qs_far, here, 2)
+    key_grad, value_grad = spread_line(kv_near, kv_far, here, 2)
     scale_one = inverse_rms(tokens_f)
     hat_one = tokens_f * scale_one
     gain_one_grad = jnp.sum(grad_norm_one * hat_one, axis=0)
     grad_tokens = (grad_resid + norm_back(grad_norm_one * gain_one, hat_one, scale_one)).astype(BF)
-
-    one_view = normed.reshape(group, HEADS, copies, shard)
-    one_views = [split_rows(one_view, turn, m, order) for m in range(copies)]
-    qs_total = reduce_copies([mm_tn(v, grad_qs) for v in one_views])
-    kv_total = reduce_copies([mm_tn(v, grad_kv) for v in one_views])
-    out_view = gated.reshape(group, 1, copies, shard)
-    out_total = reduce_copies(
-        [mm_tn(split_rows(out_view, turn, m, [0]), grad_attn) for m in range(copies)]
-    )
-    query_grad, swish_grad = finish_line(qs_total.reshape(HEADS, shard, 2 * HEAD), here, 2)
-    key_grad, value_grad = finish_line(kv_total.reshape(HEADS, shard, 2 * HEAD), here, 2)
-    out_grad = lax.psum(after(out_total.astype(BF), down_grad), "seq").astype(F32)
 
     def placed(part, width):
         whole = jnp.zeros(part.shape[:-1] + (HEADS * width,), F32)

time: 1100 us -> 1220 us (1.11)
  waiting for transfers between devices: 527 us -> 634 us
  starting transfers between devices: 114 us -> 136 us
    ppermute x72, waiting for transfers between devices: 249 us -> 361 us  [swap(): return lax.ppermute(value, axis, [(i, i ^ step) for i in range(count)])]
    ppermute x12 -> x22, waiting for transfers between devices: 149 us -> 243 us  [the longest x7 190 us: outward(): lax.ppermute(total, 'seq', [(i + 1, i), (count - 2 - i, count - 1 - i)])]
    ppermute x12, waiting for transfers between devices: 99.5 us -> 13.2 us  [chain(): total = total + lax.ppermute(sent, 'seq', [pair]).astype(F32)]
    ppermute x12 -> x22, starting transfers between devices: 19.6 us -> 41.2 us  [the longest x7 19.7 us: inward(): lax.ppermute(value, 'seq', [(i, i + 1), (count - 1 - i, count - 2 - i)])]
    add x4 -> x11, other arithmetic: 4.68 us -> 24.1 us  [the longest x7 12.5 us: across(): value + lax.ppermute(value, 'seq', [(half - 1, half), (half, half - 1)])]
    convert_element_type x3 -> x1, other arithmetic: 18.7 us -> 1.46 us  [body(): out_grad = outward(across(out_total)).astype(F32)]
    reduce_scatter x1, waiting for transfers between devices: 28.6 us -> 14.7 us  [body(): lax.psum_scatter(gu_total.reshape(HEADS, shard, 2 * hidden_width), 'seq',...]
    dot_general x10 -> x11, matrix products: 60.4 us -> 61 us  [mm_tn(): lax.dot_general(a, b, (((0,), (0,)), ((), ())), preferred_element_type=F32)]
  transfers between devices with their start and end apart: 102 -> 110, of which waited for: 32 -> 35; matrix products, arithmetic and copies ran while one was open for 27% -> 23% of each run, Pallas kernels for 8% -> 7%
where the time goes in v3:
time: 1220 us
  waiting for transfers between devices  634 us (52%)
  matrix products  169 us (14%)
  starting transfers between devices  136 us (11%)
  other arithmetic  108 us (9%)
  Pallas kernels  92.1 us (8%)
  local copies, waits for them, and re-layouts  60.6 us (5%)
  between operations  16.6 us (1%)
    ppermute x72, waiting for transfers between devices, swap(): return lax.ppermute(value, axis, [(i, i ^ step) for i in range(count)])  361 us
    ppermute x7, waiting for transfers between devices, outward(): lax.ppermute(total, 'seq', [(i + 1, i), (count - 2 - i, count - 1 - i)])  190 us
    ppermute x72, starting transfers between devices, swap(): return lax.ppermute(value, axis, [(i, i ^ step) for i in range(count)])  79.3 us
    dot_general x11, matrix products, mm_tn(): lax.dot_general(a, b, (((0,), (0,)), ((), ())), preferred_element_type=F32)  61 us
    dot_general x6, matrix products, mm_nt(): lax.dot_general(a, b, (((1,), (1,)), ((), ())), preferred_element_type=F32)  54.9 us
    ppermute x7, waiting for transfers between devices, inward(): lax.ppermute(value, 'seq', [(i, i + 1), (count - 1 - i, count - 2 - i)])  53.3 us
    dot_general x6, matrix products, mm(): lax.dot_general(a, b, (((1,), (0,)), ((), ())), preferred_element_type=F32)  51.5 us
    pallas_call x4, Pallas kernels, run(): pl.pallas_call(kernel, grid=(args[0].shape[0],), in_specs=specs, out_spec...  49.6 us
  transfers between devices with their start and end apart: 110, of which 35 were waited for; matrix products, arithmetic and copies ran while one was open for 23% of the time, Pallas kernels for 7%

profile of v3, /device:TPU:0, one launch (start us, length us, event | category | flops | bytes accessed | tf_op | source)
XLA Modules:
  0.0 1215.5 jit_solution(7202303960328741157)
XLA Ops:
  25.6 10.1 collective-permute-done.1
  66.8 11.8 collective-permute-done.20.refs_4_
  84.2 6.8 fusion.2
  101.3 5.6 shard_map.289
  106.9 7.9 convolution_convert_fusion.8
  114.8 5.5 shard_map.290
  146.8 5.2 collective-permute-done.41
  159.5 5.6 shard_map.288
  166.6 8.4 fusion.83
  175.7 43.0 %collective-permute-done.45.refs_4_ = bf16[4,64,2816]{2,1,0:T(8,128)(2,1)} collective-permute-done((bf16[4,64,2816]{2,1,0:T(8,128)(2,1)}, bf16[4,64,2816]{2,1,0:T(8,128)(2,1)}, u32[]{:S(2)}, u32[]{:S(2)}) %collective-permute-start.45) | collective-permute-done | bytes 1441824 | tf_op jit(solution)/shard_map/ppermute | solution.py:346
  224.0 14.9 %shard_map.291 = (bf16[4,256,512]{2,1,0:T(8,128)(2,1)}, f32[4,256,512]{2,1,0:T(8,128)}, f32[4,256,64]{2,1,0:T(8,128)}, bf16[4,256,256]{2,1,0:T(8,128)(2,1)}) custom-call(f32[4,256,1024]{2,1,0:T(8,128)} %bitcast.220, bf16[4,256,1024]{2,1,0:T(8,128)(2,1)} %bitcast.223, f32[4,256,128]{2,1,0:T(8,128)} %bitcast.193, f32[4,64,1024]{2,1,0:T(8,128)} %pad_maximum_fusion.6.init_ref, ...), custom_call_target="tpu_custom_call" | custom-call | flops 12000000000 | bytes 16000000 | tf_op jit(solution)/shard_map/pallas_call | solution.py:258
  255.8 13.7 %fusion.65 = f32[1024,1408]{1,0:T(8,128)} fusion(bf16[1408,2048]{1,0:T(8,128)(2,1)} %all-gather.6.cloned.1.call-done, bf16[256,2048]{1,0:T(8,128)(2,1)} %collective-permute-done.35, bf16[256,2048]{1,0:T(8,128)(2,1)} %collective-permute-done.34, bf16[256,2048]{1,0:T(8,128)(2,1)} %collective-permute-done.33, bf16[256,2048]{1,0:T(8,128)(2,1)} %param.33, ...), kind=kOutput, calls=%fused_computation.234 | convolution fusion | flops 5926551552 | bytes 15732736 | tf_op jit(solution)/shard_map/dot_general | solution.py:23
  273.4 22.6 %collective-permute-done.31 = bf16[256,2048]{1,0:T(8,128)(2,1)} collective-permute-done((bf16[256,2048]{1,0:T(8,128)(2,1)S(1)}, bf16[256,2048]{1,0:T(8,128)(2,1)}, u32[]{:S(2)}, u32[]{:S(2)}) %collective-permute-start.31) | collective-permute-done | bytes 1048608 | tf_op jit(solution)/shard_map/ppermute | solution.py:346
  303.1 13.7 %shard_map.292 = bf16[2048,2816]{1,0:T(8,128)(2,1)} custom-call(s32[32]{0:T(128)} %stack.279.spot_ref, bf16[4,64,2816]{2,1,0:T(8,128)(2,1)} %pad_maximum_fusion.5.refs_0_, bf16[4,64,2816]{2,1,0:T(8,128)(2,1)} %collective-permute-done.42.refs_1_, bf16[4,64,2816]{2,1,0:T(8,128)(2,1)} %collective-permute-done.43.refs_2_, ...), custom_call_target="tpu_custom_call" | custom-call | bytes 23068672 | tf_op jit(solution)/shard_map/pallas_call | solution.py:382
  316.8 9.0 collective-permute-done.36
  325.7 23.0 %collective-permute-done.38 = bf16[256,2048]{1,0:T(8,128)(2,1)} collective-permute-done((bf16[256,2048]{1,0:T(8,128)(2,1)S(1)}, bf16[256,2048]{1,0:T(8,128)(2,1)}, u32[]{:S(2)}, u32[]{:S(2)}) %collective-permute-start.38) | collective-permute-done | bytes 1048608 | tf_op jit(solution)/shard_map/ppermute | solution.py:346
  348.8 21.2 %fusion.64 = f32[1024,2816]{1,0:T(8,128)} fusion(bf16[2048,2816]{1,0:T(8,128)(2,1)} %shard_map.292, bf16[256,2048]{1,0:T(8,128)(2,1)} %collective-permute-done.38, bf16[256,2048]{1,0:T(8,128)(2,1)} %collective-permute-done.37, bf16[256,2048]{1,0:T(8,128)(2,1)} %collective-permute-done.36, bf16[256,2048]{1,0:T(8,128)(2,1)S(1)} %multiply_convert_fusion.5), kind=kOutput, calls=%fused_computation.233 | convolution fusion | flops 11827937280 | bytes 27262976 | tf_op jit(solution)/shard_map/dot_general | solution.py:19
  370.0 7.2 multiply_convert_fusion.2
  380.1 7.4 convolution_convert_fusion.4
  391.9 8.5 convolution_convert_fusion
  400.4 6.9 add_convert_fusion.2
  415.2 15.5 %convolution_convert_fusion.1 = bf16[1024,2048]{1,0:T(8,128)(2,1)} fusion(bf16[1024,2816]{1,0:T(8,128)(2,1)} %pad_maximum_fusion, bf16[2048,2816]{1,0:T(8,128)(2,1)S(1)} %bitcast.173), kind=kOutput, calls=%fused_computation.21 | convolution fusion | flops 11813257216 | bytes 21495808 | tf_op jit(solution)/shard_map/dot_general | solution.py:23
  435.4 8.4 collective-permute-done.54
  445.8 28.0 %collective-permute-done.56 = bf16[352,2048]{1,0:T(8,128)(2,1)} collective-permute-done((bf16[352,2048]{1,0:T(8,128)(2,1)}, bf16[352,2048]{1,0:T(8,128)(2,1)}, u32[]{:S(2)}, u32[]{:S(2)}) %collective-permute-start.56) | collective-permute-done | bytes 1441824 | tf_op jit(solution)/shard_map/ppermute | solution.py:541
  477.6 10.2 add_convert_fusion
  506.2 8.6 convolution_convert_fusion.2
  519.0 8.0 collective-permute-done.57
  527.0 21.2 %collective-permute-done.58 = bf16[256,2048]{1,0:T(8,128)(2,1)} collective-permute-done((bf16[256,2048]{1,0:T(8,128)(2,1)S(1)}, bf16[256,2048]{1,0:T(8,128)(2,1)}, u32[]{:S(2)}, u32[]{:S(2)}) %collective-permute-start.58) | collective-permute-done | bytes 1048608 | tf_op jit(solution)/shard_map/ppermute | solution.py:346
  565.6 20.0 %shard_map.293 = (bf16[4,256,1024]{2,1,0:T(8,128)(2,1)}, f32[4,256,1024]{2,1,0:T(8,128)}, f32[4,256,128]{2,1,0:T(8,128)}, f32[4,64,1024]{2,1,0:T(8,128)}, f32[8,512]{1,0:T(8,128)}) custom-call(f32[4,256,1024]{2,1,0:T(8,128)} %bitcast.221, bf16[4,256,1024]{2,1,0:T(8,128)(2,1)} %bitcast.224, f32[4,256,128]{2,1,0:T(8,128)} %bitcast.194, ...), custom_call_target="tpu_custom_call" | custom-call | flops 24000000000 | bytes 20000000 | tf_op jit(solution)/shard_map/pallas_call | solution.py:258
  585.6 8.5 fusion.86
  600.3 7.6 collective-permute-done.62
  611.9 14.7 %reduce-scatter.2.cloned.1.call-done = bf16[1,256,2816]{2,1,0:T(8,128)(2,1)} async-done(((bf16[4,256,2816]{2,1,0:T(8,128)(2,1)}), bf16[1,256,2816]{2,1,0:T(8,128)(2,1)}) %reduce-scatter.2.cloned.1.call-update) | async-done | bytes 1441808 | tf_op jit(solution)/shard_map/reduce_scatter | solution.py:685
  637.6 87.0 %collective-permute-done.103 = bf16[352,2048]{1,0:T(8,128)(2,1)} collective-permute-done((bf16[352,2048]{1,0:T(8,128)(2,1)}, bf16[352,2048]{1,0:T(8,128)(2,1)}, u32[]{:S(2)}, u32[]{:S(2)}) %collective-permute-start.103) | collective-permute-done | bytes 1441824 | tf_op jit(solution)/shard_map/ppermute | solution.py:553
  736.9 18.5 %collective-permute-done.105 = bf16[352,2048]{1,0:T(8,128)(2,1)S(1)} collective-permute-done((bf16[352,2048]{1,0:T(8,128)(2,1)S(1)}, bf16[352,2048]{1,0:T(8,128)(2,1)S(1)}, u32[]{:S(2)}, u32[]{:S(2)}) %collective-permute-start.105) | collective-permute-done | bytes 1441824 | tf_op jit(solution)/shard_map/ppermute | solution.py:553
  775.9 9.2 shard_map.294
  785.2 5.3 convolution_convert_fusion.6
  797.8 12.2 %add_convert_fusion.1 = bf16[1024,2048]{1,0:T(8,128)(2,1)} fusion(f32[1024,2048]{1,0:T(8,128)S(1)} %fusion.87, f32[1024,2048]{1,0:T(8,128)} %fusion.86, bf16[1024,1024]{1,0:T(8,128)(2,1)} %bitcast.230, bf16[2048,1024]{1,0:T(8,128)(2,1)} %shard_map.289), kind=kOutput, calls=%fused_computation.7 | convolution fusion | flops 4301258752 | bytes 27262976 | tf_op jit(solution)/shard_map/dot_general | solution.py:23
  820.0 16.8 %collective-permute-done.76 = bf16[256,2048]{1,0:T(8,128)(2,1)} collective-permute-done((bf16[256,2048]{1,0:T(8,128)(2,1)}, bf16[256,2048]{1,0:T(8,128)(2,1)}, u32[]{:S(2)}, u32[]{:S(2)}) %collective-permute-start.76) | collective-permute-done | bytes 1048608 | tf_op jit(solution)/shard_map/ppermute | solution.py:541
  849.8 33.1 %collective-permute-done.73 = bf16[256,2048]{1,0:T(8,128)(2,1)S(1)} collective-permute-done((bf16[256,2048]{1,0:T(8,128)(2,1)}, bf16[256,2048]{1,0:T(8,128)(2,1)S(1)}, u32[]{:S(2)}, u32[]{:S(2)}) %collective-permute-start.73) | collective-permute-done | bytes 1048608 | tf_op jit(solution)/shard_map/ppermute | solution.py:346
  898.1 5.3 collective-permute-start.92
  907.6 86.8 %collective-permute-done.83 = f32[1,5408]{1,0:T(1,128)S(1)} collective-permute-done((f32[1,5408]{1,0:T(1,128)S(1)}, f32[1,5408]{1,0:T(1,128)S(1)}, u32[]{:S(2)}, u32[]{:S(2)}) %collective-permute-start.83) | collective-permute-done | bytes 21664 | tf_op jit(solution)/shard_map/ppermute | solution.py:346
  1005.7 57.6 %collective-permute-done.84 = f32[1,5408]{1,0:T(1,128)S(1)} collective-permute-done((f32[1,5408]{1,0:T(1,128)S(1)}, f32[1,5408]{1,0:T(1,128)S(1)}, u32[]{:S(2)}, u32[]{:S(2)}) %collective-permute-start.84) | collective-permute-done | bytes 21664 | tf_op jit(solution)/shard_map/ppermute | solution.py:346
  1082.7 8.6 collective-permute-done.86
  1093.2 20.5 %collective-permute-done.88 = bf16[2,256,1024]{2,1,0:T(8,128)(2,1)} collective-permute-done((bf16[2,256,1024]{2,1,0:T(8,128)(2,1)S(1)}, bf16[2,256,1024]{2,1,0:T(8,128)(2,1)}, u32[]{:S(2)}, u32[]{:S(2)}) %collective-permute-start.88) | collective-permute-done | bytes 1048608 | tf_op jit(solution)/shard_map/ppermute | solution.py:553
  1116.5 42.0 %collective-permute-done.94 = bf16[2,256,1024]{2,1,0:T(8,128)(2,1)S(1)} collective-permute-done((bf16[2,256,1024]{2,1,0:T(8,128)(2,1)S(1)}, bf16[2,256,1024]{2,1,0:T(8,128)(2,1)S(1)}, u32[]{:S(2)}, u32[]{:S(2)}) %collective-permute-start.94) | collective-permute-done | bytes 1048608 | tf_op jit(solution)/shard_map/ppermute | solution.py:553
  1160.8 13.5 %collective-permute-done.97 = bf16[2,256,1024]{2,1,0:T(8,128)(2,1)S(1)} collective-permute-done((bf16[2,256,1024]{2,1,0:T(8,128)(2,1)S(1)}, bf16[2,256,1024]{2,1,0:T(8,128)(2,1)S(1)}, u32[]{:S(2)}, u32[]{:S(2)}) %collective-permute-start.97) | collective-permute-done | bytes 1048608 | tf_op jit(solution)/shard_map/ppermute | solution.py:553
  1188.8 5.6 collective-permute-done.100
  1200.8 8.0 shard_map.297
  (569 shorter events, 360.0 us)
Async XLA Ops:
  7.2 231.8 %all-gather.4.cloned.1.call-start = ((), (), s32[]{:S(2)}) async-start(), calls=%async_computation.1 | async-start | bytes 3145728 | tf_op jit(solution)/shard_map/all_gather | solution.py:625
  7.9 247.9 %all-gather.6.cloned.1.call-start = ((), (), s32[]{:S(2)}) async-start(), calls=%async_computation.2 | async-start | bytes 8650752 | tf_op jit(solution)/shard_map/all_gather | solution.py:626
  8.0 71.1 %collective-permute-start.4 = (bf16[256,2048]{1,0:T(8,128)(2,1)}, bf16[256,2048]{1,0:T(8,128)(2,1)S(1)}, u32[]{:S(2)}, u32[]{:S(2)}) collective-permute-start(bf16[256,2048]{1,0:T(8,128)(2,1)} %param.17), channel_id=1, source_target_pairs={{0,8},{8,0},{16,24},{24,16},{1,9},{9,1},{17,25},{25,17},{2,10},{10... | collective-permute-start | bytes 3145736 | tf_op jit(solution)/shard_map/ppermute | solution.py:346
  11.0 69.5 %collective-permute-start.5 = (bf16[256,2048]{1,0:T(8,128)(2,1)}, bf16[256,2048]{1,0:T(8,128)(2,1)}, u32[]{:S(2)}, u32[]{:S(2)}) collective-permute-start(bf16[256,2048]{1,0:T(8,128)(2,1)} %param.17), channel_id=1, source_target_pairs={{0,16},{8,24},{16,0},{24,8},{1,17},{9,25},{17,1},{25,9},{2,18},{10... | collective-permute-start | bytes 3145736 | tf_op jit(solution)/shard_map/ppermute | solution.py:346
  17.7 608.9 %reduce-scatter.2.cloned.1.call-start = ((), (), s32[]{:S(2)}) async-start(), calls=%async_computation.3 | async-start | bytes 7208960 | tf_op jit(solution)/shard_map/reduce_scatter | solution.py:685
  78.8 58.7 %collective-permute-start.15 = (bf16[256,1024]{1,0:T(8,128)(2,1)}, bf16[256,1024]{1,0:T(8,128)(2,1)}, u32[]{:S(2)}, u32[]{:S(2)}) collective-permute-start(bf16[256,1024]{1,0:T(8,128)(2,1)} %pad_maximum_fusion.11), channel_id=1, source_target_pairs={{0,24},{8,16},{16,8},{24,0},{1,25},{9,17},{17,9},{25,1},{2,26},{10... | collective-permute-start | bytes 1572872 | tf_op jit(solution)/shard_map/ppermute | solution.py:346
  155.1 63.7 %collective-permute-start.45 = (bf16[4,64,2816]{2,1,0:T(8,128)(2,1)}, bf16[4,64,2816]{2,1,0:T(8,128)(2,1)}, u32[]{:S(2)}, u32[]{:S(2)}) collective-permute-start(bf16[4,64,2816]{2,1,0:T(8,128)(2,1)} %pad_maximum_fusion.5.refs_0_), channel_id=1, source_target_pairs={{0,2},{1,3},{2,0},{3,1},{4,6},{5,7},{6,4},{7,5},{8,10},{9,11},{10,... | collective-permute-start | bytes 4325384 | tf_op jit(solution)/shard_map/ppermute | solution.py:346
  155.2 91.4 %collective-permute-start.43 = (bf16[4,64,2816]{2,1,0:T(8,128)(2,1)}, bf16[4,64,2816]{2,1,0:T(8,128)(2,1)}, u32[]{:S(2)}, u32[]{:S(2)}) collective-permute-start(bf16[4,64,2816]{2,1,0:T(8,128)(2,1)} %pad_maximum_fusion.5.refs_0_), channel_id=1, source_target_pairs={{0,1},{1,0},{2,3},{3,2},{4,5},{5,4},{6,7},{7,6},{8,9},{9,8},{10,11... | collective-permute-start | bytes 4325384 | tf_op jit(solution)/shard_map/ppermute | solution.py:346
  158.4 88.2 %collective-permute-start.33 = (bf16[256,2048]{1,0:T(8,128)(2,1)}, bf16[256,2048]{1,0:T(8,128)(2,1)}, u32[]{:S(2)}, u32[]{:S(2)}) collective-permute-start(bf16[256,2048]{1,0:T(8,128)(2,1)} %param.33), channel_id=1, source_target_pairs={{0,8},{8,0},{16,24},{24,16},{1,9},{9,1},{17,25},{25,17},{2,10},{10... | collective-permute-start | bytes 3145736 | tf_op jit(solution)/shard_map/ppermute | solution.py:346
  165.9 53.2 %collective-permute-start.29 = (bf16[4,64,512]{2,1,0:T(8,128)(2,1)S(1)}, bf16[4,64,512]{2,1,0:T(8,128)(2,1)S(1)}, u32[]{:S(2)}, u32[]{:S(2)}) collective-permute-start(bf16[4,64,512]{2,1,0:T(8,128)(2,1)S(1)} %add_convert_fusion.10), channel_id=1, source_target_pairs={{2,3},{6,7},{10,11},{14,15},{18,19},{22,23},{26,27},{30,31}} | collective-permute-start | bytes 786440 | tf_op jit(solution)/shard_map/ppermute | solution.py:465
  175.1 72.0 %collective-permute-start.34 = (bf16[256,2048]{1,0:T(8,128)(2,1)}, bf16[256,2048]{1,0:T(8,128)(2,1)}, u32[]{:S(2)}, u32[]{:S(2)}) collective-permute-start(bf16[256,2048]{1,0:T(8,128)(2,1)} %param.33), channel_id=1, source_target_pairs={{0,16},{8,24},{16,0},{24,8},{1,17},{9,25},{17,1},{25,9},{2,18},{10... | collective-permute-start | bytes 3145736 | tf_op jit(solution)/shard_map/ppermute | solution.py:346
  246.6 54.6 %collective-permute-start.42 = (bf16[4,64,2816]{2,1,0:T(8,128)(2,1)}, bf16[4,64,2816]{2,1,0:T(8,128)(2,1)}, u32[]{:S(2)}, u32[]{:S(2)}) collective-permute-start(bf16[4,64,2816]{2,1,0:T(8,128)(2,1)} %pad_maximum_fusion.5.refs_0_), channel_id=1, source_target_pairs={{0,4},{4,0},{1,5},{5,1},{2,6},{6,2},{3,7},{7,3},{8,12},{12,8},{9,1... | collective-permute-start | bytes 4325384 | tf_op jit(solution)/shard_map/ppermute | solution.py:346
  246.6 55.0 %collective-permute-start.44 = (bf16[4,64,2816]{2,1,0:T(8,128)(2,1)}, bf16[4,64,2816]{2,1,0:T(8,128)(2,1)}, u32[]{:S(2)}, u32[]{:S(2)}) collective-permute-start(bf16[4,64,2816]{2,1,0:T(8,128)(2,1)} %collective-permute-done.43.refs_2_), channel_id=1, source_target_pairs={{0,4},{4,0},{1,5},{5,1},{2,6},{6,2},{3,7},{7,3},{8,12},{12,8},{9,1... | collective-permute-start | bytes 4325384 | tf_op jit(solution)/shard_map/ppermute | solution.py:346
  248.6 47.4 %collective-permute-start.31 = (bf16[256,2048]{1,0:T(8,128)(2,1)S(1)}, bf16[256,2048]{1,0:T(8,128)(2,1)}, u32[]{:S(2)}, u32[]{:S(2)}) collective-permute-start(bf16[256,2048]{1,0:T(8,128)(2,1)S(1)} %get-tuple-element.203), channel_id=1, source_target_pairs={{0,16},{8,24},{16,0},{24,8},{1,17},{9,25},{17,1},{25,9},{2,18},{10... | collective-permute-start | bytes 3145736 | tf_op jit(solution)/shard_map/ppermute | solution.py:346
  301.6 47.2 %collective-permute-start.38 = (bf16[256,2048]{1,0:T(8,128)(2,1)S(1)}, bf16[256,2048]{1,0:T(8,128)(2,1)}, u32[]{:S(2)}, u32[]{:S(2)}) collective-permute-start(bf16[256,2048]{1,0:T(8,128)(2,1)S(1)} %multiply_convert_fusion.5), channel_id=1, source_target_pairs={{0,24},{8,16},{16,8},{24,0},{1,25},{9,17},{17,9},{25,1},{2,26},{10... | collective-permute-start | bytes 3145736 | tf_op jit(solution)/shard_map/ppermute | solution.py:346
  407.3 70.2 %collective-permute-start.53 = (bf16[1024,2816]{1,0:T(8,128)(2,1)}, bf16[1024,2816]{1,0:T(8,128)(2,1)}, u32[]{:S(2)}, u32[]{:S(2)}) collective-permute-start(bf16[1024,2816]{1,0:T(8,128)(2,1)} %convolution_convert_fusion), channel_id=1, source_target_pairs={{0,4},{4,0},{1,5},{5,1},{2,6},{6,2},{3,7},{7,3},{8,12},{12,8},{9,1... | collective-permute-start | bytes 17301512 | tf_op jit(solution)/shard_map/ppermute | solution.py:346
  412.7 61.1 %collective-permute-start.56 = (bf16[352,2048]{1,0:T(8,128)(2,1)}, bf16[352,2048]{1,0:T(8,128)(2,1)}, u32[]{:S(2)}, u32[]{:S(2)}) collective-permute-start(bf16[352,2048]{1,0:T(8,128)(2,1)} %get-tuple-element.207), channel_id=1, source_target_pairs={{0,1},{3,2},{4,5},{7,6},{8,9},{11,10},{12,13},{15,14},{16,17},{19,... | collective-permute-start | bytes 4325384 | tf_op jit(solution)/shard_map/ppermute | solution.py:541
  433.0 54.8 %collective-permute-start.50 = (bf16[256,2048]{1,0:T(8,128)(2,1)S(1)}, bf16[256,2048]{1,0:T(8,128)(2,1)}, u32[]{:S(2)}, u32[]{:S(2)}) collective-permute-start(bf16[256,2048]{1,0:T(8,128)(2,1)S(1)} %get-tuple-element.201), channel_id=1, source_target_pairs={{0,8},{8,0},{16,24},{24,16},{1,9},{9,1},{17,25},{25,17},{2,10},{10... | collective-permute-start | bytes 3145736 | tf_op jit(solution)/shard_map/ppermute | solution.py:346
  433.8 54.1 %collective-permute-start.51 = (bf16[256,2048]{1,0:T(8,128)(2,1)S(1)}, bf16[256,2048]{1,0:T(8,128)(2,1)}, u32[]{:S(2)}, u32[]{:S(2)}) collective-permute-start(bf16[256,2048]{1,0:T(8,128)(2,1)S(1)} %get-tuple-element.200), channel_id=1, source_target_pairs={{0,16},{8,24},{16,0},{24,8},{1,17},{9,25},{17,1},{25,9},{2,18},{10... | collective-permute-start | bytes 3145736 | tf_op jit(solution)/shard_map/ppermute | solution.py:346
  487.9 712.9 %all-gather.8.cloned.1.call-start = ((), (), s32[]{:S(2)}) async-start(), calls=%async_computation.4 | async-start | bytes 7208960 | tf_op jit(solution)/shard_map/all_gather | solution.py:727
  501.6 46.5 %collective-permute-start.58 = (bf16[256,2048]{1,0:T(8,128)(2,1)S(1)}, bf16[256,2048]{1,0:T(8,128)(2,1)}, u32[]{:S(2)}, u32[]{:S(2)}) collective-permute-start(bf16[256,2048]{1,0:T(8,128)(2,1)S(1)} %get-tuple-element.99), channel_id=1, source_target_pairs={{0,16},{8,24},{16,0},{24,8},{1,17},{9,25},{17,1},{25,9},{2,18},{10... | collective-permute-start | bytes 3145736 | tf_op jit(solution)/shard_map/ppermute | solution.py:346
  548.2 84.3 %collective-permute-start.104 = (bf16[352,2048]{1,0:T(8,128)(2,1)}, bf16[352,2048]{1,0:T(8,128)(2,1)}, u32[]{:S(2)}, u32[]{:S(2)}) collective-permute-start(bf16[352,2048]{1,0:T(8,128)(2,1)} %get-tuple-element.131), channel_id=1, source_target_pairs={{1,2},{2,1},{5,6},{6,5},{9,10},{10,9},{13,14},{14,13},{17,18},{18,... | collective-permute-start | bytes 4325384 | tf_op jit(solution)/shard_map/ppermute | solution.py:547
  556.6 70.9 %collective-permute-start.70 = (bf16[256,2048]{1,0:T(8,128)(2,1)}, bf16[256,2048]{1,0:T(8,128)(2,1)}, u32[]{:S(2)}, u32[]{:S(2)}) collective-permute-start(bf16[256,2048]{1,0:T(8,128)(2,1)} %convolution_convert_fusion.5), channel_id=1, source_target_pairs={{0,4},{4,0},{1,5},{5,1},{2,6},{6,2},{3,7},{7,3},{8,12},{12,8},{9,1... | collective-permute-start | bytes 3145736 | tf_op jit(solution)/shard_map/ppermute | solution.py:346
  560.4 47.5 %collective-permute-start.62 = (bf16[256,2048]{1,0:T(8,128)(2,1)}, bf16[256,2048]{1,0:T(8,128)(2,1)}, u32[]{:S(2)}, u32[]{:S(2)}) collective-permute-start(bf16[256,2048]{1,0:T(8,128)(2,1)} %get-tuple-element.189), channel_id=1, source_target_pairs={{0,24},{8,16},{16,8},{24,0},{1,25},{9,17},{17,9},{25,1},{2,26},{10... | collective-permute-start | bytes 3145736 | tf_op jit(solution)/shard_map/ppermute | solution.py:346
  598.9 125.7 %collective-permute-start.103 = (bf16[352,2048]{1,0:T(8,128)(2,1)}, bf16[352,2048]{1,0:T(8,128)(2,1)}, u32[]{:S(2)}, u32[]{:S(2)}) collective-permute-start(bf16[352,2048]{1,0:T(8,128)(2,1)} %add.795), channel_id=1, source_target_pairs={{1,0},{2,3},{5,4},{6,7},{9,8},{10,11},{13,12},{14,15},{17,16},{18,... | collective-permute-start | bytes 4325384 | tf_op jit(solution)/shard_map/ppermute | solution.py:553
  600.2 128.0 %collective-permute-start.71 = (bf16[1024,1024]{1,0:T(8,128)(2,1)}, bf16[1024,1024]{1,0:T(8,128)(2,1)}, u32[]{:S(2)}, u32[]{:S(2)}) collective-permute-start(bf16[1024,1024]{1,0:T(8,128)(2,1)} %convolution_convert_fusion.7), channel_id=1, source_target_pairs={{0,4},{4,0},{1,5},{5,1},{2,6},{6,2},{3,7},{7,3},{8,12},{12,8},{9,1... | collective-permute-start | bytes 6291464 | tf_op jit(solution)/shard_map/ppermute | solution.py:346
  634.5 120.9 %collective-permute-start.105 = (bf16[352,2048]{1,0:T(8,128)(2,1)S(1)}, bf16[352,2048]{1,0:T(8,128)(2,1)S(1)}, u32[]{:S(2)}, u32[]{:S(2)}) collective-permute-start(bf16[352,2048]{1,0:T(8,128)(2,1)S(1)} %add.845), channel_id=1, source_target_pairs={{1,0},{2,3},{5,4},{6,7},{9,8},{10,11},{13,12},{14,15},{17,16},{18,... | collective-permute-start | bytes 4325384 | tf_op jit(solution)/shard_map/ppermute | solution.py:553
  636.1 91.2 %collective-permute-start.66 = (bf16[4,64,512]{2,1,0:T(8,128)(2,1)S(1)}, bf16[4,64,512]{2,1,0:T(8,128)(2,1)S(1)}, u32[]{:S(2)}, u32[]{:S(2)}) collective-permute-start(bf16[4,64,512]{2,1,0:T(8,128)(2,1)S(1)} %get-tuple-element.228), channel_id=1, source_target_pairs={{3,2},{7,6},{11,10},{15,14},{19,18},{23,22},{27,26},{31,30}} | collective-permute-start | bytes 786440 | tf_op jit(solution)/shard_map/ppermute | solution.py:465
  636.9 90.4 %collective-permute-start.64 = (bf16[4,64,512]{2,1,0:T(8,128)(2,1)S(1)}, bf16[4,64,512]{2,1,0:T(8,128)(2,1)S(1)}, u32[]{:S(2)}, u32[]{:S(2)}) collective-permute-start(bf16[4,64,512]{2,1,0:T(8,128)(2,1)S(1)} %fusion.42), channel_id=1, source_target_pairs={{2,1},{6,5},{10,9},{14,13},{18,17},{22,21},{26,25},{30,29}} | collective-permute-start | bytes 786440 | tf_op jit(solution)/shard_map/ppermute | solution.py:465
  768.3 72.6 %collective-permute-start.77 = (bf16[2,256,1024]{2,1,0:T(8,128)(2,1)}, bf16[2,256,1024]{2,1,0:T(8,128)(2,1)}, u32[]{:S(2)}, u32[]{:S(2)}) collective-permute-start(bf16[2,256,1024]{2,1,0:T(8,128)(2,1)} %get-tuple-element.224), channel_id=1, source_target_pairs={{0,1},{3,2},{4,5},{7,6},{8,9},{11,10},{12,13},{15,14},{16,17},{19,... | collective-permute-start | bytes 3145736 | tf_op jit(solution)/shard_map/ppermute | solution.py:541
  770.8 71.8 %collective-permute-start.78 = (bf16[2,256,1024]{2,1,0:T(8,128)(2,1)}, bf16[2,256,1024]{2,1,0:T(8,128)(2,1)}, u32[]{:S(2)}, u32[]{:S(2)}) collective-permute-start(bf16[2,256,1024]{2,1,0:T(8,128)(2,1)} %get-tuple-element.223), channel_id=1, source_target_pairs={{0,1},{3,2},{4,5},{7,6},{8,9},{11,10},{12,13},{15,14},{16,17},{19,... | collective-permute-start | bytes 3145736 | tf_op jit(solution)/shard_map/ppermute | solution.py:541
  773.1 63.6 %collective-permute-start.76 = (bf16[256,2048]{1,0:T(8,128)(2,1)}, bf16[256,2048]{1,0:T(8,128)(2,1)}, u32[]{:S(2)}, u32[]{:S(2)}) collective-permute-start(bf16[256,2048]{1,0:T(8,128)(2,1)} %fusion.7), channel_id=1, source_target_pairs={{0,1},{3,2},{4,5},{7,6},{8,9},{11,10},{12,13},{15,14},{16,17},{19,... | collective-permute-start | bytes 3145736 | tf_op jit(solution)/shard_map/ppermute | solution.py:541
  790.5 55.2 %collective-permute-start.75 = (bf16[1024,1024]{1,0:T(8,128)(2,1)}, bf16[1024,1024]{1,0:T(8,128)(2,1)}, u32[]{:S(2)}, u32[]{:S(2)}) collective-permute-start(bf16[1024,1024]{1,0:T(8,128)(2,1)} %convolution_convert_fusion.6), channel_id=1, source_target_pairs={{0,4},{4,0},{1,5},{5,1},{2,6},{6,2},{3,7},{7,3},{8,12},{12,8},{9,1... | collective-permute-start | bytes 6291464 | tf_op jit(solution)/shard_map/ppermute | solution.py:346
  836.8 46.1 %collective-permute-start.73 = (bf16[256,2048]{1,0:T(8,128)(2,1)}, bf16[256,2048]{1,0:T(8,128)(2,1)S(1)}, u32[]{:S(2)}, u32[]{:S(2)}) collective-permute-start(bf16[256,2048]{1,0:T(8,128)(2,1)} %get-tuple-element.178), channel_id=1, source_target_pairs={{0,16},{8,24},{16,0},{24,8},{1,17},{9,25},{17,1},{25,9},{2,18},{10... | collective-permute-start | bytes 3145736 | tf_op jit(solution)/shard_map/ppermute | solution.py:346
  896.0 177.1 %collective-permute-start.101 = (bf16[256,2048]{1,0:T(8,128)(2,1)}, bf16[256,2048]{1,0:T(8,128)(2,1)}, u32[]{:S(2)}, u32[]{:S(2)}) collective-permute-start(bf16[256,2048]{1,0:T(8,128)(2,1)} %add.824), channel_id=1, source_target_pairs={{1,2},{2,1},{5,6},{6,5},{9,10},{10,9},{13,14},{14,13},{17,18},{18,... | collective-permute-start | bytes 3145736 | tf_op jit(solution)/shard_map/ppermute | solution.py:547
  898.1 97.1 %collective-permute-start.92 = (bf16[2,256,1024]{2,1,0:T(8,128)(2,1)S(1)}, bf16[2,256,1024]{2,1,0:T(8,128)(2,1)S(1)}, u32[]{:S(2)}, u32[]{:S(2)}) collective-permute-start(bf16[2,256,1024]{2,1,0:T(8,128)(2,1)S(1)} %get-tuple-element.219), channel_id=1, source_target_pairs={{0,1},{3,2},{4,5},{7,6},{8,9},{11,10},{12,13},{15,14},{16,17},{19,... | collective-permute-start | bytes 3145736 | tf_op jit(solution)/shard_map/ppermute | solution.py:541
  903.5 96.9 %collective-permute-start.95 = (bf16[2,256,1024]{2,1,0:T(8,128)(2,1)S(1)}, bf16[2,256,1024]{2,1,0:T(8,128)(2,1)S(1)}, u32[]{:S(2)}, u32[]{:S(2)}) collective-permute-start(bf16[2,256,1024]{2,1,0:T(8,128)(2,1)S(1)} %get-tuple-element.220), channel_id=1, source_target_pairs={{0,1},{3,2},{4,5},{7,6},{8,9},{11,10},{12,13},{15,14},{16,17},{19,... | collective-permute-start | bytes 3145736 | tf_op jit(solution)/shard_map/ppermute | solution.py:541
  904.8 98.8 %collective-permute-start.85 = (bf16[2,256,1024]{2,1,0:T(8,128)(2,1)S(1)}, bf16[2,256,1024]{2,1,0:T(8,128)(2,1)S(1)}, u32[]{:S(2)}, u32[]{:S(2)}) collective-permute-start(bf16[2,256,1024]{2,1,0:T(8,128)(2,1)S(1)} %copy-done.17), channel_id=1, source_target_pairs={{1,2},{2,1},{5,6},{6,5},{9,10},{10,9},{13,14},{14,13},{17,18},{18,... | collective-permute-start | bytes 3145736 | tf_op jit(solution)/shard_map/ppermute | solution.py:547
  905.6 88.7 %collective-permute-start.83 = (f32[1,5408]{1,0:T(1,128)S(1)}, f32[1,5408]{1,0:T(1,128)S(1)}, u32[]{:S(2)}, u32[]{:S(2)}) collective-permute-start(f32[1,5408]{1,0:T(1,128)S(1)} %dynamic-slice_add_fusion), channel_id=1, source_target_pairs={{0,1},{1,0},{2,3},{3,2},{4,5},{5,4},{6,7},{7,6},{8,9},{9,8},{10,11... | collective-permute-start | bytes 64904 | tf_op jit(solution)/shard_map/ppermute | solution.py:346
  994.4 74.3 %collective-permute-start.87 = (bf16[2,256,1024]{2,1,0:T(8,128)(2,1)S(1)}, bf16[2,256,1024]{2,1,0:T(8,128)(2,1)S(1)}, u32[]{:S(2)}, u32[]{:S(2)}) collective-permute-start(bf16[2,256,1024]{2,1,0:T(8,128)(2,1)S(1)} %copy-done.16), channel_id=1, source_target_pairs={{1,2},{2,1},{5,6},{6,5},{9,10},{10,9},{13,14},{14,13},{17,18},{18,... | collective-permute-start | bytes 3145736 | tf_op jit(solution)/shard_map/ppermute | solution.py:547
  995.2 68.1 %collective-permute-start.84 = (f32[1,5408]{1,0:T(1,128)S(1)}, f32[1,5408]{1,0:T(1,128)S(1)}, u32[]{:S(2)}, u32[]{:S(2)}) collective-permute-start(f32[1,5408]{1,0:T(1,128)S(1)} %add.836), channel_id=1, source_target_pairs={{0,2},{1,3},{2,0},{3,1},{4,6},{5,7},{6,4},{7,5},{8,10},{9,11},{10,... | collective-permute-start | bytes 64904 | tf_op jit(solution)/shard_map/ppermute | solution.py:346
  1002.0 74.0 %collective-permute-start.93 = (bf16[2,256,1024]{2,1,0:T(8,128)(2,1)}, bf16[2,256,1024]{2,1,0:T(8,128)(2,1)}, u32[]{:S(2)}, u32[]{:S(2)}) collective-permute-start(bf16[2,256,1024]{2,1,0:T(8,128)(2,1)} %get-tuple-element.217), channel_id=1, source_target_pairs={{1,2},{2,1},{5,6},{6,5},{9,10},{10,9},{13,14},{14,13},{17,18},{18,... | collective-permute-start | bytes 3145736 | tf_op jit(solution)/shard_map/ppermute | solution.py:547
  1003.6 75.6 %collective-permute-start.96 = (bf16[2,256,1024]{2,1,0:T(8,128)(2,1)}, bf16[2,256,1024]{2,1,0:T(8,128)(2,1)}, u32[]{:S(2)}, u32[]{:S(2)}) collective-permute-start(bf16[2,256,1024]{2,1,0:T(8,128)(2,1)} %get-tuple-element.218), channel_id=1, source_target_pairs={{1,2},{2,1},{5,6},{6,5},{9,10},{10,9},{13,14},{14,13},{17,18},{18,... | collective-permute-start | bytes 3145736 | tf_op jit(solution)/shard_map/ppermute | solution.py:547
  1074.7 100.9 %collective-permute-start.102 = (bf16[256,2048]{1,0:T(8,128)(2,1)S(1)}, bf16[256,2048]{1,0:T(8,128)(2,1)S(1)}, u32[]{:S(2)}, u32[]{:S(2)}) collective-permute-start(bf16[256,2048]{1,0:T(8,128)(2,1)S(1)} %add.844), channel_id=1, source_target_pairs={{1,0},{2,3},{5,4},{6,7},{9,8},{10,11},{13,12},{14,15},{17,16},{18,... | collective-permute-start | bytes 3145736 | tf_op jit(solution)/shard_map/ppermute | solution.py:553
  1077.9 80.7 %collective-permute-start.94 = (bf16[2,256,1024]{2,1,0:T(8,128)(2,1)S(1)}, bf16[2,256,1024]{2,1,0:T(8,128)(2,1)S(1)}, u32[]{:S(2)}, u32[]{:S(2)}) collective-permute-start(bf16[2,256,1024]{2,1,0:T(8,128)(2,1)S(1)} %add.841), channel_id=1, source_target_pairs={{1,0},{2,3},{5,4},{6,7},{9,8},{10,11},{13,12},{14,15},{17,16},{18,... | collective-permute-start | bytes 3145736 | tf_op jit(solution)/shard_map/ppermute | solution.py:553
  1081.2 93.2 %collective-permute-start.97 = (bf16[2,256,1024]{2,1,0:T(8,128)(2,1)S(1)}, bf16[2,256,1024]{2,1,0:T(8,128)(2,1)S(1)}, u32[]{:S(2)}, u32[]{:S(2)}) collective-permute-start(bf16[2,256,1024]{2,1,0:T(8,128)(2,1)S(1)} %add.843), channel_id=1, source_target_pairs={{1,0},{2,3},{5,4},{6,7},{9,8},{10,11},{13,12},{14,15},{17,16},{18,... | collective-permute-start | bytes 3145736 | tf_op jit(solution)/shard_map/ppermute | solution.py:553
  1092.7 84.3 %collective-permute-start.90 = (bf16[256,1024]{1,0:T(8,128)(2,1)S(1)}, bf16[256,1024]{1,0:T(8,128)(2,1)S(1)}, u32[]{:S(2)}, u32[]{:S(2)}) collective-permute-start(bf16[256,1024]{1,0:T(8,128)(2,1)S(1)} %get-tuple-element.238), channel_id=1, source_target_pairs={{0,16},{8,24},{16,0},{24,8},{1,17},{9,25},{17,1},{25,9},{2,18},{10... | collective-permute-start | bytes 1572872 | tf_op jit(solution)/shard_map/ppermute | solution.py:346
  1115.2 64.4 %collective-permute-start.89 = (bf16[256,1024]{1,0:T(8,128)(2,1)S(1)}, bf16[256,1024]{1,0:T(8,128)(2,1)S(1)}, u32[]{:S(2)}, u32[]{:S(2)}) collective-permute-start(bf16[256,1024]{1,0:T(8,128)(2,1)S(1)} %get-tuple-element.239), channel_id=1, source_target_pairs={{0,8},{8,0},{16,24},{24,16},{1,9},{9,1},{17,25},{25,17},{2,10},{10... | collective-permute-start | bytes 1572872 | tf_op jit(solution)/shard_map/ppermute | solution.py:346
  (155 other events, 3984.0 us)
Sparse Core Ops, SparseCore 0:
  9.5 13.2 all-gather.3
  24.4 17.1 all-gather.5
  488.0 138.5 reduce-scatter.1
  896.1 151.0 all-gather.7

commit v4 on v3

--- a/solution.py
+++ b/solution.py
@@ -617,7 +617,7 @@
     mask_own = masks[0][:, None]
 
     token_blocks = gather_heads(tokens)
-    weight_kv, kv_pieces = head_columns_seq([key_proj, value_proj], here)
+    weight_kv, kv_pieces = head_columns([key_proj, value_proj], here)
     late = lax.optimization_barrier((query_proj, swish_proj, mlp_gate, mlp_up) + tuple(kv_pieces))
     weight_qs, qs_pieces = head_columns(late[:2], here)
     weight_gu, gu_pieces = head_columns_seq(late[2:4], here)
@@ -651,15 +651,22 @@
     hat_two = residual * scale_two
     normed_two_own = (hat_two * gain_two).astype(BF)
     two_blocks = gather_heads(normed_two_own)
+
+    hidden_width = weight_down.shape[0]
+    hidden, grad_gu, two_parts = [], [], []
+    for k in range(HEADS):
+        block = two_blocks[k] if k == 0 else after(two_blocks[k], two_parts[-1])
+        gate_up = mm(block, weight_gu)
+        gate_pre, up_pre = gate_up[:, :hidden_width], gate_up[:, hidden_width:]
+        grad_cut = grad_act[k * rows : (k + 1) * rows]
+        hidden.append((jax.nn.silu(gate_pre) * up_pre).astype(BF))
+        grad_gate = (grad_cut * up_pre * silu_slope(gate_pre)).astype(BF)
+        grad_up = (grad_cut * jax.nn.silu(gate_pre)).astype(BF)
+        grad_gu.append(jnp.concatenate([grad_gate, grad_up], axis=1))
+        two_parts.append(mm_nt(grad_gu[k], weight_gu).astype(BF))
+    two_got = [swap(two_parts[k], "p", k) for k in range(1, HEADS)]
     normed_two = jnp.concatenate(two_blocks)
-
-    hidden_width = weight_down.shape[0]
-    gate_up = mm(normed_two, weight_gu)
-    gate_pre, up_pre = gate_up[:, :hidden_width], gate_up[:, hidden_width:]
-    hidden = (jax.nn.silu(gate_pre) * up_pre).astype(BF)
-    grad_gate = (grad_act * up_pre * silu_slope(gate_pre)).astype(BF)
-    grad_up = (grad_act * jax.nn.silu(gate_pre)).astype(BF)
-    grad_gu = jnp.concatenate([grad_gate, grad_up], axis=1)
+    hidden, grad_gu = jnp.concatenate(hidden), jnp.concatenate(grad_gu)
     order = [here ^ k for k in range(HEADS)]
     hops = range(1, copies)
     down_rows = mlp_down.shape[0]
@@ -667,35 +674,30 @@
     def down_cut(m):
         return lax.dynamic_slice_in_dim(hidden, (turn ^ m) * down_rows, down_rows, 1)
 
+    hidden, grad_gu = lax.optimization_barrier((hidden, grad_gu, two_got[0], *two_parts))[:2]
     down_away = [mm_tn(down_cut(m), grad_mlp).astype(BF) for m in hops]
     grad_gu, *down_away = lax.optimization_barrier((grad_gu,) + tuple(down_away))
     two_view = normed_two.reshape(group, HEADS, copies, shard)
     gu_away = [mm_tn(split_rows(two_view, turn, m, order), grad_gu).astype(BF) for m in hops]
+    hidden, *gu_away = lax.optimization_barrier((hidden, *gu_away, two_got[1]))[:copies]
     down_total = sum_copies(lambda: mm_tn(down_cut(0), grad_mlp), down_away)
-    down_half = down_rows // 2
     grad_gu, *gu_away, down_total = lax.optimization_barrier((grad_gu, *gu_away, down_total))
-    down_near, down_far = inward(down_total[:down_half]), inward(down_total[down_half:])
-    two_part = mm_nt(grad_gu, weight_gu).astype(BF).reshape(HEADS, rows, D)
-    gu_total = sum_copies(
-        lambda: mm_tn(split_rows(two_view, turn, 0, order), after(grad_gu, two_part)), gu_away
-    )
-    grad_norm_two, gu_total, down_near = scatter_heads(
-        [two_part[k] for k in range(HEADS)], gu_total, down_near
-    )
+    down_part = lax.psum_scatter(down_total, "seq", scatter_dimension=0, tiled=True)
+    gu_total = sum_copies(lambda: mm_tn(split_rows(two_view, turn, 0, order), grad_gu), gu_away)
+    *two_got, gu_total, down_part = lax.optimization_barrier((*two_got, gu_total, down_part))
+    grad_norm_two = two_parts[0].astype(F32)
+    for part in two_got:
+        grad_norm_two = grad_norm_two + part.astype(F32)
     gu_part = lax.psum_scatter(
         gu_total.reshape(HEADS, shard, 2 * hidden_width), "seq", scatter_dimension=0, tiled=True
     )
-    down_near = across(down_near)
     gain_two_grad = jnp.sum(grad_norm_two * hat_two, axis=0)
     grad_rows = grad_out.astype(F32)
     grad_resid = grad_rows + norm_back(grad_norm_two * gain_two, hat_two, scale_two)
     grad_attn_own = (mask_own * grad_resid).astype(BF)
     attn_blocks = gather_heads(grad_attn_own)
     mlp_part = mm(hidden, weight_down).astype(BF)
-    mlp_part, down_near, down_far, *attn_blocks = lax.optimization_barrier(
-        (mlp_part, down_near, down_far) + tuple(attn_blocks)
-    )
-    down_grad = jnp.concatenate([outward(down_near), outward(across(down_far))])
+    mlp_part, *attn_blocks = lax.optimization_barrier((mlp_part,) + tuple(attn_blocks))
     grad_attn = jnp.concatenate(attn_blocks)
     mlp_part = mlp_part.reshape(HEADS, rows, D)
     mlp_out = scatter_heads([mlp_part[k] for k in range(HEADS)])
@@ -721,10 +723,11 @@
     out_total = weight_grad(out_views, grad_attn)
     qs_total = weight_grad(one_views, grad_qs)
     ends = chain_pair(adjoint, decay, False)
-    ends, gu_part, out_total, qs_total = lax.optimization_barrier(
-        (ends, gu_part, out_total, qs_total)
+    ends, gu_part, down_part, out_total, qs_total = lax.optimization_barrier(
+        (ends, gu_part, down_part, out_total, qs_total)
     )
     gu_whole = lax.all_gather(gu_part, "seq", axis=0, tiled=True)
+    down_grad = lax.all_gather(after(down_part, ends), "seq", axis=0, tiled=True)
     qs_total = qs_total.reshape(HEADS, shard, 2 * HEAD)
     out_total, qs_near, qs_far = inward(out_total), inward(qs_total[1::2]), inward(qs_total[0::2])
     grad_kv, grad_li = mixer_finish(kv, li, init, ends, grad_kv, grad_li)

time: 1220 us -> 1320 us (1.082)
  other arithmetic: 108 us -> 162 us
  starting transfers between devices: 136 us -> 173 us
  matrix products: 169 us -> 187 us
    ppermute x7 -> x5, waiting for transfers between devices: 190 us -> 68.8 us  [outward(): lax.ppermute(total, 'seq', [(i + 1, i), (count - 2 - i, count - 1 - i)])]
    concatenate x1 -> x2, other arithmetic: 2.92 us -> 55.9 us  [body(): hidden, grad_gu = (jnp.concatenate(hidden), jnp.concatenate(grad_gu))]
    reduce_scatter x0 -> x1, waiting for transfers between devices: none -> 37.4 us  [body(): lax.psum_scatter(down_total, 'seq', scatter_dimension=0, tiled=True)]
    ppermute x7 -> x5, waiting for transfers between devices: 53.3 us -> 82 us  [inward(): lax.ppermute(value, 'seq', [(i, i + 1), (count - 1 - i, count - 2 - i)])]
    ppermute x12, waiting for transfers between devices: 13.2 us -> 41.3 us  [chain(): total = total + lax.ppermute(sent, 'seq', [pair]).astype(F32)]
    ppermute x72 -> x69, waiting for transfers between devices: 361 us -> 386 us  [swap(): return lax.ppermute(value, axis, [(i, i ^ step) for i in range(count)])]
    ppermute x7 -> x5, starting transfers between devices: 19.7 us -> 43.9 us  [inward(): lax.ppermute(value, 'seq', [(i, i + 1), (count - 1 - i, count - 2 - i)])]
    ppermute x72 -> x69, starting transfers between devices: 79.3 us -> 95.4 us  [swap(): return lax.ppermute(value, axis, [(i, i ^ step) for i in range(count)])]
  transfers between devices with their start and end apart: 110 -> 103, of which waited for: 35 -> 34; matrix products, arithmetic and copies ran while one was open for 23% -> 29% of each run, Pallas kernels for 7% -> 6%
where the time goes in v4:
time: 1320 us; the launch traced here: 1310 us
  waiting for transfers between devices  626 us (47%)
  matrix products  187 us (14%)
  starting transfers between devices  173 us (13%)
  other arithmetic  162 us (12%)
  Pallas kernels  92.3 us (7%)
  local copies, waits for them, and re-layouts  56.5 us (4%)
  between operations  17.3 us (1%)
    ppermute x69, waiting for transfers between devices, swap(): return lax.ppermute(value, axis, [(i, i ^ step) for i in range(count)])  386 us
    ppermute x69, starting transfers between devices, swap(): return lax.ppermute(value, axis, [(i, i ^ step) for i in range(count)])  95.4 us
    ppermute x5, waiting for transfers between devices, inward(): lax.ppermute(value, 'seq', [(i, i + 1), (count - 1 - i, count - 2 - i)])  82 us
    dot_general x9, matrix products, mm_nt(): lax.dot_general(a, b, (((1,), (1,)), ((), ())), preferred_element_type=F32)  70.2 us
    ppermute x5, waiting for transfers between devices, outward(): lax.ppermute(total, 'seq', [(i + 1, i), (count - 2 - i, count - 1 - i)])  68.8 us
    dot_general x11, matrix products, mm_tn(): lax.dot_general(a, b, (((0,), (0,)), ((), ())), preferred_element_type=F32)  68.7 us
    concatenate x2, other arithmetic, body(): hidden, grad_gu = (jnp.concatenate(hidden), jnp.concatenate(grad_gu))  55.9 us
    pallas_call x4, Pallas kernels, run(): pl.pallas_call(kernel, grid=(args[0].shape[0],), in_specs=specs, out_spec...  49.6 us
  transfers between devices with their start and end apart: 103, of which 34 were waited for; matrix products, arithmetic and copies ran while one was open for 29% of the time, Pallas kernels for 6%

profile of v4, /device:TPU:0, one launch (start us, length us, event | category | flops | bytes accessed | tf_op | source)
XLA Modules:
  0.0 1314.2 jit_solution(505203520608909217)
XLA Ops:
  27.2 9.8 collective-permute-done.1
  38.5 21.2 %collective-permute-done.2 = f32[2,5409]{1,0:T(2,128)S(1)} collective-permute-done((f32[2,5409]{1,0:T(2,128)S(1)}, f32[2,5409]{1,0:T(2,128)S(1)}, u32[]{:S(2)}, u32[]{:S(2)}) %collective-permute-start.2) | collective-permute-done | bytes 43304 | tf_op jit(solution)/shard_map/ppermute | solution.py:346
  69.2 15.9 %collective-permute-done.8 = bf16[256,1024]{1,0:T(8,128)(2,1)} collective-permute-done((bf16[256,1024]{1,0:T(8,128)(2,1)}, bf16[256,1024]{1,0:T(8,128)(2,1)}, u32[]{:S(2)}, u32[]{:S(2)}) %collective-permute-start.8) | collective-permute-done | bytes 524320 | tf_op jit(solution)/shard_map/ppermute | solution.py:346
  112.7 6.8 fusion.2
  156.1 26.0 %collective-permute-done.24 = bf16[4,64,512]{2,1,0:T(8,128)(2,1)S(1)} collective-permute-done((bf16[4,64,512]{2,1,0:T(8,128)(2,1)S(1)}, bf16[4,64,512]{2,1,0:T(8,128)(2,1)S(1)}, u32[]{:S(2)}, u32[]{:S(2)}) %collective-permute-start.24) | collective-permute-done | bytes 262176 | tf_op jit(solution)/shard_map/ppermute | solution.py:465
  187.5 31.4 %collective-permute-start.37 = (bf16[4,64,2816]{2,1,0:T(8,128)(2,1)S(1)}, bf16[4,64,2816]{2,1,0:T(8,128)(2,1)}, u32[]{:S(2)}, u32[]{:S(2)}) collective-permute-start(bf16[4,64,2816]{2,1,0:T(8,128)(2,1)S(1)} %pad_maximum_fusion.5.refs_0_), channel_id=1, source_target_pairs={{0,1},{1,0},{2,3},{3,2},{4,5},{5,4},{6,7},{7,6},{8,9},{9,8},{10,11... | collective-permute-start | bytes 4325384 | tf_op jit(solution)/shard_map/ppermute | solution.py:346
  218.9 6.0 shard_map.288
  228.0 8.2 fusion.95
  237.7 13.7 %collective-permute-done.37.refs_2_ = bf16[4,64,2816]{2,1,0:T(8,128)(2,1)} collective-permute-done((bf16[4,64,2816]{2,1,0:T(8,128)(2,1)S(1)}, bf16[4,64,2816]{2,1,0:T(8,128)(2,1)}, u32[]{:S(2)}, u32[]{:S(2)}) %collective-permute-start.37) | collective-permute-done | bytes 1441824 | tf_op jit(solution)/shard_map/ppermute | solution.py:346
  254.0 27.9 %collective-permute-done.41.refs_6_ = bf16[4,64,2816]{2,1,0:T(8,128)(2,1)} collective-permute-done((bf16[4,64,2816]{2,1,0:T(8,128)(2,1)}, bf16[4,64,2816]{2,1,0:T(8,128)(2,1)}, u32[]{:S(2)}, u32[]{:S(2)}) %collective-permute-start.41) | collective-permute-done | bytes 1441824 | tf_op jit(solution)/shard_map/ppermute | solution.py:346
  282.5 15.0 %shard_map.291 = (bf16[4,256,512]{2,1,0:T(8,128)(2,1)}, f32[4,256,512]{2,1,0:T(8,128)}, f32[4,256,64]{2,1,0:T(8,128)}, bf16[4,256,256]{2,1,0:T(8,128)(2,1)}) custom-call(f32[4,256,1024]{2,1,0:T(8,128)} %bitcast.222, bf16[4,256,1024]{2,1,0:T(8,128)(2,1)} %bitcast.225, f32[4,256,128]{2,1,0:T(8,128)} %bitcast.202, f32[4,64,1024]{2,1,0:T(8,128)} %pad_maximum_fusion.6.init_ref, ...), custom_call_target="tpu_custom_call" | custom-call | flops 12000000000 | bytes 16000000 | tf_op jit(solution)/shard_map/pallas_call | solution.py:258
  308.6 13.5 %shard_map.292 = bf16[2048,2816]{1,0:T(8,128)(2,1)} custom-call(s32[32]{0:T(128)} %stack.240.spot_ref, bf16[4,64,2816]{2,1,0:T(8,128)(2,1)} %copy-done.12, bf16[4,64,2816]{2,1,0:T(8,128)(2,1)} %collective-permute-done.36.refs_1_, bf16[4,64,2816]{2,1,0:T(8,128)(2,1)} %collective-permute-done.37.refs_2_, bf16[4,64,2816]{2,1,0:T(8,128)(2,1)} %collective-permute-done.38.refs_3_, ...), custom_call_target="tpu_custom_call" | custom-call | bytes 23068672 | tf_op jit(solution)/shard_map/pallas_call | solution.py:382
  325.0 13.6 %fusion.81 = f32[1024,1408]{1,0:T(8,128)} fusion(bf16[1408,2048]{1,0:T(8,128)(2,1)} %all-gather.7.cloned.1.call-done, bf16[256,2048]{1,0:T(8,128)(2,1)} %collective-permute-done.32, bf16[256,2048]{1,0:T(8,128)(2,1)} %collective-permute-done.31, bf16[256,2048]{1,0:T(8,128)(2,1)} %collective-permute-done.30, bf16[256,2048]{1,0:T(8,128)(2,1)} %param.33, ...), kind=kOutput, calls=%fused_computation.270 | convolution fusion | flops 5926551552 | bytes 15732736 | tf_op jit(solution)/shard_map/dot_general | solution.py:23
  338.5 8.8 collective-permute-done.27
  348.3 21.3 %collective-permute-done.29 = bf16[256,2048]{1,0:T(8,128)(2,1)} collective-permute-done((bf16[256,2048]{1,0:T(8,128)(2,1)S(1)}, bf16[256,2048]{1,0:T(8,128)(2,1)}, u32[]{:S(2)}, u32[]{:S(2)}) %collective-permute-start.29) | collective-permute-done | bytes 1048608 | tf_op jit(solution)/shard_map/ppermute | solution.py:346
  385.7 9.0 convolution_convert_fusion.7
  394.7 27.0 %collective-permute-done.43 = bf16[256,2048]{1,0:T(8,128)(2,1)} collective-permute-done((bf16[256,2048]{1,0:T(8,128)(2,1)}, bf16[256,2048]{1,0:T(8,128)(2,1)}, u32[]{:S(2)}, u32[]{:S(2)}) %collective-permute-start.43) | collective-permute-done | bytes 1048608 | tf_op jit(solution)/shard_map/ppermute | solution.py:346
  429.5 5.7 convolution_convert_fusion.6
  456.3 50.0 %maximum_maximum_fusion = bf16[1024,2816]{1,0:T(8,128)(2,1)} fusion(bf16[256,1408]{1,0:T(8,128)(2,1)S(1)} %get-tuple-element.189, bf16[256,1408]{1,0:T(8,128)(2,1)S(1)} %get-tuple-element.188, bf16[256,1408]{1,0:T(8,128)(2,1)S(1)} %copy-done.39, bf16[256,1408]{1,0:T(8,128)(2,1)S(1)} %copy-done.38, bf16[256,1408]{1,0:T(8,128)(2,1)S(1)} %copy-done.34, ...), kind=kLoop, calls=%fused_computation.9 | loop fusion | flops 46137344 | bytes 11534336 | tf_op jit(solution)/shard_map/concatenate | solution.py:669
  506.4 5.9 pad_maximum_fusion.2
  517.7 7.9 convolution_convert_fusion.3
  531.2 8.9 convolution_convert_fusion
  540.1 11.3 collective-permute-done.47
  551.4 8.7 add_convert_fusion.2
  561.8 8.1 collective-permute-done.50
  569.9 11.8 add_convert_fusion
  587.1 37.4 %reduce-scatter.3.cloned.1.call-done = bf16[176,2048]{1,0:T(8,128)(2,1)} async-done(((bf16[704,2048]{1,0:T(8,128)(2,1)}), bf16[176,2048]{1,0:T(8,128)(2,1)}) %reduce-scatter.3.cloned.1.call-update) | async-done | bytes 720912 | tf_op jit(solution)/shard_map/reduce_scatter | solution.py:685
  641.7 8.6 convolution_convert_fusion.1
  650.4 14.0 %collective-permute-done.51 = bf16[256,2048]{1,0:T(8,128)(2,1)} collective-permute-done((bf16[256,2048]{1,0:T(8,128)(2,1)S(1)}, bf16[256,2048]{1,0:T(8,128)(2,1)}, u32[]{:S(2)}, u32[]{:S(2)}) %collective-permute-start.51) | collective-permute-done | bytes 1048608 | tf_op jit(solution)/shard_map/ppermute | solution.py:346
  664.3 22.7 %collective-permute-done.52 = bf16[256,2048]{1,0:T(8,128)(2,1)} collective-permute-done((bf16[256,2048]{1,0:T(8,128)(2,1)S(1)}, bf16[256,2048]{1,0:T(8,128)(2,1)}, u32[]{:S(2)}, u32[]{:S(2)}) %collective-permute-start.52) | collective-permute-done | bytes 1048608 | tf_op jit(solution)/shard_map/ppermute | solution.py:346
  694.9 19.9 %shard_map.293 = (bf16[4,256,1024]{2,1,0:T(8,128)(2,1)}, f32[4,256,1024]{2,1,0:T(8,128)}, f32[4,256,128]{2,1,0:T(8,128)}, f32[4,64,1024]{2,1,0:T(8,128)}, f32[8,512]{1,0:T(8,128)}) custom-call(f32[4,256,1024]{2,1,0:T(8,128)} %bitcast.223, bf16[4,256,1024]{2,1,0:T(8,128)(2,1)} %bitcast.226, f32[4,256,128]{2,1,0:T(8,128)} %bitcast.203, ...), custom_call_target="tpu_custom_call" | custom-call | flops 24000000000 | bytes 20000000 | tf_op jit(solution)/shard_map/pallas_call | solution.py:258
  720.3 9.0 reduce-scatter.5.cloned.1.call-done
  762.0 9.8 collective-permute-done.59
  776.0 9.2 shard_map.294
  785.2 8.6 fusion.102
  807.8 27.4 %collective-permute-start.70 = (bf16[256,2048]{1,0:T(8,128)(2,1)}, bf16[256,2048]{1,0:T(8,128)(2,1)}, u32[]{:S(2)}, u32[]{:S(2)}) collective-permute-start(bf16[256,2048]{1,0:T(8,128)(2,1)} %fusion.6), channel_id=1, source_target_pairs={{0,1},{3,2},{4,5},{7,6},{8,9},{11,10},{12,13},{15,14},{16,17},{19,... | collective-permute-start | bytes 3145736 | tf_op jit(solution)/shard_map/ppermute | solution.py:541
  841.6 14.3 %add_convert_fusion.1 = bf16[1024,2048]{1,0:T(8,128)(2,1)} fusion(f32[1024,2048]{1,0:T(8,128)} %fusion.103, f32[1024,2048]{1,0:T(8,128)} %fusion.102, bf16[1024,1024]{1,0:T(8,128)(2,1)} %bitcast.229, bf16[2048,1024]{1,0:T(8,128)(2,1)} %shard_map.288), kind=kOutput, calls=%fused_computation.7 | convolution fusion | flops 4301258752 | bytes 27262976 | tf_op jit(solution)/shard_map/dot_general | solution.py:23
  867.3 40.8 %collective-permute-done.72 = bf16[2,256,1024]{2,1,0:T(8,128)(2,1)} collective-permute-done((bf16[2,256,1024]{2,1,0:T(8,128)(2,1)}, bf16[2,256,1024]{2,1,0:T(8,128)(2,1)}, u32[]{:S(2)}, u32[]{:S(2)}) %collective-permute-start.72) | collective-permute-done | bytes 1048608 | tf_op jit(solution)/shard_map/ppermute | solution.py:541
  908.1 40.8 %collective-permute-done.71 = bf16[2,256,1024]{2,1,0:T(8,128)(2,1)} collective-permute-done((bf16[2,256,1024]{2,1,0:T(8,128)(2,1)}, bf16[2,256,1024]{2,1,0:T(8,128)(2,1)}, u32[]{:S(2)}, u32[]{:S(2)}) %collective-permute-start.71) | collective-permute-done | bytes 1048608 | tf_op jit(solution)/shard_map/ppermute | solution.py:541
  961.1 15.0 %collective-permute-done.68 = bf16[256,2048]{1,0:T(8,128)(2,1)S(1)} collective-permute-done((bf16[256,2048]{1,0:T(8,128)(2,1)S(1)}, bf16[256,2048]{1,0:T(8,128)(2,1)S(1)}, u32[]{:S(2)}, u32[]{:S(2)}) %collective-permute-start.68) | collective-permute-done | bytes 1048608 | tf_op jit(solution)/shard_map/ppermute | solution.py:346
  983.6 14.2 %collective-permute-done.55 = bf16[256,2048]{1,0:T(8,128)(2,1)} collective-permute-done((bf16[256,2048]{1,0:T(8,128)(2,1)}, bf16[256,2048]{1,0:T(8,128)(2,1)}, u32[]{:S(2)}, u32[]{:S(2)}) %collective-permute-start.55) | collective-permute-done | bytes 1048608 | tf_op jit(solution)/shard_map/ppermute | solution.py:346
  1004.9 10.6 collective-permute-start.86
  1017.7 89.3 %collective-permute-done.77 = f32[1,5408]{1,0:T(1,128)S(1)} collective-permute-done((f32[1,5408]{1,0:T(1,128)S(1)}, f32[1,5408]{1,0:T(1,128)S(1)}, u32[]{:S(2)}, u32[]{:S(2)}) %collective-permute-start.77) | collective-permute-done | bytes 21664 | tf_op jit(solution)/shard_map/ppermute | solution.py:346
  1121.9 51.7 %collective-permute-done.78 = f32[1,5408]{1,0:T(1,128)S(1)} collective-permute-done((f32[1,5408]{1,0:T(1,128)S(1)}, f32[1,5408]{1,0:T(1,128)S(1)}, u32[]{:S(2)}, u32[]{:S(2)}) %collective-permute-start.78) | collective-permute-done | bytes 21664 | tf_op jit(solution)/shard_map/ppermute | solution.py:346
  1194.1 9.3 collective-permute-done.80
  1205.9 42.3 %collective-permute-done.91 = bf16[2,256,1024]{2,1,0:T(8,128)(2,1)S(1)} collective-permute-done((bf16[2,256,1024]{2,1,0:T(8,128)(2,1)S(1)}, bf16[2,256,1024]{2,1,0:T(8,128)(2,1)S(1)}, u32[]{:S(2)}, u32[]{:S(2)}) %collective-permute-start.91) | collective-permute-done | bytes 1048608 | tf_op jit(solution)/shard_map/ppermute | solution.py:553
  1250.0 17.2 %collective-permute-done.88 = bf16[2,256,1024]{2,1,0:T(8,128)(2,1)S(1)} collective-permute-done((bf16[2,256,1024]{2,1,0:T(8,128)(2,1)S(1)}, bf16[2,256,1024]{2,1,0:T(8,128)(2,1)S(1)}, u32[]{:S(2)}, u32[]{:S(2)}) %collective-permute-start.88) | collective-permute-done | bytes 1048608 | tf_op jit(solution)/shard_map/ppermute | solution.py:553
  1298.9 8.0 shard_map.297
  (592 shorter events, 383.6 us)
Async XLA Ops:
  7.2 292.4 %all-gather.5.cloned.1.call-start = ((), (), s32[]{:S(2)}) async-start(), calls=%async_computation.2 | async-start | bytes 3145728 | tf_op jit(solution)/shard_map/all_gather | solution.py:625
  7.9 317.0 %all-gather.7.cloned.1.call-start = ((), (), s32[]{:S(2)}) async-start(), calls=%async_computation.3 | async-start | bytes 8650752 | tf_op jit(solution)/shard_map/all_gather | solution.py:626
  8.0 90.4 %collective-permute-start.6 = (bf16[256,2048]{1,0:T(8,128)(2,1)}, bf16[256,2048]{1,0:T(8,128)(2,1)S(1)}, u32[]{:S(2)}, u32[]{:S(2)}) collective-permute-start(bf16[256,2048]{1,0:T(8,128)(2,1)} %param.17), channel_id=1, source_target_pairs={{0,24},{8,16},{16,8},{24,0},{1,25},{9,17},{17,9},{25,1},{2,26},{10... | collective-permute-start | bytes 3145736 | tf_op jit(solution)/shard_map/ppermute | solution.py:346
  12.0 86.6 %collective-permute-start.5 = (bf16[256,2048]{1,0:T(8,128)(2,1)}, bf16[256,2048]{1,0:T(8,128)(2,1)}, u32[]{:S(2)}, u32[]{:S(2)}) collective-permute-start(bf16[256,2048]{1,0:T(8,128)(2,1)} %param.17), channel_id=1, source_target_pairs={{0,16},{8,24},{16,0},{24,8},{1,17},{9,25},{17,1},{25,9},{2,18},{10... | collective-permute-start | bytes 3145736 | tf_op jit(solution)/shard_map/ppermute | solution.py:346
  17.7 606.8 %reduce-scatter.3.cloned.1.call-start = ((), (), s32[]{:S(2)}) async-start(), calls=%async_computation.4 | async-start | bytes 3604480 | tf_op jit(solution)/shard_map/reduce_scatter | solution.py:685
  90.1 61.6 %collective-permute-start.11 = (bf16[256,1024]{1,0:T(8,128)(2,1)}, bf16[256,1024]{1,0:T(8,128)(2,1)}, u32[]{:S(2)}, u32[]{:S(2)}) collective-permute-start(bf16[256,1024]{1,0:T(8,128)(2,1)} %pad_maximum_fusion.12), channel_id=1, source_target_pairs={{0,8},{8,0},{16,24},{24,16},{1,9},{9,1},{17,25},{25,17},{2,10},{10... | collective-permute-start | bytes 1572872 | tf_op jit(solution)/shard_map/ppermute | solution.py:346
  102.3 51.0 %collective-permute-start.13 = (bf16[256,1024]{1,0:T(8,128)(2,1)}, bf16[256,1024]{1,0:T(8,128)(2,1)}, u32[]{:S(2)}, u32[]{:S(2)}) collective-permute-start(bf16[256,1024]{1,0:T(8,128)(2,1)} %pad_maximum_fusion.13), channel_id=1, source_target_pairs={{0,16},{8,24},{16,0},{24,8},{1,17},{9,25},{17,1},{25,9},{2,18},{10... | collective-permute-start | bytes 1572872 | tf_op jit(solution)/shard_map/ppermute | solution.py:346
  141.9 86.0 %collective-permute-start.39 = (bf16[4,64,2816]{2,1,0:T(8,128)(2,1)S(1)}, bf16[4,64,2816]{2,1,0:T(8,128)(2,1)}, u32[]{:S(2)}, u32[]{:S(2)}) collective-permute-start(bf16[4,64,2816]{2,1,0:T(8,128)(2,1)S(1)} %pad_maximum_fusion.5.refs_0_), channel_id=1, source_target_pairs={{0,2},{1,3},{2,0},{3,1},{4,6},{5,7},{6,4},{7,5},{8,10},{9,11},{10,... | collective-permute-start | bytes 4325384 | tf_op jit(solution)/shard_map/ppermute | solution.py:346
  184.6 41.0 %collective-permute-start.25 = (bf16[4,64,512]{2,1,0:T(8,128)(2,1)}, bf16[4,64,512]{2,1,0:T(8,128)(2,1)}, u32[]{:S(2)}, u32[]{:S(2)}) collective-permute-start(bf16[4,64,512]{2,1,0:T(8,128)(2,1)} %get-tuple-element.246), channel_id=1, source_target_pairs={{1,2},{5,6},{9,10},{13,14},{17,18},{21,22},{25,26},{29,30}} | collective-permute-start | bytes 786440 | tf_op jit(solution)/shard_map/ppermute | solution.py:465
  187.5 110.1 %collective-permute-start.36 = (bf16[4,64,2816]{2,1,0:T(8,128)(2,1)S(1)}, bf16[4,64,2816]{2,1,0:T(8,128)(2,1)}, u32[]{:S(2)}, u32[]{:S(2)}) collective-permute-start(bf16[4,64,2816]{2,1,0:T(8,128)(2,1)S(1)} %pad_maximum_fusion.5.refs_0_), channel_id=1, source_target_pairs={{0,4},{4,0},{1,5},{5,1},{2,6},{6,2},{3,7},{7,3},{8,12},{12,8},{9,1... | collective-permute-start | bytes 4325384 | tf_op jit(solution)/shard_map/ppermute | solution.py:346
  187.5 63.9 %collective-permute-start.37 = (bf16[4,64,2816]{2,1,0:T(8,128)(2,1)S(1)}, bf16[4,64,2816]{2,1,0:T(8,128)(2,1)}, u32[]{:S(2)}, u32[]{:S(2)}) collective-permute-start(bf16[4,64,2816]{2,1,0:T(8,128)(2,1)S(1)} %pad_maximum_fusion.5.refs_0_), channel_id=1, source_target_pairs={{0,1},{1,0},{2,3},{3,2},{4,5},{5,4},{6,7},{7,6},{8,9},{9,8},{10,11... | collective-permute-start | bytes 4325384 | tf_op jit(solution)/shard_map/ppermute | solution.py:346
  227.9 54.0 %collective-permute-start.41 = (bf16[4,64,2816]{2,1,0:T(8,128)(2,1)}, bf16[4,64,2816]{2,1,0:T(8,128)(2,1)}, u32[]{:S(2)}, u32[]{:S(2)}) collective-permute-start(bf16[4,64,2816]{2,1,0:T(8,128)(2,1)} %collective-permute-done.39.refs_4_), channel_id=1, source_target_pairs={{0,1},{1,0},{2,3},{3,2},{4,5},{5,4},{6,7},{7,6},{8,9},{9,8},{10,11... | collective-permute-start | bytes 4325384 | tf_op jit(solution)/shard_map/ppermute | solution.py:346
  236.2 85.9 %collective-permute-start.32 = (bf16[256,2048]{1,0:T(8,128)(2,1)}, bf16[256,2048]{1,0:T(8,128)(2,1)}, u32[]{:S(2)}, u32[]{:S(2)}) collective-permute-start(bf16[256,2048]{1,0:T(8,128)(2,1)} %param.33), channel_id=1, source_target_pairs={{0,24},{8,16},{16,8},{24,0},{1,25},{9,17},{17,9},{25,1},{2,26},{10... | collective-permute-start | bytes 3145736 | tf_op jit(solution)/shard_map/ppermute | solution.py:346
  251.4 47.2 %collective-permute-start.38 = (bf16[4,64,2816]{2,1,0:T(8,128)(2,1)}, bf16[4,64,2816]{2,1,0:T(8,128)(2,1)}, u32[]{:S(2)}, u32[]{:S(2)}) collective-permute-start(bf16[4,64,2816]{2,1,0:T(8,128)(2,1)} %collective-permute-done.37.refs_2_), channel_id=1, source_target_pairs={{0,4},{4,0},{1,5},{5,1},{2,6},{6,2},{3,7},{7,3},{8,12},{12,8},{9,1... | collective-permute-start | bytes 4325384 | tf_op jit(solution)/shard_map/ppermute | solution.py:346
  253.5 53.0 %collective-permute-start.40 = (bf16[4,64,2816]{2,1,0:T(8,128)(2,1)}, bf16[4,64,2816]{2,1,0:T(8,128)(2,1)}, u32[]{:S(2)}, u32[]{:S(2)}) collective-permute-start(bf16[4,64,2816]{2,1,0:T(8,128)(2,1)} %collective-permute-done.39.refs_4_), channel_id=1, source_target_pairs={{0,4},{4,0},{1,5},{5,1},{2,6},{6,2},{3,7},{7,3},{8,12},{12,8},{9,1... | collective-permute-start | bytes 4325384 | tf_op jit(solution)/shard_map/ppermute | solution.py:346
  306.5 40.8 %collective-permute-start.27 = (bf16[256,2048]{1,0:T(8,128)(2,1)}, bf16[256,2048]{1,0:T(8,128)(2,1)S(1)}, u32[]{:S(2)}, u32[]{:S(2)}) collective-permute-start(bf16[256,2048]{1,0:T(8,128)(2,1)} %get-tuple-element.220), channel_id=1, source_target_pairs={{0,8},{8,0},{16,24},{24,16},{1,9},{9,1},{17,25},{25,17},{2,10},{10... | collective-permute-start | bytes 3145736 | tf_op jit(solution)/shard_map/ppermute | solution.py:346
  322.1 47.5 %collective-permute-start.29 = (bf16[256,2048]{1,0:T(8,128)(2,1)S(1)}, bf16[256,2048]{1,0:T(8,128)(2,1)}, u32[]{:S(2)}, u32[]{:S(2)}) collective-permute-start(bf16[256,2048]{1,0:T(8,128)(2,1)S(1)} %get-tuple-element.218), channel_id=1, source_target_pairs={{0,24},{8,16},{16,8},{24,0},{1,25},{9,17},{17,9},{25,1},{2,26},{10... | collective-permute-start | bytes 3145736 | tf_op jit(solution)/shard_map/ppermute | solution.py:346
  374.0 75.3 %collective-permute-start.45 = (bf16[256,2048]{1,0:T(8,128)(2,1)}, bf16[256,2048]{1,0:T(8,128)(2,1)}, u32[]{:S(2)}, u32[]{:S(2)}) collective-permute-start(bf16[256,2048]{1,0:T(8,128)(2,1)} %multiply_convert_fusion.2), channel_id=1, source_target_pairs={{0,24},{8,16},{16,8},{24,0},{1,25},{9,17},{17,9},{25,1},{2,26},{10... | collective-permute-start | bytes 3145736 | tf_op jit(solution)/shard_map/ppermute | solution.py:346
  375.5 60.7 %collective-permute-start.44 = (bf16[256,2048]{1,0:T(8,128)(2,1)}, bf16[256,2048]{1,0:T(8,128)(2,1)}, u32[]{:S(2)}, u32[]{:S(2)}) collective-permute-start(bf16[256,2048]{1,0:T(8,128)(2,1)} %multiply_convert_fusion.2), channel_id=1, source_target_pairs={{0,16},{8,24},{16,0},{24,8},{1,17},{9,25},{17,1},{25,9},{2,18},{10... | collective-permute-start | bytes 3145736 | tf_op jit(solution)/shard_map/ppermute | solution.py:346
  376.5 45.2 %collective-permute-start.43 = (bf16[256,2048]{1,0:T(8,128)(2,1)}, bf16[256,2048]{1,0:T(8,128)(2,1)}, u32[]{:S(2)}, u32[]{:S(2)}) collective-permute-start(bf16[256,2048]{1,0:T(8,128)(2,1)} %multiply_convert_fusion.2), channel_id=1, source_target_pairs={{0,8},{8,0},{16,24},{24,16},{1,9},{9,1},{17,25},{25,17},{2,10},{10... | collective-permute-start | bytes 3145736 | tf_op jit(solution)/shard_map/ppermute | solution.py:346
  435.2 82.5 %collective-permute-start.46 = (bf16[256,2048]{1,0:T(8,128)(2,1)}, bf16[256,2048]{1,0:T(8,128)(2,1)}, u32[]{:S(2)}, u32[]{:S(2)}) collective-permute-start(bf16[256,2048]{1,0:T(8,128)(2,1)} %convolution_convert_fusion.6), channel_id=1, source_target_pairs={{0,8},{8,0},{16,24},{24,16},{1,9},{9,1},{17,25},{25,17},{2,10},{10... | collective-permute-start | bytes 3145736 | tf_op jit(solution)/shard_map/ppermute | solution.py:346
  560.2 169.1 %reduce-scatter.5.cloned.1.call-start = ((), (), s32[]{:S(2)}) async-start(), calls=%async_computation.5 | async-start | bytes 7208960 | tf_op jit(solution)/shard_map/reduce_scatter | solution.py:691
  624.5 648.8 %all-gather.11.cloned.1.call-start = ((), (), s32[]{:S(2)}) async-start(), calls=%async_computation.7 | async-start | bytes 3604480 | tf_op jit(solution)/shard_map/all_gather | solution.py:730
  639.9 47.1 %collective-permute-start.52 = (bf16[256,2048]{1,0:T(8,128)(2,1)S(1)}, bf16[256,2048]{1,0:T(8,128)(2,1)}, u32[]{:S(2)}, u32[]{:S(2)}) collective-permute-start(bf16[256,2048]{1,0:T(8,128)(2,1)S(1)} %get-tuple-element.112), channel_id=1, source_target_pairs={{0,16},{8,24},{16,0},{24,8},{1,17},{9,25},{17,1},{25,9},{2,18},{10... | collective-permute-start | bytes 3145736 | tf_op jit(solution)/shard_map/ppermute | solution.py:346
  641.4 45.7 %collective-permute-start.53 = (bf16[256,2048]{1,0:T(8,128)(2,1)S(1)}, bf16[256,2048]{1,0:T(8,128)(2,1)}, u32[]{:S(2)}, u32[]{:S(2)}) collective-permute-start(bf16[256,2048]{1,0:T(8,128)(2,1)S(1)} %get-tuple-element.112), channel_id=1, source_target_pairs={{0,24},{8,16},{16,8},{24,0},{1,25},{9,17},{17,9},{25,1},{2,26},{10... | collective-permute-start | bytes 3145736 | tf_op jit(solution)/shard_map/ppermute | solution.py:346
  741.4 241.6 %collective-permute-start.56 = (bf16[256,2048]{1,0:T(8,128)(2,1)}, bf16[256,2048]{1,0:T(8,128)(2,1)}, u32[]{:S(2)}, u32[]{:S(2)}) collective-permute-start(bf16[256,2048]{1,0:T(8,128)(2,1)} %get-tuple-element.208), channel_id=1, source_target_pairs={{0,24},{8,16},{16,8},{24,0},{1,25},{9,17},{17,9},{25,1},{2,26},{10... | collective-permute-start | bytes 3145736 | tf_op jit(solution)/shard_map/ppermute | solution.py:346
  807.8 145.8 %collective-permute-start.69 = (bf16[1024,1024]{1,0:T(8,128)(2,1)}, bf16[1024,1024]{1,0:T(8,128)(2,1)}, u32[]{:S(2)}, u32[]{:S(2)}) collective-permute-start(bf16[1024,1024]{1,0:T(8,128)(2,1)} %convolution_convert_fusion.9), channel_id=1, source_target_pairs={{0,4},{4,0},{1,5},{5,1},{2,6},{6,2},{3,7},{7,3},{8,12},{12,8},{9,1... | collective-permute-start | bytes 6291464 | tf_op jit(solution)/shard_map/ppermute | solution.py:346
  807.8 55.3 %collective-permute-start.70 = (bf16[256,2048]{1,0:T(8,128)(2,1)}, bf16[256,2048]{1,0:T(8,128)(2,1)}, u32[]{:S(2)}, u32[]{:S(2)}) collective-permute-start(bf16[256,2048]{1,0:T(8,128)(2,1)} %fusion.6), channel_id=1, source_target_pairs={{0,1},{3,2},{4,5},{7,6},{8,9},{11,10},{12,13},{15,14},{16,17},{19,... | collective-permute-start | bytes 3145736 | tf_op jit(solution)/shard_map/ppermute | solution.py:541
  836.8 71.4 %collective-permute-start.72 = (bf16[2,256,1024]{2,1,0:T(8,128)(2,1)}, bf16[2,256,1024]{2,1,0:T(8,128)(2,1)}, u32[]{:S(2)}, u32[]{:S(2)}) collective-permute-start(bf16[2,256,1024]{2,1,0:T(8,128)(2,1)} %get-tuple-element.239), channel_id=1, source_target_pairs={{0,1},{3,2},{4,5},{7,6},{8,9},{11,10},{12,13},{15,14},{16,17},{19,... | collective-permute-start | bytes 3145736 | tf_op jit(solution)/shard_map/ppermute | solution.py:541
  839.0 110.0 %collective-permute-start.71 = (bf16[2,256,1024]{2,1,0:T(8,128)(2,1)}, bf16[2,256,1024]{2,1,0:T(8,128)(2,1)}, u32[]{:S(2)}, u32[]{:S(2)}) collective-permute-start(bf16[2,256,1024]{2,1,0:T(8,128)(2,1)} %get-tuple-element.240), channel_id=1, source_target_pairs={{0,1},{3,2},{4,5},{7,6},{8,9},{11,10},{12,13},{15,14},{16,17},{19,... | collective-permute-start | bytes 3145736 | tf_op jit(solution)/shard_map/ppermute | solution.py:541
  841.3 457.6 %all-gather.9.cloned.1.call-start = ((), (), s32[]{:S(2)}) async-start(), calls=%async_computation.6 | async-start | bytes 7208960 | tf_op jit(solution)/shard_map/all_gather | solution.py:729
  863.2 97.3 %collective-permute-start.66 = (bf16[256,2048]{1,0:T(8,128)(2,1)S(1)}, bf16[256,2048]{1,0:T(8,128)(2,1)S(1)}, u32[]{:S(2)}, u32[]{:S(2)}) collective-permute-start(bf16[256,2048]{1,0:T(8,128)(2,1)S(1)} %get-tuple-element.198), channel_id=1, source_target_pairs={{0,8},{8,0},{16,24},{24,16},{1,9},{9,1},{17,25},{25,17},{2,10},{10... | collective-permute-start | bytes 3145736 | tf_op jit(solution)/shard_map/ppermute | solution.py:346
  908.1 52.9 %collective-permute-start.67 = (bf16[256,2048]{1,0:T(8,128)(2,1)S(1)}, bf16[256,2048]{1,0:T(8,128)(2,1)S(1)}, u32[]{:S(2)}, u32[]{:S(2)}) collective-permute-start(bf16[256,2048]{1,0:T(8,128)(2,1)S(1)} %get-tuple-element.197), channel_id=1, source_target_pairs={{0,16},{8,24},{16,0},{24,8},{1,17},{9,25},{17,1},{25,9},{2,18},{10... | collective-permute-start | bytes 3145736 | tf_op jit(solution)/shard_map/ppermute | solution.py:346
  953.6 44.2 %collective-permute-start.55 = (bf16[256,2048]{1,0:T(8,128)(2,1)}, bf16[256,2048]{1,0:T(8,128)(2,1)}, u32[]{:S(2)}, u32[]{:S(2)}) collective-permute-start(bf16[256,2048]{1,0:T(8,128)(2,1)} %get-tuple-element.209), channel_id=1, source_target_pairs={{0,16},{8,24},{16,0},{24,8},{1,17},{9,25},{17,1},{25,9},{2,18},{10... | collective-permute-start | bytes 3145736 | tf_op jit(solution)/shard_map/ppermute | solution.py:346
  1001.9 106.8 %collective-permute-start.81 = (bf16[2,256,1024]{2,1,0:T(8,128)(2,1)}, bf16[2,256,1024]{2,1,0:T(8,128)(2,1)S(1)}, u32[]{:S(2)}, u32[]{:S(2)}) collective-permute-start(bf16[2,256,1024]{2,1,0:T(8,128)(2,1)} %get-tuple-element.134), channel_id=1, source_target_pairs={{1,2},{2,1},{5,6},{6,5},{9,10},{10,9},{13,14},{14,13},{17,18},{18,... | collective-permute-start | bytes 3145736 | tf_op jit(solution)/shard_map/ppermute | solution.py:547
  1004.9 108.6 %collective-permute-start.86 = (bf16[2,256,1024]{2,1,0:T(8,128)(2,1)S(1)}, bf16[2,256,1024]{2,1,0:T(8,128)(2,1)S(1)}, u32[]{:S(2)}, u32[]{:S(2)}) collective-permute-start(bf16[2,256,1024]{2,1,0:T(8,128)(2,1)S(1)} %get-tuple-element.235), channel_id=1, source_target_pairs={{0,1},{3,2},{4,5},{7,6},{8,9},{11,10},{12,13},{15,14},{16,17},{19,... | collective-permute-start | bytes 3145736 | tf_op jit(solution)/shard_map/ppermute | solution.py:541
  1015.5 99.6 %collective-permute-start.89 = (bf16[2,256,1024]{2,1,0:T(8,128)(2,1)S(1)}, bf16[2,256,1024]{2,1,0:T(8,128)(2,1)S(1)}, u32[]{:S(2)}, u32[]{:S(2)}) collective-permute-start(bf16[2,256,1024]{2,1,0:T(8,128)(2,1)S(1)} %get-tuple-element.236), channel_id=1, source_target_pairs={{0,1},{3,2},{4,5},{7,6},{8,9},{11,10},{12,13},{15,14},{16,17},{19,... | collective-permute-start | bytes 3145736 | tf_op jit(solution)/shard_map/ppermute | solution.py:541
  1016.9 90.1 %collective-permute-start.77 = (f32[1,5408]{1,0:T(1,128)S(1)}, f32[1,5408]{1,0:T(1,128)S(1)}, u32[]{:S(2)}, u32[]{:S(2)}) collective-permute-start(f32[1,5408]{1,0:T(1,128)S(1)} %dynamic-slice_add_fusion), channel_id=1, source_target_pairs={{0,1},{1,0},{2,3},{3,2},{4,5},{5,4},{6,7},{7,6},{8,9},{9,8},{10,11... | collective-permute-start | bytes 64904 | tf_op jit(solution)/shard_map/ppermute | solution.py:346
  1017.0 156.7 %collective-permute-start.79 = (bf16[2,256,1024]{2,1,0:T(8,128)(2,1)}, bf16[2,256,1024]{2,1,0:T(8,128)(2,1)S(1)}, u32[]{:S(2)}, u32[]{:S(2)}) collective-permute-start(bf16[2,256,1024]{2,1,0:T(8,128)(2,1)} %get-tuple-element.133), channel_id=1, source_target_pairs={{1,2},{2,1},{5,6},{6,5},{9,10},{10,9},{13,14},{14,13},{17,18},{18,... | collective-permute-start | bytes 3145736 | tf_op jit(solution)/shard_map/ppermute | solution.py:547
  1107.0 73.9 %collective-permute-start.95 = (bf16[256,2048]{1,0:T(8,128)(2,1)S(1)}, bf16[256,2048]{1,0:T(8,128)(2,1)}, u32[]{:S(2)}, u32[]{:S(2)}) collective-permute-start(bf16[256,2048]{1,0:T(8,128)(2,1)S(1)} %copy-done.15), channel_id=1, source_target_pairs={{1,2},{2,1},{5,6},{6,5},{9,10},{10,9},{13,14},{14,13},{17,18},{18,... | collective-permute-start | bytes 3145736 | tf_op jit(solution)/shard_map/ppermute | solution.py:547
  1108.7 64.9 %collective-permute-start.78 = (f32[1,5408]{1,0:T(1,128)S(1)}, f32[1,5408]{1,0:T(1,128)S(1)}, u32[]{:S(2)}, u32[]{:S(2)}) collective-permute-start(f32[1,5408]{1,0:T(1,128)S(1)} %add.779), channel_id=1, source_target_pairs={{0,2},{1,3},{2,0},{3,1},{4,6},{5,7},{6,4},{7,5},{8,10},{9,11},{10,... | collective-permute-start | bytes 64904 | tf_op jit(solution)/shard_map/ppermute | solution.py:346
  1113.4 73.9 %collective-permute-start.82 = (bf16[2,256,1024]{2,1,0:T(8,128)(2,1)S(1)}, bf16[2,256,1024]{2,1,0:T(8,128)(2,1)}, u32[]{:S(2)}, u32[]{:S(2)}) collective-permute-start(bf16[2,256,1024]{2,1,0:T(8,128)(2,1)S(1)} %add.782), channel_id=1, source_target_pairs={{1,0},{2,3},{5,4},{6,7},{9,8},{10,11},{13,12},{14,15},{17,16},{18,... | collective-permute-start | bytes 3145736 | tf_op jit(solution)/shard_map/ppermute | solution.py:553
  1116.6 67.2 %collective-permute-start.90 = (bf16[2,256,1024]{2,1,0:T(8,128)(2,1)}, bf16[2,256,1024]{2,1,0:T(8,128)(2,1)}, u32[]{:S(2)}, u32[]{:S(2)}) collective-permute-start(bf16[2,256,1024]{2,1,0:T(8,128)(2,1)} %get-tuple-element.234), channel_id=1, source_target_pairs={{1,2},{2,1},{5,6},{6,5},{9,10},{10,9},{13,14},{14,13},{17,18},{18,... | collective-permute-start | bytes 3145736 | tf_op jit(solution)/shard_map/ppermute | solution.py:547
  1182.5 88.4 %collective-permute-start.96 = (bf16[256,2048]{1,0:T(8,128)(2,1)S(1)}, bf16[256,2048]{1,0:T(8,128)(2,1)S(1)}, u32[]{:S(2)}, u32[]{:S(2)}) collective-permute-start(bf16[256,2048]{1,0:T(8,128)(2,1)S(1)} %add.787), channel_id=1, source_target_pairs={{1,0},{2,3},{5,4},{6,7},{9,8},{10,11},{13,12},{14,15},{17,16},{18,... | collective-permute-start | bytes 3145736 | tf_op jit(solution)/shard_map/ppermute | solution.py:553
  1185.8 62.4 %collective-permute-start.91 = (bf16[2,256,1024]{2,1,0:T(8,128)(2,1)S(1)}, bf16[2,256,1024]{2,1,0:T(8,128)(2,1)S(1)}, u32[]{:S(2)}, u32[]{:S(2)}) collective-permute-start(bf16[2,256,1024]{2,1,0:T(8,128)(2,1)S(1)} %add.786), channel_id=1, source_target_pairs={{1,0},{2,3},{5,4},{6,7},{9,8},{10,11},{13,12},{14,15},{17,16},{18,... | collective-permute-start | bytes 3145736 | tf_op jit(solution)/shard_map/ppermute | solution.py:553
  1188.8 82.3 %collective-permute-start.85 = (bf16[256,1024]{1,0:T(8,128)(2,1)S(1)}, bf16[256,1024]{1,0:T(8,128)(2,1)S(1)}, u32[]{:S(2)}, u32[]{:S(2)}) collective-permute-start(bf16[256,1024]{1,0:T(8,128)(2,1)S(1)} %get-tuple-element.256), channel_id=1, source_target_pairs={{0,24},{8,16},{16,8},{24,0},{1,25},{9,17},{17,9},{25,1},{2,26},{10... | collective-permute-start | bytes 1572872 | tf_op jit(solution)/shard_map/ppermute | solution.py:346
  1192.8 74.4 %collective-permute-start.88 = (bf16[2,256,1024]{2,1,0:T(8,128)(2,1)S(1)}, bf16[2,256,1024]{2,1,0:T(8,128)(2,1)S(1)}, u32[]{:S(2)}, u32[]{:S(2)}) collective-permute-start(bf16[2,256,1024]{2,1,0:T(8,128)(2,1)S(1)} %add.784), channel_id=1, source_target_pairs={{1,0},{2,3},{5,4},{6,7},{9,8},{10,11},{13,12},{14,15},{17,16},{18,... | collective-permute-start | bytes 3145736 | tf_op jit(solution)/shard_map/ppermute | solution.py:553
  1204.8 73.7 %collective-permute-start.84 = (bf16[256,1024]{1,0:T(8,128)(2,1)S(1)}, bf16[256,1024]{1,0:T(8,128)(2,1)}, u32[]{:S(2)}, u32[]{:S(2)}) collective-permute-start(bf16[256,1024]{1,0:T(8,128)(2,1)S(1)} %get-tuple-element.254), channel_id=1, source_target_pairs={{0,16},{8,24},{16,0},{24,8},{1,17},{9,25},{17,1},{25,9},{2,18},{10... | collective-permute-start | bytes 1572872 | tf_op jit(solution)/shard_map/ppermute | solution.py:346
  (165 other events, 3899.5 us)
Sparse Core Ops, SparseCore 0:
  9.5 13.2 all-gather.4
  24.4 17.1 all-gather.6
  560.3 64.1 reduce-scatter.2
  627.2 102.0 reduce-scatter.4
  841.4 104.3 all-gather.10
  1002.0 157.0 all-gather.8

commit v5 on v3

--- a/solution.py
+++ b/solution.py
@@ -415,21 +415,25 @@
     return place(parts, spots), pieces[1:]
 
 
-def head_columns_seq(shards, here):
-    copies, count = lax.axis_size("r"), lax.axis_size("seq")
-    turn, spot = lax.axis_index("r"), lax.axis_index("seq")
+def seq_pieces(shards, here):
+    count, spot = lax.axis_size("seq"), lax.axis_index("seq")
     rows = shards[0].shape[0] // count
     shards = [lax.dynamic_slice_in_dim(shard, spot * rows, rows, 0) for shard in shards]
     own = column_cuts(shards, here, 0)
-    pieces = [own] + [swap(column_cuts(shards, here, k), "p", k) for k in range(1, HEADS)]
+    return jnp.stack([own] + [swap(column_cuts(shards, here, k), "p", k) for k in range(1, HEADS)])
+
+
+def seq_columns(pieces, here):
+    copies, count = lax.axis_size("r"), lax.axis_size("seq")
+    turn, spot = lax.axis_index("r"), lax.axis_index("seq")
     parts, spots = [], []
-    for j, part in enumerate(gather_seq(jnp.stack(pieces))):
+    for j, part in enumerate(gather_seq(pieces)):
         for m in range(copies):
             parts.append(part if m == 0 else swap(part, "r", m))
             spots.append(
                 [(((here ^ k) * copies + (turn ^ m)) * count + (spot ^ j)) for k in range(HEADS)]
             )
-    return place(parts, spots), pieces[1:]
+    return place(parts, spots)
 
 
 def gather_small(packed, here, turn):
@@ -533,31 +537,6 @@
         ),
         compiler_params=pltpu.CompilerParams(vmem_limit_bytes=56 << 20),
     )(spots, *([parts] * spans))
-
-
-def inward(value):
-    count = lax.axis_size("seq")
-    for i in range(count // 2 - 1):
-        value = value + lax.ppermute(value, "seq", [(i, i + 1), (count - 1 - i, count - 2 - i)])
-    return value
-
-
-def across(value):
-    half = lax.axis_size("seq") // 2
-    return value + lax.ppermute(value, "seq", [(half - 1, half), (half, half - 1)])
-
-
-def outward(total):
-    count, spot = lax.axis_size("seq"), lax.axis_index("seq")
-    for i in range(count // 2 - 2, -1, -1):
-        got = lax.ppermute(total, "seq", [(i + 1, i), (count - 2 - i, count - 1 - i)])
-        total = jnp.where((spot == i) | (spot == count - 1 - i), got, total)
-    return total
-
-
-def spread_line(near, far, here, n_out):
-    got = [far[0], swap(near[0], "p", 1), swap(far[1], "p", 2), swap(near[1], "p", 3)]
-    return assemble(jnp.stack(got)[None], [here ^ k for k in range(HEADS)], n_out)
 
 
 def swap_diagonal(part):
@@ -617,10 +596,10 @@
     mask_own = masks[0][:, None]
 
     token_blocks = gather_heads(tokens)
-    weight_kv, kv_pieces = head_columns_seq([key_proj, value_proj], here)
+    weight_kv, kv_pieces = head_columns([key_proj, value_proj], here)
     late = lax.optimization_barrier((query_proj, swish_proj, mlp_gate, mlp_up) + tuple(kv_pieces))
     weight_qs, qs_pieces = head_columns(late[:2], here)
-    weight_gu, gu_pieces = head_columns_seq(late[2:4], here)
+    gu_pieces = seq_pieces(late[2:4], here)
     grad_blocks = gather_heads(after(grad_out, *qs_pieces))
     weight_out = lax.all_gather(out_proj, "r", axis=0, tiled=True)
     weight_down = lax.all_gather(mlp_down, "r", axis=0, tiled=True)
@@ -636,6 +615,8 @@
     state, decay = chunk_states(kv, li)
     decay = decay[:, :, :1]
     init = chain_pair(state, decay, True)
+    init, gu_pieces = lax.optimization_barrier((init, gu_pieces))
+    weight_gu = seq_columns(gu_pieces, here)
     qs = mm(normed, weight_qs).reshape(HEADS, rows, 2 * HEAD)
     gated, mixer_out, probs, mix = mixer_forward(qs, kv, li, init, gain_head8)
     gated = gated.reshape(group, HEAD)
@@ -650,8 +631,7 @@
     scale_two = inverse_rms(residual)
     hat_two = residual * scale_two
     normed_two_own = (hat_two * gain_two).astype(BF)
-    two_blocks = gather_heads(normed_two_own)
-    normed_two = jnp.concatenate(two_blocks)
+    normed_two = jnp.concatenate(gather_heads(normed_two_own))
 
     hidden_width = weight_down.shape[0]
     gate_up = mm(normed_two, weight_gu)
@@ -663,39 +643,33 @@
     order = [here ^ k for k in range(HEADS)]
     hops = range(1, copies)
     down_rows = mlp_down.shape[0]
-
-    def down_cut(m):
-        return lax.dynamic_slice_in_dim(hidden, (turn ^ m) * down_rows, down_rows, 1)
-
-    down_away = [mm_tn(down_cut(m), grad_mlp).astype(BF) for m in hops]
-    grad_gu, *down_away = lax.optimization_barrier((grad_gu,) + tuple(down_away))
     two_view = normed_two.reshape(group, HEADS, copies, shard)
     gu_away = [mm_tn(split_rows(two_view, turn, m, order), grad_gu).astype(BF) for m in hops]
-    down_total = sum_copies(lambda: mm_tn(down_cut(0), grad_mlp), down_away)
-    down_half = down_rows // 2
-    grad_gu, *gu_away, down_total = lax.optimization_barrier((grad_gu, *gu_away, down_total))
-    down_near, down_far = inward(down_total[:down_half]), inward(down_total[down_half:])
-    two_part = mm_nt(grad_gu, weight_gu).astype(BF).reshape(HEADS, rows, D)
+    two_part = mm_nt(after(grad_gu, *gu_away), weight_gu).astype(BF)
     gu_total = sum_copies(
         lambda: mm_tn(split_rows(two_view, turn, 0, order), after(grad_gu, two_part)), gu_away
     )
-    grad_norm_two, gu_total, down_near = scatter_heads(
-        [two_part[k] for k in range(HEADS)], gu_total, down_near
-    )
     gu_part = lax.psum_scatter(
         gu_total.reshape(HEADS, shard, 2 * hidden_width), "seq", scatter_dimension=0, tiled=True
     )
-    down_near = across(down_near)
+    hidden_late = after(hidden, gu_total)
+
+    def down_grad_part(m):
+        cut = lax.dynamic_slice_in_dim(hidden_late, (turn ^ m) * down_rows, down_rows, 1)
+        return mm_tn(cut, grad_mlp)
+
+    down_total = sum_copies(
+        lambda: down_grad_part(0), [down_grad_part(m).astype(BF) for m in hops]
+    )
+    two_part = two_part.reshape(HEADS, rows, D)
+    grad_norm_two, down_total = scatter_heads([two_part[k] for k in range(HEADS)], down_total)
     gain_two_grad = jnp.sum(grad_norm_two * hat_two, axis=0)
     grad_rows = grad_out.astype(F32)
     grad_resid = grad_rows + norm_back(grad_norm_two * gain_two, hat_two, scale_two)
     grad_attn_own = (mask_own * grad_resid).astype(BF)
     attn_blocks = gather_heads(grad_attn_own)
     mlp_part = mm(hidden, weight_down).astype(BF)
-    mlp_part, down_near, down_far, *attn_blocks = lax.optimization_barrier(
-        (mlp_part, down_near, down_far) + tuple(attn_blocks)
-    )
-    down_grad = jnp.concatenate([outward(down_near), outward(across(down_far))])
+    mlp_part, *attn_blocks = lax.optimization_barrier((mlp_part,) + tuple(attn_blocks))
     grad_attn = jnp.concatenate(attn_blocks)
     mlp_part = mlp_part.reshape(HEADS, rows, D)
     mlp_out = scatter_heads([mlp_part[k] for k in range(HEADS)])
@@ -724,9 +698,6 @@
     ends, gu_part, out_total, qs_total = lax.optimization_barrier(
         (ends, gu_part, out_total, qs_total)
     )
-    gu_whole = lax.all_gather(gu_part, "seq", axis=0, tiled=True)
-    qs_total = qs_total.reshape(HEADS, shard, 2 * HEAD)
-    out_total, qs_near, qs_far = inward(out_total), inward(qs_total[1::2]), inward(qs_total[0::2])
     grad_kv, grad_li = mixer_finish(kv, li, init, ends, grad_kv, grad_li)
     grad_kv = grad_kv.reshape(group, 2 * HEAD)
     grad_li = grad_li.reshape(group, 2 * SLOTS)
@@ -751,17 +722,25 @@
         .reshape(HEADS, rows, D)
     )
     kv_total = weight_grad(one_views, grad_kv)
-    grad_norm_one, kv_total, out_total, qs_near, qs_far = scatter_heads(
-        [one_part[k] for k in range(HEADS)], kv_total, out_total, qs_near, qs_far
-    )
+    grad_norm_one, kv_total = scatter_heads([one_part[k] for k in range(HEADS)], kv_total)
+
+    qs_total = qs_total.reshape(HEADS, shard, 2 * HEAD)
     kv_total = kv_total.reshape(HEADS, shard, 2 * HEAD)
-    kv_near, kv_far = inward(kv_total[1::2]), inward(kv_total[0::2])
-    out_grad = outward(across(out_total)).astype(F32)
-    qs_near, qs_far = outward(across(qs_near)), outward(across(qs_far))
-    kv_near, kv_far = outward(across(kv_near)), outward(across(kv_far))
+    gu_whole = lax.all_gather(gu_part, "seq", axis=0, tiled=True)
+    qs_part = lax.psum_scatter(
+        after(qs_total, gu_whole), "seq", scatter_dimension=0, tiled=True
+    )
+    down_grad = lax.psum(after(down_total, qs_part), "seq")
+    qs_whole = lax.all_gather(after(swap_diagonal(qs_part), down_grad), "seq", axis=0, tiled=True)
+    kv_part = lax.psum_scatter(
+        after(kv_total, qs_whole), "seq", scatter_dimension=0, tiled=True
+    )
+    out_grad = lax.psum(after(out_total, kv_part), "seq")
+    kv_whole = lax.all_gather(after(swap_diagonal(kv_part), out_grad), "seq", axis=0, tiled=True)
     gate_grad, up_grad = assemble(gu_whole[None], order, 2)
-    query_grad, swish_grad = spread_line(qs_near, qs_far, here, 2)
-    key_grad, value_grad = spread_line(kv_near, kv_far, here, 2)
+    query_grad, swish_grad = assemble(qs_whole[None], order, 2)
+    key_grad, value_grad = assemble(kv_whole[None], order, 2)
+    out_grad = out_grad.astype(F32)
     scale_one = inverse_rms(tokens_f)
     hat_one = tokens_f * scale_one
     gain_one_grad = jnp.sum(grad_norm_one * hat_one, axis=0)

time: 1220 us -> 1110 us (0.910)
  waiting for transfers between devices: 634 us -> 585 us
  starting transfers between devices: 136 us -> 95 us
  other arithmetic: 108 us -> 83.9 us
    ppermute x21 -> x0, waiting for transfers between devices: 243 us -> none  [the longest x7 190 us: outward(): lax.ppermute(total, 'seq', [(i + 1, i), (count - 2 - i, count - 1 - i)])]
    psum x0 -> x2, waiting for transfers between devices: none -> 128 us  [the longest x1 81.6 us: body(): down_grad = lax.psum(after(down_total, qs_part), 'seq')]
    all_gather x1, waiting for transfers between devices: 0.01 us -> 123 us  [body(): gu_whole = lax.all_gather(gu_part, 'seq', axis=0, tiled=True)]
    ppermute x72 -> x63, waiting for transfers between devices: 361 us -> 254 us  [swap(): return lax.ppermute(value, axis, [(i, i ^ step) for i in range(count)])]
    reduce_scatter x0 -> x2, waiting for transfers between devices: none -> 59.9 us  [the longest x1 44.6 us: body(): lax.psum_scatter(after(qs_total, gu_whole), 'seq', scatter_dimension=0, t...]
    ppermute x21 -> x0, starting transfers between devices: 39.4 us -> none  [the longest x7 19.7 us: inward(): lax.ppermute(value, 'seq', [(i, i + 1), (count - 1 - i, count - 2 - i)])]
    add x11 -> x0, other arithmetic: 24.1 us -> none  [the longest x7 12.5 us: across(): value + lax.ppermute(value, 'seq', [(half - 1, half), (half, half - 1)])]
    ppermute x72 -> x63, starting transfers between devices: 79.3 us -> 58.2 us  [swap(): return lax.ppermute(value, axis, [(i, i ^ step) for i in range(count)])]
  transfers between devices with their start and end apart: 110 -> 88, of which waited for: 35 -> 29; matrix products, arithmetic and copies ran while one was open for 23% -> 23% of each run, Pallas kernels for 7% -> 8%
where the time goes in v5:
time: 1110 us
  waiting for transfers between devices  585 us (53%)
  matrix products  181 us (16%)
  starting transfers between devices  95 us (9%)
  Pallas kernels  92.3 us (8%)
  other arithmetic  83.9 us (8%)
  local copies, waits for them, and re-layouts  52.1 us (5%)
  between operations  16.6 us (1%)
    ppermute x63, waiting for transfers between devices, swap(): return lax.ppermute(value, axis, [(i, i ^ step) for i in range(count)])  254 us
    all_gather x1, waiting for transfers between devices, body(): gu_whole = lax.all_gather(gu_part, 'seq', axis=0, tiled=True)  123 us
    psum x1, waiting for transfers between devices, body(): down_grad = lax.psum(after(down_total, qs_part), 'seq')  81.6 us
    dot_general x11, matrix products, mm_tn(): lax.dot_general(a, b, (((0,), (0,)), ((), ())), preferred_element_type=F32)  70.9 us
    ppermute x63, starting transfers between devices, swap(): return lax.ppermute(value, axis, [(i, i ^ step) for i in range(count)])  58.2 us
    dot_general x6, matrix products, mm_nt(): lax.dot_general(a, b, (((1,), (1,)), ((), ())), preferred_element_type=F32)  57.4 us
    pallas_call x4, Pallas kernels, run(): pl.pallas_call(kernel, grid=(args[0].shape[0],), in_specs=specs, out_spec...  49.4 us
    dot_general x6, matrix products, mm(): lax.dot_general(a, b, (((1,), (0,)), ((), ())), preferred_element_type=F32)  49.4 us
  transfers between devices with their start and end apart: 88, of which 29 were waited for; matrix products, arithmetic and copies ran while one was open for 23% of the time, Pallas kernels for 8%

profile of v5, /device:TPU:0, one launch (start us, length us, event | category | flops | bytes accessed | tf_op | source)
XLA Modules:
  0.0 1106.2 jit_solution(2891455885849780600)
XLA Ops:
  27.4 9.6 collective-permute-done.1
  38.5 21.2 %collective-permute-done.2 = f32[2,5409]{1,0:T(2,128)S(1)} collective-permute-done((f32[2,5409]{1,0:T(2,128)S(1)}, f32[2,5409]{1,0:T(2,128)S(1)}, u32[]{:S(2)}, u32[]{:S(2)}) %collective-permute-start.2) | collective-permute-done | bytes 43304 | tf_op jit(solution)/shard_map/ppermute | solution.py:346
  68.7 16.4 %collective-permute-done.8 = bf16[256,1024]{1,0:T(8,128)(2,1)} collective-permute-done((bf16[256,1024]{1,0:T(8,128)(2,1)}, bf16[256,1024]{1,0:T(8,128)(2,1)}, u32[]{:S(2)}, u32[]{:S(2)}) %collective-permute-start.8) | collective-permute-done | bytes 524320 | tf_op jit(solution)/shard_map/ppermute | solution.py:346
  106.5 5.6 shard_map.289
  112.2 6.8 fusion.2
  118.9 5.7 convolution_convert_fusion.8
  128.3 5.5 shard_map.290
  155.2 5.7 collective-permute-done.15
  173.6 6.0 shard_map.288
  181.1 8.4 fusion.77
  194.5 15.0 %shard_map.291 = (bf16[4,256,512]{2,1,0:T(8,128)(2,1)}, f32[4,256,512]{2,1,0:T(8,128)}, f32[4,256,64]{2,1,0:T(8,128)}, bf16[4,256,256]{2,1,0:T(8,128)(2,1)}) custom-call(f32[4,256,1024]{2,1,0:T(8,128)} %bitcast.194, bf16[4,256,1024]{2,1,0:T(8,128)(2,1)} %bitcast.197, f32[4,256,128]{2,1,0:T(8,128)} %bitcast.175, f32[4,64,1024]{2,1,0:T(8,128)} %pad_maximum_fusion.6.init_ref, ...), custom_call_target="tpu_custom_call" | custom-call | flops 12000000000 | bytes 16000000 | tf_op jit(solution)/shard_map/pallas_call | solution.py:258
  219.3 20.7 %collective-permute-done.30 = bf16[256,2048]{1,0:T(8,128)(2,1)S(1)} collective-permute-done((bf16[256,2048]{1,0:T(8,128)(2,1)S(1)}, bf16[256,2048]{1,0:T(8,128)(2,1)S(1)}, u32[]{:S(2)}, u32[]{:S(2)}) %collective-permute-start.30) | collective-permute-done | bytes 1048608 | tf_op jit(solution)/shard_map/ppermute | solution.py:346
  241.9 7.3 collective-permute-done.40.refs_2_
  249.2 7.2 collective-permute-done.42.refs_4_
  256.5 13.7 %fusion.66 = f32[1024,1408]{1,0:T(8,128)} fusion(bf16[1408,2048]{1,0:T(8,128)(2,1)} %all-gather.8.cloned.1.call-done, bf16[256,2048]{1,0:T(8,128)(2,1)} %collective-permute-done.35, bf16[256,2048]{1,0:T(8,128)(2,1)} %collective-permute-done.34, bf16[256,2048]{1,0:T(8,128)(2,1)} %collective-permute-done.33, bf16[256,2048]{1,0:T(8,128)(2,1)} %param.33, ...), kind=kOutput, calls=%fused_computation.220 | convolution fusion | flops 5926551552 | bytes 15732736 | tf_op jit(solution)/shard_map/dot_general | solution.py:23
  270.3 17.0 %collective-permute-done.44.refs_6_ = bf16[4,64,2816]{2,1,0:T(8,128)(2,1)} collective-permute-done((bf16[4,64,2816]{2,1,0:T(8,128)(2,1)}, bf16[4,64,2816]{2,1,0:T(8,128)(2,1)}, u32[]{:S(2)}, u32[]{:S(2)}) %collective-permute-start.44) | collective-permute-done | bytes 1441824 | tf_op jit(solution)/shard_map/ppermute | solution.py:346
  295.5 13.7 %shard_map.292 = bf16[2048,2816]{1,0:T(8,128)(2,1)} custom-call(s32[32]{0:T(128)} %stack.221.spot_ref, bf16[4,64,2816]{2,1,0:T(8,128)(2,1)} %pad_maximum_fusion.5.refs_0_, bf16[4,64,2816]{2,1,0:T(8,128)(2,1)} %collective-permute-done.39.refs_1_, bf16[4,64,2816]{2,1,0:T(8,128)(2,1)} %collective-permute-done.40.refs_2_, ...), custom_call_target="tpu_custom_call" | custom-call | bytes 23068672 | tf_op jit(solution)/shard_map/pallas_call | solution.py:382
  309.2 9.2 collective-permute-done.38
  318.4 22.0 %collective-permute-done.37 = bf16[256,2048]{1,0:T(8,128)(2,1)} collective-permute-done((bf16[256,2048]{1,0:T(8,128)(2,1)S(1)}, bf16[256,2048]{1,0:T(8,128)(2,1)}, u32[]{:S(2)}, u32[]{:S(2)}) %collective-permute-start.37) | collective-permute-done | bytes 1048608 | tf_op jit(solution)/shard_map/ppermute | solution.py:346
  340.4 21.2 %fusion.65 = f32[1024,2816]{1,0:T(8,128)} fusion(bf16[2048,2816]{1,0:T(8,128)(2,1)} %shard_map.292, bf16[256,2048]{1,0:T(8,128)(2,1)} %collective-permute-done.38, bf16[256,2048]{1,0:T(8,128)(2,1)} %collective-permute-done.37, bf16[256,2048]{1,0:T(8,128)(2,1)} %collective-permute-done.36, bf16[256,2048]{1,0:T(8,128)(2,1)S(1)} %multiply_convert_fusion.5), kind=kOutput, calls=%fused_computation.219 | convolution fusion | flops 11827937280 | bytes 27262976 | tf_op jit(solution)/shard_map/dot_general | solution.py:19
  361.6 7.1 multiply_convert_fusion.2
  374.5 8.9 convolution_convert_fusion
  386.6 16.4 %convolution_convert_fusion.1 = bf16[1024,2048]{1,0:T(8,128)(2,1)} fusion(bf16[1024,2816]{1,0:T(8,128)(2,1)S(1)} %pad_maximum_fusion, bf16[2048,2816]{1,0:T(8,128)(2,1)} %shard_map.292), kind=kOutput, calls=%fused_computation.21 | convolution fusion | flops 11813257216 | bytes 21495808 | tf_op jit(solution)/shard_map/dot_general | solution.py:23
  403.0 10.6 add_convert_fusion
  413.6 7.5 convolution_convert_fusion.4
  431.6 8.4 add_convert_fusion.2
  439.9 14.4 %collective-permute-done.46 = bf16[256,2048]{1,0:T(8,128)(2,1)S(1)} collective-permute-done((bf16[256,2048]{1,0:T(8,128)(2,1)}, bf16[256,2048]{1,0:T(8,128)(2,1)S(1)}, u32[]{:S(2)}, u32[]{:S(2)}) %collective-permute-start.46) | collective-permute-done | bytes 1048608 | tf_op jit(solution)/shard_map/ppermute | solution.py:346
  454.3 21.8 %collective-permute-done.47 = bf16[256,2048]{1,0:T(8,128)(2,1)} collective-permute-done((bf16[256,2048]{1,0:T(8,128)(2,1)}, bf16[256,2048]{1,0:T(8,128)(2,1)}, u32[]{:S(2)}, u32[]{:S(2)}) %collective-permute-start.47) | collective-permute-done | bytes 1048608 | tf_op jit(solution)/shard_map/ppermute | solution.py:346
  487.6 8.6 convolution_convert_fusion.2
  496.2 13.9 %collective-permute-done.51 = bf16[256,2048]{1,0:T(8,128)(2,1)S(1)} collective-permute-done((bf16[256,2048]{1,0:T(8,128)(2,1)S(1)}, bf16[256,2048]{1,0:T(8,128)(2,1)S(1)}, u32[]{:S(2)}, u32[]{:S(2)}) %collective-permute-start.51) | collective-permute-done | bytes 1048608 | tf_op jit(solution)/shard_map/ppermute | solution.py:346
  510.1 19.9 %collective-permute-done.52 = bf16[256,2048]{1,0:T(8,128)(2,1)S(1)} collective-permute-done((bf16[256,2048]{1,0:T(8,128)(2,1)S(1)}, bf16[256,2048]{1,0:T(8,128)(2,1)S(1)}, u32[]{:S(2)}, u32[]{:S(2)}) %collective-permute-start.52) | collective-permute-done | bytes 1048608 | tf_op jit(solution)/shard_map/ppermute | solution.py:346
  535.9 19.8 %shard_map.293 = (bf16[4,256,1024]{2,1,0:T(8,128)(2,1)}, f32[4,256,1024]{2,1,0:T(8,128)}, f32[4,256,128]{2,1,0:T(8,128)}, f32[4,64,1024]{2,1,0:T(8,128)}, f32[8,512]{1,0:T(8,128)}) custom-call(f32[4,256,1024]{2,1,0:T(8,128)} %bitcast.195, bf16[4,256,1024]{2,1,0:T(8,128)(2,1)} %bitcast.198, f32[4,256,128]{2,1,0:T(8,128)} %bitcast.176, ...), custom_call_target="tpu_custom_call" | custom-call | flops 24000000000 | bytes 20000000 | tf_op jit(solution)/shard_map/pallas_call | solution.py:258
  555.8 5.4 convolution_convert_fusion.7
  577.5 12.4 %collective-permute-start.63 = (bf16[1,256,2816]{2,1,0:T(8,128)(2,1)}, bf16[1,256,2816]{2,1,0:T(8,128)(2,1)}, u32[]{:S(2)}, u32[]{:S(2)}) collective-permute-start(bf16[1,256,2816]{2,1,0:T(8,128)(2,1)} %reduce-scatter.4.cloned.1.call-done), channel_id=1, source_target_pairs={{0,0},{1,9},{2,18},{3,27},{8,8},{9,1},{10,26},{11,19},{16,16},{17,... | collective-permute-start | bytes 4325384 | tf_op jit(solution)/shard_map/ppermute | solution.py:545
  593.6 6.6 add_convert_fusion.4
  608.1 122.9 %all-gather.10.cloned.1.call-done = bf16[4,256,2816]{2,1,0:T(8,128)(2,1)} async-done(((bf16[1,256,2816]{2,1,0:T(8,128)(2,1)}), bf16[4,256,2816]{2,1,0:T(8,128)(2,1)}) %all-gather.10.cloned.1.call-update) | async-done | bytes 5767184 | tf_op jit(solution)/shard_map/all_gather | solution.py:729
  731.0 44.6 %reduce-scatter.6.cloned.1.call-done = bf16[1,256,1024]{2,1,0:T(8,128)(2,1)} async-done(((bf16[4,256,1024]{2,1,0:T(8,128)(2,1)}), bf16[1,256,1024]{2,1,0:T(8,128)(2,1)}) %reduce-scatter.6.cloned.1.call-update) | async-done | bytes 524304 | tf_op jit(solution)/shard_map/reduce_scatter | solution.py:730
  775.7 9.1 shard_map.294
  789.2 6.1 convolution_convert_fusion.6
  795.4 6.8 fusion.80
  808.1 81.6 %all-reduce.3.cloned.1.call-done = bf16[704,2048]{1,0:T(8,128)(2,1)} async-done(((bf16[704,2048]{1,0:T(8,128)(2,1)}), bf16[704,2048]{1,0:T(8,128)(2,1)}) %all-reduce.3.cloned.1.call-update) | async-done | bytes 2883600 | tf_op jit(solution)/shard_map/psum | solution.py:733
  889.7 12.2 %add_convert_fusion.1 = bf16[1024,2048]{1,0:T(8,128)(2,1)S(1)} fusion(f32[1024,2048]{1,0:T(8,128)} %fusion.81, f32[1024,2048]{1,0:T(8,128)} %fusion.80, bf16[1024,1024]{1,0:T(8,128)(2,1)} %bitcast.202, bf16[2048,1024]{1,0:T(8,128)(2,1)} %shard_map.288), kind=kOutput, calls=%fused_computation.7 | convolution fusion | flops 4301258752 | bytes 27262976 | tf_op jit(solution)/shard_map/dot_general | solution.py:23
  911.4 17.2 %collective-permute-done.66 = bf16[256,2048]{1,0:T(8,128)(2,1)S(1)} collective-permute-done((bf16[256,2048]{1,0:T(8,128)(2,1)S(1)}, bf16[256,2048]{1,0:T(8,128)(2,1)S(1)}, u32[]{:S(2)}, u32[]{:S(2)}) %collective-permute-start.66) | collective-permute-done | bytes 1048608 | tf_op jit(solution)/shard_map/ppermute | solution.py:346
  929.5 21.4 %collective-permute-done.67 = bf16[256,2048]{1,0:T(8,128)(2,1)S(1)} collective-permute-done((bf16[256,2048]{1,0:T(8,128)(2,1)S(1)}, bf16[256,2048]{1,0:T(8,128)(2,1)S(1)}, u32[]{:S(2)}, u32[]{:S(2)}) %collective-permute-start.67) | collective-permute-done | bytes 1048608 | tf_op jit(solution)/shard_map/ppermute | solution.py:346
  978.7 15.3 %reduce-scatter.8.cloned.1.call-done = bf16[1,256,1024]{2,1,0:T(8,128)(2,1)} async-done(((bf16[4,256,1024]{2,1,0:T(8,128)(2,1)}), bf16[1,256,1024]{2,1,0:T(8,128)(2,1)}) %reduce-scatter.8.cloned.1.call-update) | async-done | bytes 524304 | tf_op jit(solution)/shard_map/reduce_scatter | solution.py:735
  1001.2 46.3 %all-reduce.5.cloned.1.call-done = bf16[256,2048]{1,0:T(8,128)(2,1)} async-done(((bf16[256,2048]{1,0:T(8,128)(2,1)}), bf16[256,2048]{1,0:T(8,128)(2,1)}) %all-reduce.5.cloned.1.call-update) | async-done | bytes 1048592 | tf_op jit(solution)/shard_map/psum | solution.py:738
  1065.3 8.0 shard_map.297
  1084.9 9.5 all-gather.14.cloned.1.call-done
  (478 shorter events, 269.2 us)
Async XLA Ops:
  7.2 202.3 %all-gather.6.cloned.1.call-start = ((), (), s32[]{:S(2)}) async-start(), calls=%async_computation.3 | async-start | bytes 3145728 | tf_op jit(solution)/shard_map/all_gather | solution.py:604
  7.9 248.5 %all-gather.8.cloned.1.call-start = ((), (), s32[]{:S(2)}) async-start(), calls=%async_computation.4 | async-start | bytes 8650752 | tf_op jit(solution)/shard_map/all_gather | solution.py:605
  8.0 90.2 %collective-permute-start.6 = (bf16[256,2048]{1,0:T(8,128)(2,1)}, bf16[256,2048]{1,0:T(8,128)(2,1)S(1)}, u32[]{:S(2)}, u32[]{:S(2)}) collective-permute-start(bf16[256,2048]{1,0:T(8,128)(2,1)} %param.17), channel_id=1, source_target_pairs={{0,24},{8,16},{16,8},{24,0},{1,25},{9,17},{17,9},{25,1},{2,26},{10... | collective-permute-start | bytes 3145736 | tf_op jit(solution)/shard_map/ppermute | solution.py:346
  12.0 86.4 %collective-permute-start.5 = (bf16[256,2048]{1,0:T(8,128)(2,1)}, bf16[256,2048]{1,0:T(8,128)(2,1)}, u32[]{:S(2)}, u32[]{:S(2)}) collective-permute-start(bf16[256,2048]{1,0:T(8,128)(2,1)} %param.17), channel_id=1, source_target_pairs={{0,16},{8,24},{16,0},{24,8},{1,17},{9,25},{17,1},{25,9},{2,18},{10... | collective-permute-start | bytes 3145736 | tf_op jit(solution)/shard_map/ppermute | solution.py:346
  17.7 546.3 %reduce-scatter.4.cloned.1.call-start = ((), (), s32[]{:S(2)}) async-start(), calls=%async_computation.5 | async-start | bytes 7208960 | tf_op jit(solution)/shard_map/reduce_scatter | solution.py:652
  23.4 36.3 %collective-permute-start.2 = (f32[2,5409]{1,0:T(2,128)S(1)}, f32[2,5409]{1,0:T(2,128)S(1)}, u32[]{:S(2)}, u32[]{:S(2)}) collective-permute-start(f32[2,5409]{1,0:T(2,128)S(1)} %pad_maximum_fusion.28), channel_id=1, source_target_pairs={{0,16},{8,24},{16,0},{24,8},{1,17},{9,25},{17,1},{25,9},{2,18},{10... | collective-permute-start | bytes 129824 | tf_op jit(solution)/shard_map/ppermute | solution.py:346
  25.3 36.1 %collective-permute-start.3 = (f32[2,5409]{1,0:T(2,128)S(1)}, f32[2,5409]{1,0:T(2,128)S(1)}, u32[]{:S(2)}, u32[]{:S(2)}) collective-permute-start(f32[2,5409]{1,0:T(2,128)S(1)} %pad_maximum_fusion.28), channel_id=1, source_target_pairs={{0,24},{8,16},{16,8},{24,0},{1,25},{9,17},{17,9},{25,1},{2,26},{10... | collective-permute-start | bytes 129824 | tf_op jit(solution)/shard_map/ppermute | solution.py:346
  37.0 31.2 %collective-permute-start.7 = (bf16[256,1024]{1,0:T(8,128)(2,1)}, bf16[256,1024]{1,0:T(8,128)(2,1)S(1)}, u32[]{:S(2)}, u32[]{:S(2)}) collective-permute-start(bf16[256,1024]{1,0:T(8,128)(2,1)} %pad_maximum_fusion.8), channel_id=1, source_target_pairs={{0,8},{8,0},{16,24},{24,16},{1,9},{9,1},{17,25},{25,17},{2,10},{10... | collective-permute-start | bytes 1572872 | tf_op jit(solution)/shard_map/ppermute | solution.py:346
  68.3 30.4 %collective-permute-start.4 = (bf16[256,2048]{1,0:T(8,128)(2,1)S(1)}, bf16[256,2048]{1,0:T(8,128)(2,1)S(1)}, u32[]{:S(2)}, u32[]{:S(2)}) collective-permute-start(bf16[256,2048]{1,0:T(8,128)(2,1)S(1)} %copy-done.2), channel_id=1, source_target_pairs={{0,8},{8,0},{16,24},{24,16},{1,9},{9,1},{17,25},{25,17},{2,10},{10... | collective-permute-start | bytes 3145736 | tf_op jit(solution)/shard_map/ppermute | solution.py:346
  89.3 63.5 %collective-permute-start.11 = (bf16[256,1024]{1,0:T(8,128)(2,1)}, bf16[256,1024]{1,0:T(8,128)(2,1)}, u32[]{:S(2)}, u32[]{:S(2)}) collective-permute-start(bf16[256,1024]{1,0:T(8,128)(2,1)} %pad_maximum_fusion.12), channel_id=1, source_target_pairs={{0,8},{8,0},{16,24},{24,16},{1,9},{9,1},{17,25},{25,17},{2,10},{10... | collective-permute-start | bytes 1572872 | tf_op jit(solution)/shard_map/ppermute | solution.py:346
  102.1 53.1 %collective-permute-start.13 = (bf16[256,1024]{1,0:T(8,128)(2,1)}, bf16[256,1024]{1,0:T(8,128)(2,1)}, u32[]{:S(2)}, u32[]{:S(2)}) collective-permute-start(bf16[256,1024]{1,0:T(8,128)(2,1)} %pad_maximum_fusion.13), channel_id=1, source_target_pairs={{0,16},{8,24},{16,0},{24,8},{1,17},{9,25},{17,1},{25,9},{2,18},{10... | collective-permute-start | bytes 1572872 | tf_op jit(solution)/shard_map/ppermute | solution.py:346
  103.6 44.0 %collective-permute-start.29 = (bf16[64,2816]{1,0:T(8,128)(2,1)}, bf16[64,2816]{1,0:T(8,128)(2,1)}, u32[]{:S(2)}, u32[]{:S(2)}) collective-permute-start(bf16[64,2816]{1,0:T(8,128)(2,1)} %pad_maximum_fusion.19), channel_id=1, source_target_pairs={{0,24},{8,16},{16,8},{24,0},{1,25},{9,17},{17,9},{25,1},{2,26},{10... | collective-permute-start | bytes 1081352 | tf_op jit(solution)/shard_map/ppermute | solution.py:346
  105.0 47.0 %collective-permute-start.28 = (bf16[64,2816]{1,0:T(8,128)(2,1)}, bf16[64,2816]{1,0:T(8,128)(2,1)}, u32[]{:S(2)}, u32[]{:S(2)}) collective-permute-start(bf16[64,2816]{1,0:T(8,128)(2,1)} %pad_maximum_fusion.18), channel_id=1, source_target_pairs={{0,16},{8,24},{16,0},{24,8},{1,17},{9,25},{17,1},{25,9},{2,18},{10... | collective-permute-start | bytes 1081352 | tf_op jit(solution)/shard_map/ppermute | solution.py:346
  169.3 47.7 %collective-permute-start.35 = (bf16[256,2048]{1,0:T(8,128)(2,1)}, bf16[256,2048]{1,0:T(8,128)(2,1)}, u32[]{:S(2)}, u32[]{:S(2)}) collective-permute-start(bf16[256,2048]{1,0:T(8,128)(2,1)} %param.33), channel_id=1, source_target_pairs={{0,24},{8,16},{16,8},{24,0},{1,25},{9,17},{17,9},{25,1},{2,26},{10... | collective-permute-start | bytes 3145736 | tf_op jit(solution)/shard_map/ppermute | solution.py:346
  170.8 46.7 %collective-permute-start.34 = (bf16[256,2048]{1,0:T(8,128)(2,1)}, bf16[256,2048]{1,0:T(8,128)(2,1)}, u32[]{:S(2)}, u32[]{:S(2)}) collective-permute-start(bf16[256,2048]{1,0:T(8,128)(2,1)} %param.33), channel_id=1, source_target_pairs={{0,16},{8,24},{16,0},{24,8},{1,17},{9,25},{17,1},{25,9},{2,18},{10... | collective-permute-start | bytes 3145736 | tf_op jit(solution)/shard_map/ppermute | solution.py:346
  171.2 46.4 %collective-permute-start.33 = (bf16[256,2048]{1,0:T(8,128)(2,1)}, bf16[256,2048]{1,0:T(8,128)(2,1)}, u32[]{:S(2)}, u32[]{:S(2)}) collective-permute-start(bf16[256,2048]{1,0:T(8,128)(2,1)} %param.33), channel_id=1, source_target_pairs={{0,8},{8,0},{16,24},{24,16},{1,9},{9,1},{17,25},{25,17},{2,10},{10... | collective-permute-start | bytes 3145736 | tf_op jit(solution)/shard_map/ppermute | solution.py:346
  190.8 58.4 %collective-permute-start.40 = (bf16[4,64,2816]{2,1,0:T(8,128)(2,1)}, bf16[4,64,2816]{2,1,0:T(8,128)(2,1)}, u32[]{:S(2)}, u32[]{:S(2)}) collective-permute-start(bf16[4,64,2816]{2,1,0:T(8,128)(2,1)} %pad_maximum_fusion.5.refs_0_), channel_id=1, source_target_pairs={{0,1},{1,0},{2,3},{3,2},{4,5},{5,4},{6,7},{7,6},{8,9},{9,8},{10,11... | collective-permute-start | bytes 4325384 | tf_op jit(solution)/shard_map/ppermute | solution.py:346
  193.9 62.6 %collective-permute-start.42 = (bf16[4,64,2816]{2,1,0:T(8,128)(2,1)}, bf16[4,64,2816]{2,1,0:T(8,128)(2,1)}, u32[]{:S(2)}, u32[]{:S(2)}) collective-permute-start(bf16[4,64,2816]{2,1,0:T(8,128)(2,1)} %pad_maximum_fusion.5.refs_0_), channel_id=1, source_target_pairs={{0,2},{1,3},{2,0},{3,1},{4,6},{5,7},{6,4},{7,5},{8,10},{9,11},{10,... | collective-permute-start | bytes 4325384 | tf_op jit(solution)/shard_map/ppermute | solution.py:346
  217.5 75.3 %collective-permute-start.39 = (bf16[4,64,2816]{2,1,0:T(8,128)(2,1)}, bf16[4,64,2816]{2,1,0:T(8,128)(2,1)}, u32[]{:S(2)}, u32[]{:S(2)}) collective-permute-start(bf16[4,64,2816]{2,1,0:T(8,128)(2,1)} %pad_maximum_fusion.5.refs_0_), channel_id=1, source_target_pairs={{0,4},{4,0},{1,5},{5,1},{2,6},{6,2},{3,7},{7,3},{8,12},{12,8},{9,1... | collective-permute-start | bytes 4325384 | tf_op jit(solution)/shard_map/ppermute | solution.py:346
  217.6 52.6 %collective-permute-start.31 = (bf16[256,2048]{1,0:T(8,128)(2,1)}, bf16[256,2048]{1,0:T(8,128)(2,1)}, u32[]{:S(2)}, u32[]{:S(2)}) collective-permute-start(bf16[256,2048]{1,0:T(8,128)(2,1)} %get-tuple-element.203), channel_id=1, source_target_pairs={{0,16},{8,24},{16,0},{24,8},{1,17},{9,25},{17,1},{25,9},{2,18},{10... | collective-permute-start | bytes 3145736 | tf_op jit(solution)/shard_map/ppermute | solution.py:346
  240.0 47.3 %collective-permute-start.32 = (bf16[256,2048]{1,0:T(8,128)(2,1)S(1)}, bf16[256,2048]{1,0:T(8,128)(2,1)}, u32[]{:S(2)}, u32[]{:S(2)}) collective-permute-start(bf16[256,2048]{1,0:T(8,128)(2,1)S(1)} %get-tuple-element.202), channel_id=1, source_target_pairs={{0,24},{8,16},{16,8},{24,0},{1,25},{9,17},{17,9},{25,1},{2,26},{10... | collective-permute-start | bytes 3145736 | tf_op jit(solution)/shard_map/ppermute | solution.py:346
  249.2 44.1 %collective-permute-start.41 = (bf16[4,64,2816]{2,1,0:T(8,128)(2,1)}, bf16[4,64,2816]{2,1,0:T(8,128)(2,1)}, u32[]{:S(2)}, u32[]{:S(2)}) collective-permute-start(bf16[4,64,2816]{2,1,0:T(8,128)(2,1)} %collective-permute-done.40.refs_2_), channel_id=1, source_target_pairs={{0,4},{4,0},{1,5},{5,1},{2,6},{6,2},{3,7},{7,3},{8,12},{12,8},{9,1... | collective-permute-start | bytes 4325384 | tf_op jit(solution)/shard_map/ppermute | solution.py:346
  256.5 30.8 %collective-permute-start.44 = (bf16[4,64,2816]{2,1,0:T(8,128)(2,1)}, bf16[4,64,2816]{2,1,0:T(8,128)(2,1)}, u32[]{:S(2)}, u32[]{:S(2)}) collective-permute-start(bf16[4,64,2816]{2,1,0:T(8,128)(2,1)} %collective-permute-done.42.refs_4_), channel_id=1, source_target_pairs={{0,1},{1,0},{2,3},{3,2},{4,5},{5,4},{6,7},{7,6},{8,9},{9,8},{10,11... | collective-permute-start | bytes 4325384 | tf_op jit(solution)/shard_map/ppermute | solution.py:346
  291.3 27.1 %collective-permute-start.38 = (bf16[256,2048]{1,0:T(8,128)(2,1)S(1)}, bf16[256,2048]{1,0:T(8,128)(2,1)}, u32[]{:S(2)}, u32[]{:S(2)}) collective-permute-start(bf16[256,2048]{1,0:T(8,128)(2,1)S(1)} %multiply_convert_fusion.5), channel_id=1, source_target_pairs={{0,24},{8,16},{16,8},{24,0},{1,25},{9,17},{17,9},{25,1},{2,26},{10... | collective-permute-start | bytes 3145736 | tf_op jit(solution)/shard_map/ppermute | solution.py:346
  292.8 47.6 %collective-permute-start.37 = (bf16[256,2048]{1,0:T(8,128)(2,1)S(1)}, bf16[256,2048]{1,0:T(8,128)(2,1)}, u32[]{:S(2)}, u32[]{:S(2)}) collective-permute-start(bf16[256,2048]{1,0:T(8,128)(2,1)S(1)} %multiply_convert_fusion.5), channel_id=1, source_target_pairs={{0,16},{8,24},{16,0},{24,8},{1,17},{9,25},{17,1},{25,9},{2,18},{10... | collective-permute-start | bytes 3145736 | tf_op jit(solution)/shard_map/ppermute | solution.py:346
  293.3 47.1 %collective-permute-start.36 = (bf16[256,2048]{1,0:T(8,128)(2,1)S(1)}, bf16[256,2048]{1,0:T(8,128)(2,1)}, u32[]{:S(2)}, u32[]{:S(2)}) collective-permute-start(bf16[256,2048]{1,0:T(8,128)(2,1)S(1)} %multiply_convert_fusion.5), channel_id=1, source_target_pairs={{0,8},{8,0},{16,24},{24,16},{1,9},{9,1},{17,25},{25,17},{2,10},{10... | collective-permute-start | bytes 3145736 | tf_op jit(solution)/shard_map/ppermute | solution.py:346
  421.5 309.4 %all-gather.10.cloned.1.call-start = ((), (), s32[]{:S(2)}) async-start(), calls=%async_computation.6 | async-start | bytes 7208960 | tf_op jit(solution)/shard_map/all_gather | solution.py:729
  428.1 26.2 %collective-permute-start.46 = (bf16[256,2048]{1,0:T(8,128)(2,1)}, bf16[256,2048]{1,0:T(8,128)(2,1)S(1)}, u32[]{:S(2)}, u32[]{:S(2)}) collective-permute-start(bf16[256,2048]{1,0:T(8,128)(2,1)} %get-tuple-element.201), channel_id=1, source_target_pairs={{0,8},{8,0},{16,24},{24,16},{1,9},{9,1},{17,25},{25,17},{2,10},{10... | collective-permute-start | bytes 3145736 | tf_op jit(solution)/shard_map/ppermute | solution.py:346
  428.5 47.7 %collective-permute-start.47 = (bf16[256,2048]{1,0:T(8,128)(2,1)}, bf16[256,2048]{1,0:T(8,128)(2,1)}, u32[]{:S(2)}, u32[]{:S(2)}) collective-permute-start(bf16[256,2048]{1,0:T(8,128)(2,1)} %get-tuple-element.200), channel_id=1, source_target_pairs={{0,16},{8,24},{16,0},{24,8},{1,17},{9,25},{17,1},{25,9},{2,18},{10... | collective-permute-start | bytes 3145736 | tf_op jit(solution)/shard_map/ppermute | solution.py:346
  429.9 46.3 %collective-permute-start.48 = (bf16[256,2048]{1,0:T(8,128)(2,1)}, bf16[256,2048]{1,0:T(8,128)(2,1)}, u32[]{:S(2)}, u32[]{:S(2)}) collective-permute-start(bf16[256,2048]{1,0:T(8,128)(2,1)} %get-tuple-element.199), channel_id=1, source_target_pairs={{0,24},{8,16},{16,8},{24,0},{1,25},{9,17},{17,9},{25,1},{2,26},{10... | collective-permute-start | bytes 3145736 | tf_op jit(solution)/shard_map/ppermute | solution.py:346
  485.8 44.2 %collective-permute-start.52 = (bf16[256,2048]{1,0:T(8,128)(2,1)S(1)}, bf16[256,2048]{1,0:T(8,128)(2,1)S(1)}, u32[]{:S(2)}, u32[]{:S(2)}) collective-permute-start(bf16[256,2048]{1,0:T(8,128)(2,1)S(1)} %get-tuple-element.98), channel_id=1, source_target_pairs={{0,16},{8,24},{16,0},{24,8},{1,17},{9,25},{17,1},{25,9},{2,18},{10... | collective-permute-start | bytes 3145736 | tf_op jit(solution)/shard_map/ppermute | solution.py:346
  486.1 45.8 %collective-permute-start.53 = (bf16[256,2048]{1,0:T(8,128)(2,1)S(1)}, bf16[256,2048]{1,0:T(8,128)(2,1)S(1)}, u32[]{:S(2)}, u32[]{:S(2)}) collective-permute-start(bf16[256,2048]{1,0:T(8,128)(2,1)S(1)} %get-tuple-element.98), channel_id=1, source_target_pairs={{0,24},{8,16},{16,8},{24,0},{1,25},{9,17},{17,9},{25,1},{2,26},{10... | collective-permute-start | bytes 3145736 | tf_op jit(solution)/shard_map/ppermute | solution.py:346
  561.2 32.4 %collective-permute-start.65 = (bf16[1024,1024]{1,0:T(8,128)(2,1)}, bf16[1024,1024]{1,0:T(8,128)(2,1)}, u32[]{:S(2)}, u32[]{:S(2)}) collective-permute-start(bf16[1024,1024]{1,0:T(8,128)(2,1)} %convolution_convert_fusion.7), channel_id=1, source_target_pairs={{0,4},{4,0},{1,5},{5,1},{2,6},{6,2},{3,7},{7,3},{8,12},{12,8},{9,1... | collective-permute-start | bytes 6291464 | tf_op jit(solution)/shard_map/ppermute | solution.py:346
  577.5 30.5 %collective-permute-start.63 = (bf16[1,256,2816]{2,1,0:T(8,128)(2,1)}, bf16[1,256,2816]{2,1,0:T(8,128)(2,1)}, u32[]{:S(2)}, u32[]{:S(2)}) collective-permute-start(bf16[1,256,2816]{2,1,0:T(8,128)(2,1)} %reduce-scatter.4.cloned.1.call-done), channel_id=1, source_target_pairs={{0,0},{1,9},{2,18},{3,27},{8,8},{9,1},{10,26},{11,19},{16,16},{17,... | collective-permute-start | bytes 4325384 | tf_op jit(solution)/shard_map/ppermute | solution.py:545
  608.0 167.6 %reduce-scatter.6.cloned.1.call-start = ((), (), s32[]{:S(2)}) async-start(), calls=%async_computation.7 | async-start | bytes 2621440 | tf_op jit(solution)/shard_map/reduce_scatter | solution.py:730
  731.0 158.7 %all-reduce.3.cloned.1.call-start = ((), (), s32[]{:S(2)}) async-start(), calls=%async_computation.8 | async-start | bytes 5767168 | tf_op jit(solution)/shard_map/psum | solution.py:733
  775.6 176.2 %all-gather.12.cloned.1.call-start = ((), (), s32[]{:S(2)}) async-start(), calls=%async_computation.9 | async-start | bytes 2621440 | tf_op jit(solution)/shard_map/all_gather | solution.py:734
  803.4 102.6 %collective-permute-start.69 = (bf16[1024,1024]{1,0:T(8,128)(2,1)}, bf16[1024,1024]{1,0:T(8,128)(2,1)}, u32[]{:S(2)}, u32[]{:S(2)}) collective-permute-start(bf16[1024,1024]{1,0:T(8,128)(2,1)} %convolution_convert_fusion.6), channel_id=1, source_target_pairs={{0,4},{4,0},{1,5},{5,1},{2,6},{6,2},{3,7},{7,3},{8,12},{12,8},{9,1... | collective-permute-start | bytes 6291464 | tf_op jit(solution)/shard_map/ppermute | solution.py:346
  889.7 104.3 %reduce-scatter.8.cloned.1.call-start = ((), (), s32[]{:S(2)}) async-start(), calls=%async_computation.10 | async-start | bytes 2621440 | tf_op jit(solution)/shard_map/reduce_scatter | solution.py:735
  902.4 26.1 %collective-permute-start.66 = (bf16[256,2048]{1,0:T(8,128)(2,1)S(1)}, bf16[256,2048]{1,0:T(8,128)(2,1)S(1)}, u32[]{:S(2)}, u32[]{:S(2)}) collective-permute-start(bf16[256,2048]{1,0:T(8,128)(2,1)S(1)} %get-tuple-element.179), channel_id=1, source_target_pairs={{0,8},{8,0},{16,24},{24,16},{1,9},{9,1},{17,25},{25,17},{2,10},{10... | collective-permute-start | bytes 3145736 | tf_op jit(solution)/shard_map/ppermute | solution.py:346
  904.0 46.9 %collective-permute-start.67 = (bf16[256,2048]{1,0:T(8,128)(2,1)S(1)}, bf16[256,2048]{1,0:T(8,128)(2,1)S(1)}, u32[]{:S(2)}, u32[]{:S(2)}) collective-permute-start(bf16[256,2048]{1,0:T(8,128)(2,1)S(1)} %get-tuple-element.178), channel_id=1, source_target_pairs={{0,16},{8,24},{16,0},{24,8},{1,17},{9,25},{17,1},{25,9},{2,18},{10... | collective-permute-start | bytes 3145736 | tf_op jit(solution)/shard_map/ppermute | solution.py:346
  905.4 46.4 %collective-permute-start.68 = (bf16[256,2048]{1,0:T(8,128)(2,1)S(1)}, bf16[256,2048]{1,0:T(8,128)(2,1)}, u32[]{:S(2)}, u32[]{:S(2)}) collective-permute-start(bf16[256,2048]{1,0:T(8,128)(2,1)S(1)} %get-tuple-element.177), channel_id=1, source_target_pairs={{0,24},{8,16},{16,8},{24,0},{1,25},{9,17},{17,9},{25,1},{2,26},{10... | collective-permute-start | bytes 3145736 | tf_op jit(solution)/shard_map/ppermute | solution.py:346
  951.9 95.6 %all-reduce.5.cloned.1.call-start = ((), (), s32[]{:S(2)}) async-start(), calls=%async_computation.11 | async-start | bytes 2097152 | tf_op jit(solution)/shard_map/psum | solution.py:738
  977.3 70.3 %collective-permute-start.56 = (bf16[256,2048]{1,0:T(8,128)(2,1)}, bf16[256,2048]{1,0:T(8,128)(2,1)}, u32[]{:S(2)}, u32[]{:S(2)}) collective-permute-start(bf16[256,2048]{1,0:T(8,128)(2,1)} %get-tuple-element.189), channel_id=1, source_target_pairs={{0,24},{8,16},{16,8},{24,0},{1,25},{9,17},{17,9},{25,1},{2,26},{10... | collective-permute-start | bytes 3145736 | tf_op jit(solution)/shard_map/ppermute | solution.py:346
  978.3 69.2 %collective-permute-start.55 = (bf16[256,2048]{1,0:T(8,128)(2,1)}, bf16[256,2048]{1,0:T(8,128)(2,1)}, u32[]{:S(2)}, u32[]{:S(2)}) collective-permute-start(bf16[256,2048]{1,0:T(8,128)(2,1)} %get-tuple-element.190), channel_id=1, source_target_pairs={{0,16},{8,24},{16,0},{24,8},{1,17},{9,25},{17,1},{25,9},{2,18},{10... | collective-permute-start | bytes 3145736 | tf_op jit(solution)/shard_map/ppermute | solution.py:346
  994.0 100.3 %all-gather.14.cloned.1.call-start = ((), (), s32[]{:S(2)}) async-start(), calls=%async_computation.12 | async-start | bytes 2621440 | tf_op jit(solution)/shard_map/all_gather | solution.py:739
  994.1 53.5 %collective-permute-start.54 = (bf16[256,2048]{1,0:T(8,128)(2,1)}, bf16[256,2048]{1,0:T(8,128)(2,1)}, u32[]{:S(2)}, u32[]{:S(2)}) collective-permute-start(bf16[256,2048]{1,0:T(8,128)(2,1)} %get-tuple-element.188), channel_id=1, source_target_pairs={{0,8},{8,0},{16,24},{24,16},{1,9},{9,1},{17,25},{25,17},{2,10},{10... | collective-permute-start | bytes 3145736 | tf_op jit(solution)/shard_map/ppermute | solution.py:346
  1001.1 50.7 %collective-permute-start.73 = (f32[1,5408]{1,0:T(1,128)S(1)}, f32[1,5408]{1,0:T(1,128)S(1)}, u32[]{:S(2)}, u32[]{:S(2)}) collective-permute-start(f32[1,5408]{1,0:T(1,128)S(1)} %constant_dynamic-slice_fusion), channel_id=1, source_target_pairs={{0,4},{4,0},{1,5},{5,1},{2,6},{6,2},{3,7},{7,3},{8,12},{12,8},{9,1... | collective-permute-start | bytes 64904 | tf_op jit(solution)/shard_map/ppermute | solution.py:346
  (121 other events, 2264.3 us)
Sparse Core Ops, SparseCore 0:
  9.5 13.2 all-gather.5
  24.4 17.1 all-gather.7
  421.7 99.5 reduce-scatter.3
  608.1 122.7 all-gather.9
  733.7 41.8 reduce-scatter.5
  777.8 111.7 all-reduce.2
  891.8 44.6 all-gather.11
  952.0 41.9 reduce-scatter.7
  996.4 51.0 all-reduce.4
  1048.9 45.3 all-gather.13

commit v6 on v5

--- a/solution.py
+++ b/solution.py
@@ -539,6 +539,35 @@
     )(spots, *([parts] * spans))
 
 
+def line_sum(chunks):
+    count, spot = lax.axis_size("seq"), lax.axis_index("seq")
+    half = count // 2
+    totals, last = [], {}
+
+    def send(value, key, pairs):
+        if key in last:
+            value = after(value, last[key])
+        last[key] = lax.ppermute(value, "seq", pairs)
+        return value, last[key]
+
+    for value in chunks:
+        for i in range(half - 1):
+            value, got = send(value, ("in", i), [(i, i + 1), (count - 1 - i, count - 2 - i)])
+            value = value + got
+        value, got = send(value, "across", [(half - 1, half), (half, half - 1)])
+        value = value + got
+        for i in range(half - 2, -1, -1):
+            value, got = send(value, ("out", i), [(i + 1, i), (count - 2 - i, count - 1 - i)])
+            value = jnp.where((spot == i) | (spot == count - 1 - i), got, value)
+        totals.append(value)
+    return totals
+
+
+def spread_line(near, far, here):
+    got = [far[0], swap(near[0], "p", 1), swap(far[1], "p", 2), swap(near[1], "p", 3)]
+    return assemble(jnp.stack(got)[None], [here ^ k for k in range(HEADS)], 2)
+
+
 def swap_diagonal(part):
     count = lax.axis_size("seq")
     sends = [(p * count + z, (p ^ z) * count + z) for p in range(HEADS) for z in range(count)]
@@ -669,7 +698,8 @@
     grad_attn_own = (mask_own * grad_resid).astype(BF)
     attn_blocks = gather_heads(grad_attn_own)
     mlp_part = mm(hidden, weight_down).astype(BF)
-    mlp_part, *attn_blocks = lax.optimization_barrier((mlp_part,) + tuple(attn_blocks))
+    mlp_part, gu_part, *attn_blocks = lax.optimization_barrier((mlp_part, gu_part, *attn_blocks))
+    gu_part = swap_diagonal(gu_part)
     grad_attn = jnp.concatenate(attn_blocks)
     mlp_part = mlp_part.reshape(HEADS, rows, D)
     mlp_out = scatter_heads([mlp_part[k] for k in range(HEADS)])
@@ -680,7 +710,7 @@
         qs, kv, li, init, gain_head8, mixer_out, probs, mix, grad_gated
     )
     adjoint, gu_part = lax.optimization_barrier((adjoint, gu_part))
-    gu_part = swap_diagonal(gu_part)
+    gu_whole = lax.all_gather(gu_part, "seq", axis=0, tiled=True)
     one_view = normed.reshape(group, HEADS, copies, shard)
     one_views = [split_rows(one_view, turn, m, order) for m in range(copies)]
     out_view = gated.reshape(group, 1, copies, shard)
@@ -695,9 +725,7 @@
     out_total = weight_grad(out_views, grad_attn)
     qs_total = weight_grad(one_views, grad_qs)
     ends = chain_pair(adjoint, decay, False)
-    ends, gu_part, out_total, qs_total = lax.optimization_barrier(
-        (ends, gu_part, out_total, qs_total)
-    )
+    ends, out_total, qs_total = lax.optimization_barrier((ends, out_total, qs_total))
     grad_kv, grad_li = mixer_finish(kv, li, init, ends, grad_kv, grad_li)
     grad_kv = grad_kv.reshape(group, 2 * HEAD)
     grad_li = grad_li.reshape(group, 2 * SLOTS)
@@ -726,20 +754,15 @@
 
     qs_total = qs_total.reshape(HEADS, shard, 2 * HEAD)
     kv_total = kv_total.reshape(HEADS, shard, 2 * HEAD)
-    gu_whole = lax.all_gather(gu_part, "seq", axis=0, tiled=True)
-    qs_part = lax.psum_scatter(
-        after(qs_total, gu_whole), "seq", scatter_dimension=0, tiled=True
-    )
-    down_grad = lax.psum(after(down_total, qs_part), "seq")
-    qs_whole = lax.all_gather(after(swap_diagonal(qs_part), down_grad), "seq", axis=0, tiled=True)
-    kv_part = lax.psum_scatter(
-        after(kv_total, qs_whole), "seq", scatter_dimension=0, tiled=True
-    )
-    out_grad = lax.psum(after(out_total, kv_part), "seq")
-    kv_whole = lax.all_gather(after(swap_diagonal(kv_part), out_grad), "seq", axis=0, tiled=True)
+    half_rows = down_rows // 2
+    first = after(down_total[:half_rows], gu_whole, one_part)
+    chunks = [first, down_total[half_rows:], out_total]
+    chunks += [qs_total[1::2], qs_total[0::2], kv_total[1::2], kv_total[0::2]]
+    near, far, out_grad, *wide = line_sum(chunks)
+    down_grad = jnp.concatenate([near, far])
     gate_grad, up_grad = assemble(gu_whole[None], order, 2)
-    query_grad, swish_grad = assemble(qs_whole[None], order, 2)
-    key_grad, value_grad = assemble(kv_whole[None], order, 2)
+    query_grad, swish_grad = spread_line(wide[0], wide[1], here)
+    key_grad, value_grad = spread_line(wide[2], wide[3], here)
     out_grad = out_grad.astype(F32)
     scale_one = inverse_rms(tokens_f)
     hat_one = tokens_f * scale_one

time: 1110 us -> 993 us (0.89)
  waiting for transfers between devices: 585 us -> 403 us
  starting transfers between devices: 95 us -> 145 us
  other arithmetic: 83.9 us -> 98 us
  matrix products: 181 us -> 168 us
  local copies, waits for them, and re-layouts: 52.1 us -> 63.7 us
    psum x2 -> x0, waiting for transfers between devices: 128 us -> none  [the longest x1 81.6 us: body(): down_grad = lax.psum(after(down_total, qs_part), 'seq')]
    all_gather x1, waiting for transfers between devices: 123 us -> 6.12 us  [body(): gu_whole = lax.all_gather(gu_part, 'seq', axis=0, tiled=True)]
    ppermute x12, waiting for transfers between devices: 9.88 us -> 77.9 us  [chain(): total = total + lax.ppermute(sent, 'seq', [pair]).astype(F32)]
    ppermute x0 -> x21, waiting for transfers between devices: none -> 62.5 us  [send(): last[key] = lax.ppermute(value, 'seq', pairs)]
    reduce_scatter x2 -> x0, waiting for transfers between devices: 59.9 us -> none  [the longest x1 44.6 us: body(): lax.psum_scatter(after(qs_total, gu_whole), 'seq', scatter_dimension=0, t...]
    ppermute x0 -> x21, starting transfers between devices: none -> 57.6 us  [send(): last[key] = lax.ppermute(value, 'seq', pairs)]
    add x0 -> x14, other arithmetic: none -> 21.6 us  [line_sum(): value = value + got]
    ppermute x3 -> x1, starting transfers between devices: 18.7 us -> 2.19 us  [swap_diagonal(): return lax.ppermute(part, ('p', 'seq'), sends)]
  transfers between devices with their start and end apart: 88 -> 107, of which waited for: 29 -> 33; matrix products, arithmetic and copies ran while one was open for 23% -> 27% of each run, Pallas kernels for 8% -> 9%
where the time goes in v6:
time: 993 us; the launch traced here: 986 us
  waiting for transfers between devices  403 us (41%)
  matrix products  168 us (17%)
  starting transfers between devices  145 us (15%)
  other arithmetic  98 us (10%)
  Pallas kernels  92.2 us (9%)
  local copies, waits for them, and re-layouts  63.7 us (6%)
  between operations  16.5 us (2%)
    ppermute x69, waiting for transfers between devices, swap(): return lax.ppermute(value, axis, [(i, i ^ step) for i in range(count)])  256 us
    ppermute x12, waiting for transfers between devices, chain(): total = total + lax.ppermute(sent, 'seq', [pair]).astype(F32)  77.9 us
    ppermute x69, starting transfers between devices, swap(): return lax.ppermute(value, axis, [(i, i ^ step) for i in range(count)])  68.3 us
    ppermute x21, waiting for transfers between devices, send(): last[key] = lax.ppermute(value, 'seq', pairs)  62.5 us
    dot_general x11, matrix products, mm_tn(): lax.dot_general(a, b, (((0,), (0,)), ((), ())), preferred_element_type=F32)  57.8 us
    ppermute x21, starting transfers between devices, send(): last[key] = lax.ppermute(value, 'seq', pairs)  57.6 us
    dot_general x6, matrix products, mm_nt(): lax.dot_general(a, b, (((1,), (1,)), ((), ())), preferred_element_type=F32)  55.7 us
    dot_general x6, matrix products, mm(): lax.dot_general(a, b, (((1,), (0,)), ((), ())), preferred_element_type=F32)  51.6 us
  transfers between devices with their start and end apart: 107, of which 33 were waited for; matrix products, arithmetic and copies ran while one was open for 27% of the time, Pallas kernels for 9%

profile of v6, /device:TPU:0, one launch (start us, length us, event | category | flops | bytes accessed | tf_op | source)
XLA Modules:
  0.0 986.1 jit_solution(15431721691409197231)
XLA Ops:
  26.7 9.1 collective-permute-done.1
  44.7 6.2 collective-permute-done.7
  53.6 30.1 %collective-permute-done.8 = bf16[256,1024]{1,0:T(8,128)(2,1)} collective-permute-done((bf16[256,1024]{1,0:T(8,128)(2,1)}, bf16[256,1024]{1,0:T(8,128)(2,1)}, u32[]{:S(2)}, u32[]{:S(2)}) %collective-permute-start.8) | collective-permute-done | bytes 524320 | tf_op jit(solution)/shard_map/ppermute | solution.py:346
  100.4 6.8 fusion.2
  114.7 6.2 shard_map.289
  120.9 7.9 convolution_convert_fusion.8
  154.4 5.7 collective-permute-done.11
  179.9 8.4 fusion.82
  193.4 15.0 %shard_map.291 = (bf16[4,256,512]{2,1,0:T(8,128)(2,1)}, f32[4,256,512]{2,1,0:T(8,128)}, f32[4,256,64]{2,1,0:T(8,128)}, bf16[4,256,256]{2,1,0:T(8,128)(2,1)}) custom-call(f32[4,256,1024]{2,1,0:T(8,128)} %bitcast.213, bf16[4,256,1024]{2,1,0:T(8,128)(2,1)} %bitcast.216, f32[4,256,128]{2,1,0:T(8,128)} %bitcast.188, f32[4,64,1024]{2,1,0:T(8,128)} %pad_maximum_fusion.6.init_ref, ...), custom_call_target="tpu_custom_call" | custom-call | flops 12000000000 | bytes 16000000 | tf_op jit(solution)/shard_map/pallas_call | solution.py:258
  217.2 20.2 %collective-permute-done.30 = bf16[256,2048]{1,0:T(8,128)(2,1)} collective-permute-done((bf16[256,2048]{1,0:T(8,128)(2,1)S(1)}, bf16[256,2048]{1,0:T(8,128)(2,1)}, u32[]{:S(2)}, u32[]{:S(2)}) %collective-permute-start.30) | collective-permute-done | bytes 1048608 | tf_op jit(solution)/shard_map/ppermute | solution.py:346
  239.5 12.7 %collective-permute-done.42.refs_4_ = bf16[4,64,2816]{2,1,0:T(8,128)(2,1)} collective-permute-done((bf16[4,64,2816]{2,1,0:T(8,128)(2,1)}, bf16[4,64,2816]{2,1,0:T(8,128)(2,1)}, u32[]{:S(2)}, u32[]{:S(2)}) %collective-permute-start.42) | collective-permute-done | bytes 1441824 | tf_op jit(solution)/shard_map/ppermute | solution.py:346
  252.3 13.7 %fusion.66 = f32[1024,1408]{1,0:T(8,128)} fusion(bf16[1408,2048]{1,0:T(8,128)(2,1)} %all-gather.6.cloned.1.call-done, bf16[256,2048]{1,0:T(8,128)(2,1)} %collective-permute-done.35, bf16[256,2048]{1,0:T(8,128)(2,1)} %collective-permute-done.34, bf16[256,2048]{1,0:T(8,128)(2,1)} %collective-permute-done.33, bf16[256,2048]{1,0:T(8,128)(2,1)} %param.33, ...), kind=kOutput, calls=%fused_computation.236 | convolution fusion | flops 5926551552 | bytes 15732736 | tf_op jit(solution)/shard_map/dot_general | solution.py:23
  266.5 17.1 %collective-permute-done.44.refs_6_ = bf16[4,64,2816]{2,1,0:T(8,128)(2,1)} collective-permute-done((bf16[4,64,2816]{2,1,0:T(8,128)(2,1)}, bf16[4,64,2816]{2,1,0:T(8,128)(2,1)}, u32[]{:S(2)}, u32[]{:S(2)}) %collective-permute-start.44) | collective-permute-done | bytes 1441824 | tf_op jit(solution)/shard_map/ppermute | solution.py:346
  291.8 13.7 %shard_map.292 = bf16[2048,2816]{1,0:T(8,128)(2,1)} custom-call(s32[32]{0:T(128)} %stack.245.spot_ref, bf16[4,64,2816]{2,1,0:T(8,128)(2,1)} %pad_maximum_fusion.5.refs_0_, bf16[4,64,2816]{2,1,0:T(8,128)(2,1)} %collective-permute-done.39.refs_1_, bf16[4,64,2816]{2,1,0:T(8,128)(2,1)} %collective-permute-done.40.refs_2_, ...), custom_call_target="tpu_custom_call" | custom-call | bytes 23068672 | tf_op jit(solution)/shard_map/pallas_call | solution.py:382
  305.5 8.3 collective-permute-done.36
  313.8 23.1 %collective-permute-done.38 = bf16[256,2048]{1,0:T(8,128)(2,1)} collective-permute-done((bf16[256,2048]{1,0:T(8,128)(2,1)S(1)}, bf16[256,2048]{1,0:T(8,128)(2,1)}, u32[]{:S(2)}, u32[]{:S(2)}) %collective-permute-start.38) | collective-permute-done | bytes 1048608 | tf_op jit(solution)/shard_map/ppermute | solution.py:346
  336.8 21.2 %fusion.65 = f32[1024,2816]{1,0:T(8,128)} fusion(bf16[2048,2816]{1,0:T(8,128)(2,1)} %shard_map.292, bf16[256,2048]{1,0:T(8,128)(2,1)} %collective-permute-done.38, bf16[256,2048]{1,0:T(8,128)(2,1)} %collective-permute-done.37, bf16[256,2048]{1,0:T(8,128)(2,1)} %collective-permute-done.36, bf16[256,2048]{1,0:T(8,128)(2,1)S(1)} %multiply_convert_fusion.5), kind=kOutput, calls=%fused_computation.235 | convolution fusion | flops 11827937280 | bytes 27262976 | tf_op jit(solution)/shard_map/dot_general | solution.py:19
  358.0 7.1 multiply_convert_fusion.2
  367.8 8.9 convolution_convert_fusion
  377.2 16.3 %convolution_convert_fusion.1 = bf16[1024,2048]{1,0:T(8,128)(2,1)} fusion(bf16[1024,2816]{1,0:T(8,128)(2,1)S(1)} %pad_maximum_fusion, bf16[2048,2816]{1,0:T(8,128)(2,1)} %shard_map.292), kind=kOutput, calls=%fused_computation.21 | convolution fusion | flops 11813257216 | bytes 21495808 | tf_op jit(solution)/shard_map/dot_general | solution.py:23
  393.5 10.4 %add_convert_fusion = bf16[1024,2816]{1,0:T(8,128)(2,1)} fusion(bf16[1024,2816]{1,0:T(8,128)(2,1)} %collective-permute-done.46, bf16[1024,2816]{1,0:T(8,128)(2,1)S(1)} %pad_maximum_fusion, bf16[1024,256]{1,0:T(8,128)(2,1)S(1)} %get-tuple-element.224, bf16[1024,256]{1,0:T(8,128)(2,1)S(1)} %get-tuple-element.225, ...), kind=kOutput, calls=%fused_computation.1 | convolution fusion | flops 5922619392 | bytes 19398656 | tf_op jit(solution)/shard_map/dot_general | solution.py:27
  404.2 8.0 convolution_convert_fusion.4
  418.8 8.8 add_convert_fusion.2
  427.5 13.7 %collective-permute-done.47 = bf16[256,2048]{1,0:T(8,128)(2,1)S(1)} collective-permute-done((bf16[256,2048]{1,0:T(8,128)(2,1)S(1)}, bf16[256,2048]{1,0:T(8,128)(2,1)S(1)}, u32[]{:S(2)}, u32[]{:S(2)}) %collective-permute-start.47) | collective-permute-done | bytes 1048608 | tf_op jit(solution)/shard_map/ppermute | solution.py:346
  441.3 22.3 %collective-permute-done.48 = bf16[256,2048]{1,0:T(8,128)(2,1)S(1)} collective-permute-done((bf16[256,2048]{1,0:T(8,128)(2,1)S(1)}, bf16[256,2048]{1,0:T(8,128)(2,1)S(1)}, u32[]{:S(2)}, u32[]{:S(2)}) %collective-permute-start.48) | collective-permute-done | bytes 1048608 | tf_op jit(solution)/shard_map/ppermute | solution.py:346
  472.5 8.7 convolution_convert_fusion.2
  481.1 13.9 %collective-permute-done.51 = bf16[256,2048]{1,0:T(8,128)(2,1)S(1)} collective-permute-done((bf16[256,2048]{1,0:T(8,128)(2,1)S(1)}, bf16[256,2048]{1,0:T(8,128)(2,1)S(1)}, u32[]{:S(2)}, u32[]{:S(2)}) %collective-permute-start.51) | collective-permute-done | bytes 1048608 | tf_op jit(solution)/shard_map/ppermute | solution.py:346
  495.0 21.7 %collective-permute-done.52 = bf16[256,2048]{1,0:T(8,128)(2,1)S(1)} collective-permute-done((bf16[256,2048]{1,0:T(8,128)(2,1)S(1)}, bf16[256,2048]{1,0:T(8,128)(2,1)S(1)}, u32[]{:S(2)}, u32[]{:S(2)}) %collective-permute-start.52) | collective-permute-done | bytes 1048608 | tf_op jit(solution)/shard_map/ppermute | solution.py:346
  526.4 19.7 %shard_map.293 = (bf16[4,256,1024]{2,1,0:T(8,128)(2,1)}, f32[4,256,1024]{2,1,0:T(8,128)}, f32[4,256,128]{2,1,0:T(8,128)}, f32[4,64,1024]{2,1,0:T(8,128)}, f32[8,512]{1,0:T(8,128)}) custom-call(f32[4,256,1024]{2,1,0:T(8,128)} %bitcast.214, bf16[4,256,1024]{2,1,0:T(8,128)(2,1)} %bitcast.217, f32[4,256,128]{2,1,0:T(8,128)} %bitcast.189, ...), custom_call_target="tpu_custom_call" | custom-call | flops 24000000000 | bytes 20000000 | tf_op jit(solution)/shard_map/pallas_call | solution.py:258
  569.0 48.2 %collective-permute-done.60 = bf16[4,64,512]{2,1,0:T(8,128)(2,1)S(1)} collective-permute-done((bf16[4,64,512]{2,1,0:T(8,128)(2,1)S(1)}, bf16[4,64,512]{2,1,0:T(8,128)(2,1)S(1)}, u32[]{:S(2)}, u32[]{:S(2)}) %collective-permute-start.60) | collective-permute-done | bytes 262176 | tf_op jit(solution)/shard_map/ppermute | solution.py:469
  617.3 24.6 %collective-permute-done.63 = bf16[4,64,512]{2,1,0:T(8,128)(2,1)S(1)} collective-permute-done((bf16[4,64,512]{2,1,0:T(8,128)(2,1)S(1)}, bf16[4,64,512]{2,1,0:T(8,128)(2,1)S(1)}, u32[]{:S(2)}, u32[]{:S(2)}) %collective-permute-start.63) | collective-permute-done | bytes 262176 | tf_op jit(solution)/shard_map/ppermute | solution.py:469
  643.0 9.1 shard_map.294
  665.1 6.1 all-gather.8.cloned.1.call-done
  674.7 5.8 fusion.86
  680.6 6.7 fusion.85
  687.3 16.3 %collective-permute-done.76 = bf16[352,2048]{1,0:T(8,128)(2,1)S(1)} collective-permute-done((bf16[352,2048]{1,0:T(8,128)(2,1)S(1)}, bf16[352,2048]{1,0:T(8,128)(2,1)S(1)}, u32[]{:S(2)}, u32[]{:S(2)}) %collective-permute-start.76) | collective-permute-done | bytes 1441824 | tf_op jit(solution)/shard_map/ppermute | solution.py:550
  705.9 5.9 collective-permute-start.77
  711.8 9.5 add_convert_fusion.1
  751.5 8.1 collective-permute-start.78
  770.6 5.8 collective-permute-done.68
  779.5 7.9 collective-permute-start.79
  799.6 21.0 %collective-permute-done.55 = bf16[256,2048]{1,0:T(8,128)(2,1)} collective-permute-done((bf16[256,2048]{1,0:T(8,128)(2,1)}, bf16[256,2048]{1,0:T(8,128)(2,1)}, u32[]{:S(2)}, u32[]{:S(2)}) %collective-permute-start.55) | collective-permute-done | bytes 1048608 | tf_op jit(solution)/shard_map/ppermute | solution.py:346
  830.3 6.7 collective-permute-start.80
  840.8 15.1 %collective-permute-done.80 = bf16[2,256,1024]{2,1,0:T(8,128)(2,1)S(1)} collective-permute-done((bf16[2,256,1024]{2,1,0:T(8,128)(2,1)S(1)}, bf16[2,256,1024]{2,1,0:T(8,128)(2,1)S(1)}, u32[]{:S(2)}, u32[]{:S(2)}) %collective-permute-start.80) | collective-permute-done | bytes 1048608 | tf_op jit(solution)/shard_map/ppermute | solution.py:550
  867.2 14.9 %collective-permute-done.74 = f32[1,5408]{1,0:T(1,128)S(1)} collective-permute-done((f32[1,5408]{1,0:T(1,128)S(1)}, f32[1,5408]{1,0:T(1,128)S(1)}, u32[]{:S(2)}, u32[]{:S(2)}) %collective-permute-start.74) | collective-permute-done | bytes 21664 | tf_op jit(solution)/shard_map/ppermute | solution.py:346
  901.3 8.0 shard_map.297
  927.1 14.0 %collective-permute-done.98 = bf16[2,256,1024]{2,1,0:T(8,128)(2,1)S(1)} collective-permute-done((bf16[2,256,1024]{2,1,0:T(8,128)(2,1)S(1)}, bf16[2,256,1024]{2,1,0:T(8,128)(2,1)S(1)}, u32[]{:S(2)}, u32[]{:S(2)}) %collective-permute-start.98) | collective-permute-done | bytes 1048608 | tf_op jit(solution)/shard_map/ppermute | solution.py:550
  946.2 13.2 %collective-permute-done.99 = bf16[2,256,1024]{2,1,0:T(8,128)(2,1)S(1)} collective-permute-done((bf16[2,256,1024]{2,1,0:T(8,128)(2,1)S(1)}, bf16[2,256,1024]{2,1,0:T(8,128)(2,1)S(1)}, u32[]{:S(2)}, u32[]{:S(2)}) %collective-permute-start.99) | collective-permute-done | bytes 1048608 | tf_op jit(solution)/shard_map/ppermute | solution.py:550
  (545 shorter events, 338.1 us)
Async XLA Ops:
  7.2 201.2 %all-gather.4.cloned.1.call-start = ((), (), s32[]{:S(2)}) async-start(), calls=%async_computation.1 | async-start | bytes 3145728 | tf_op jit(solution)/shard_map/all_gather | solution.py:633
  7.9 244.3 %all-gather.6.cloned.1.call-start = ((), (), s32[]{:S(2)}) async-start(), calls=%async_computation.2 | async-start | bytes 8650752 | tf_op jit(solution)/shard_map/all_gather | solution.py:634
  8.0 88.5 %collective-permute-start.4 = (bf16[256,2048]{1,0:T(8,128)(2,1)}, bf16[256,2048]{1,0:T(8,128)(2,1)S(1)}, u32[]{:S(2)}, u32[]{:S(2)}) collective-permute-start(bf16[256,2048]{1,0:T(8,128)(2,1)} %param.17), channel_id=1, source_target_pairs={{0,8},{8,0},{16,24},{24,16},{1,9},{9,1},{17,25},{25,17},{2,10},{10... | collective-permute-start | bytes 3145736 | tf_op jit(solution)/shard_map/ppermute | solution.py:346
  11.0 85.7 %collective-permute-start.5 = (bf16[256,2048]{1,0:T(8,128)(2,1)}, bf16[256,2048]{1,0:T(8,128)(2,1)}, u32[]{:S(2)}, u32[]{:S(2)}) collective-permute-start(bf16[256,2048]{1,0:T(8,128)(2,1)} %param.17), channel_id=1, source_target_pairs={{0,16},{8,24},{16,0},{24,8},{1,17},{9,25},{17,1},{25,9},{2,18},{10... | collective-permute-start | bytes 3145736 | tf_op jit(solution)/shard_map/ppermute | solution.py:346
  17.7 500.0 %reduce-scatter.2.cloned.1.call-start = ((), (), s32[]{:S(2)}) async-start(), calls=%async_computation.3 | async-start | bytes 7208960 | tf_op jit(solution)/shard_map/reduce_scatter | solution.py:681
  37.7 46.0 %collective-permute-start.8 = (bf16[256,1024]{1,0:T(8,128)(2,1)}, bf16[256,1024]{1,0:T(8,128)(2,1)}, u32[]{:S(2)}, u32[]{:S(2)}) collective-permute-start(bf16[256,1024]{1,0:T(8,128)(2,1)} %pad_maximum_fusion.9), channel_id=1, source_target_pairs={{0,16},{8,24},{16,0},{24,8},{1,17},{9,25},{17,1},{25,9},{2,18},{10... | collective-permute-start | bytes 1572872 | tf_op jit(solution)/shard_map/ppermute | solution.py:346
  39.2 44.5 %collective-permute-start.9 = (bf16[256,1024]{1,0:T(8,128)(2,1)S(1)}, bf16[256,1024]{1,0:T(8,128)(2,1)}, u32[]{:S(2)}, u32[]{:S(2)}) collective-permute-start(bf16[256,1024]{1,0:T(8,128)(2,1)S(1)} %pad_maximum_fusion.10), channel_id=1, source_target_pairs={{0,24},{8,16},{16,8},{24,0},{1,25},{9,17},{17,9},{25,1},{2,26},{10... | collective-permute-start | bytes 1572872 | tf_op jit(solution)/shard_map/ppermute | solution.py:346
  50.9 46.1 %collective-permute-start.6 = (bf16[256,2048]{1,0:T(8,128)(2,1)S(1)}, bf16[256,2048]{1,0:T(8,128)(2,1)S(1)}, u32[]{:S(2)}, u32[]{:S(2)}) collective-permute-start(bf16[256,2048]{1,0:T(8,128)(2,1)S(1)} %copy-done.3), channel_id=1, source_target_pairs={{0,24},{8,16},{16,8},{24,0},{1,25},{9,17},{17,9},{25,1},{2,26},{10... | collective-permute-start | bytes 3145736 | tf_op jit(solution)/shard_map/ppermute | solution.py:346
  87.9 64.1 %collective-permute-start.15 = (bf16[256,1024]{1,0:T(8,128)(2,1)}, bf16[256,1024]{1,0:T(8,128)(2,1)}, u32[]{:S(2)}, u32[]{:S(2)}) collective-permute-start(bf16[256,1024]{1,0:T(8,128)(2,1)} %pad_maximum_fusion.14), channel_id=1, source_target_pairs={{0,24},{8,16},{16,8},{24,0},{1,25},{9,17},{17,9},{25,1},{2,26},{10... | collective-permute-start | bytes 1572872 | tf_op jit(solution)/shard_map/ppermute | solution.py:346
  110.9 43.5 %collective-permute-start.13 = (bf16[256,1024]{1,0:T(8,128)(2,1)}, bf16[256,1024]{1,0:T(8,128)(2,1)}, u32[]{:S(2)}, u32[]{:S(2)}) collective-permute-start(bf16[256,1024]{1,0:T(8,128)(2,1)} %pad_maximum_fusion.13), channel_id=1, source_target_pairs={{0,16},{8,24},{16,0},{24,8},{1,17},{9,25},{17,1},{25,9},{2,18},{10... | collective-permute-start | bytes 1572872 | tf_op jit(solution)/shard_map/ppermute | solution.py:346
  111.5 35.4 %collective-permute-start.27 = (bf16[64,2816]{1,0:T(8,128)(2,1)}, bf16[64,2816]{1,0:T(8,128)(2,1)}, u32[]{:S(2)}, u32[]{:S(2)}) collective-permute-start(bf16[64,2816]{1,0:T(8,128)(2,1)} %pad_maximum_fusion.17), channel_id=1, source_target_pairs={{0,8},{8,0},{16,24},{24,16},{1,9},{9,1},{17,25},{25,17},{2,10},{10... | collective-permute-start | bytes 1081352 | tf_op jit(solution)/shard_map/ppermute | solution.py:346
  113.0 38.3 %collective-permute-start.28 = (bf16[64,2816]{1,0:T(8,128)(2,1)}, bf16[64,2816]{1,0:T(8,128)(2,1)}, u32[]{:S(2)}, u32[]{:S(2)}) collective-permute-start(bf16[64,2816]{1,0:T(8,128)(2,1)} %pad_maximum_fusion.18), channel_id=1, source_target_pairs={{0,16},{8,24},{16,0},{24,8},{1,17},{9,25},{17,1},{25,9},{2,18},{10... | collective-permute-start | bytes 1081352 | tf_op jit(solution)/shard_map/ppermute | solution.py:346
  168.3 46.7 %collective-permute-start.33 = (bf16[256,2048]{1,0:T(8,128)(2,1)}, bf16[256,2048]{1,0:T(8,128)(2,1)}, u32[]{:S(2)}, u32[]{:S(2)}) collective-permute-start(bf16[256,2048]{1,0:T(8,128)(2,1)} %param.33), channel_id=1, source_target_pairs={{0,8},{8,0},{16,24},{24,16},{1,9},{9,1},{17,25},{25,17},{2,10},{10... | collective-permute-start | bytes 3145736 | tf_op jit(solution)/shard_map/ppermute | solution.py:346
  168.7 46.7 %collective-permute-start.34 = (bf16[256,2048]{1,0:T(8,128)(2,1)}, bf16[256,2048]{1,0:T(8,128)(2,1)}, u32[]{:S(2)}, u32[]{:S(2)}) collective-permute-start(bf16[256,2048]{1,0:T(8,128)(2,1)} %param.33), channel_id=1, source_target_pairs={{0,16},{8,24},{16,0},{24,8},{1,17},{9,25},{17,1},{25,9},{2,18},{10... | collective-permute-start | bytes 3145736 | tf_op jit(solution)/shard_map/ppermute | solution.py:346
  170.4 45.1 %collective-permute-start.35 = (bf16[256,2048]{1,0:T(8,128)(2,1)}, bf16[256,2048]{1,0:T(8,128)(2,1)}, u32[]{:S(2)}, u32[]{:S(2)}) collective-permute-start(bf16[256,2048]{1,0:T(8,128)(2,1)} %param.33), channel_id=1, source_target_pairs={{0,24},{8,16},{16,8},{24,0},{1,25},{9,17},{17,9},{25,1},{2,26},{10... | collective-permute-start | bytes 3145736 | tf_op jit(solution)/shard_map/ppermute | solution.py:346
  189.6 62.6 %collective-permute-start.42 = (bf16[4,64,2816]{2,1,0:T(8,128)(2,1)}, bf16[4,64,2816]{2,1,0:T(8,128)(2,1)}, u32[]{:S(2)}, u32[]{:S(2)}) collective-permute-start(bf16[4,64,2816]{2,1,0:T(8,128)(2,1)} %pad_maximum_fusion.5.refs_0_), channel_id=1, source_target_pairs={{0,2},{1,3},{2,0},{3,1},{4,6},{5,7},{6,4},{7,5},{8,10},{9,11},{10,... | collective-permute-start | bytes 4325384 | tf_op jit(solution)/shard_map/ppermute | solution.py:346
  189.6 62.6 %collective-permute-start.40 = (bf16[4,64,2816]{2,1,0:T(8,128)(2,1)}, bf16[4,64,2816]{2,1,0:T(8,128)(2,1)}, u32[]{:S(2)}, u32[]{:S(2)}) collective-permute-start(bf16[4,64,2816]{2,1,0:T(8,128)(2,1)} %pad_maximum_fusion.5.refs_0_), channel_id=1, source_target_pairs={{0,1},{1,0},{2,3},{3,2},{4,5},{5,4},{6,7},{7,6},{8,9},{9,8},{10,11... | collective-permute-start | bytes 4325384 | tf_op jit(solution)/shard_map/ppermute | solution.py:346
  215.4 72.8 %collective-permute-start.39 = (bf16[4,64,2816]{2,1,0:T(8,128)(2,1)}, bf16[4,64,2816]{2,1,0:T(8,128)(2,1)}, u32[]{:S(2)}, u32[]{:S(2)}) collective-permute-start(bf16[4,64,2816]{2,1,0:T(8,128)(2,1)} %pad_maximum_fusion.5.refs_0_), channel_id=1, source_target_pairs={{0,4},{4,0},{1,5},{5,1},{2,6},{6,2},{3,7},{7,3},{8,12},{12,8},{9,1... | collective-permute-start | bytes 4325384 | tf_op jit(solution)/shard_map/ppermute | solution.py:346
  215.5 50.5 %collective-permute-start.31 = (bf16[256,2048]{1,0:T(8,128)(2,1)S(1)}, bf16[256,2048]{1,0:T(8,128)(2,1)}, u32[]{:S(2)}, u32[]{:S(2)}) collective-permute-start(bf16[256,2048]{1,0:T(8,128)(2,1)S(1)} %get-tuple-element.229), channel_id=1, source_target_pairs={{0,16},{8,24},{16,0},{24,8},{1,17},{9,25},{17,1},{25,9},{2,18},{10... | collective-permute-start | bytes 3145736 | tf_op jit(solution)/shard_map/ppermute | solution.py:346
  237.4 46.2 %collective-permute-start.32 = (bf16[256,2048]{1,0:T(8,128)(2,1)S(1)}, bf16[256,2048]{1,0:T(8,128)(2,1)}, u32[]{:S(2)}, u32[]{:S(2)}) collective-permute-start(bf16[256,2048]{1,0:T(8,128)(2,1)S(1)} %get-tuple-element.228), channel_id=1, source_target_pairs={{0,24},{8,16},{16,8},{24,0},{1,25},{9,17},{17,9},{25,1},{2,26},{10... | collective-permute-start | bytes 3145736 | tf_op jit(solution)/shard_map/ppermute | solution.py:346
  252.2 31.3 %collective-permute-start.44 = (bf16[4,64,2816]{2,1,0:T(8,128)(2,1)}, bf16[4,64,2816]{2,1,0:T(8,128)(2,1)}, u32[]{:S(2)}, u32[]{:S(2)}) collective-permute-start(bf16[4,64,2816]{2,1,0:T(8,128)(2,1)} %collective-permute-done.42.refs_4_), channel_id=1, source_target_pairs={{0,1},{1,0},{2,3},{3,2},{4,5},{5,4},{6,7},{7,6},{8,9},{9,8},{10,11... | collective-permute-start | bytes 4325384 | tf_op jit(solution)/shard_map/ppermute | solution.py:346
  252.2 37.4 %collective-permute-start.41 = (bf16[4,64,2816]{2,1,0:T(8,128)(2,1)}, bf16[4,64,2816]{2,1,0:T(8,128)(2,1)}, u32[]{:S(2)}, u32[]{:S(2)}) collective-permute-start(bf16[4,64,2816]{2,1,0:T(8,128)(2,1)} %collective-permute-done.40.refs_2_), channel_id=1, source_target_pairs={{0,4},{4,0},{1,5},{5,1},{2,6},{6,2},{3,7},{7,3},{8,12},{12,8},{9,1... | collective-permute-start | bytes 4325384 | tf_op jit(solution)/shard_map/ppermute | solution.py:346
  289.6 47.2 %collective-permute-start.38 = (bf16[256,2048]{1,0:T(8,128)(2,1)S(1)}, bf16[256,2048]{1,0:T(8,128)(2,1)}, u32[]{:S(2)}, u32[]{:S(2)}) collective-permute-start(bf16[256,2048]{1,0:T(8,128)(2,1)S(1)} %multiply_convert_fusion.5), channel_id=1, source_target_pairs={{0,24},{8,16},{16,8},{24,0},{1,25},{9,17},{17,9},{25,1},{2,26},{10... | collective-permute-start | bytes 3145736 | tf_op jit(solution)/shard_map/ppermute | solution.py:346
  404.0 267.3 %all-gather.8.cloned.1.call-start = ((), (), s32[]{:S(2)}) async-start(), calls=%async_computation.4 | async-start | bytes 7208960 | tf_op jit(solution)/shard_map/all_gather | solution.py:713
  416.2 47.3 %collective-permute-start.48 = (bf16[256,2048]{1,0:T(8,128)(2,1)S(1)}, bf16[256,2048]{1,0:T(8,128)(2,1)S(1)}, u32[]{:S(2)}, u32[]{:S(2)}) collective-permute-start(bf16[256,2048]{1,0:T(8,128)(2,1)S(1)} %get-tuple-element.218), channel_id=1, source_target_pairs={{0,16},{8,24},{16,0},{24,8},{1,17},{9,25},{17,1},{25,9},{2,18},{10... | collective-permute-start | bytes 3145736 | tf_op jit(solution)/shard_map/ppermute | solution.py:346
  417.9 45.7 %collective-permute-start.49 = (bf16[256,2048]{1,0:T(8,128)(2,1)S(1)}, bf16[256,2048]{1,0:T(8,128)(2,1)S(1)}, u32[]{:S(2)}, u32[]{:S(2)}) collective-permute-start(bf16[256,2048]{1,0:T(8,128)(2,1)S(1)} %get-tuple-element.217), channel_id=1, source_target_pairs={{0,24},{8,16},{16,8},{24,0},{1,25},{9,17},{17,9},{25,1},{2,26},{10... | collective-permute-start | bytes 3145736 | tf_op jit(solution)/shard_map/ppermute | solution.py:346
  470.2 46.5 %collective-permute-start.52 = (bf16[256,2048]{1,0:T(8,128)(2,1)S(1)}, bf16[256,2048]{1,0:T(8,128)(2,1)S(1)}, u32[]{:S(2)}, u32[]{:S(2)}) collective-permute-start(bf16[256,2048]{1,0:T(8,128)(2,1)S(1)} %get-tuple-element.111), channel_id=1, source_target_pairs={{0,16},{8,24},{16,0},{24,8},{1,17},{9,25},{17,1},{25,9},{2,18},{10... | collective-permute-start | bytes 3145736 | tf_op jit(solution)/shard_map/ppermute | solution.py:346
  470.9 46.8 %collective-permute-start.53 = (bf16[256,2048]{1,0:T(8,128)(2,1)S(1)}, bf16[256,2048]{1,0:T(8,128)(2,1)}, u32[]{:S(2)}, u32[]{:S(2)}) collective-permute-start(bf16[256,2048]{1,0:T(8,128)(2,1)S(1)} %get-tuple-element.111), channel_id=1, source_target_pairs={{0,24},{8,16},{16,8},{24,0},{1,25},{9,17},{17,9},{25,1},{2,26},{10... | collective-permute-start | bytes 3145736 | tf_op jit(solution)/shard_map/ppermute | solution.py:346
  517.8 28.3 %collective-permute-start.57 = (bf16[1,256,2816]{2,1,0:T(8,128)(2,1)}, bf16[1,256,2816]{2,1,0:T(8,128)(2,1)S(1)}, u32[]{:S(2)}, u32[]{:S(2)}) collective-permute-start(bf16[1,256,2816]{2,1,0:T(8,128)(2,1)} %reduce-scatter.2.cloned.1.call-done), channel_id=1, source_target_pairs={{0,0},{1,9},{2,18},{3,27},{8,8},{9,1},{10,26},{11,19},{16,16},{17,... | collective-permute-start | bytes 4325384 | tf_op jit(solution)/shard_map/ppermute | solution.py:574
  562.5 54.7 %collective-permute-start.60 = (bf16[4,64,512]{2,1,0:T(8,128)(2,1)S(1)}, bf16[4,64,512]{2,1,0:T(8,128)(2,1)S(1)}, u32[]{:S(2)}, u32[]{:S(2)}) collective-permute-start(bf16[4,64,512]{2,1,0:T(8,128)(2,1)S(1)} %get-tuple-element.245), channel_id=1, source_target_pairs={{1,0},{5,4},{9,8},{13,12},{17,16},{21,20},{25,24},{29,28}} | collective-permute-start | bytes 786440 | tf_op jit(solution)/shard_map/ppermute | solution.py:469
  563.9 78.0 %collective-permute-start.63 = (bf16[4,64,512]{2,1,0:T(8,128)(2,1)S(1)}, bf16[4,64,512]{2,1,0:T(8,128)(2,1)S(1)}, u32[]{:S(2)}, u32[]{:S(2)}) collective-permute-start(bf16[4,64,512]{2,1,0:T(8,128)(2,1)S(1)} %add_convert_fusion.6), channel_id=1, source_target_pairs={{1,0},{5,4},{9,8},{13,12},{17,16},{21,20},{25,24},{29,28}} | collective-permute-start | bytes 786440 | tf_op jit(solution)/shard_map/ppermute | solution.py:469
  657.5 107.2 %collective-permute-start.69 = (bf16[1024,1024]{1,0:T(8,128)(2,1)}, bf16[1024,1024]{1,0:T(8,128)(2,1)}, u32[]{:S(2)}, u32[]{:S(2)}) collective-permute-start(bf16[1024,1024]{1,0:T(8,128)(2,1)} %convolution_convert_fusion.6), channel_id=1, source_target_pairs={{0,4},{4,0},{1,5},{5,1},{2,6},{6,2},{3,7},{7,3},{8,12},{12,8},{9,1... | collective-permute-start | bytes 6291464 | tf_op jit(solution)/shard_map/ppermute | solution.py:346
  671.2 32.3 %collective-permute-start.76 = (bf16[352,2048]{1,0:T(8,128)(2,1)S(1)}, bf16[352,2048]{1,0:T(8,128)(2,1)S(1)}, u32[]{:S(2)}, u32[]{:S(2)}) collective-permute-start(bf16[352,2048]{1,0:T(8,128)(2,1)S(1)} %get-tuple-element.132), channel_id=1, source_target_pairs={{0,1},{3,2},{4,5},{7,6},{8,9},{11,10},{12,13},{15,14},{16,17},{19,... | collective-permute-start | bytes 4325384 | tf_op jit(solution)/shard_map/ppermute | solution.py:550
  704.1 31.6 %collective-permute-start.81 = (bf16[352,2048]{1,0:T(8,128)(2,1)S(1)}, bf16[352,2048]{1,0:T(8,128)(2,1)}, u32[]{:S(2)}, u32[]{:S(2)}) collective-permute-start(bf16[352,2048]{1,0:T(8,128)(2,1)S(1)} %add.762), channel_id=1, source_target_pairs={{1,2},{2,1},{5,6},{6,5},{9,10},{10,9},{13,14},{14,13},{17,18},{18,... | collective-permute-start | bytes 4325384 | tf_op jit(solution)/shard_map/ppermute | solution.py:550
  705.9 35.1 %collective-permute-start.77 = (bf16[352,2048]{1,0:T(8,128)(2,1)}, bf16[352,2048]{1,0:T(8,128)(2,1)}, u32[]{:S(2)}, u32[]{:S(2)}) collective-permute-start(bf16[352,2048]{1,0:T(8,128)(2,1)} %get-tuple-element.133), channel_id=1, source_target_pairs={{0,1},{3,2},{4,5},{7,6},{8,9},{11,10},{12,13},{15,14},{16,17},{19,... | collective-permute-start | bytes 4325384 | tf_op jit(solution)/shard_map/ppermute | solution.py:550
  738.9 52.0 %collective-permute-start.86 = (bf16[352,2048]{1,0:T(8,128)(2,1)}, bf16[352,2048]{1,0:T(8,128)(2,1)}, u32[]{:S(2)}, u32[]{:S(2)}) collective-permute-start(bf16[352,2048]{1,0:T(8,128)(2,1)} %add.767), channel_id=1, source_target_pairs={{1,0},{2,3},{5,4},{6,7},{9,8},{10,11},{13,12},{14,15},{17,16},{18,... | collective-permute-start | bytes 4325384 | tf_op jit(solution)/shard_map/ppermute | solution.py:550
  744.5 35.0 %collective-permute-start.82 = (bf16[352,2048]{1,0:T(8,128)(2,1)}, bf16[352,2048]{1,0:T(8,128)(2,1)}, u32[]{:S(2)}, u32[]{:S(2)}) collective-permute-start(bf16[352,2048]{1,0:T(8,128)(2,1)} %add.761), channel_id=1, source_target_pairs={{1,2},{2,1},{5,6},{6,5},{9,10},{10,9},{13,14},{14,13},{17,18},{18,... | collective-permute-start | bytes 4325384 | tf_op jit(solution)/shard_map/ppermute | solution.py:550
  764.7 34.2 %collective-permute-start.54 = (bf16[256,2048]{1,0:T(8,128)(2,1)}, bf16[256,2048]{1,0:T(8,128)(2,1)}, u32[]{:S(2)}, u32[]{:S(2)}) collective-permute-start(bf16[256,2048]{1,0:T(8,128)(2,1)} %get-tuple-element.214), channel_id=1, source_target_pairs={{0,8},{8,0},{16,24},{24,16},{1,9},{9,1},{17,25},{25,17},{2,10},{10... | collective-permute-start | bytes 3145736 | tf_op jit(solution)/shard_map/ppermute | solution.py:346
  776.4 44.2 %collective-permute-start.55 = (bf16[256,2048]{1,0:T(8,128)(2,1)}, bf16[256,2048]{1,0:T(8,128)(2,1)}, u32[]{:S(2)}, u32[]{:S(2)}) collective-permute-start(bf16[256,2048]{1,0:T(8,128)(2,1)} %get-tuple-element.216), channel_id=1, source_target_pairs={{0,16},{8,24},{16,0},{24,8},{1,17},{9,25},{17,1},{25,9},{2,18},{10... | collective-permute-start | bytes 3145736 | tf_op jit(solution)/shard_map/ppermute | solution.py:346
  778.9 43.1 %collective-permute-start.56 = (bf16[256,2048]{1,0:T(8,128)(2,1)}, bf16[256,2048]{1,0:T(8,128)(2,1)}, u32[]{:S(2)}, u32[]{:S(2)}) collective-permute-start(bf16[256,2048]{1,0:T(8,128)(2,1)} %get-tuple-element.215), channel_id=1, source_target_pairs={{0,24},{8,16},{16,8},{24,0},{1,25},{9,17},{17,9},{25,1},{2,26},{10... | collective-permute-start | bytes 3145736 | tf_op jit(solution)/shard_map/ppermute | solution.py:346
  779.5 44.1 %collective-permute-start.79 = (bf16[2,256,1024]{2,1,0:T(8,128)(2,1)}, bf16[2,256,1024]{2,1,0:T(8,128)(2,1)}, u32[]{:S(2)}, u32[]{:S(2)}) collective-permute-start(bf16[2,256,1024]{2,1,0:T(8,128)(2,1)} %get-tuple-element.135), channel_id=1, source_target_pairs={{0,1},{3,2},{4,5},{7,6},{8,9},{11,10},{12,13},{15,14},{16,17},{19,... | collective-permute-start | bytes 3145736 | tf_op jit(solution)/shard_map/ppermute | solution.py:550
  790.9 46.5 %collective-permute-start.87 = (bf16[352,2048]{1,0:T(8,128)(2,1)}, bf16[352,2048]{1,0:T(8,128)(2,1)}, u32[]{:S(2)}, u32[]{:S(2)}) collective-permute-start(bf16[352,2048]{1,0:T(8,128)(2,1)} %add.766), channel_id=1, source_target_pairs={{1,0},{2,3},{5,4},{6,7},{9,8},{10,11},{13,12},{14,15},{17,16},{18,... | collective-permute-start | bytes 4325384 | tf_op jit(solution)/shard_map/ppermute | solution.py:550
  798.8 31.4 %collective-permute-start.83 = (bf16[256,2048]{1,0:T(8,128)(2,1)S(1)}, bf16[256,2048]{1,0:T(8,128)(2,1)S(1)}, u32[]{:S(2)}, u32[]{:S(2)}) collective-permute-start(bf16[256,2048]{1,0:T(8,128)(2,1)S(1)} %add.760), channel_id=1, source_target_pairs={{1,2},{2,1},{5,6},{6,5},{9,10},{10,9},{13,14},{14,13},{17,18},{18,... | collective-permute-start | bytes 3145736 | tf_op jit(solution)/shard_map/ppermute | solution.py:550
  855.8 31.7 %collective-permute-start.94 = (bf16[2,256,1024]{2,1,0:T(8,128)(2,1)S(1)}, bf16[2,256,1024]{2,1,0:T(8,128)(2,1)S(1)}, u32[]{:S(2)}, u32[]{:S(2)}) collective-permute-start(bf16[2,256,1024]{2,1,0:T(8,128)(2,1)S(1)} %get-tuple-element.147), channel_id=1, source_target_pairs={{0,1},{3,2},{4,5},{7,6},{8,9},{11,10},{12,13},{15,14},{16,17},{19,... | collective-permute-start | bytes 3145736 | tf_op jit(solution)/shard_map/ppermute | solution.py:550
  860.7 32.6 %collective-permute-start.85 = (bf16[2,256,1024]{2,1,0:T(8,128)(2,1)S(1)}, bf16[2,256,1024]{2,1,0:T(8,128)(2,1)S(1)}, u32[]{:S(2)}, u32[]{:S(2)}) collective-permute-start(bf16[2,256,1024]{2,1,0:T(8,128)(2,1)S(1)} %add.758), channel_id=1, source_target_pairs={{1,2},{2,1},{5,6},{6,5},{9,10},{10,9},{13,14},{14,13},{17,18},{18,... | collective-permute-start | bytes 3145736 | tf_op jit(solution)/shard_map/ppermute | solution.py:550
  862.9 33.6 %collective-permute-start.89 = (bf16[2,256,1024]{2,1,0:T(8,128)(2,1)S(1)}, bf16[2,256,1024]{2,1,0:T(8,128)(2,1)S(1)}, u32[]{:S(2)}, u32[]{:S(2)}) collective-permute-start(bf16[2,256,1024]{2,1,0:T(8,128)(2,1)S(1)} %add.764), channel_id=1, source_target_pairs={{1,0},{2,3},{5,4},{6,7},{9,8},{10,11},{13,12},{14,15},{17,16},{18,... | collective-permute-start | bytes 3145736 | tf_op jit(solution)/shard_map/ppermute | solution.py:550
  923.5 36.5 %collective-permute-start.91 = (bf16[256,1024]{1,0:T(8,128)(2,1)S(1)}, bf16[256,1024]{1,0:T(8,128)(2,1)S(1)}, u32[]{:S(2)}, u32[]{:S(2)}) collective-permute-start(bf16[256,1024]{1,0:T(8,128)(2,1)S(1)} %get-tuple-element.259), channel_id=1, source_target_pairs={{0,8},{8,0},{16,24},{24,16},{1,9},{9,1},{17,25},{25,17},{2,10},{10... | collective-permute-start | bytes 1572872 | tf_op jit(solution)/shard_map/ppermute | solution.py:346
  924.7 38.3 %collective-permute-start.93 = (bf16[256,1024]{1,0:T(8,128)(2,1)S(1)}, bf16[256,1024]{1,0:T(8,128)(2,1)S(1)}, u32[]{:S(2)}, u32[]{:S(2)}) collective-permute-start(bf16[256,1024]{1,0:T(8,128)(2,1)S(1)} %get-tuple-element.260), channel_id=1, source_target_pairs={{0,24},{8,16},{16,8},{24,0},{1,25},{9,17},{17,9},{25,1},{2,26},{10... | collective-permute-start | bytes 1572872 | tf_op jit(solution)/shard_map/ppermute | solution.py:346
  (143 other events, 3018.7 us)
Sparse Core Ops, SparseCore 0:
  9.5 13.2 all-gather.3
  24.4 17.1 all-gather.5
  404.1 103.0 reduce-scatter.1
  547.4 123.7 all-gather.7

commit v7 on v6

--- a/solution.py
+++ b/solution.py
@@ -416,22 +416,21 @@
 
 
 def seq_pieces(shards, here):
-    count, spot = lax.axis_size("seq"), lax.axis_index("seq")
-    rows = shards[0].shape[0] // count
-    shards = [lax.dynamic_slice_in_dim(shard, spot * rows, rows, 0) for shard in shards]
+    rows = shards[0].shape[0] // 2
+    start = lax.axis_index("seq") % 2 * rows
+    shards = [lax.dynamic_slice_in_dim(shard, start, rows, 0) for shard in shards]
     own = column_cuts(shards, here, 0)
     return jnp.stack([own] + [swap(column_cuts(shards, here, k), "p", k) for k in range(1, HEADS)])
 
 
 def seq_columns(pieces, here):
-    copies, count = lax.axis_size("r"), lax.axis_size("seq")
-    turn, spot = lax.axis_index("r"), lax.axis_index("seq")
+    copies, turn, half = lax.axis_size("r"), lax.axis_index("r"), lax.axis_index("seq") % 2
     parts, spots = [], []
-    for j, part in enumerate(gather_seq(pieces)):
+    for j, part in enumerate([pieces, swap(pieces, "seq", 1)]):
         for m in range(copies):
             parts.append(part if m == 0 else swap(part, "r", m))
             spots.append(
-                [(((here ^ k) * copies + (turn ^ m)) * count + (spot ^ j)) for k in range(HEADS)]
+                [((here ^ k) * copies + (turn ^ m)) * 2 + (half ^ j) for k in range(HEADS)]
             )
     return place(parts, spots)
 
@@ -453,10 +452,6 @@
     kept = lax.dynamic_index_in_dim(total, turn, 0, True)
     for m in range(1, copies):
         kept = kept + swap(lax.dynamic_index_in_dim(total, turn ^ m, 0, True), "r", m)
-    step = 1
-    while step < lax.axis_size("seq"):
-        kept = kept + swap(kept, "seq", step)
-        step *= 2
     return kept[0]
 
 
@@ -492,17 +487,6 @@
     for part in got:
         total = total + part.astype(F32)
     return total.astype(BF)
-
-
-def gather_seq(value):
-    count = lax.axis_size("seq")
-    found = {0: value}
-    step = count // 2
-    while step >= 1:
-        for j in list(found):
-            found[j ^ step] = swap(found[j], "seq", step)
-        step //= 2
-    return [found[j] for j in range(count)]
 
 
 def assemble_kernel(counts, spot_ref, *refs):
@@ -703,7 +687,6 @@
     grad_attn = jnp.concatenate(attn_blocks)
     mlp_part = mlp_part.reshape(HEADS, rows, D)
     mlp_out = scatter_heads([mlp_part[k] for k in range(HEADS)])
-    result = (residual + mask_own * mlp_out).astype(BF)
 
     grad_gated = mm_nt(grad_attn, weight_out).reshape(HEADS, rows, HEAD)
     grad_qs, grad_kv, grad_li, adjoint, slot_part = mixer_backward(
@@ -725,7 +708,10 @@
     out_total = weight_grad(out_views, grad_attn)
     qs_total = weight_grad(one_views, grad_qs)
     ends = chain_pair(adjoint, decay, False)
-    ends, out_total, qs_total = lax.optimization_barrier((ends, out_total, qs_total))
+    ends, mlp_out, out_total, qs_total = lax.optimization_barrier(
+        (ends, mlp_out, out_total, qs_total)
+    )
+    result = (residual + mask_own * mlp_out).astype(BF)
     grad_kv, grad_li = mixer_finish(kv, li, init, ends, grad_kv, grad_li)
     grad_kv = grad_kv.reshape(group, 2 * HEAD)
     grad_li = grad_li.reshape(group, 2 * SLOTS)
@@ -752,18 +738,6 @@
     kv_total = weight_grad(one_views, grad_kv)
     grad_norm_one, kv_total = scatter_heads([one_part[k] for k in range(HEADS)], kv_total)
 
-    qs_total = qs_total.reshape(HEADS, shard, 2 * HEAD)
-    kv_total = kv_total.reshape(HEADS, shard, 2 * HEAD)
-    half_rows = down_rows // 2
-    first = after(down_total[:half_rows], gu_whole, one_part)
-    chunks = [first, down_total[half_rows:], out_total]
-    chunks += [qs_total[1::2], qs_total[0::2], kv_total[1::2], kv_total[0::2]]
-    near, far, out_grad, *wide = line_sum(chunks)
-    down_grad = jnp.concatenate([near, far])
-    gate_grad, up_grad = assemble(gu_whole[None], order, 2)
-    query_grad, swish_grad = spread_line(wide[0], wide[1], here)
-    key_grad, value_grad = spread_line(wide[2], wide[3], here)
-    out_grad = out_grad.astype(F32)
     scale_one = inverse_rms(tokens_f)
     hat_one = tokens_f * scale_one
     gain_one_grad = jnp.sum(grad_norm_one * hat_one, axis=0)
@@ -784,6 +758,22 @@
     ]
     flat = jnp.concatenate([a.reshape(HEADS, copies, -1) for a in sums], axis=2)
     flat = sum_small(flat, here, turn)
+    lanes = D * 8
+    flat = jnp.pad(flat, (0, -flat.size % lanes)).astype(BF).reshape(-1, D)
+
+    qs_total = qs_total.reshape(HEADS, shard, 2 * HEAD)
+    kv_total = kv_total.reshape(HEADS, shard, 2 * HEAD)
+    half_rows = down_rows // 2
+    first = after(down_total[:half_rows], gu_whole, one_part)
+    chunks = [first, down_total[half_rows:]]
+    chunks += [qs_total[1::2], qs_total[0::2], kv_total[1::2], kv_total[0::2]]
+    near, far, *wide, last = line_sum(chunks + [jnp.concatenate([out_total, flat])])
+    down_grad = jnp.concatenate([near, far])
+    gate_grad, up_grad = assemble(gu_whole[None], order, 2)
+    query_grad, swish_grad = spread_line(wide[0], wide[1], here)
+    key_grad, value_grad = spread_line(wide[2], wide[3], here)
+    out_grad = last[:shard].astype(F32)
+    flat = last[shard:].reshape(-1).astype(F32)
     totals, offset = [], 0
     for a in sums:
         size = a.size // owners

time: 993 us -> 999 us (level)
    ppermute x12, waiting for transfers between devices: 77.9 us -> 62.1 us  [chain(): total = total + lax.ppermute(sent, 'seq', [pair]).astype(F32)]
    ppermute x21, starting transfers between devices: 57.6 us -> 69.3 us  [send(): last[key] = lax.ppermute(value, 'seq', pairs)]
    ppermute x21, waiting for transfers between devices: 62.5 us -> 73 us  [send(): last[key] = lax.ppermute(value, 'seq', pairs)]
    ppermute x69 -> x63, waiting for transfers between devices: 256 us -> 264 us  [swap(): return lax.ppermute(value, axis, [(i, i ^ step) for i in range(count)])]
    ppermute x69 -> x63, starting transfers between devices: 68.3 us -> 60.2 us  [swap(): return lax.ppermute(value, axis, [(i, i ^ step) for i in range(count)])]
  transfers between devices with their start and end apart: 107 -> 101, of which waited for: 33 -> 28; matrix products, arithmetic and copies ran while one was open for 27% -> 27% of each run, Pallas kernels for 9% -> 8%
where the time goes in v7:
time: 999 us; the launch traced here: 992 us
  waiting for transfers between devices  400 us (40%)
  matrix products  170 us (17%)
  starting transfers between devices  145 us (15%)
  other arithmetic  96.5 us (10%)
  Pallas kernels  91.8 us (9%)
  local copies, waits for them, and re-layouts  71.1 us (7%)
  between operations  16.8 us (2%)
    ppermute x63, waiting for transfers between devices, swap(): return lax.ppermute(value, axis, [(i, i ^ step) for i in range(count)])  264 us
    ppermute x21, waiting for transfers between devices, send(): last[key] = lax.ppermute(value, 'seq', pairs)  73 us
    ppermute x21, starting transfers between devices, send(): last[key] = lax.ppermute(value, 'seq', pairs)  69.3 us
    ppermute x12, waiting for transfers between devices, chain(): total = total + lax.ppermute(sent, 'seq', [pair]).astype(F32)  62.1 us
    dot_general x11, matrix products, mm_tn(): lax.dot_general(a, b, (((0,), (0,)), ((), ())), preferred_element_type=F32)  61.2 us
    ppermute x63, starting transfers between devices, swap(): return lax.ppermute(value, axis, [(i, i ^ step) for i in range(count)])  60.2 us
    dot_general x6, matrix products, mm_nt(): lax.dot_general(a, b, (((1,), (1,)), ((), ())), preferred_element_type=F32)  55.7 us
    pallas_call x4, Pallas kernels, run(): pl.pallas_call(kernel, grid=(args[0].shape[0],), in_specs=specs, out_spec...  49.4 us
  transfers between devices with their start and end apart: 101, of which 28 were waited for; matrix products, arithmetic and copies ran while one was open for 27% of the time, Pallas kernels for 8%

profile of v7, /device:TPU:0, one launch (start us, length us, event | category | flops | bytes accessed | tf_op | source)
XLA Modules:
  0.0 991.9 jit_solution(8246073377325475757)
XLA Ops:
  27.4 9.6 collective-permute-done.1
  38.5 21.2 %collective-permute-done.2 = f32[2,5409]{1,0:T(2,128)S(1)} collective-permute-done((f32[2,5409]{1,0:T(2,128)S(1)}, f32[2,5409]{1,0:T(2,128)S(1)}, u32[]{:S(2)}, u32[]{:S(2)}) %collective-permute-start.2) | collective-permute-done | bytes 43304 | tf_op jit(solution)/shard_map/ppermute | solution.py:346
  68.8 16.3 %collective-permute-done.8 = bf16[256,1024]{1,0:T(8,128)(2,1)} collective-permute-done((bf16[256,1024]{1,0:T(8,128)(2,1)}, bf16[256,1024]{1,0:T(8,128)(2,1)}, u32[]{:S(2)}, u32[]{:S(2)}) %collective-permute-start.8) | collective-permute-done | bytes 524320 | tf_op jit(solution)/shard_map/ppermute | solution.py:346
  106.0 5.6 shard_map.289
  111.7 6.8 fusion.2
  118.5 5.7 convolution_convert_fusion.8
  154.4 13.6 %collective-permute-done.29 = bf16[128,2816]{1,0:T(8,128)(2,1)S(1)} collective-permute-done((bf16[128,2816]{1,0:T(8,128)(2,1)S(1)}, bf16[128,2816]{1,0:T(8,128)(2,1)S(1)}, u32[]{:S(2)}, u32[]{:S(2)}) %collective-permute-start.29) | collective-permute-done | bytes 720928 | tf_op jit(solution)/shard_map/ppermute | solution.py:346
  168.7 11.9 %collective-permute-done.28 = bf16[128,2816]{1,0:T(8,128)(2,1)S(1)} collective-permute-done((bf16[128,2816]{1,0:T(8,128)(2,1)S(1)}, bf16[128,2816]{1,0:T(8,128)(2,1)S(1)}, u32[]{:S(2)}, u32[]{:S(2)}) %collective-permute-start.28) | collective-permute-done | bytes 720928 | tf_op jit(solution)/shard_map/ppermute | solution.py:346
  197.4 8.2 fusion.83
  206.3 15.0 %shard_map.291 = (bf16[4,256,512]{2,1,0:T(8,128)(2,1)}, f32[4,256,512]{2,1,0:T(8,128)}, f32[4,256,64]{2,1,0:T(8,128)}, bf16[4,256,256]{2,1,0:T(8,128)(2,1)}) custom-call(f32[4,256,1024]{2,1,0:T(8,128)} %bitcast.200, bf16[4,256,1024]{2,1,0:T(8,128)(2,1)} %bitcast.203, f32[4,256,128]{2,1,0:T(8,128)} %bitcast.177, f32[4,64,1024]{2,1,0:T(8,128)} %pad_maximum_fusion.7.init_ref, ...), custom_call_target="tpu_custom_call" | custom-call | flops 12000000000 | bytes 16000000 | tf_op jit(solution)/shard_map/pallas_call | solution.py:258
  234.9 24.7 %collective-permute-done.40.refs_2_ = bf16[4,128,2816]{2,1,0:T(8,128)(2,1)} collective-permute-done((bf16[4,128,2816]{2,1,0:T(8,128)(2,1)}, bf16[4,128,2816]{2,1,0:T(8,128)(2,1)}, u32[]{:S(2)}, u32[]{:S(2)}) %collective-permute-start.40) | collective-permute-done | bytes 2883616 | tf_op jit(solution)/shard_map/ppermute | solution.py:346
  259.6 13.4 %fusion.66 = f32[1024,1408]{1,0:T(8,128)} fusion(bf16[1408,2048]{1,0:T(8,128)(2,1)} %all-gather.6.cloned.1.call-done, bf16[256,2048]{1,0:T(8,128)(2,1)} %collective-permute-done.35, bf16[256,2048]{1,0:T(8,128)(2,1)} %collective-permute-done.34, bf16[256,2048]{1,0:T(8,128)(2,1)} %collective-permute-done.33, bf16[256,2048]{1,0:T(8,128)(2,1)} %param.33, ...), kind=kOutput, calls=%fused_computation.239 | convolution fusion | flops 5926551552 | bytes 15732736 | tf_op jit(solution)/shard_map/dot_general | solution.py:23
  273.1 7.6 collective-permute-done.31
  288.9 23.0 %collective-permute-done.38 = bf16[256,2048]{1,0:T(8,128)(2,1)} collective-permute-done((bf16[256,2048]{1,0:T(8,128)(2,1)S(1)}, bf16[256,2048]{1,0:T(8,128)(2,1)}, u32[]{:S(2)}, u32[]{:S(2)}) %collective-permute-start.38) | collective-permute-done | bytes 1048608 | tf_op jit(solution)/shard_map/ppermute | solution.py:346
  311.9 20.6 %collective-permute-done.37 = bf16[256,2048]{1,0:T(8,128)(2,1)} collective-permute-done((bf16[256,2048]{1,0:T(8,128)(2,1)S(1)}, bf16[256,2048]{1,0:T(8,128)(2,1)}, u32[]{:S(2)}, u32[]{:S(2)}) %collective-permute-start.37) | collective-permute-done | bytes 1048608 | tf_op jit(solution)/shard_map/ppermute | solution.py:346
  336.6 13.6 %shard_map.292 = bf16[2048,2816]{1,0:T(8,128)(2,1)} custom-call(s32[16]{0:T(128)} %stack.181.spot_ref, bf16[4,128,2816]{2,1,0:T(8,128)(2,1)} %pad_maximum_fusion.3.refs_0_, bf16[4,128,2816]{2,1,0:T(8,128)(2,1)} %collective-permute-done.39.refs_1_, bf16[4,128,2816]{2,1,0:T(8,128)(2,1)} %collective-permute-done.40.refs_2_, ...), custom_call_target="tpu_custom_call" | custom-call | bytes 23068672 | tf_op jit(solution)/shard_map/pallas_call | solution.py:382
  350.2 21.3 %fusion.65 = f32[1024,2816]{1,0:T(8,128)} fusion(bf16[2048,2816]{1,0:T(8,128)(2,1)} %shard_map.292, bf16[256,2048]{1,0:T(8,128)(2,1)} %collective-permute-done.38, bf16[256,2048]{1,0:T(8,128)(2,1)} %collective-permute-done.37, bf16[256,2048]{1,0:T(8,128)(2,1)} %collective-permute-done.36, bf16[256,2048]{1,0:T(8,128)(2,1)S(1)} %multiply_convert_fusion.5), kind=kOutput, calls=%fused_computation.238 | convolution fusion | flops 11827937280 | bytes 27262976 | tf_op jit(solution)/shard_map/dot_general | solution.py:19
  371.6 7.3 multiply_convert_fusion.2
  378.9 8.9 convolution_convert_fusion
  388.4 16.4 %convolution_convert_fusion.1 = bf16[1024,2048]{1,0:T(8,128)(2,1)} fusion(bf16[1024,2816]{1,0:T(8,128)(2,1)S(1)} %pad_maximum_fusion, bf16[2048,2816]{1,0:T(8,128)(2,1)} %shard_map.292), kind=kOutput, calls=%fused_computation.21 | convolution fusion | flops 11813257216 | bytes 21495808 | tf_op jit(solution)/shard_map/dot_general | solution.py:23
  404.8 10.4 %add_convert_fusion = bf16[1024,2816]{1,0:T(8,128)(2,1)} fusion(bf16[1024,2816]{1,0:T(8,128)(2,1)} %collective-permute-done.42, bf16[1024,2816]{1,0:T(8,128)(2,1)S(1)} %pad_maximum_fusion, bf16[1024,256]{1,0:T(8,128)(2,1)S(1)} %get-tuple-element.242, bf16[1024,256]{1,0:T(8,128)(2,1)S(1)} %copy-done.71, bf16[1024,256]{1,0:T(8,128)(2,1)S(1)} %copy-done.72, ...), kind=kOutput, calls=%fused_computation.1 | convolution fusion | flops 5922619392 | bytes 19398656 | tf_op jit(solution)/shard_map/dot_general | solution.py:27
  415.7 8.0 convolution_convert_fusion.4
  430.2 8.5 add_convert_fusion.2
  438.7 14.0 %collective-permute-done.43 = bf16[256,2048]{1,0:T(8,128)(2,1)S(1)} collective-permute-done((bf16[256,2048]{1,0:T(8,128)(2,1)S(1)}, bf16[256,2048]{1,0:T(8,128)(2,1)S(1)}, u32[]{:S(2)}, u32[]{:S(2)}) %collective-permute-start.43) | collective-permute-done | bytes 1048608 | tf_op jit(solution)/shard_map/ppermute | solution.py:346
  452.8 21.9 %collective-permute-done.44 = bf16[256,2048]{1,0:T(8,128)(2,1)S(1)} collective-permute-done((bf16[256,2048]{1,0:T(8,128)(2,1)S(1)}, bf16[256,2048]{1,0:T(8,128)(2,1)S(1)}, u32[]{:S(2)}, u32[]{:S(2)}) %collective-permute-start.44) | collective-permute-done | bytes 1048608 | tf_op jit(solution)/shard_map/ppermute | solution.py:346
  483.6 8.3 convolution_convert_fusion.2
  491.9 14.3 %collective-permute-done.47 = bf16[256,2048]{1,0:T(8,128)(2,1)S(1)} collective-permute-done((bf16[256,2048]{1,0:T(8,128)(2,1)S(1)}, bf16[256,2048]{1,0:T(8,128)(2,1)S(1)}, u32[]{:S(2)}, u32[]{:S(2)}) %collective-permute-start.47) | collective-permute-done | bytes 1048608 | tf_op jit(solution)/shard_map/ppermute | solution.py:346
  506.2 21.7 %collective-permute-done.48 = bf16[256,2048]{1,0:T(8,128)(2,1)S(1)} collective-permute-done((bf16[256,2048]{1,0:T(8,128)(2,1)S(1)}, bf16[256,2048]{1,0:T(8,128)(2,1)S(1)}, u32[]{:S(2)}, u32[]{:S(2)}) %collective-permute-start.48) | collective-permute-done | bytes 1048608 | tf_op jit(solution)/shard_map/ppermute | solution.py:346
  537.6 19.9 %shard_map.293 = (bf16[4,256,1024]{2,1,0:T(8,128)(2,1)}, f32[4,256,1024]{2,1,0:T(8,128)}, f32[4,256,128]{2,1,0:T(8,128)}, f32[4,64,1024]{2,1,0:T(8,128)}, f32[8,512]{1,0:T(8,128)}) custom-call(f32[4,256,1024]{2,1,0:T(8,128)} %bitcast.201, bf16[4,256,1024]{2,1,0:T(8,128)(2,1)} %bitcast.204, f32[4,256,128]{2,1,0:T(8,128)} %bitcast.178, ...), custom_call_target="tpu_custom_call" | custom-call | flops 24000000000 | bytes 20000000 | tf_op jit(solution)/shard_map/pallas_call | solution.py:258
  575.9 18.1 %collective-permute-done.59 = bf16[256,2048]{1,0:T(8,128)(2,1)S(1)} collective-permute-done((bf16[256,2048]{1,0:T(8,128)(2,1)S(1)}, bf16[256,2048]{1,0:T(8,128)(2,1)S(1)}, u32[]{:S(2)}, u32[]{:S(2)}) %collective-permute-start.59) | collective-permute-done | bytes 1048608 | tf_op jit(solution)/shard_map/ppermute | solution.py:346
  594.7 17.6 %collective-permute-done.58 = bf16[256,2048]{1,0:T(8,128)(2,1)S(1)} collective-permute-done((bf16[256,2048]{1,0:T(8,128)(2,1)S(1)}, bf16[256,2048]{1,0:T(8,128)(2,1)S(1)}, u32[]{:S(2)}, u32[]{:S(2)}) %collective-permute-start.58) | collective-permute-done | bytes 1048608 | tf_op jit(solution)/shard_map/ppermute | solution.py:346
  624.8 41.1 %collective-permute-done.53 = bf16[4,64,512]{2,1,0:T(8,128)(2,1)S(1)} collective-permute-done((bf16[4,64,512]{2,1,0:T(8,128)(2,1)S(1)}, bf16[4,64,512]{2,1,0:T(8,128)(2,1)S(1)}, u32[]{:S(2)}, u32[]{:S(2)}) %collective-permute-start.53) | collective-permute-done | bytes 262176 | tf_op jit(solution)/shard_map/ppermute | solution.py:464
  666.0 15.5 %collective-permute-done.56 = bf16[4,64,512]{2,1,0:T(8,128)(2,1)S(1)} collective-permute-done((bf16[4,64,512]{2,1,0:T(8,128)(2,1)S(1)}, bf16[4,64,512]{2,1,0:T(8,128)(2,1)S(1)}, u32[]{:S(2)}, u32[]{:S(2)}) %collective-permute-start.56) | collective-permute-done | bytes 262176 | tf_op jit(solution)/shard_map/ppermute | solution.py:464
  682.7 9.1 shard_map.294
  700.6 5.9 convolution_convert_fusion.6
  710.0 5.9 fusion.87
  715.9 6.8 fusion.86
  722.7 12.5 %collective-permute-done.70 = bf16[352,2048]{1,0:T(8,128)(2,1)S(1)} collective-permute-done((bf16[352,2048]{1,0:T(8,128)(2,1)S(1)}, bf16[352,2048]{1,0:T(8,128)(2,1)S(1)}, u32[]{:S(2)}, u32[]{:S(2)}) %collective-permute-start.70) | collective-permute-done | bytes 1441824 | tf_op jit(solution)/shard_map/ppermute | solution.py:534
  735.2 5.5 collective-permute-start.71
  743.4 9.5 add_convert_fusion.1
  801.8 7.0 collective-permute-done.72
  808.8 5.5 collective-permute-start.73
  833.4 24.1 %collective-permute-start.74 = (bf16[2,256,1024]{2,1,0:T(8,128)(2,1)S(1)}, bf16[2,256,1024]{2,1,0:T(8,128)(2,1)S(1)}, u32[]{:S(2)}, u32[]{:S(2)}) collective-permute-start(bf16[2,256,1024]{2,1,0:T(8,128)(2,1)S(1)} %get-tuple-element.139), channel_id=1, source_target_pairs={{0,1},{3,2},{4,5},{7,6},{8,9},{11,10},{12,13},{15,14},{16,17},{19,... | collective-permute-start | bytes 3145736 | tf_op jit(solution)/shard_map/ppermute | solution.py:534
  861.0 12.2 %collective-permute-done.74 = bf16[2,256,1024]{2,1,0:T(8,128)(2,1)S(1)} collective-permute-done((bf16[2,256,1024]{2,1,0:T(8,128)(2,1)S(1)}, bf16[2,256,1024]{2,1,0:T(8,128)(2,1)S(1)}, u32[]{:S(2)}, u32[]{:S(2)}) %collective-permute-start.74) | collective-permute-done | bytes 1048608 | tf_op jit(solution)/shard_map/ppermute | solution.py:534
  890.2 8.0 shard_map.297
  898.3 5.6 collective-permute-start.76
  918.1 16.0 %collective-permute-done.88 = bf16[2,256,1024]{2,1,0:T(8,128)(2,1)S(1)} collective-permute-done((bf16[2,256,1024]{2,1,0:T(8,128)(2,1)S(1)}, bf16[2,256,1024]{2,1,0:T(8,128)(2,1)S(1)}, u32[]{:S(2)}, u32[]{:S(2)}) %collective-permute-start.88) | collective-permute-done | bytes 1048608 | tf_op jit(solution)/shard_map/ppermute | solution.py:534
  939.0 21.8 %collective-permute-done.89 = bf16[2,256,1024]{2,1,0:T(8,128)(2,1)S(1)} collective-permute-done((bf16[2,256,1024]{2,1,0:T(8,128)(2,1)S(1)}, bf16[2,256,1024]{2,1,0:T(8,128)(2,1)S(1)}, u32[]{:S(2)}, u32[]{:S(2)}) %collective-permute-start.89) | collective-permute-done | bytes 1048608 | tf_op jit(solution)/shard_map/ppermute | solution.py:534
  (586 shorter events, 329.6 us)
Async XLA Ops:
  7.2 214.1 %all-gather.4.cloned.1.call-start = ((), (), s32[]{:S(2)}) async-start(), calls=%async_computation.1 | async-start | bytes 3145728 | tf_op jit(solution)/shard_map/all_gather | solution.py:617
  7.9 251.7 %all-gather.6.cloned.1.call-start = ((), (), s32[]{:S(2)}) async-start(), calls=%async_computation.2 | async-start | bytes 8650752 | tf_op jit(solution)/shard_map/all_gather | solution.py:618
  8.0 89.9 %collective-permute-start.6 = (bf16[256,2048]{1,0:T(8,128)(2,1)}, bf16[256,2048]{1,0:T(8,128)(2,1)S(1)}, u32[]{:S(2)}, u32[]{:S(2)}) collective-permute-start(bf16[256,2048]{1,0:T(8,128)(2,1)} %param.17), channel_id=1, source_target_pairs={{0,24},{8,16},{16,8},{24,0},{1,25},{9,17},{17,9},{25,1},{2,26},{10... | collective-permute-start | bytes 3145736 | tf_op jit(solution)/shard_map/ppermute | solution.py:346
  12.0 86.1 %collective-permute-start.5 = (bf16[256,2048]{1,0:T(8,128)(2,1)}, bf16[256,2048]{1,0:T(8,128)(2,1)}, u32[]{:S(2)}, u32[]{:S(2)}) collective-permute-start(bf16[256,2048]{1,0:T(8,128)(2,1)} %param.17), channel_id=1, source_target_pairs={{0,16},{8,24},{16,0},{24,8},{1,17},{9,25},{17,1},{25,9},{2,18},{10... | collective-permute-start | bytes 3145736 | tf_op jit(solution)/shard_map/ppermute | solution.py:346
  17.7 511.2 %reduce-scatter.2.cloned.1.call-start = ((), (), s32[]{:S(2)}) async-start(), calls=%async_computation.3 | async-start | bytes 7208960 | tf_op jit(solution)/shard_map/reduce_scatter | solution.py:665
  23.4 36.3 %collective-permute-start.2 = (f32[2,5409]{1,0:T(2,128)S(1)}, f32[2,5409]{1,0:T(2,128)S(1)}, u32[]{:S(2)}, u32[]{:S(2)}) collective-permute-start(f32[2,5409]{1,0:T(2,128)S(1)} %pad_maximum_fusion.29), channel_id=1, source_target_pairs={{0,16},{8,24},{16,0},{24,8},{1,17},{9,25},{17,1},{25,9},{2,18},{10... | collective-permute-start | bytes 129824 | tf_op jit(solution)/shard_map/ppermute | solution.py:346
  25.3 36.1 %collective-permute-start.3 = (f32[2,5409]{1,0:T(2,128)S(1)}, f32[2,5409]{1,0:T(2,128)S(1)}, u32[]{:S(2)}, u32[]{:S(2)}) collective-permute-start(f32[2,5409]{1,0:T(2,128)S(1)} %pad_maximum_fusion.29), channel_id=1, source_target_pairs={{0,24},{8,16},{16,8},{24,0},{1,25},{9,17},{17,9},{25,1},{2,26},{10... | collective-permute-start | bytes 129824 | tf_op jit(solution)/shard_map/ppermute | solution.py:346
  37.0 31.3 %collective-permute-start.7 = (bf16[256,1024]{1,0:T(8,128)(2,1)}, bf16[256,1024]{1,0:T(8,128)(2,1)S(1)}, u32[]{:S(2)}, u32[]{:S(2)}) collective-permute-start(bf16[256,1024]{1,0:T(8,128)(2,1)} %pad_maximum_fusion.12), channel_id=1, source_target_pairs={{0,8},{8,0},{16,24},{24,16},{1,9},{9,1},{17,25},{25,17},{2,10},{10... | collective-permute-start | bytes 1572872 | tf_op jit(solution)/shard_map/ppermute | solution.py:346
  68.4 30.3 %collective-permute-start.4 = (bf16[256,2048]{1,0:T(8,128)(2,1)S(1)}, bf16[256,2048]{1,0:T(8,128)(2,1)S(1)}, u32[]{:S(2)}, u32[]{:S(2)}) collective-permute-start(bf16[256,2048]{1,0:T(8,128)(2,1)S(1)} %copy-done.2), channel_id=1, source_target_pairs={{0,8},{8,0},{16,24},{24,16},{1,9},{9,1},{17,25},{25,17},{2,10},{10... | collective-permute-start | bytes 3145736 | tf_op jit(solution)/shard_map/ppermute | solution.py:346
  90.1 57.9 %collective-permute-start.11 = (bf16[256,1024]{1,0:T(8,128)(2,1)}, bf16[256,1024]{1,0:T(8,128)(2,1)}, u32[]{:S(2)}, u32[]{:S(2)}) collective-permute-start(bf16[256,1024]{1,0:T(8,128)(2,1)} %pad_maximum_fusion.16), channel_id=1, source_target_pairs={{0,8},{8,0},{16,24},{24,16},{1,9},{9,1},{17,25},{25,17},{2,10},{10... | collective-permute-start | bytes 1572872 | tf_op jit(solution)/shard_map/ppermute | solution.py:346
  101.9 48.6 %collective-permute-start.13 = (bf16[256,1024]{1,0:T(8,128)(2,1)}, bf16[256,1024]{1,0:T(8,128)(2,1)}, u32[]{:S(2)}, u32[]{:S(2)}) collective-permute-start(bf16[256,1024]{1,0:T(8,128)(2,1)} %pad_maximum_fusion.17), channel_id=1, source_target_pairs={{0,16},{8,24},{16,0},{24,8},{1,17},{9,25},{17,1},{25,9},{2,18},{10... | collective-permute-start | bytes 1572872 | tf_op jit(solution)/shard_map/ppermute | solution.py:346
  103.6 50.0 %collective-permute-start.15 = (bf16[256,1024]{1,0:T(8,128)(2,1)}, bf16[256,1024]{1,0:T(8,128)(2,1)}, u32[]{:S(2)}, u32[]{:S(2)}) collective-permute-start(bf16[256,1024]{1,0:T(8,128)(2,1)} %pad_maximum_fusion.18), channel_id=1, source_target_pairs={{0,24},{8,16},{16,8},{24,0},{1,25},{9,17},{17,9},{25,1},{2,26},{10... | collective-permute-start | bytes 1572872 | tf_op jit(solution)/shard_map/ppermute | solution.py:346
  184.1 45.1 %collective-permute-start.35 = (bf16[256,2048]{1,0:T(8,128)(2,1)}, bf16[256,2048]{1,0:T(8,128)(2,1)}, u32[]{:S(2)}, u32[]{:S(2)}) collective-permute-start(bf16[256,2048]{1,0:T(8,128)(2,1)} %param.33), channel_id=1, source_target_pairs={{0,24},{8,16},{16,8},{24,0},{1,25},{9,17},{17,9},{25,1},{2,26},{10... | collective-permute-start | bytes 3145736 | tf_op jit(solution)/shard_map/ppermute | solution.py:346
  185.6 47.3 %collective-permute-start.34 = (bf16[256,2048]{1,0:T(8,128)(2,1)}, bf16[256,2048]{1,0:T(8,128)(2,1)}, u32[]{:S(2)}, u32[]{:S(2)}) collective-permute-start(bf16[256,2048]{1,0:T(8,128)(2,1)} %param.33), channel_id=1, source_target_pairs={{0,16},{8,24},{16,0},{24,8},{1,17},{9,25},{17,1},{25,9},{2,18},{10... | collective-permute-start | bytes 3145736 | tf_op jit(solution)/shard_map/ppermute | solution.py:346
  186.1 47.6 %collective-permute-start.33 = (bf16[256,2048]{1,0:T(8,128)(2,1)}, bf16[256,2048]{1,0:T(8,128)(2,1)}, u32[]{:S(2)}, u32[]{:S(2)}) collective-permute-start(bf16[256,2048]{1,0:T(8,128)(2,1)} %param.33), channel_id=1, source_target_pairs={{0,8},{8,0},{16,24},{24,16},{1,9},{9,1},{17,25},{25,17},{2,10},{10... | collective-permute-start | bytes 3145736 | tf_op jit(solution)/shard_map/ppermute | solution.py:346
  194.3 65.3 %collective-permute-start.40 = (bf16[4,128,2816]{2,1,0:T(8,128)(2,1)}, bf16[4,128,2816]{2,1,0:T(8,128)(2,1)}, u32[]{:S(2)}, u32[]{:S(2)}) collective-permute-start(bf16[4,128,2816]{2,1,0:T(8,128)(2,1)} %pad_maximum_fusion.3.refs_0_), channel_id=1, source_target_pairs={{0,1},{1,0},{2,3},{3,2},{4,5},{5,4},{6,7},{7,6},{8,9},{9,8},{10,11... | collective-permute-start | bytes 8650760 | tf_op jit(solution)/shard_map/ppermute | solution.py:346
  205.7 130.9 %collective-permute-start.39 = (bf16[4,128,2816]{2,1,0:T(8,128)(2,1)}, bf16[4,128,2816]{2,1,0:T(8,128)(2,1)}, u32[]{:S(2)}, u32[]{:S(2)}) collective-permute-start(bf16[4,128,2816]{2,1,0:T(8,128)(2,1)} %pad_maximum_fusion.3.refs_0_), channel_id=1, source_target_pairs={{0,4},{4,0},{1,5},{5,1},{2,6},{6,2},{3,7},{7,3},{8,12},{12,8},{9,1... | collective-permute-start | bytes 8650760 | tf_op jit(solution)/shard_map/ppermute | solution.py:346
  229.1 44.0 %collective-permute-start.30 = (bf16[256,2048]{1,0:T(8,128)(2,1)}, bf16[256,2048]{1,0:T(8,128)(2,1)S(1)}, u32[]{:S(2)}, u32[]{:S(2)}) collective-permute-start(bf16[256,2048]{1,0:T(8,128)(2,1)} %get-tuple-element.248), channel_id=1, source_target_pairs={{0,8},{8,0},{16,24},{24,16},{1,9},{9,1},{17,25},{25,17},{2,10},{10... | collective-permute-start | bytes 3145736 | tf_op jit(solution)/shard_map/ppermute | solution.py:346
  232.9 47.9 %collective-permute-start.31 = (bf16[256,2048]{1,0:T(8,128)(2,1)}, bf16[256,2048]{1,0:T(8,128)(2,1)}, u32[]{:S(2)}, u32[]{:S(2)}) collective-permute-start(bf16[256,2048]{1,0:T(8,128)(2,1)} %get-tuple-element.247), channel_id=1, source_target_pairs={{0,16},{8,24},{16,0},{24,8},{1,17},{9,25},{17,1},{25,9},{2,18},{10... | collective-permute-start | bytes 3145736 | tf_op jit(solution)/shard_map/ppermute | solution.py:346
  233.7 47.1 %collective-permute-start.32 = (bf16[256,2048]{1,0:T(8,128)(2,1)S(1)}, bf16[256,2048]{1,0:T(8,128)(2,1)}, u32[]{:S(2)}, u32[]{:S(2)}) collective-permute-start(bf16[256,2048]{1,0:T(8,128)(2,1)S(1)} %get-tuple-element.246), channel_id=1, source_target_pairs={{0,24},{8,16},{16,8},{24,0},{1,25},{9,17},{17,9},{25,1},{2,26},{10... | collective-permute-start | bytes 3145736 | tf_op jit(solution)/shard_map/ppermute | solution.py:346
  259.6 76.9 %collective-permute-start.41 = (bf16[4,128,2816]{2,1,0:T(8,128)(2,1)}, bf16[4,128,2816]{2,1,0:T(8,128)(2,1)}, u32[]{:S(2)}, u32[]{:S(2)}) collective-permute-start(bf16[4,128,2816]{2,1,0:T(8,128)(2,1)} %collective-permute-done.40.refs_2_), channel_id=1, source_target_pairs={{0,4},{4,0},{1,5},{5,1},{2,6},{6,2},{3,7},{7,3},{8,12},{12,8},{9,1... | collective-permute-start | bytes 8650760 | tf_op jit(solution)/shard_map/ppermute | solution.py:346
  286.3 46.2 %collective-permute-start.37 = (bf16[256,2048]{1,0:T(8,128)(2,1)S(1)}, bf16[256,2048]{1,0:T(8,128)(2,1)}, u32[]{:S(2)}, u32[]{:S(2)}) collective-permute-start(bf16[256,2048]{1,0:T(8,128)(2,1)S(1)} %multiply_convert_fusion.5), channel_id=1, source_target_pairs={{0,16},{8,24},{16,0},{24,8},{1,17},{9,25},{17,1},{25,9},{2,18},{10... | collective-permute-start | bytes 3145736 | tf_op jit(solution)/shard_map/ppermute | solution.py:346
  286.8 45.7 %collective-permute-start.36 = (bf16[256,2048]{1,0:T(8,128)(2,1)S(1)}, bf16[256,2048]{1,0:T(8,128)(2,1)}, u32[]{:S(2)}, u32[]{:S(2)}) collective-permute-start(bf16[256,2048]{1,0:T(8,128)(2,1)S(1)} %multiply_convert_fusion.5), channel_id=1, source_target_pairs={{0,8},{8,0},{16,24},{24,16},{1,9},{9,1},{17,25},{25,17},{2,10},{10... | collective-permute-start | bytes 3145736 | tf_op jit(solution)/shard_map/ppermute | solution.py:346
  415.3 291.3 %all-gather.8.cloned.1.call-start = ((), (), s32[]{:S(2)}) async-start(), calls=%async_computation.4 | async-start | bytes 7208960 | tf_op jit(solution)/shard_map/all_gather | solution.py:696
  427.4 47.3 %collective-permute-start.44 = (bf16[256,2048]{1,0:T(8,128)(2,1)S(1)}, bf16[256,2048]{1,0:T(8,128)(2,1)S(1)}, u32[]{:S(2)}, u32[]{:S(2)}) collective-permute-start(bf16[256,2048]{1,0:T(8,128)(2,1)S(1)} %get-tuple-element.236), channel_id=1, source_target_pairs={{0,16},{8,24},{16,0},{24,8},{1,17},{9,25},{17,1},{25,9},{2,18},{10... | collective-permute-start | bytes 3145736 | tf_op jit(solution)/shard_map/ppermute | solution.py:346
  428.8 45.9 %collective-permute-start.45 = (bf16[256,2048]{1,0:T(8,128)(2,1)S(1)}, bf16[256,2048]{1,0:T(8,128)(2,1)S(1)}, u32[]{:S(2)}, u32[]{:S(2)}) collective-permute-start(bf16[256,2048]{1,0:T(8,128)(2,1)S(1)} %get-tuple-element.235), channel_id=1, source_target_pairs={{0,24},{8,16},{16,8},{24,0},{1,25},{9,17},{17,9},{25,1},{2,26},{10... | collective-permute-start | bytes 3145736 | tf_op jit(solution)/shard_map/ppermute | solution.py:346
  481.5 46.4 %collective-permute-start.48 = (bf16[256,2048]{1,0:T(8,128)(2,1)S(1)}, bf16[256,2048]{1,0:T(8,128)(2,1)S(1)}, u32[]{:S(2)}, u32[]{:S(2)}) collective-permute-start(bf16[256,2048]{1,0:T(8,128)(2,1)S(1)} %get-tuple-element.111), channel_id=1, source_target_pairs={{0,16},{8,24},{16,0},{24,8},{1,17},{9,25},{17,1},{25,9},{2,18},{10... | collective-permute-start | bytes 3145736 | tf_op jit(solution)/shard_map/ppermute | solution.py:346
  482.2 46.6 %collective-permute-start.49 = (bf16[256,2048]{1,0:T(8,128)(2,1)S(1)}, bf16[256,2048]{1,0:T(8,128)(2,1)}, u32[]{:S(2)}, u32[]{:S(2)}) collective-permute-start(bf16[256,2048]{1,0:T(8,128)(2,1)S(1)} %get-tuple-element.111), channel_id=1, source_target_pairs={{0,24},{8,16},{16,8},{24,0},{1,25},{9,17},{17,9},{25,1},{2,26},{10... | collective-permute-start | bytes 3145736 | tf_op jit(solution)/shard_map/ppermute | solution.py:346
  568.4 43.9 %collective-permute-start.58 = (bf16[256,2048]{1,0:T(8,128)(2,1)S(1)}, bf16[256,2048]{1,0:T(8,128)(2,1)S(1)}, u32[]{:S(2)}, u32[]{:S(2)}) collective-permute-start(bf16[256,2048]{1,0:T(8,128)(2,1)S(1)} %get-tuple-element.234), channel_id=1, source_target_pairs={{0,16},{8,24},{16,0},{24,8},{1,17},{9,25},{17,1},{25,9},{2,18},{10... | collective-permute-start | bytes 3145736 | tf_op jit(solution)/shard_map/ppermute | solution.py:346
  569.2 43.7 %collective-permute-start.57 = (bf16[256,2048]{1,0:T(8,128)(2,1)S(1)}, bf16[256,2048]{1,0:T(8,128)(2,1)S(1)}, u32[]{:S(2)}, u32[]{:S(2)}) collective-permute-start(bf16[256,2048]{1,0:T(8,128)(2,1)S(1)} %get-tuple-element.232), channel_id=1, source_target_pairs={{0,8},{8,0},{16,24},{24,16},{1,9},{9,1},{17,25},{25,17},{2,10},{10... | collective-permute-start | bytes 3145736 | tf_op jit(solution)/shard_map/ppermute | solution.py:346
  573.0 48.0 %collective-permute-start.61 = (bf16[1024,1024]{1,0:T(8,128)(2,1)S(1)}, bf16[1024,1024]{1,0:T(8,128)(2,1)S(1)}, u32[]{:S(2)}, u32[]{:S(2)}) collective-permute-start(bf16[1024,1024]{1,0:T(8,128)(2,1)S(1)} %convolution_convert_fusion.7), channel_id=1, source_target_pairs={{0,4},{4,0},{1,5},{5,1},{2,6},{6,2},{3,7},{7,3},{8,12},{12,8},{9,1... | collective-permute-start | bytes 6291464 | tf_op jit(solution)/shard_map/ppermute | solution.py:346
  575.3 40.5 %collective-permute-start.60 = (bf16[256,2048]{1,0:T(8,128)(2,1)S(1)}, bf16[256,2048]{1,0:T(8,128)(2,1)S(1)}, u32[]{:S(2)}, u32[]{:S(2)}) collective-permute-start(bf16[256,2048]{1,0:T(8,128)(2,1)S(1)} %convolution_convert_fusion.5), channel_id=1, source_target_pairs={{0,4},{4,0},{1,5},{5,1},{2,6},{6,2},{3,7},{7,3},{8,12},{12,8},{9,1... | collective-permute-start | bytes 3145736 | tf_op jit(solution)/shard_map/ppermute | solution.py:346
  618.1 47.8 %collective-permute-start.53 = (bf16[4,64,512]{2,1,0:T(8,128)(2,1)S(1)}, bf16[4,64,512]{2,1,0:T(8,128)(2,1)S(1)}, u32[]{:S(2)}, u32[]{:S(2)}) collective-permute-start(bf16[4,64,512]{2,1,0:T(8,128)(2,1)S(1)} %get-tuple-element.265), channel_id=1, source_target_pairs={{1,0},{5,4},{9,8},{13,12},{17,16},{21,20},{25,24},{29,28}} | collective-permute-start | bytes 786440 | tf_op jit(solution)/shard_map/ppermute | solution.py:464
  619.5 62.0 %collective-permute-start.56 = (bf16[4,64,512]{2,1,0:T(8,128)(2,1)S(1)}, bf16[4,64,512]{2,1,0:T(8,128)(2,1)S(1)}, u32[]{:S(2)}, u32[]{:S(2)}) collective-permute-start(bf16[4,64,512]{2,1,0:T(8,128)(2,1)S(1)} %add_convert_fusion.6), channel_id=1, source_target_pairs={{1,0},{5,4},{9,8},{13,12},{17,16},{21,20},{25,24},{29,28}} | collective-permute-start | bytes 786440 | tf_op jit(solution)/shard_map/ppermute | solution.py:464
  709.4 76.2 %collective-permute-start.65 = (bf16[1024,1024]{1,0:T(8,128)(2,1)}, bf16[1024,1024]{1,0:T(8,128)(2,1)}, u32[]{:S(2)}, u32[]{:S(2)}) collective-permute-start(bf16[1024,1024]{1,0:T(8,128)(2,1)} %convolution_convert_fusion.6), channel_id=1, source_target_pairs={{0,4},{4,0},{1,5},{5,1},{2,6},{6,2},{3,7},{7,3},{8,12},{12,8},{9,1... | collective-permute-start | bytes 6291464 | tf_op jit(solution)/shard_map/ppermute | solution.py:346
  735.2 40.5 %collective-permute-start.71 = (bf16[352,2048]{1,0:T(8,128)(2,1)}, bf16[352,2048]{1,0:T(8,128)(2,1)}, u32[]{:S(2)}, u32[]{:S(2)}) collective-permute-start(bf16[352,2048]{1,0:T(8,128)(2,1)} %get-tuple-element.136), channel_id=1, source_target_pairs={{0,1},{3,2},{4,5},{7,6},{8,9},{11,10},{12,13},{15,14},{16,17},{19,... | collective-permute-start | bytes 4325384 | tf_op jit(solution)/shard_map/ppermute | solution.py:534
  741.2 37.1 %collective-permute-start.77 = (bf16[352,2048]{1,0:T(8,128)(2,1)S(1)}, bf16[352,2048]{1,0:T(8,128)(2,1)}, u32[]{:S(2)}, u32[]{:S(2)}) collective-permute-start(bf16[352,2048]{1,0:T(8,128)(2,1)S(1)} %add.684), channel_id=1, source_target_pairs={{1,2},{2,1},{5,6},{6,5},{9,10},{10,9},{13,14},{14,13},{17,18},{18,... | collective-permute-start | bytes 4325384 | tf_op jit(solution)/shard_map/ppermute | solution.py:534
  759.9 37.0 %collective-permute-start.63 = (bf16[256,2048]{1,0:T(8,128)(2,1)}, bf16[256,2048]{1,0:T(8,128)(2,1)}, u32[]{:S(2)}, u32[]{:S(2)}) collective-permute-start(bf16[256,2048]{1,0:T(8,128)(2,1)} %get-tuple-element.222), channel_id=1, source_target_pairs={{0,16},{8,24},{16,0},{24,8},{1,17},{9,25},{17,1},{25,9},{2,18},{10... | collective-permute-start | bytes 3145736 | tf_op jit(solution)/shard_map/ppermute | solution.py:346
  778.3 36.1 %collective-permute-start.78 = (bf16[352,2048]{1,0:T(8,128)(2,1)S(1)}, bf16[352,2048]{1,0:T(8,128)(2,1)S(1)}, u32[]{:S(2)}, u32[]{:S(2)}) collective-permute-start(bf16[352,2048]{1,0:T(8,128)(2,1)S(1)} %add.683), channel_id=1, source_target_pairs={{1,2},{2,1},{5,6},{6,5},{9,10},{10,9},{13,14},{14,13},{17,18},{18,... | collective-permute-start | bytes 4325384 | tf_op jit(solution)/shard_map/ppermute | solution.py:534
  781.5 34.6 %collective-permute-start.84 = (bf16[352,2048]{1,0:T(8,128)(2,1)S(1)}, bf16[352,2048]{1,0:T(8,128)(2,1)S(1)}, u32[]{:S(2)}, u32[]{:S(2)}) collective-permute-start(bf16[352,2048]{1,0:T(8,128)(2,1)S(1)} %add.691), channel_id=1, source_target_pairs={{1,0},{2,3},{5,4},{6,7},{9,8},{10,11},{13,12},{14,15},{17,16},{18,... | collective-permute-start | bytes 4325384 | tf_op jit(solution)/shard_map/ppermute | solution.py:534
  817.2 40.8 %collective-permute-start.85 = (bf16[352,2048]{1,0:T(8,128)(2,1)}, bf16[352,2048]{1,0:T(8,128)(2,1)}, u32[]{:S(2)}, u32[]{:S(2)}) collective-permute-start(bf16[352,2048]{1,0:T(8,128)(2,1)} %add.690), channel_id=1, source_target_pairs={{1,0},{2,3},{5,4},{6,7},{9,8},{10,11},{13,12},{14,15},{17,16},{18,... | collective-permute-start | bytes 4325384 | tf_op jit(solution)/shard_map/ppermute | solution.py:534
  826.7 32.0 %collective-permute-start.68 = (f32[2,5408]{1,0:T(2,128)S(1)}, f32[2,5408]{1,0:T(2,128)S(1)}, u32[]{:S(2)}, u32[]{:S(2)}) collective-permute-start(f32[2,5408]{1,0:T(2,128)S(1)} %get-tuple-element.307), channel_id=1, source_target_pairs={{0,24},{8,16},{16,8},{24,0},{1,25},{9,17},{17,9},{25,1},{2,26},{10... | collective-permute-start | bytes 129800 | tf_op jit(solution)/shard_map/ppermute | solution.py:346
  828.2 31.8 %collective-permute-start.67 = (f32[2,5408]{1,0:T(2,128)S(1)}, f32[2,5408]{1,0:T(2,128)S(1)}, u32[]{:S(2)}, u32[]{:S(2)}) collective-permute-start(f32[2,5408]{1,0:T(2,128)S(1)} %get-tuple-element.308), channel_id=1, source_target_pairs={{0,16},{8,24},{16,0},{24,8},{1,17},{9,25},{17,1},{25,9},{2,18},{10... | collective-permute-start | bytes 129800 | tf_op jit(solution)/shard_map/ppermute | solution.py:346
  833.4 39.7 %collective-permute-start.74 = (bf16[2,256,1024]{2,1,0:T(8,128)(2,1)S(1)}, bf16[2,256,1024]{2,1,0:T(8,128)(2,1)S(1)}, u32[]{:S(2)}, u32[]{:S(2)}) collective-permute-start(bf16[2,256,1024]{2,1,0:T(8,128)(2,1)S(1)} %get-tuple-element.139), channel_id=1, source_target_pairs={{0,1},{3,2},{4,5},{7,6},{8,9},{11,10},{12,13},{15,14},{16,17},{19,... | collective-permute-start | bytes 3145736 | tf_op jit(solution)/shard_map/ppermute | solution.py:534
  911.5 50.9 %collective-permute-start.93 = (bf16[256,1024]{1,0:T(8,128)(2,1)S(1)}, bf16[256,1024]{1,0:T(8,128)(2,1)S(1)}, u32[]{:S(2)}, u32[]{:S(2)}) collective-permute-start(bf16[256,1024]{1,0:T(8,128)(2,1)S(1)} %get-tuple-element.280), channel_id=1, source_target_pairs={{0,24},{8,16},{16,8},{24,0},{1,25},{9,17},{17,9},{25,1},{2,26},{10... | collective-permute-start | bytes 1572872 | tf_op jit(solution)/shard_map/ppermute | solution.py:346
  913.0 49.4 %collective-permute-start.91 = (bf16[256,1024]{1,0:T(8,128)(2,1)S(1)}, bf16[256,1024]{1,0:T(8,128)(2,1)S(1)}, u32[]{:S(2)}, u32[]{:S(2)}) collective-permute-start(bf16[256,1024]{1,0:T(8,128)(2,1)S(1)} %get-tuple-element.279), channel_id=1, source_target_pairs={{0,8},{8,0},{16,24},{24,16},{1,9},{9,1},{17,25},{25,17},{2,10},{10... | collective-permute-start | bytes 1572872 | tf_op jit(solution)/shard_map/ppermute | solution.py:346
  936.8 31.0 %collective-permute-start.92 = (bf16[256,1024]{1,0:T(8,128)(2,1)S(1)}, bf16[256,1024]{1,0:T(8,128)(2,1)S(1)}, u32[]{:S(2)}, u32[]{:S(2)}) collective-permute-start(bf16[256,1024]{1,0:T(8,128)(2,1)S(1)} %get-tuple-element.278), channel_id=1, source_target_pairs={{0,16},{8,24},{16,0},{24,8},{1,17},{9,25},{17,1},{25,9},{2,18},{10... | collective-permute-start | bytes 1572872 | tf_op jit(solution)/shard_map/ppermute | solution.py:346
  937.1 37.1 %collective-permute-start.96 = (bf16[256,1024]{1,0:T(8,128)(2,1)S(1)}, bf16[256,1024]{1,0:T(8,128)(2,1)S(1)}, u32[]{:S(2)}, u32[]{:S(2)}) collective-permute-start(bf16[256,1024]{1,0:T(8,128)(2,1)S(1)} %get-tuple-element.276), channel_id=1, source_target_pairs={{0,24},{8,16},{16,8},{24,0},{1,25},{9,17},{17,9},{25,1},{2,26},{10... | collective-permute-start | bytes 1572872 | tf_op jit(solution)/shard_map/ppermute | solution.py:346
  (161 other events, 3055.1 us)
Sparse Core Ops, SparseCore 0:
  9.5 13.2 all-gather.3
  24.4 17.1 all-gather.5
  415.4 102.2 reduce-scatter.1
  558.8 121.4 all-gather.7

commit v8 on v7

--- a/solution.py
+++ b/solution.py
@@ -420,7 +420,7 @@
     start = lax.axis_index("seq") % 2 * rows
     shards = [lax.dynamic_slice_in_dim(shard, start, rows, 0) for shard in shards]
     own = column_cuts(shards, here, 0)
-    return jnp.stack([own] + [swap(column_cuts(shards, here, k), "p", k) for k in range(1, HEADS)])
+    return [own] + [swap(column_cuts(shards, here, k), "p", k) for k in range(1, HEADS)]
 
 
 def seq_columns(pieces, here):
@@ -523,28 +523,37 @@
     )(spots, *([parts] * spans))
 
 
-def line_sum(chunks):
+def line_pairs(i):
+    count = lax.axis_size("seq")
+    return [(i, i + 1), (count - 1 - i, count - 2 - i)]
+
+
+def inward(value, last):
+    for i in range(lax.axis_size("seq") // 2 - 1):
+        if i in last:
+            value = after(value, last[i])
+        last[i] = lax.ppermute(value, "seq", line_pairs(i))
+        value = value + last[i]
+    return value
+
+
+def across(value, last):
+    half = lax.axis_size("seq") // 2
+    if "across" in last:
+        value = after(value, last["across"])
+    last["across"] = lax.ppermute(value, "seq", [(half - 1, half), (half, half - 1)])
+    return value + last["across"]
+
+
+def outward(value, last):
     count, spot = lax.axis_size("seq"), lax.axis_index("seq")
-    half = count // 2
-    totals, last = [], {}
-
-    def send(value, key, pairs):
-        if key in last:
-            value = after(value, last[key])
-        last[key] = lax.ppermute(value, "seq", pairs)
-        return value, last[key]
-
-    for value in chunks:
-        for i in range(half - 1):
-            value, got = send(value, ("in", i), [(i, i + 1), (count - 1 - i, count - 2 - i)])
-            value = value + got
-        value, got = send(value, "across", [(half - 1, half), (half, half - 1)])
-        value = value + got
-        for i in range(half - 2, -1, -1):
-            value, got = send(value, ("out", i), [(i + 1, i), (count - 2 - i, count - 1 - i)])
-            value = jnp.where((spot == i) | (spot == count - 1 - i), got, value)
-        totals.append(value)
-    return totals
+    for i in range(count // 2 - 2, -1, -1):
+        if ("out", i) in last:
+            value = after(value, last["out", i])
+        got = lax.ppermute(value, "seq", [(b, a) for a, b in line_pairs(i)])
+        last["out", i] = got
+        value = jnp.where((spot == i) | (spot == count - 1 - i), got, value)
+    return value
 
 
 def spread_line(near, far, here):
@@ -613,7 +622,7 @@
     late = lax.optimization_barrier((query_proj, swish_proj, mlp_gate, mlp_up) + tuple(kv_pieces))
     weight_qs, qs_pieces = head_columns(late[:2], here)
     gu_pieces = seq_pieces(late[2:4], here)
-    grad_blocks = gather_heads(after(grad_out, *qs_pieces))
+    grad_all = lax.all_gather(after(grad_out, *qs_pieces), "p", axis=0, tiled=False)
     weight_out = lax.all_gather(out_proj, "r", axis=0, tiled=True)
     weight_down = lax.all_gather(mlp_down, "r", axis=0, tiled=True)
 
@@ -628,12 +637,15 @@
     state, decay = chunk_states(kv, li)
     decay = decay[:, :, :1]
     init = chain_pair(state, decay, True)
-    init, gu_pieces = lax.optimization_barrier((init, gu_pieces))
-    weight_gu = seq_columns(gu_pieces, here)
+    *gu_pieces, _ = lax.optimization_barrier((*gu_pieces, init))
+    weight_gu = seq_columns(jnp.stack(gu_pieces), here)
     qs = mm(normed, weight_qs).reshape(HEADS, rows, 2 * HEAD)
     gated, mixer_out, probs, mix = mixer_forward(qs, kv, li, init, gain_head8)
     gated = gated.reshape(group, HEAD)
     attn_part = mm(gated, weight_out).astype(BF).reshape(HEADS, rows, D)
+    grad_blocks = [
+        lax.dynamic_index_in_dim(grad_all, here ^ k, 0, False) for k in range(HEADS)
+    ]
     grad_mlp = (mask_all * jnp.concatenate(grad_blocks).astype(F32)).astype(BF)
     attn_out, grad_act = scatter_heads(
         [attn_part[k] for k in range(HEADS)], mm_nt(grad_mlp, weight_down)
@@ -644,7 +656,8 @@
     scale_two = inverse_rms(residual)
     hat_two = residual * scale_two
     normed_two_own = (hat_two * gain_two).astype(BF)
-    normed_two = jnp.concatenate(gather_heads(normed_two_own))
+    weight_gu, *two_blocks = lax.optimization_barrier((weight_gu, *gather_heads(normed_two_own)))
+    normed_two = jnp.concatenate(two_blocks)
 
     hidden_width = weight_down.shape[0]
     gate_up = mm(normed_two, weight_gu)
@@ -684,6 +697,8 @@
     mlp_part = mm(hidden, weight_down).astype(BF)
     mlp_part, gu_part, *attn_blocks = lax.optimization_barrier((mlp_part, gu_part, *attn_blocks))
     gu_part = swap_diagonal(gu_part)
+    half_rows, line = down_rows // 2, {}
+    down_near = inward(after(down_total[:half_rows], *attn_blocks), line)
     grad_attn = jnp.concatenate(attn_blocks)
     mlp_part = mlp_part.reshape(HEADS, rows, D)
     mlp_out = scatter_heads([mlp_part[k] for k in range(HEADS)])
@@ -692,7 +707,7 @@
     grad_qs, grad_kv, grad_li, adjoint, slot_part = mixer_backward(
         qs, kv, li, init, gain_head8, mixer_out, probs, mix, grad_gated
     )
-    adjoint, gu_part = lax.optimization_barrier((adjoint, gu_part))
+    adjoint, gu_part, down_near = lax.optimization_barrier((adjoint, gu_part, down_near))
     gu_whole = lax.all_gather(gu_part, "seq", axis=0, tiled=True)
     one_view = normed.reshape(group, HEADS, copies, shard)
     one_views = [split_rows(one_view, turn, m, order) for m in range(copies)]
@@ -708,10 +723,12 @@
     out_total = weight_grad(out_views, grad_attn)
     qs_total = weight_grad(one_views, grad_qs)
     ends = chain_pair(adjoint, decay, False)
-    ends, mlp_out, out_total, qs_total = lax.optimization_barrier(
-        (ends, mlp_out, out_total, qs_total)
+    ends, mlp_out, out_total, qs_total, down_near, gu_whole = lax.optimization_barrier(
+        (ends, mlp_out, out_total, qs_total, down_near, gu_whole)
     )
     result = (residual + mask_own * mlp_out).astype(BF)
+    down_near = across(down_near, line)
+    grad_qs = after(grad_qs, down_near)
     grad_kv, grad_li = mixer_finish(kv, li, init, ends, grad_kv, grad_li)
     grad_kv = grad_kv.reshape(group, 2 * HEAD)
     grad_li = grad_li.reshape(group, 2 * SLOTS)
@@ -763,17 +780,18 @@
 
     qs_total = qs_total.reshape(HEADS, shard, 2 * HEAD)
     kv_total = kv_total.reshape(HEADS, shard, 2 * HEAD)
-    half_rows = down_rows // 2
-    first = after(down_total[:half_rows], gu_whole, one_part)
-    chunks = [first, down_total[half_rows:]]
-    chunks += [qs_total[1::2], qs_total[0::2], kv_total[1::2], kv_total[0::2]]
-    near, far, *wide, last = line_sum(chunks + [jnp.concatenate([out_total, flat])])
+    chunks = [down_total[half_rows:], qs_total[1::2], qs_total[0::2], out_total]
+    chunks += [kv_total[1::2], kv_total[0::2], flat]
+    summed = [outward(down_near, line)]
+    for chunk in chunks:
+        summed.append(outward(across(inward(chunk, line), line), line))
+    near, far, *wide, out_grad, kv_near, kv_far, flat = summed
     down_grad = jnp.concatenate([near, far])
     gate_grad, up_grad = assemble(gu_whole[None], order, 2)
     query_grad, swish_grad = spread_line(wide[0], wide[1], here)
-    key_grad, value_grad = spread_line(wide[2], wide[3], here)
-    out_grad = last[:shard].astype(F32)
-    flat = last[shard:].reshape(-1).astype(F32)
+    key_grad, value_grad = spread_line(kv_near, kv_far, here)
+    out_grad = out_grad.astype(F32)
+    flat = flat.reshape(-1).astype(F32)
     totals, offset = [], 0
     for a in sums:
         size = a.size // owners

time: 999 us -> 1070 us (1.071)
  starting transfers between devices: 145 us -> 208 us
    ppermute x21 -> x24, starting transfers between devices: 69.3 us -> 112 us  [the longest x8 92.5 us: inward(): last[i] = lax.ppermute(value, 'seq', line_pairs(i))]
    ppermute x63 -> x60, waiting for transfers between devices: 264 us -> 304 us  [swap(): return lax.ppermute(value, axis, [(i, i ^ step) for i in range(count)])]
    ppermute x12, waiting for transfers between devices: 62.1 us -> 22.2 us  [chain(): total = total + lax.ppermute(sent, 'seq', [pair]).astype(F32)]
    ppermute x1, starting transfers between devices: 2.19 us -> 13 us  [swap_diagonal(): return lax.ppermute(part, ('p', 'seq'), sends)]
    ppermute x63 -> x60, starting transfers between devices: 60.2 us -> 70.2 us  [swap(): return lax.ppermute(value, axis, [(i, i ^ step) for i in range(count)])]
    add x14 -> x16, other arithmetic: 18.1 us -> 25 us  [the longest x8 13.9 us: inward(): value = value + last[i]]
    ppermute x21 -> x24, waiting for transfers between devices: 73 us -> 76.2 us  [the longest x8 39.3 us: inward(): last[i] = lax.ppermute(value, 'seq', line_pairs(i))]
  transfers between devices with their start and end apart: 101 -> 102, of which waited for: 28 -> 36; matrix products, arithmetic and copies ran while one was open for 27% -> 25% of each run, Pallas kernels for 8% -> 7%
where the time goes in v8:
time: 1070 us; the launch traced here: 1050 us
  waiting for transfers between devices  404 us (38%)
  starting transfers between devices  208 us (19%)
  matrix products  165 us (15%)
  other arithmetic  93.5 us (9%)
  Pallas kernels  92.2 us (9%)
  local copies, waits for them, and re-layouts  74.5 us (7%)
  between operations  17.1 us (2%)
    ppermute x60, waiting for transfers between devices, swap(): return lax.ppermute(value, axis, [(i, i ^ step) for i in range(count)])  304 us
    ppermute x8, starting transfers between devices, inward(): last[i] = lax.ppermute(value, 'seq', line_pairs(i))  92.5 us
    ppermute x60, starting transfers between devices, swap(): return lax.ppermute(value, axis, [(i, i ^ step) for i in range(count)])  70.2 us
    dot_general x6, matrix products, mm_nt(): lax.dot_general(a, b, (((1,), (1,)), ((), ())), preferred_element_type=F32)  61.9 us
    dot_general x11, matrix products, mm_tn(): lax.dot_general(a, b, (((0,), (0,)), ((), ())), preferred_element_type=F32)  58 us
    pallas_call x4, Pallas kernels, run(): pl.pallas_call(kernel, grid=(args[0].shape[0],), in_specs=specs, out_spec...  49.4 us
    dot_general x6, matrix products, mm(): lax.dot_general(a, b, (((1,), (0,)), ((), ())), preferred_element_type=F32)  42.9 us
    ppermute x8, waiting for transfers between devices, inward(): last[i] = lax.ppermute(value, 'seq', line_pairs(i))  39.3 us
  transfers between devices with their start and end apart: 102, of which 36 were waited for; matrix products, arithmetic and copies ran while one was open for 25% of the time, Pallas kernels for 7%

profile of v8, /device:TPU:0, one launch (start us, length us, event | category | flops | bytes accessed | tf_op | source)
XLA Modules:
  0.0 1053.6 jit_solution(18135399613191021202)
XLA Ops:
  15.5 10.9 %collective-permute-done.7 = bf16[256,1024]{1,0:T(8,128)(2,1)S(1)} collective-permute-done((bf16[256,1024]{1,0:T(8,128)(2,1)S(1)}, bf16[256,1024]{1,0:T(8,128)(2,1)S(1)}, u32[]{:S(2)}, u32[]{:S(2)}) %collective-permute-start.7) | collective-permute-done | bytes 524320 | tf_op jit(solution)/shard_map/ppermute | solution.py:346
  26.4 12.0 %collective-permute-done.8 = bf16[256,1024]{1,0:T(8,128)(2,1)S(1)} collective-permute-done((bf16[256,1024]{1,0:T(8,128)(2,1)S(1)}, bf16[256,1024]{1,0:T(8,128)(2,1)S(1)}, u32[]{:S(2)}, u32[]{:S(2)}) %collective-permute-start.8) | collective-permute-done | bytes 524320 | tf_op jit(solution)/shard_map/ppermute | solution.py:346
  43.2 11.0 %collective-permute-done.11 = bf16[256,1024]{1,0:T(8,128)(2,1)S(1)} collective-permute-done((bf16[256,1024]{1,0:T(8,128)(2,1)S(1)}, bf16[256,1024]{1,0:T(8,128)(2,1)S(1)}, u32[]{:S(2)}, u32[]{:S(2)}) %collective-permute-start.11) | collective-permute-done | bytes 524320 | tf_op jit(solution)/shard_map/ppermute | solution.py:346
  54.3 8.2 collective-permute-done.13
  75.1 25.9 %collective-permute-done.1 = f32[2,5409]{1,0:T(2,128)S(1)} collective-permute-done((f32[2,5409]{1,0:T(2,128)S(1)}, f32[2,5409]{1,0:T(2,128)S(1)}, u32[]{:S(2)}, u32[]{:S(2)}) %collective-permute-start.1) | collective-permute-done | bytes 43304 | tf_op jit(solution)/shard_map/ppermute | solution.py:346
  103.5 25.4 %collective-permute-done.2 = f32[2,5409]{1,0:T(2,128)S(1)} collective-permute-done((f32[2,5409]{1,0:T(2,128)S(1)}, f32[2,5409]{1,0:T(2,128)S(1)}, u32[]{:S(2)}, u32[]{:S(2)}) %collective-permute-start.2) | collective-permute-done | bytes 43304 | tf_op jit(solution)/shard_map/ppermute | solution.py:346
  205.3 15.4 %collective-permute-done.31 = bf16[128,2816]{1,0:T(8,128)(2,1)} collective-permute-done((bf16[128,2816]{1,0:T(8,128)(2,1)S(1)}, bf16[128,2816]{1,0:T(8,128)(2,1)}, u32[]{:S(2)}, u32[]{:S(2)}) %collective-permute-start.31) | collective-permute-done | bytes 720928 | tf_op jit(solution)/shard_map/ppermute | solution.py:346
  223.6 9.2 collective-permute-start.34
  232.7 6.0 fusion.81
  239.3 14.9 %shard_map.291 = (bf16[4,256,512]{2,1,0:T(8,128)(2,1)}, f32[4,256,512]{2,1,0:T(8,128)}, f32[4,256,64]{2,1,0:T(8,128)}, bf16[4,256,256]{2,1,0:T(8,128)(2,1)}) custom-call(f32[4,256,1024]{2,1,0:T(8,128)} %bitcast.211, bf16[4,256,1024]{2,1,0:T(8,128)(2,1)} %bitcast.214, f32[4,256,128]{2,1,0:T(8,128)} %bitcast.189, f32[4,64,1024]{2,1,0:T(8,128)} %pad_maximum_fusion.5.init_ref, ...), custom_call_target="tpu_custom_call" | custom-call | flops 12000000000 | bytes 16000000 | tf_op jit(solution)/shard_map/pallas_call | solution.py:258
  265.8 25.5 %collective-permute-done.34.refs_2_ = bf16[4,128,2816]{2,1,0:T(8,128)(2,1)} collective-permute-done((bf16[4,128,2816]{2,1,0:T(8,128)(2,1)}, bf16[4,128,2816]{2,1,0:T(8,128)(2,1)}, u32[]{:S(2)}, u32[]{:S(2)}) %collective-permute-start.34) | collective-permute-done | bytes 2883616 | tf_op jit(solution)/shard_map/ppermute | solution.py:346
  295.2 14.2 %fusion.65 = f32[1024,1408]{1,0:T(8,128)} fusion(bf16[1408,2048]{1,0:T(8,128)(2,1)} %all-gather.8.cloned.1.call-done, bf16[256,2048]{1,0:T(8,128)(2,1)S(1)} %get-tuple-element.277, bf16[256,2048]{1,0:T(8,128)(2,1)} %get-tuple-element.278, bf16[256,2048]{1,0:T(8,128)(2,1)} %get-tuple-element.279, bf16[256,2048]{1,0:T(8,128)(2,1)S(1)} %get-tuple-element.276, ...), kind=kOutput, calls=%fused_computation.244 | convolution fusion | flops 5926551552 | bytes 15732736 | tf_op jit(solution)/shard_map/dot_general | solution.py:23
  320.3 13.5 %shard_map.292 = bf16[2048,2816]{1,0:T(8,128)(2,1)} custom-call(s32[16]{0:T(128)} %stack.176.spot_ref, bf16[4,128,2816]{2,1,0:T(8,128)(2,1)} %pad_maximum_fusion.2.refs_0_, bf16[4,128,2816]{2,1,0:T(8,128)(2,1)} %collective-permute-done.33.refs_1_, bf16[4,128,2816]{2,1,0:T(8,128)(2,1)} %collective-permute-done.34.refs_2_, ...), custom_call_target="tpu_custom_call" | custom-call | bytes 23068672 | tf_op jit(solution)/shard_map/pallas_call | solution.py:382
  333.8 8.5 collective-permute-done.36
  342.3 20.0 %collective-permute-done.37 = bf16[256,2048]{1,0:T(8,128)(2,1)} collective-permute-done((bf16[256,2048]{1,0:T(8,128)(2,1)S(1)}, bf16[256,2048]{1,0:T(8,128)(2,1)}, u32[]{:S(2)}, u32[]{:S(2)}) %collective-permute-start.37) | collective-permute-done | bytes 1048608 | tf_op jit(solution)/shard_map/ppermute | solution.py:346
  367.6 17.6 %fusion.83 = f32[1024,2816]{1,0:T(8,128)} fusion(bf16[1024,2048]{1,0:T(8,128)(2,1)S(1)} %constant_dynamic-update-slice_fusion, bf16[2048,2816]{1,0:T(8,128)(2,1)} %shard_map.292), kind=kOutput, calls=%fused_computation.262 | convolution fusion | flops 11811160064 | bytes 27262976 | tf_op jit(solution)/shard_map/dot_general | solution.py:19
  385.2 7.1 multiply_convert_fusion.2
  392.9 8.8 convolution_convert_fusion
  402.0 16.6 %convolution_convert_fusion.1 = bf16[1024,2048]{1,0:T(8,128)(2,1)} fusion(bf16[1024,2816]{1,0:T(8,128)(2,1)S(1)} %pad_maximum_fusion, bf16[2048,2816]{1,0:T(8,128)(2,1)} %shard_map.292), kind=kOutput, calls=%fused_computation.20 | convolution fusion | flops 11813257216 | bytes 21495808 | tf_op jit(solution)/shard_map/dot_general | solution.py:23
  418.6 10.4 add_convert_fusion
  430.2 7.7 convolution_convert_fusion.4
  444.5 5.9 add_convert_fusion.2
  450.5 16.6 %collective-permute-done.40 = bf16[256,2048]{1,0:T(8,128)(2,1)S(1)} collective-permute-done((bf16[256,2048]{1,0:T(8,128)(2,1)S(1)}, bf16[256,2048]{1,0:T(8,128)(2,1)S(1)}, u32[]{:S(2)}, u32[]{:S(2)}) %collective-permute-start.40) | collective-permute-done | bytes 1048608 | tf_op jit(solution)/shard_map/ppermute | solution.py:346
  467.0 21.3 %collective-permute-done.41 = bf16[256,2048]{1,0:T(8,128)(2,1)S(1)} collective-permute-done((bf16[256,2048]{1,0:T(8,128)(2,1)S(1)}, bf16[256,2048]{1,0:T(8,128)(2,1)S(1)}, u32[]{:S(2)}, u32[]{:S(2)}) %collective-permute-start.41) | collective-permute-done | bytes 1048608 | tf_op jit(solution)/shard_map/ppermute | solution.py:346
  496.6 8.3 convolution_convert_fusion.2
  506.8 12.3 %collective-permute-done.44 = bf16[256,2048]{1,0:T(8,128)(2,1)S(1)} collective-permute-done((bf16[256,2048]{1,0:T(8,128)(2,1)S(1)}, bf16[256,2048]{1,0:T(8,128)(2,1)S(1)}, u32[]{:S(2)}, u32[]{:S(2)}) %collective-permute-start.44) | collective-permute-done | bytes 1048608 | tf_op jit(solution)/shard_map/ppermute | solution.py:346
  519.2 21.4 %collective-permute-done.45 = bf16[256,2048]{1,0:T(8,128)(2,1)S(1)} collective-permute-done((bf16[256,2048]{1,0:T(8,128)(2,1)S(1)}, bf16[256,2048]{1,0:T(8,128)(2,1)S(1)}, u32[]{:S(2)}, u32[]{:S(2)}) %collective-permute-start.45) | collective-permute-done | bytes 1048608 | tf_op jit(solution)/shard_map/ppermute | solution.py:346
  541.7 13.0 %collective-permute-start.47 = (bf16[1,256,2816]{2,1,0:T(8,128)(2,1)}, bf16[1,256,2816]{2,1,0:T(8,128)(2,1)}, u32[]{:S(2)}, u32[]{:S(2)}) collective-permute-start(bf16[1,256,2816]{2,1,0:T(8,128)(2,1)} %reduce-scatter.2.cloned.1.call-done), channel_id=1, source_target_pairs={{0,0},{1,9},{2,18},{3,27},{8,8},{9,1},{10,26},{11,19},{16,16},{17,... | collective-permute-start | bytes 4325384 | tf_op jit(solution)/shard_map/ppermute | solution.py:567
  562.5 19.9 %shard_map.293 = (bf16[4,256,1024]{2,1,0:T(8,128)(2,1)}, f32[4,256,1024]{2,1,0:T(8,128)}, f32[4,256,128]{2,1,0:T(8,128)}, f32[4,64,1024]{2,1,0:T(8,128)}, f32[8,512]{1,0:T(8,128)}) custom-call(f32[4,256,1024]{2,1,0:T(8,128)} %bitcast.212, bf16[4,256,1024]{2,1,0:T(8,128)(2,1)} %bitcast.215, f32[4,256,128]{2,1,0:T(8,128)} %bitcast.190, ...), custom_call_target="tpu_custom_call" | custom-call | flops 24000000000 | bytes 20000000 | tf_op jit(solution)/shard_map/pallas_call | solution.py:258
  612.2 13.1 %collective-permute-done.57 = bf16[256,2048]{1,0:T(8,128)(2,1)} collective-permute-done((bf16[256,2048]{1,0:T(8,128)(2,1)}, bf16[256,2048]{1,0:T(8,128)(2,1)}, u32[]{:S(2)}, u32[]{:S(2)}) %collective-permute-start.57) | collective-permute-done | bytes 1048608 | tf_op jit(solution)/shard_map/ppermute | solution.py:346
  626.1 18.2 %collective-permute-done.56 = bf16[256,2048]{1,0:T(8,128)(2,1)} collective-permute-done((bf16[256,2048]{1,0:T(8,128)(2,1)}, bf16[256,2048]{1,0:T(8,128)(2,1)}, u32[]{:S(2)}, u32[]{:S(2)}) %collective-permute-start.56) | collective-permute-done | bytes 1048608 | tf_op jit(solution)/shard_map/ppermute | solution.py:346
  652.6 28.2 %collective-permute-start.69 = (bf16[352,2048]{1,0:T(8,128)(2,1)S(1)}, bf16[352,2048]{1,0:T(8,128)(2,1)S(1)}, u32[]{:S(2)}, u32[]{:S(2)}) collective-permute-start(bf16[352,2048]{1,0:T(8,128)(2,1)S(1)} %copy-done.10), channel_id=1, source_target_pairs={{0,1},{3,2},{4,5},{7,6},{8,9},{11,10},{12,13},{15,14},{16,17},{19,... | collective-permute-start | bytes 4325384 | tf_op jit(solution)/shard_map/ppermute | solution.py:535
  689.2 6.7 collective-permute-done.51
  696.0 7.7 collective-permute-done.54
  704.9 16.6 %collective-permute-done.69 = bf16[352,2048]{1,0:T(8,128)(2,1)S(1)} collective-permute-done((bf16[352,2048]{1,0:T(8,128)(2,1)S(1)}, bf16[352,2048]{1,0:T(8,128)(2,1)S(1)}, u32[]{:S(2)}, u32[]{:S(2)}) %collective-permute-start.69) | collective-permute-done | bytes 1441824 | tf_op jit(solution)/shard_map/ppermute | solution.py:535
  723.4 9.1 shard_map.294
  750.2 19.4 %collective-permute-start.70 = (bf16[2,256,1024]{2,1,0:T(8,128)(2,1)}, bf16[2,256,1024]{2,1,0:T(8,128)(2,1)}, u32[]{:S(2)}, u32[]{:S(2)}) collective-permute-start(bf16[2,256,1024]{2,1,0:T(8,128)(2,1)} %get-tuple-element.161), channel_id=1, source_target_pairs={{0,1},{3,2},{4,5},{7,6},{8,9},{11,10},{12,13},{15,14},{16,17},{19,... | collective-permute-start | bytes 3145736 | tf_op jit(solution)/shard_map/ppermute | solution.py:535
  774.3 8.5 shard_map.297
  782.9 10.7 %fusion.85 = f32[1024,2048]{1,0:T(8,128)} fusion(bf16[1024,1024]{1,0:T(8,128)(2,1)} %bitcast.220, bf16[2048,1024]{1,0:T(8,128)(2,1)} %shard_map.289), kind=kOutput, calls=%fused_computation.264 | convolution fusion | flops 4294967296 | bytes 14680064 | tf_op jit(solution)/shard_map/dot_general | solution.py:23
  803.0 12.2 %add_convert_fusion.1 = bf16[1024,2048]{1,0:T(8,128)(2,1)} fusion(f32[1024,2048]{1,0:T(8,128)S(1)} %bitcast.167, f32[1024,2048]{1,0:T(8,128)} %fusion.85, bf16[1024,1024]{1,0:T(8,128)(2,1)} %bitcast.217, bf16[2048,1024]{1,0:T(8,128)(2,1)} %shard_map.288), kind=kOutput, calls=%fused_computation.7 | convolution fusion | flops 4301258752 | bytes 27262976 | tf_op jit(solution)/shard_map/dot_general | solution.py:23
  832.8 10.9 %collective-permute-done.61 = bf16[256,2048]{1,0:T(8,128)(2,1)S(1)} collective-permute-done((bf16[256,2048]{1,0:T(8,128)(2,1)S(1)}, bf16[256,2048]{1,0:T(8,128)(2,1)S(1)}, u32[]{:S(2)}, u32[]{:S(2)}) %collective-permute-start.61) | collective-permute-done | bytes 1048608 | tf_op jit(solution)/shard_map/ppermute | solution.py:346
  843.7 7.1 collective-permute-start.72
  850.8 15.8 %collective-permute-done.62 = bf16[256,2048]{1,0:T(8,128)(2,1)S(1)} collective-permute-done((bf16[256,2048]{1,0:T(8,128)(2,1)S(1)}, bf16[256,2048]{1,0:T(8,128)(2,1)S(1)}, u32[]{:S(2)}, u32[]{:S(2)}) %collective-permute-start.62) | collective-permute-done | bytes 1048608 | tf_op jit(solution)/shard_map/ppermute | solution.py:346
  884.2 24.1 %collective-permute-start.73 = (bf16[2,256,1024]{2,1,0:T(8,128)(2,1)S(1)}, bf16[2,256,1024]{2,1,0:T(8,128)(2,1)S(1)}, u32[]{:S(2)}, u32[]{:S(2)}) collective-permute-start(bf16[2,256,1024]{2,1,0:T(8,128)(2,1)S(1)} %get-tuple-element.164), channel_id=1, source_target_pairs={{0,1},{3,2},{4,5},{7,6},{8,9},{11,10},{12,13},{15,14},{16,17},{19,... | collective-permute-start | bytes 3145736 | tf_op jit(solution)/shard_map/ppermute | solution.py:535
  914.6 13.2 %collective-permute-done.73 = bf16[2,256,1024]{2,1,0:T(8,128)(2,1)S(1)} collective-permute-done((bf16[2,256,1024]{2,1,0:T(8,128)(2,1)S(1)}, bf16[2,256,1024]{2,1,0:T(8,128)(2,1)S(1)}, u32[]{:S(2)}, u32[]{:S(2)}) %collective-permute-start.73) | collective-permute-done | bytes 1048608 | tf_op jit(solution)/shard_map/ppermute | solution.py:535
  969.7 13.4 %collective-permute-done.87 = bf16[256,2048]{1,0:T(8,128)(2,1)S(1)} collective-permute-done((bf16[256,2048]{1,0:T(8,128)(2,1)S(1)}, bf16[256,2048]{1,0:T(8,128)(2,1)S(1)}, u32[]{:S(2)}, u32[]{:S(2)}) %collective-permute-start.87) | collective-permute-done | bytes 1048608 | tf_op jit(solution)/shard_map/ppermute | solution.py:553
  997.4 9.7 collective-permute-done.88
  1016.4 11.5 %collective-permute-done.89 = bf16[2,256,1024]{2,1,0:T(8,128)(2,1)S(1)} collective-permute-done((bf16[2,256,1024]{2,1,0:T(8,128)(2,1)S(1)}, bf16[2,256,1024]{2,1,0:T(8,128)(2,1)S(1)}, u32[]{:S(2)}, u32[]{:S(2)}) %collective-permute-start.89) | collective-permute-done | bytes 1048608 | tf_op jit(solution)/shard_map/ppermute | solution.py:553
  (616 shorter events, 373.3 us)
Async XLA Ops:
  7.2 247.1 %all-gather.6.cloned.1.call-start = ((), (), s32[]{:S(2)}) async-start(), calls=%async_computation.1 | async-start | bytes 3145728 | tf_op jit(solution)/shard_map/all_gather | solution.py:626
  7.9 283.3 %all-gather.12.cloned.1.call-start = ((), (), s32[]{:S(2)}) async-start(), calls=%async_computation.5 | async-start | bytes 5242880 | tf_op jit(solution)/shard_map/all_gather | solution.py:625
  65.0 230.2 %all-gather.8.cloned.1.call-start = ((), (), s32[]{:S(2)}) async-start(), calls=%async_computation.2 | async-start | bytes 8650752 | tf_op jit(solution)/shard_map/all_gather | solution.py:627
  65.0 76.3 %collective-permute-start.6 = (bf16[256,2048]{1,0:T(8,128)(2,1)S(1)}, bf16[256,2048]{1,0:T(8,128)(2,1)S(1)}, u32[]{:S(2)}, u32[]{:S(2)}) collective-permute-start(bf16[256,2048]{1,0:T(8,128)(2,1)S(1)} %copy-done.3), channel_id=1, source_target_pairs={{0,24},{8,16},{16,8},{24,0},{1,25},{9,17},{17,9},{25,1},{2,26},{10... | collective-permute-start | bytes 3145736 | tf_op jit(solution)/shard_map/ppermute | solution.py:346
  67.0 74.3 %collective-permute-start.5 = (bf16[256,2048]{1,0:T(8,128)(2,1)S(1)}, bf16[256,2048]{1,0:T(8,128)(2,1)}, u32[]{:S(2)}, u32[]{:S(2)}) collective-permute-start(bf16[256,2048]{1,0:T(8,128)(2,1)S(1)} %copy-done.3), channel_id=1, source_target_pairs={{0,16},{8,24},{16,0},{24,8},{1,17},{9,25},{17,1},{25,9},{2,18},{10... | collective-permute-start | bytes 3145736 | tf_op jit(solution)/shard_map/ppermute | solution.py:346
  68.5 473.1 %reduce-scatter.2.cloned.1.call-start = ((), (), s32[]{:S(2)}) async-start(), calls=%async_computation.3 | async-start | bytes 7208960 | tf_op jit(solution)/shard_map/reduce_scatter | solution.py:678
  70.9 30.0 %collective-permute-start.1 = (f32[2,5409]{1,0:T(2,128)S(1)}, f32[2,5409]{1,0:T(2,128)S(1)}, u32[]{:S(2)}, u32[]{:S(2)}) collective-permute-start(f32[2,5409]{1,0:T(2,128)S(1)} %pad_maximum_fusion.28), channel_id=1, source_target_pairs={{0,8},{8,0},{16,24},{24,16},{1,9},{9,1},{17,25},{25,17},{2,10},{10... | collective-permute-start | bytes 129824 | tf_op jit(solution)/shard_map/ppermute | solution.py:346
  72.2 56.6 %collective-permute-start.2 = (f32[2,5409]{1,0:T(2,128)S(1)}, f32[2,5409]{1,0:T(2,128)S(1)}, u32[]{:S(2)}, u32[]{:S(2)}) collective-permute-start(f32[2,5409]{1,0:T(2,128)S(1)} %pad_maximum_fusion.28), channel_id=1, source_target_pairs={{0,16},{8,24},{16,0},{24,8},{1,17},{9,25},{17,1},{25,9},{2,18},{10... | collective-permute-start | bytes 129824 | tf_op jit(solution)/shard_map/ppermute | solution.py:346
  73.0 55.8 %collective-permute-start.3 = (f32[2,5409]{1,0:T(2,128)S(1)}, f32[2,5409]{1,0:T(2,128)S(1)}, u32[]{:S(2)}, u32[]{:S(2)}) collective-permute-start(f32[2,5409]{1,0:T(2,128)S(1)} %pad_maximum_fusion.28), channel_id=1, source_target_pairs={{0,24},{8,16},{16,8},{24,0},{1,25},{9,17},{17,9},{25,1},{2,26},{10... | collective-permute-start | bytes 129824 | tf_op jit(solution)/shard_map/ppermute | solution.py:346
  101.0 40.8 %collective-permute-start.4 = (bf16[256,2048]{1,0:T(8,128)(2,1)S(1)}, bf16[256,2048]{1,0:T(8,128)(2,1)}, u32[]{:S(2)}, u32[]{:S(2)}) collective-permute-start(bf16[256,2048]{1,0:T(8,128)(2,1)S(1)} %copy-done.3), channel_id=1, source_target_pairs={{0,8},{8,0},{16,24},{24,16},{1,9},{9,1},{17,25},{25,17},{2,10},{10... | collective-permute-start | bytes 3145736 | tf_op jit(solution)/shard_map/ppermute | solution.py:346
  135.7 50.8 %collective-permute-start.10 = (bf16[256,1024]{1,0:T(8,128)(2,1)}, bf16[256,1024]{1,0:T(8,128)(2,1)}, u32[]{:S(2)}, u32[]{:S(2)}) collective-permute-start(bf16[256,1024]{1,0:T(8,128)(2,1)} %get-tuple-element.334), channel_id=1, source_target_pairs={{0,4},{4,0},{1,5},{5,1},{2,6},{6,2},{3,7},{7,3},{8,12},{12,8},{9,1... | collective-permute-start | bytes 1572872 | tf_op jit(solution)/shard_map/ppermute | solution.py:346
  186.5 34.2 %collective-permute-start.31 = (bf16[128,2816]{1,0:T(8,128)(2,1)S(1)}, bf16[128,2816]{1,0:T(8,128)(2,1)}, u32[]{:S(2)}, u32[]{:S(2)}) collective-permute-start(bf16[128,2816]{1,0:T(8,128)(2,1)S(1)} %pad_maximum_fusion.9), channel_id=1, source_target_pairs={{0,16},{8,24},{16,0},{24,8},{1,17},{9,25},{17,1},{25,9},{2,18},{10... | collective-permute-start | bytes 2162696 | tf_op jit(solution)/shard_map/ppermute | solution.py:346
  188.6 32.1 %collective-permute-start.32 = (bf16[128,2816]{1,0:T(8,128)(2,1)S(1)}, bf16[128,2816]{1,0:T(8,128)(2,1)}, u32[]{:S(2)}, u32[]{:S(2)}) collective-permute-start(bf16[128,2816]{1,0:T(8,128)(2,1)S(1)} %pad_maximum_fusion.10), channel_id=1, source_target_pairs={{0,24},{8,16},{16,8},{24,0},{1,25},{9,17},{17,9},{25,1},{2,26},{10... | collective-permute-start | bytes 2162696 | tf_op jit(solution)/shard_map/ppermute | solution.py:346
  223.6 67.7 %collective-permute-start.34 = (bf16[4,128,2816]{2,1,0:T(8,128)(2,1)}, bf16[4,128,2816]{2,1,0:T(8,128)(2,1)}, u32[]{:S(2)}, u32[]{:S(2)}) collective-permute-start(bf16[4,128,2816]{2,1,0:T(8,128)(2,1)} %pad_maximum_fusion.2.refs_0_), channel_id=1, source_target_pairs={{0,1},{1,0},{2,3},{3,2},{4,5},{5,4},{6,7},{7,6},{8,9},{9,8},{10,11... | collective-permute-start | bytes 8650760 | tf_op jit(solution)/shard_map/ppermute | solution.py:346
  238.7 81.5 %collective-permute-start.33 = (bf16[4,128,2816]{2,1,0:T(8,128)(2,1)}, bf16[4,128,2816]{2,1,0:T(8,128)(2,1)}, u32[]{:S(2)}, u32[]{:S(2)}) collective-permute-start(bf16[4,128,2816]{2,1,0:T(8,128)(2,1)} %pad_maximum_fusion.2.refs_0_), channel_id=1, source_target_pairs={{0,4},{4,0},{1,5},{5,1},{2,6},{6,2},{3,7},{7,3},{8,12},{12,8},{9,1... | collective-permute-start | bytes 8650760 | tf_op jit(solution)/shard_map/ppermute | solution.py:346
  262.3 47.2 %collective-permute-start.27 = (bf16[256,2048]{1,0:T(8,128)(2,1)}, bf16[256,2048]{1,0:T(8,128)(2,1)}, u32[]{:S(2)}, u32[]{:S(2)}) collective-permute-start(bf16[256,2048]{1,0:T(8,128)(2,1)} %get-tuple-element.282), channel_id=1, source_target_pairs={{0,8},{8,0},{16,24},{24,16},{1,9},{9,1},{17,25},{25,17},{2,10},{10... | collective-permute-start | bytes 3145736 | tf_op jit(solution)/shard_map/ppermute | solution.py:346
  264.0 48.1 %collective-permute-start.28 = (bf16[256,2048]{1,0:T(8,128)(2,1)}, bf16[256,2048]{1,0:T(8,128)(2,1)}, u32[]{:S(2)}, u32[]{:S(2)}) collective-permute-start(bf16[256,2048]{1,0:T(8,128)(2,1)} %get-tuple-element.281), channel_id=1, source_target_pairs={{0,16},{8,24},{16,0},{24,8},{1,17},{9,25},{17,1},{25,9},{2,18},{10... | collective-permute-start | bytes 3145736 | tf_op jit(solution)/shard_map/ppermute | solution.py:346
  264.3 47.8 %collective-permute-start.29 = (bf16[256,2048]{1,0:T(8,128)(2,1)}, bf16[256,2048]{1,0:T(8,128)(2,1)}, u32[]{:S(2)}, u32[]{:S(2)}) collective-permute-start(bf16[256,2048]{1,0:T(8,128)(2,1)} %get-tuple-element.280), channel_id=1, source_target_pairs={{0,24},{8,16},{16,8},{24,0},{1,25},{9,17},{17,9},{25,1},{2,26},{10... | collective-permute-start | bytes 3145736 | tf_op jit(solution)/shard_map/ppermute | solution.py:346
  291.2 29.0 %collective-permute-start.35 = (bf16[4,128,2816]{2,1,0:T(8,128)(2,1)}, bf16[4,128,2816]{2,1,0:T(8,128)(2,1)}, u32[]{:S(2)}, u32[]{:S(2)}) collective-permute-start(bf16[4,128,2816]{2,1,0:T(8,128)(2,1)} %collective-permute-done.34.refs_2_), channel_id=1, source_target_pairs={{0,4},{4,0},{1,5},{5,1},{2,6},{6,2},{3,7},{7,3},{8,12},{12,8},{9,1... | collective-permute-start | bytes 8650760 | tf_op jit(solution)/shard_map/ppermute | solution.py:346
  316.5 45.9 %collective-permute-start.37 = (bf16[256,2048]{1,0:T(8,128)(2,1)S(1)}, bf16[256,2048]{1,0:T(8,128)(2,1)}, u32[]{:S(2)}, u32[]{:S(2)}) collective-permute-start(bf16[256,2048]{1,0:T(8,128)(2,1)S(1)} %multiply_convert_fusion.5), channel_id=1, source_target_pairs={{0,16},{8,24},{16,0},{24,8},{1,17},{9,25},{17,1},{25,9},{2,18},{10... | collective-permute-start | bytes 3145736 | tf_op jit(solution)/shard_map/ppermute | solution.py:346
  317.9 45.5 %collective-permute-start.38 = (bf16[256,2048]{1,0:T(8,128)(2,1)S(1)}, bf16[256,2048]{1,0:T(8,128)(2,1)}, u32[]{:S(2)}, u32[]{:S(2)}) collective-permute-start(bf16[256,2048]{1,0:T(8,128)(2,1)S(1)} %multiply_convert_fusion.5), channel_id=1, source_target_pairs={{0,24},{8,16},{16,8},{24,0},{1,25},{9,17},{17,9},{25,1},{2,26},{10... | collective-permute-start | bytes 3145736 | tf_op jit(solution)/shard_map/ppermute | solution.py:346
  429.0 294.3 %all-gather.10.cloned.1.call-start = ((), (), s32[]{:S(2)}) async-start(), calls=%async_computation.4 | async-start | bytes 7208960 | tf_op jit(solution)/shard_map/all_gather | solution.py:711
  442.2 46.0 %collective-permute-start.41 = (bf16[256,2048]{1,0:T(8,128)(2,1)S(1)}, bf16[256,2048]{1,0:T(8,128)(2,1)S(1)}, u32[]{:S(2)}, u32[]{:S(2)}) collective-permute-start(bf16[256,2048]{1,0:T(8,128)(2,1)S(1)} %get-tuple-element.266), channel_id=1, source_target_pairs={{0,16},{8,24},{16,0},{24,8},{1,17},{9,25},{17,1},{25,9},{2,18},{10... | collective-permute-start | bytes 3145736 | tf_op jit(solution)/shard_map/ppermute | solution.py:346
  443.5 46.1 %collective-permute-start.42 = (bf16[256,2048]{1,0:T(8,128)(2,1)S(1)}, bf16[256,2048]{1,0:T(8,128)(2,1)S(1)}, u32[]{:S(2)}, u32[]{:S(2)}) collective-permute-start(bf16[256,2048]{1,0:T(8,128)(2,1)S(1)} %get-tuple-element.265), channel_id=1, source_target_pairs={{0,24},{8,16},{16,8},{24,0},{1,25},{9,17},{17,9},{25,1},{2,26},{10... | collective-permute-start | bytes 3145736 | tf_op jit(solution)/shard_map/ppermute | solution.py:346
  494.0 46.5 %collective-permute-start.45 = (bf16[256,2048]{1,0:T(8,128)(2,1)S(1)}, bf16[256,2048]{1,0:T(8,128)(2,1)S(1)}, u32[]{:S(2)}, u32[]{:S(2)}) collective-permute-start(bf16[256,2048]{1,0:T(8,128)(2,1)S(1)} %get-tuple-element.132), channel_id=1, source_target_pairs={{0,16},{8,24},{16,0},{24,8},{1,17},{9,25},{17,1},{25,9},{2,18},{10... | collective-permute-start | bytes 3145736 | tf_op jit(solution)/shard_map/ppermute | solution.py:346
  495.4 46.2 %collective-permute-start.46 = (bf16[256,2048]{1,0:T(8,128)(2,1)S(1)}, bf16[256,2048]{1,0:T(8,128)(2,1)}, u32[]{:S(2)}, u32[]{:S(2)}) collective-permute-start(bf16[256,2048]{1,0:T(8,128)(2,1)S(1)} %get-tuple-element.132), channel_id=1, source_target_pairs={{0,24},{8,16},{16,8},{24,0},{1,25},{9,17},{17,9},{25,1},{2,26},{10... | collective-permute-start | bytes 3145736 | tf_op jit(solution)/shard_map/ppermute | solution.py:346
  541.7 46.1 %collective-permute-start.47 = (bf16[1,256,2816]{2,1,0:T(8,128)(2,1)}, bf16[1,256,2816]{2,1,0:T(8,128)(2,1)}, u32[]{:S(2)}, u32[]{:S(2)}) collective-permute-start(bf16[1,256,2816]{2,1,0:T(8,128)(2,1)} %reduce-scatter.2.cloned.1.call-done), channel_id=1, source_target_pairs={{0,0},{1,9},{2,18},{3,27},{8,8},{9,1},{10,26},{11,19},{16,16},{17,... | collective-permute-start | bytes 4325384 | tf_op jit(solution)/shard_map/ppermute | solution.py:567
  557.4 28.6 %collective-permute-start.48 = (bf16[352,2048]{1,0:T(8,128)(2,1)S(1)}, bf16[352,2048]{1,0:T(8,128)(2,1)S(1)}, u32[]{:S(2)}, u32[]{:S(2)}) collective-permute-start(bf16[352,2048]{1,0:T(8,128)(2,1)S(1)} %copy-done.11), channel_id=1, source_target_pairs={{0,1},{3,2},{4,5},{7,6},{8,9},{11,10},{12,13},{15,14},{16,17},{19,... | collective-permute-start | bytes 4325384 | tf_op jit(solution)/shard_map/ppermute | solution.py:535
  600.7 43.6 %collective-permute-start.56 = (bf16[256,2048]{1,0:T(8,128)(2,1)}, bf16[256,2048]{1,0:T(8,128)(2,1)}, u32[]{:S(2)}, u32[]{:S(2)}) collective-permute-start(bf16[256,2048]{1,0:T(8,128)(2,1)} %get-tuple-element.264), channel_id=1, source_target_pairs={{0,16},{8,24},{16,0},{24,8},{1,17},{9,25},{17,1},{25,9},{2,18},{10... | collective-permute-start | bytes 3145736 | tf_op jit(solution)/shard_map/ppermute | solution.py:346
  601.3 43.6 %collective-permute-start.55 = (bf16[256,2048]{1,0:T(8,128)(2,1)}, bf16[256,2048]{1,0:T(8,128)(2,1)}, u32[]{:S(2)}, u32[]{:S(2)}) collective-permute-start(bf16[256,2048]{1,0:T(8,128)(2,1)} %get-tuple-element.262), channel_id=1, source_target_pairs={{0,8},{8,0},{16,24},{24,16},{1,9},{9,1},{17,25},{25,17},{2,10},{10... | collective-permute-start | bytes 3145736 | tf_op jit(solution)/shard_map/ppermute | solution.py:346
  605.5 78.4 %collective-permute-start.59 = (bf16[1024,1024]{1,0:T(8,128)(2,1)}, bf16[1024,1024]{1,0:T(8,128)(2,1)}, u32[]{:S(2)}, u32[]{:S(2)}) collective-permute-start(bf16[1024,1024]{1,0:T(8,128)(2,1)} %convolution_convert_fusion.7), channel_id=1, source_target_pairs={{0,4},{4,0},{1,5},{5,1},{2,6},{6,2},{3,7},{7,3},{8,12},{12,8},{9,1... | collective-permute-start | bytes 6291464 | tf_op jit(solution)/shard_map/ppermute | solution.py:346
  611.5 38.7 %collective-permute-start.58 = (bf16[256,2048]{1,0:T(8,128)(2,1)S(1)}, bf16[256,2048]{1,0:T(8,128)(2,1)S(1)}, u32[]{:S(2)}, u32[]{:S(2)}) collective-permute-start(bf16[256,2048]{1,0:T(8,128)(2,1)S(1)} %convolution_convert_fusion.5), channel_id=1, source_target_pairs={{0,4},{4,0},{1,5},{5,1},{2,6},{6,2},{3,7},{7,3},{8,12},{12,8},{9,1... | collective-permute-start | bytes 3145736 | tf_op jit(solution)/shard_map/ppermute | solution.py:346
  649.4 32.6 %collective-permute-start.53 = (bf16[4,64,512]{2,1,0:T(8,128)(2,1)S(1)}, bf16[4,64,512]{2,1,0:T(8,128)(2,1)S(1)}, u32[]{:S(2)}, u32[]{:S(2)}) collective-permute-start(bf16[4,64,512]{2,1,0:T(8,128)(2,1)S(1)} %get-tuple-element.298), channel_id=1, source_target_pairs={{2,1},{6,5},{10,9},{14,13},{18,17},{22,21},{26,25},{30,29}} | collective-permute-start | bytes 786440 | tf_op jit(solution)/shard_map/ppermute | solution.py:464
  652.6 69.0 %collective-permute-start.69 = (bf16[352,2048]{1,0:T(8,128)(2,1)S(1)}, bf16[352,2048]{1,0:T(8,128)(2,1)S(1)}, u32[]{:S(2)}, u32[]{:S(2)}) collective-permute-start(bf16[352,2048]{1,0:T(8,128)(2,1)S(1)} %copy-done.10), channel_id=1, source_target_pairs={{0,1},{3,2},{4,5},{7,6},{8,9},{11,10},{12,13},{15,14},{16,17},{19,... | collective-permute-start | bytes 4325384 | tf_op jit(solution)/shard_map/ppermute | solution.py:535
  743.1 53.1 %collective-permute-start.60 = (bf16[352,2048]{1,0:T(8,128)(2,1)}, bf16[352,2048]{1,0:T(8,128)(2,1)}, u32[]{:S(2)}, u32[]{:S(2)}) collective-permute-start(bf16[352,2048]{1,0:T(8,128)(2,1)} %add.657), channel_id=1, source_target_pairs={{1,2},{2,1},{5,6},{6,5},{9,10},{10,9},{13,14},{14,13},{17,18},{18,... | collective-permute-start | bytes 4325384 | tf_op jit(solution)/shard_map/ppermute | solution.py:544
  750.2 43.4 %collective-permute-start.70 = (bf16[2,256,1024]{2,1,0:T(8,128)(2,1)}, bf16[2,256,1024]{2,1,0:T(8,128)(2,1)}, u32[]{:S(2)}, u32[]{:S(2)}) collective-permute-start(bf16[2,256,1024]{2,1,0:T(8,128)(2,1)} %get-tuple-element.161), channel_id=1, source_target_pairs={{0,1},{3,2},{4,5},{7,6},{8,9},{11,10},{12,13},{15,14},{16,17},{19,... | collective-permute-start | bytes 3145736 | tf_op jit(solution)/shard_map/ppermute | solution.py:535
  771.2 47.8 %collective-permute-start.64 = (bf16[1024,1024]{1,0:T(8,128)(2,1)}, bf16[1024,1024]{1,0:T(8,128)(2,1)}, u32[]{:S(2)}, u32[]{:S(2)}) collective-permute-start(bf16[1024,1024]{1,0:T(8,128)(2,1)} %convolution_convert_fusion.6), channel_id=1, source_target_pairs={{0,4},{4,0},{1,5},{5,1},{2,6},{6,2},{3,7},{7,3},{8,12},{12,8},{9,1... | collective-permute-start | bytes 6291464 | tf_op jit(solution)/shard_map/ppermute | solution.py:346
  799.7 69.9 %collective-permute-start.83 = (bf16[352,2048]{1,0:T(8,128)(2,1)}, bf16[352,2048]{1,0:T(8,128)(2,1)}, u32[]{:S(2)}, u32[]{:S(2)}) collective-permute-start(bf16[352,2048]{1,0:T(8,128)(2,1)} %add.677), channel_id=1, source_target_pairs={{1,0},{2,3},{5,4},{6,7},{9,8},{10,11},{13,12},{14,15},{17,16},{18,... | collective-permute-start | bytes 4325384 | tf_op jit(solution)/shard_map/ppermute | solution.py:553
  801.0 65.5 %collective-permute-start.76 = (bf16[352,2048]{1,0:T(8,128)(2,1)}, bf16[352,2048]{1,0:T(8,128)(2,1)}, u32[]{:S(2)}, u32[]{:S(2)}) collective-permute-start(bf16[352,2048]{1,0:T(8,128)(2,1)} %add.697), channel_id=1, source_target_pairs={{1,2},{2,1},{5,6},{6,5},{9,10},{10,9},{13,14},{14,13},{17,18},{18,... | collective-permute-start | bytes 4325384 | tf_op jit(solution)/shard_map/ppermute | solution.py:544
  818.9 47.6 %collective-permute-start.62 = (bf16[256,2048]{1,0:T(8,128)(2,1)S(1)}, bf16[256,2048]{1,0:T(8,128)(2,1)S(1)}, u32[]{:S(2)}, u32[]{:S(2)}) collective-permute-start(bf16[256,2048]{1,0:T(8,128)(2,1)S(1)} %get-tuple-element.252), channel_id=1, source_target_pairs={{0,16},{8,24},{16,0},{24,8},{1,17},{9,25},{17,1},{25,9},{2,18},{10... | collective-permute-start | bytes 3145736 | tf_op jit(solution)/shard_map/ppermute | solution.py:346
  820.2 46.3 %collective-permute-start.63 = (bf16[256,2048]{1,0:T(8,128)(2,1)S(1)}, bf16[256,2048]{1,0:T(8,128)(2,1)S(1)}, u32[]{:S(2)}, u32[]{:S(2)}) collective-permute-start(bf16[256,2048]{1,0:T(8,128)(2,1)S(1)} %get-tuple-element.251), channel_id=1, source_target_pairs={{0,24},{8,16},{16,8},{24,0},{1,25},{9,17},{17,9},{25,1},{2,26},{10... | collective-permute-start | bytes 3145736 | tf_op jit(solution)/shard_map/ppermute | solution.py:346
  843.7 39.1 %collective-permute-start.72 = (bf16[256,2048]{1,0:T(8,128)(2,1)}, bf16[256,2048]{1,0:T(8,128)(2,1)}, u32[]{:S(2)}, u32[]{:S(2)}) collective-permute-start(bf16[256,2048]{1,0:T(8,128)(2,1)} %fusion.7), channel_id=1, source_target_pairs={{0,1},{3,2},{4,5},{7,6},{8,9},{11,10},{12,13},{15,14},{16,17},{19,... | collective-permute-start | bytes 3145736 | tf_op jit(solution)/shard_map/ppermute | solution.py:535
  869.6 39.1 %collective-permute-start.84 = (bf16[352,2048]{1,0:T(8,128)(2,1)S(1)}, bf16[352,2048]{1,0:T(8,128)(2,1)}, u32[]{:S(2)}, u32[]{:S(2)}) collective-permute-start(bf16[352,2048]{1,0:T(8,128)(2,1)S(1)} %add.704), channel_id=1, source_target_pairs={{1,0},{2,3},{5,4},{6,7},{9,8},{10,11},{13,12},{14,15},{17,16},{18,... | collective-permute-start | bytes 4325384 | tf_op jit(solution)/shard_map/ppermute | solution.py:553
  877.9 31.6 %collective-permute-start.67 = (f32[2,5408]{1,0:T(2,128)S(1)}, f32[2,5408]{1,0:T(2,128)S(1)}, u32[]{:S(2)}, u32[]{:S(2)}) collective-permute-start(f32[2,5408]{1,0:T(2,128)S(1)} %get-tuple-element.339), channel_id=1, source_target_pairs={{0,24},{8,16},{16,8},{24,0},{1,25},{9,17},{17,9},{25,1},{2,26},{10... | collective-permute-start | bytes 129800 | tf_op jit(solution)/shard_map/ppermute | solution.py:346
  879.3 31.5 %collective-permute-start.66 = (f32[2,5408]{1,0:T(2,128)S(1)}, f32[2,5408]{1,0:T(2,128)S(1)}, u32[]{:S(2)}, u32[]{:S(2)}) collective-permute-start(f32[2,5408]{1,0:T(2,128)S(1)} %get-tuple-element.340), channel_id=1, source_target_pairs={{0,16},{8,24},{16,0},{24,8},{1,17},{9,25},{17,1},{25,9},{2,18},{10... | collective-permute-start | bytes 129800 | tf_op jit(solution)/shard_map/ppermute | solution.py:346
  884.2 43.7 %collective-permute-start.73 = (bf16[2,256,1024]{2,1,0:T(8,128)(2,1)S(1)}, bf16[2,256,1024]{2,1,0:T(8,128)(2,1)S(1)}, u32[]{:S(2)}, u32[]{:S(2)}) collective-permute-start(bf16[2,256,1024]{2,1,0:T(8,128)(2,1)S(1)} %get-tuple-element.164), channel_id=1, source_target_pairs={{0,1},{3,2},{4,5},{7,6},{8,9},{11,10},{12,13},{15,14},{16,17},{19,... | collective-permute-start | bytes 3145736 | tf_op jit(solution)/shard_map/ppermute | solution.py:535
  911.6 29.9 %collective-permute-start.68 = (f32[1,5408]{1,0:T(1,128)S(1)}, f32[1,5408]{1,0:T(1,128)S(1)}, u32[]{:S(2)}, u32[]{:S(2)}) collective-permute-start(f32[1,5408]{1,0:T(1,128)S(1)} %constant_dynamic-slice_fusion), channel_id=1, source_target_pairs={{0,4},{4,0},{1,5},{5,1},{2,6},{6,2},{3,7},{7,3},{8,12},{12,8},{9,1... | collective-permute-start | bytes 64904 | tf_op jit(solution)/shard_map/ppermute | solution.py:346
  951.4 32.3 %collective-permute-start.75 = (bf16[8,2048]{1,0:T(8,128)(2,1)S(1)}, bf16[8,2048]{1,0:T(8,128)(2,1)S(1)}, u32[]{:S(2)}, u32[]{:S(2)}) collective-permute-start(bf16[8,2048]{1,0:T(8,128)(2,1)S(1)} %copy-done.88), channel_id=1, source_target_pairs={{0,1},{3,2},{4,5},{7,6},{8,9},{11,10},{12,13},{15,14},{16,17},{19,... | collective-permute-start | bytes 98312 | tf_op jit(solution)/shard_map/ppermute | solution.py:535
  (173 other events, 3017.4 us)
Sparse Core Ops, SparseCore 0:
  9.5 13.2 all-gather.5
  64.4 82.5 all-gather.11
  148.5 15.0 all-gather.7
  429.2 103.4 reduce-scatter.1
  587.9 112.6 all-gather.9

commit v9 on v8

--- a/solution.py
+++ b/solution.py
@@ -416,21 +416,22 @@
 
 
 def seq_pieces(shards, here):
-    rows = shards[0].shape[0] // 2
-    start = lax.axis_index("seq") % 2 * rows
-    shards = [lax.dynamic_slice_in_dim(shard, start, rows, 0) for shard in shards]
+    count, spot = lax.axis_size("seq"), lax.axis_index("seq")
+    rows = shards[0].shape[0] // count
+    shards = [lax.dynamic_slice_in_dim(shard, spot * rows, rows, 0) for shard in shards]
     own = column_cuts(shards, here, 0)
-    return [own] + [swap(column_cuts(shards, here, k), "p", k) for k in range(1, HEADS)]
+    return jnp.stack([own] + [swap(column_cuts(shards, here, k), "p", k) for k in range(1, HEADS)])
 
 
 def seq_columns(pieces, here):
-    copies, turn, half = lax.axis_size("r"), lax.axis_index("r"), lax.axis_index("seq") % 2
+    copies, count = lax.axis_size("r"), lax.axis_size("seq")
+    turn, spot = lax.axis_index("r"), lax.axis_index("seq")
     parts, spots = [], []
-    for j, part in enumerate([pieces, swap(pieces, "seq", 1)]):
+    for j, part in enumerate(gather_seq(pieces)):
         for m in range(copies):
             parts.append(part if m == 0 else swap(part, "r", m))
             spots.append(
-                [((here ^ k) * copies + (turn ^ m)) * 2 + (half ^ j) for k in range(HEADS)]
+                [(((here ^ k) * copies + (turn ^ m)) * count + (spot ^ j)) for k in range(HEADS)]
             )
     return place(parts, spots)
 
@@ -487,6 +488,17 @@
     for part in got:
         total = total + part.astype(F32)
     return total.astype(BF)
+
+
+def gather_seq(value):
+    count = lax.axis_size("seq")
+    found = {0: value}
+    step = count // 2
+    while step >= 1:
+        for j in list(found):
+            found[j ^ step] = swap(found[j], "seq", step)
+        step //= 2
+    return [found[j] for j in range(count)]
 
 
 def assemble_kernel(counts, spot_ref, *refs):
@@ -622,7 +634,7 @@
     late = lax.optimization_barrier((query_proj, swish_proj, mlp_gate, mlp_up) + tuple(kv_pieces))
     weight_qs, qs_pieces = head_columns(late[:2], here)
     gu_pieces = seq_pieces(late[2:4], here)
-    grad_all = lax.all_gather(after(grad_out, *qs_pieces), "p", axis=0, tiled=False)
+    grad_blocks = gather_heads(after(grad_out, *qs_pieces))
     weight_out = lax.all_gather(out_proj, "r", axis=0, tiled=True)
     weight_down = lax.all_gather(mlp_down, "r", axis=0, tiled=True)
 
@@ -637,15 +649,12 @@
     state, decay = chunk_states(kv, li)
     decay = decay[:, :, :1]
     init = chain_pair(state, decay, True)
-    *gu_pieces, _ = lax.optimization_barrier((*gu_pieces, init))
-    weight_gu = seq_columns(jnp.stack(gu_pieces), here)
+    init, gu_pieces = lax.optimization_barrier((init, gu_pieces))
+    weight_gu = seq_columns(gu_pieces, here)
     qs = mm(normed, weight_qs).reshape(HEADS, rows, 2 * HEAD)
     gated, mixer_out, probs, mix = mixer_forward(qs, kv, li, init, gain_head8)
     gated = gated.reshape(group, HEAD)
     attn_part = mm(gated, weight_out).astype(BF).reshape(HEADS, rows, D)
-    grad_blocks = [
-        lax.dynamic_index_in_dim(grad_all, here ^ k, 0, False) for k in range(HEADS)
-    ]
     grad_mlp = (mask_all * jnp.concatenate(grad_blocks).astype(F32)).astype(BF)
     attn_out, grad_act = scatter_heads(
         [attn_part[k] for k in range(HEADS)], mm_nt(grad_mlp, weight_down)
@@ -656,8 +665,7 @@
     scale_two = inverse_rms(residual)
     hat_two = residual * scale_two
     normed_two_own = (hat_two * gain_two).astype(BF)
-    weight_gu, *two_blocks = lax.optimization_barrier((weight_gu, *gather_heads(normed_two_own)))
-    normed_two = jnp.concatenate(two_blocks)
+    normed_two = jnp.concatenate(gather_heads(normed_two_own))
 
     hidden_width = weight_down.shape[0]
     gate_up = mm(normed_two, weight_gu)
@@ -697,17 +705,17 @@
     mlp_part = mm(hidden, weight_down).astype(BF)
     mlp_part, gu_part, *attn_blocks = lax.optimization_barrier((mlp_part, gu_part, *attn_blocks))
     gu_part = swap_diagonal(gu_part)
-    half_rows, line = down_rows // 2, {}
-    down_near = inward(after(down_total[:half_rows], *attn_blocks), line)
     grad_attn = jnp.concatenate(attn_blocks)
     mlp_part = mlp_part.reshape(HEADS, rows, D)
-    mlp_out = scatter_heads([mlp_part[k] for k in range(HEADS)])
+    mlp_part = jnp.stack(
+        [lax.dynamic_index_in_dim(mlp_part, here ^ k, 0, False) for k in range(HEADS)]
+    )
 
     grad_gated = mm_nt(grad_attn, weight_out).reshape(HEADS, rows, HEAD)
     grad_qs, grad_kv, grad_li, adjoint, slot_part = mixer_backward(
         qs, kv, li, init, gain_head8, mixer_out, probs, mix, grad_gated
     )
-    adjoint, gu_part, down_near = lax.optimization_barrier((adjoint, gu_part, down_near))
+    adjoint, gu_part = lax.optimization_barrier((adjoint, gu_part))
     gu_whole = lax.all_gather(gu_part, "seq", axis=0, tiled=True)
     one_view = normed.reshape(group, HEADS, copies, shard)
     one_views = [split_rows(one_view, turn, m, order) for m in range(copies)]
@@ -723,13 +731,16 @@
     out_total = weight_grad(out_views, grad_attn)
     qs_total = weight_grad(one_views, grad_qs)
     ends = chain_pair(adjoint, decay, False)
-    ends, mlp_out, out_total, qs_total, down_near, gu_whole = lax.optimization_barrier(
-        (ends, mlp_out, out_total, qs_total, down_near, gu_whole)
-    )
+    ends, out_total, qs_total = lax.optimization_barrier((ends, out_total, qs_total))
+    grad_kv, grad_li = mixer_finish(kv, li, init, ends, grad_kv, grad_li)
+    half_rows, line = down_rows // 2, {}
+    grad_kv, mlp_part, gu_whole, down_total = lax.optimization_barrier(
+        (grad_kv, mlp_part, gu_whole, down_total)
+    )
+    mlp_out = lax.psum_scatter(mlp_part, "p", scatter_dimension=0, tiled=False).astype(F32)
+    down_near = inward(down_total[:half_rows], line)
+    grad_qs, down_near = lax.optimization_barrier((grad_qs, down_near))
     result = (residual + mask_own * mlp_out).astype(BF)
-    down_near = across(down_near, line)
-    grad_qs = after(grad_qs, down_near)
-    grad_kv, grad_li = mixer_finish(kv, li, init, ends, grad_kv, grad_li)
     grad_kv = grad_kv.reshape(group, 2 * HEAD)
     grad_li = grad_li.reshape(group, 2 * SLOTS)
     grad_decay = (
@@ -780,18 +791,18 @@
 
     qs_total = qs_total.reshape(HEADS, shard, 2 * HEAD)
     kv_total = kv_total.reshape(HEADS, shard, 2 * HEAD)
-    chunks = [down_total[half_rows:], qs_total[1::2], qs_total[0::2], out_total]
-    chunks += [kv_total[1::2], kv_total[0::2], flat]
-    summed = [outward(down_near, line)]
+    chunks = [down_total[half_rows:], qs_total[1::2], qs_total[0::2]]
+    chunks += [kv_total[1::2], kv_total[0::2], jnp.concatenate([out_total, flat])]
+    summed = [outward(across(down_near, line), line)]
     for chunk in chunks:
         summed.append(outward(across(inward(chunk, line), line), line))
-    near, far, *wide, out_grad, kv_near, kv_far, flat = summed
+    near, far, *wide, tail = summed
     down_grad = jnp.concatenate([near, far])
     gate_grad, up_grad = assemble(gu_whole[None], order, 2)
     query_grad, swish_grad = spread_line(wide[0], wide[1], here)
-    key_grad, value_grad = spread_line(kv_near, kv_far, here)
-    out_grad = out_grad.astype(F32)
-    flat = flat.reshape(-1).astype(F32)
+    key_grad, value_grad = spread_line(wide[2], wide[3], here)
+    out_grad = tail[:shard].astype(F32)
+    flat = tail[shard:].reshape(-1).astype(F32)
     totals, offset = [], 0
     for a in sums:
         size = a.size // owners

time: 1070 us -> 999 us (0.934)
  starting transfers between devices: 208 us -> 134 us
  other arithmetic: 93.5 us -> 108 us
  local copies, waits for them, and re-layouts: 74.5 us -> 63.6 us
    ppermute x60 -> x64, waiting for transfers between devices: 304 us -> 243 us  [swap(): return lax.ppermute(value, axis, [(i, i ^ step) for i in range(count)])]
    ppermute x8 -> x7, starting transfers between devices: 92.5 us -> 35 us  [inward(): last[i] = lax.ppermute(value, 'seq', line_pairs(i))]
    ppermute x12, waiting for transfers between devices: 22.2 us -> 76 us  [chain(): total = total + lax.ppermute(sent, 'seq', [pair]).astype(F32)]
    ppermute x1, starting transfers between devices: 13 us -> 2.19 us  [swap_diagonal(): return lax.ppermute(part, ('p', 'seq'), sends)]
    ppermute x60 -> x64, starting transfers between devices: 70.2 us -> 61.1 us  [swap(): return lax.ppermute(value, axis, [(i, i ^ step) for i in range(count)])]
    ppermute x8 -> x7, waiting for transfers between devices: 39.3 us -> 43.7 us  [inward(): last[i] = lax.ppermute(value, 'seq', line_pairs(i))]
    ppermute x8 -> x7, waiting for transfers between devices: 36.9 us -> 40.5 us  [outward(): got = lax.ppermute(value, 'seq', [(b, a) for a, b in line_pairs(i)])]
  transfers between devices with their start and end apart: 102 -> 103, of which waited for: 36 -> 32; matrix products, arithmetic and copies ran while one was open for 25% -> 28% of each run, Pallas kernels for 7% -> 9%
where the time goes in v9:
time: 999 us; the launch traced here: 993 us
  waiting for transfers between devices  404 us (40%)
  matrix products  175 us (18%)
  starting transfers between devices  134 us (13%)
  other arithmetic  108 us (11%)
  Pallas kernels  92.1 us (9%)
  local copies, waits for them, and re-layouts  63.6 us (6%)
  between operations  16.6 us (2%)
    ppermute x64, waiting for transfers between devices, swap(): return lax.ppermute(value, axis, [(i, i ^ step) for i in range(count)])  243 us
    ppermute x12, waiting for transfers between devices, chain(): total = total + lax.ppermute(sent, 'seq', [pair]).astype(F32)  76 us
    dot_general x11, matrix products, mm_tn(): lax.dot_general(a, b, (((0,), (0,)), ((), ())), preferred_element_type=F32)  67 us
    ppermute x64, starting transfers between devices, swap(): return lax.ppermute(value, axis, [(i, i ^ step) for i in range(count)])  61.1 us
    dot_general x6, matrix products, mm_nt(): lax.dot_general(a, b, (((1,), (1,)), ((), ())), preferred_element_type=F32)  57 us
    dot_general x6, matrix products, mm(): lax.dot_general(a, b, (((1,), (0,)), ((), ())), preferred_element_type=F32)  49.4 us
    pallas_call x4, Pallas kernels, run(): pl.pallas_call(kernel, grid=(args[0].shape[0],), in_specs=specs, out_spec...  49.2 us
    ppermute x7, waiting for transfers between devices, inward(): last[i] = lax.ppermute(value, 'seq', line_pairs(i))  43.7 us
  transfers between devices with their start and end apart: 103, of which 32 were waited for; matrix products, arithmetic and copies ran while one was open for 28% of the time, Pallas kernels for 9%

profile of v9, /device:TPU:0, one launch (start us, length us, event | category | flops | bytes accessed | tf_op | source)
XLA Modules:
  0.0 992.6 jit_solution(1620465782039679264)
XLA Ops:
  27.4 9.6 collective-permute-done.1
  38.5 21.2 %collective-permute-done.2 = f32[2,5409]{1,0:T(2,128)S(1)} collective-permute-done((f32[2,5409]{1,0:T(2,128)S(1)}, f32[2,5409]{1,0:T(2,128)S(1)}, u32[]{:S(2)}, u32[]{:S(2)}) %collective-permute-start.2) | collective-permute-done | bytes 43304 | tf_op jit(solution)/shard_map/ppermute | solution.py:346
  68.7 16.4 %collective-permute-done.8 = bf16[256,1024]{1,0:T(8,128)(2,1)} collective-permute-done((bf16[256,1024]{1,0:T(8,128)(2,1)}, bf16[256,1024]{1,0:T(8,128)(2,1)}, u32[]{:S(2)}, u32[]{:S(2)}) %collective-permute-start.8) | collective-permute-done | bytes 524320 | tf_op jit(solution)/shard_map/ppermute | solution.py:346
  106.6 5.6 shard_map.289
  112.2 6.8 fusion.2
  119.0 5.7 convolution_convert_fusion.8
  155.3 5.7 collective-permute-done.15
  173.7 6.0 shard_map.288
  181.2 8.6 fusion.84
  194.8 15.0 %shard_map.291 = (bf16[4,256,512]{2,1,0:T(8,128)(2,1)}, f32[4,256,512]{2,1,0:T(8,128)}, f32[4,256,64]{2,1,0:T(8,128)}, bf16[4,256,256]{2,1,0:T(8,128)(2,1)}) custom-call(f32[4,256,1024]{2,1,0:T(8,128)} %bitcast.220, bf16[4,256,1024]{2,1,0:T(8,128)(2,1)} %bitcast.223, f32[4,256,128]{2,1,0:T(8,128)} %bitcast.199, f32[4,64,1024]{2,1,0:T(8,128)} %pad_maximum_fusion.8.init_ref, ...), custom_call_target="tpu_custom_call" | custom-call | flops 12000000000 | bytes 16000000 | tf_op jit(solution)/shard_map/pallas_call | solution.py:258
  219.5 20.8 %collective-permute-done.30 = bf16[256,2048]{1,0:T(8,128)(2,1)S(1)} collective-permute-done((bf16[256,2048]{1,0:T(8,128)(2,1)S(1)}, bf16[256,2048]{1,0:T(8,128)(2,1)S(1)}, u32[]{:S(2)}, u32[]{:S(2)}) %collective-permute-start.30) | collective-permute-done | bytes 1048608 | tf_op jit(solution)/shard_map/ppermute | solution.py:346
  242.2 7.4 collective-permute-done.40.refs_2_
  249.5 7.2 collective-permute-done.42.refs_4_
  256.8 13.4 %fusion.68 = f32[1024,1408]{1,0:T(8,128)} fusion(bf16[1408,2048]{1,0:T(8,128)(2,1)} %all-gather.6.cloned.1.call-done, bf16[256,2048]{1,0:T(8,128)(2,1)} %collective-permute-done.35, bf16[256,2048]{1,0:T(8,128)(2,1)} %collective-permute-done.34, bf16[256,2048]{1,0:T(8,128)(2,1)} %collective-permute-done.33, bf16[256,2048]{1,0:T(8,128)(2,1)} %param.33, ...), kind=kOutput, calls=%fused_computation.246 | convolution fusion | flops 5926551552 | bytes 15732736 | tf_op jit(solution)/shard_map/dot_general | solution.py:23
  270.3 17.2 %collective-permute-done.44.refs_6_ = bf16[4,64,2816]{2,1,0:T(8,128)(2,1)} collective-permute-done((bf16[4,64,2816]{2,1,0:T(8,128)(2,1)}, bf16[4,64,2816]{2,1,0:T(8,128)(2,1)}, u32[]{:S(2)}, u32[]{:S(2)}) %collective-permute-start.44) | collective-permute-done | bytes 1441824 | tf_op jit(solution)/shard_map/ppermute | solution.py:346
  295.8 13.7 %shard_map.292 = bf16[2048,2816]{1,0:T(8,128)(2,1)} custom-call(s32[32]{0:T(128)} %stack.252.spot_ref, bf16[4,64,2816]{2,1,0:T(8,128)(2,1)} %pad_maximum_fusion.6.refs_0_, bf16[4,64,2816]{2,1,0:T(8,128)(2,1)} %collective-permute-done.39.refs_1_, bf16[4,64,2816]{2,1,0:T(8,128)(2,1)} %collective-permute-done.40.refs_2_, ...), custom_call_target="tpu_custom_call" | custom-call | bytes 23068672 | tf_op jit(solution)/shard_map/pallas_call | solution.py:382
  309.5 9.3 collective-permute-done.38
  318.7 22.0 %collective-permute-done.37 = bf16[256,2048]{1,0:T(8,128)(2,1)} collective-permute-done((bf16[256,2048]{1,0:T(8,128)(2,1)S(1)}, bf16[256,2048]{1,0:T(8,128)(2,1)}, u32[]{:S(2)}, u32[]{:S(2)}) %collective-permute-start.37) | collective-permute-done | bytes 1048608 | tf_op jit(solution)/shard_map/ppermute | solution.py:346
  340.7 21.2 %fusion.67 = f32[1024,2816]{1,0:T(8,128)} fusion(bf16[2048,2816]{1,0:T(8,128)(2,1)} %shard_map.292, bf16[256,2048]{1,0:T(8,128)(2,1)} %collective-permute-done.38, bf16[256,2048]{1,0:T(8,128)(2,1)} %collective-permute-done.37, bf16[256,2048]{1,0:T(8,128)(2,1)} %collective-permute-done.36, bf16[256,2048]{1,0:T(8,128)(2,1)S(1)} %multiply_convert_fusion.5), kind=kOutput, calls=%fused_computation.245 | convolution fusion | flops 11827937280 | bytes 27262976 | tf_op jit(solution)/shard_map/dot_general | solution.py:19
  362.0 7.1 multiply_convert_fusion.2
  371.8 8.9 convolution_convert_fusion
  381.2 16.3 %convolution_convert_fusion.1 = bf16[1024,2048]{1,0:T(8,128)(2,1)} fusion(bf16[1024,2816]{1,0:T(8,128)(2,1)S(1)} %pad_maximum_fusion, bf16[2048,2816]{1,0:T(8,128)(2,1)} %shard_map.292), kind=kOutput, calls=%fused_computation.22 | convolution fusion | flops 11813257216 | bytes 21495808 | tf_op jit(solution)/shard_map/dot_general | solution.py:23
  397.5 10.4 %add_convert_fusion = bf16[1024,2816]{1,0:T(8,128)(2,1)} fusion(bf16[1024,2816]{1,0:T(8,128)(2,1)} %collective-permute-done.46, bf16[1024,2816]{1,0:T(8,128)(2,1)S(1)} %pad_maximum_fusion, bf16[1024,256]{1,0:T(8,128)(2,1)S(1)} %get-tuple-element.251, bf16[1024,256]{1,0:T(8,128)(2,1)S(1)} %get-tuple-element.252, ...), kind=kOutput, calls=%fused_computation.1 | convolution fusion | flops 5922619392 | bytes 19398656 | tf_op jit(solution)/shard_map/dot_general | solution.py:27
  408.4 8.0 convolution_convert_fusion.4
  422.9 8.4 add_convert_fusion.2
  431.3 14.1 %collective-permute-done.47 = bf16[256,2048]{1,0:T(8,128)(2,1)S(1)} collective-permute-done((bf16[256,2048]{1,0:T(8,128)(2,1)S(1)}, bf16[256,2048]{1,0:T(8,128)(2,1)S(1)}, u32[]{:S(2)}, u32[]{:S(2)}) %collective-permute-start.47) | collective-permute-done | bytes 1048608 | tf_op jit(solution)/shard_map/ppermute | solution.py:346
  445.5 21.9 %collective-permute-done.48 = bf16[256,2048]{1,0:T(8,128)(2,1)S(1)} collective-permute-done((bf16[256,2048]{1,0:T(8,128)(2,1)S(1)}, bf16[256,2048]{1,0:T(8,128)(2,1)S(1)}, u32[]{:S(2)}, u32[]{:S(2)}) %collective-permute-start.48) | collective-permute-done | bytes 1048608 | tf_op jit(solution)/shard_map/ppermute | solution.py:346
  475.8 8.5 convolution_convert_fusion.2
  484.3 14.1 %collective-permute-done.51 = bf16[256,2048]{1,0:T(8,128)(2,1)S(1)} collective-permute-done((bf16[256,2048]{1,0:T(8,128)(2,1)S(1)}, bf16[256,2048]{1,0:T(8,128)(2,1)S(1)}, u32[]{:S(2)}, u32[]{:S(2)}) %collective-permute-start.51) | collective-permute-done | bytes 1048608 | tf_op jit(solution)/shard_map/ppermute | solution.py:346
  498.3 21.7 %collective-permute-done.52 = bf16[256,2048]{1,0:T(8,128)(2,1)S(1)} collective-permute-done((bf16[256,2048]{1,0:T(8,128)(2,1)S(1)}, bf16[256,2048]{1,0:T(8,128)(2,1)S(1)}, u32[]{:S(2)}, u32[]{:S(2)}) %collective-permute-start.52) | collective-permute-done | bytes 1048608 | tf_op jit(solution)/shard_map/ppermute | solution.py:346
  529.7 19.7 %shard_map.293 = (bf16[4,256,1024]{2,1,0:T(8,128)(2,1)}, f32[4,256,1024]{2,1,0:T(8,128)}, f32[4,256,128]{2,1,0:T(8,128)}, f32[4,64,1024]{2,1,0:T(8,128)}, f32[8,512]{1,0:T(8,128)}) custom-call(f32[4,256,1024]{2,1,0:T(8,128)} %bitcast.221, bf16[4,256,1024]{2,1,0:T(8,128)(2,1)} %bitcast.224, f32[4,256,128]{2,1,0:T(8,128)} %bitcast.200, ...), custom_call_target="tpu_custom_call" | custom-call | flops 24000000000 | bytes 20000000 | tf_op jit(solution)/shard_map/pallas_call | solution.py:258
  586.4 46.1 %collective-permute-done.57 = bf16[4,64,512]{2,1,0:T(8,128)(2,1)S(1)} collective-permute-done((bf16[4,64,512]{2,1,0:T(8,128)(2,1)S(1)}, bf16[4,64,512]{2,1,0:T(8,128)(2,1)S(1)}, u32[]{:S(2)}, u32[]{:S(2)}) %collective-permute-start.57) | collective-permute-done | bytes 262176 | tf_op jit(solution)/shard_map/ppermute | solution.py:465
  633.6 24.6 %collective-permute-done.60 = bf16[4,64,512]{2,1,0:T(8,128)(2,1)S(1)} collective-permute-done((bf16[4,64,512]{2,1,0:T(8,128)(2,1)S(1)}, bf16[4,64,512]{2,1,0:T(8,128)(2,1)S(1)}, u32[]{:S(2)}, u32[]{:S(2)}) %collective-permute-start.60) | collective-permute-done | bytes 262176 | tf_op jit(solution)/shard_map/ppermute | solution.py:465
  659.4 9.1 shard_map.294
  683.0 5.9 convolution_convert_fusion.6
  688.9 6.8 fusion.87
  695.7 16.7 %collective-permute-done.63 = bf16[352,2048]{1,0:T(8,128)(2,1)S(1)} collective-permute-done((bf16[352,2048]{1,0:T(8,128)(2,1)S(1)}, bf16[352,2048]{1,0:T(8,128)(2,1)S(1)}, u32[]{:S(2)}, u32[]{:S(2)}) %collective-permute-start.63) | collective-permute-done | bytes 1441824 | tf_op jit(solution)/shard_map/ppermute | solution.py:547
  714.2 5.5 collective-permute-start.72
  721.7 12.2 %add_convert_fusion.1 = bf16[1024,2048]{1,0:T(8,128)(2,1)} fusion(f32[1024,2048]{1,0:T(8,128)S(1)} %bitcast.179, f32[1024,2048]{1,0:T(8,128)} %fusion.87, bf16[1024,1024]{1,0:T(8,128)(2,1)} %bitcast.226, bf16[2048,1024]{1,0:T(8,128)(2,1)} %shard_map.288), kind=kOutput, calls=%fused_computation.7 | convolution fusion | flops 4301258752 | bytes 27262976 | tf_op jit(solution)/shard_map/dot_general | solution.py:23
  755.0 8.1 shard_map.297
  784.4 9.2 collective-permute-done.65
  793.7 12.7 %collective-permute-done.66 = bf16[256,2048]{1,0:T(8,128)(2,1)} collective-permute-done((bf16[256,2048]{1,0:T(8,128)(2,1)}, bf16[256,2048]{1,0:T(8,128)(2,1)}, u32[]{:S(2)}, u32[]{:S(2)}) %collective-permute-start.66) | collective-permute-done | bytes 1048608 | tf_op jit(solution)/shard_map/ppermute | solution.py:346
  839.4 12.3 %collective-permute-done.86 = bf16[352,2048]{1,0:T(8,128)(2,1)S(1)} collective-permute-done((bf16[352,2048]{1,0:T(8,128)(2,1)S(1)}, bf16[352,2048]{1,0:T(8,128)(2,1)S(1)}, u32[]{:S(2)}, u32[]{:S(2)}) %collective-permute-start.86) | collective-permute-done | bytes 1441824 | tf_op jit(solution)/shard_map/ppermute | solution.py:565
  854.1 11.0 %collective-permute-start.76 = (bf16[2,256,1024]{2,1,0:T(8,128)(2,1)}, bf16[2,256,1024]{2,1,0:T(8,128)(2,1)}, u32[]{:S(2)}, u32[]{:S(2)}) collective-permute-start(bf16[2,256,1024]{2,1,0:T(8,128)(2,1)} %get-tuple-element.146), channel_id=1, source_target_pairs={{0,1},{3,2},{4,5},{7,6},{8,9},{11,10},{12,13},{15,14},{16,17},{19,... | collective-permute-start | bytes 3145736 | tf_op jit(solution)/shard_map/ppermute | solution.py:547
  878.5 9.0 collective-permute-done.76
  904.4 10.4 %collective-permute-done.77 = bf16[264,2048]{1,0:T(8,128)(2,1)S(1)} collective-permute-done((bf16[264,2048]{1,0:T(8,128)(2,1)S(1)}, bf16[264,2048]{1,0:T(8,128)(2,1)S(1)}, u32[]{:S(2)}, u32[]{:S(2)}) %collective-permute-start.77) | collective-permute-done | bytes 1081376 | tf_op jit(solution)/shard_map/ppermute | solution.py:547
  917.5 11.7 %collective-permute-done.89 = bf16[2,256,1024]{2,1,0:T(8,128)(2,1)S(1)} collective-permute-done((bf16[2,256,1024]{2,1,0:T(8,128)(2,1)S(1)}, bf16[2,256,1024]{2,1,0:T(8,128)(2,1)S(1)}, u32[]{:S(2)}, u32[]{:S(2)}) %collective-permute-start.89) | collective-permute-done | bytes 1048608 | tf_op jit(solution)/shard_map/ppermute | solution.py:565
  944.2 10.6 %collective-permute-done.90 = bf16[2,256,1024]{2,1,0:T(8,128)(2,1)} collective-permute-done((bf16[2,256,1024]{2,1,0:T(8,128)(2,1)S(1)}, bf16[2,256,1024]{2,1,0:T(8,128)(2,1)}, u32[]{:S(2)}, u32[]{:S(2)}) %collective-permute-start.90) | collective-permute-done | bytes 1048608 | tf_op jit(solution)/shard_map/ppermute | solution.py:565
  (548 shorter events, 362.5 us)
Async XLA Ops:
  7.2 202.6 %all-gather.4.cloned.1.call-start = ((), (), s32[]{:S(2)}) async-start(), calls=%async_computation.2 | async-start | bytes 3145728 | tf_op jit(solution)/shard_map/all_gather | solution.py:638
  7.9 248.9 %all-gather.6.cloned.1.call-start = ((), (), s32[]{:S(2)}) async-start(), calls=%async_computation.3 | async-start | bytes 8650752 | tf_op jit(solution)/shard_map/all_gather | solution.py:639
  8.0 90.2 %collective-permute-start.6 = (bf16[256,2048]{1,0:T(8,128)(2,1)}, bf16[256,2048]{1,0:T(8,128)(2,1)S(1)}, u32[]{:S(2)}, u32[]{:S(2)}) collective-permute-start(bf16[256,2048]{1,0:T(8,128)(2,1)} %param.17), channel_id=1, source_target_pairs={{0,24},{8,16},{16,8},{24,0},{1,25},{9,17},{17,9},{25,1},{2,26},{10... | collective-permute-start | bytes 3145736 | tf_op jit(solution)/shard_map/ppermute | solution.py:346
  12.0 86.4 %collective-permute-start.5 = (bf16[256,2048]{1,0:T(8,128)(2,1)}, bf16[256,2048]{1,0:T(8,128)(2,1)}, u32[]{:S(2)}, u32[]{:S(2)}) collective-permute-start(bf16[256,2048]{1,0:T(8,128)(2,1)} %param.17), channel_id=1, source_target_pairs={{0,16},{8,24},{16,0},{24,8},{1,17},{9,25},{17,1},{25,9},{2,18},{10... | collective-permute-start | bytes 3145736 | tf_op jit(solution)/shard_map/ppermute | solution.py:346
  17.7 503.3 %reduce-scatter.5.cloned.1.call-start = ((), (), s32[]{:S(2)}) async-start(), calls=%async_computation.4 | async-start | bytes 7208960 | tf_op jit(solution)/shard_map/reduce_scatter | solution.py:686
  23.4 36.3 %collective-permute-start.2 = (f32[2,5409]{1,0:T(2,128)S(1)}, f32[2,5409]{1,0:T(2,128)S(1)}, u32[]{:S(2)}, u32[]{:S(2)}) collective-permute-start(f32[2,5409]{1,0:T(2,128)S(1)} %pad_maximum_fusion.30), channel_id=1, source_target_pairs={{0,16},{8,24},{16,0},{24,8},{1,17},{9,25},{17,1},{25,9},{2,18},{10... | collective-permute-start | bytes 129824 | tf_op jit(solution)/shard_map/ppermute | solution.py:346
  25.3 36.1 %collective-permute-start.3 = (f32[2,5409]{1,0:T(2,128)S(1)}, f32[2,5409]{1,0:T(2,128)S(1)}, u32[]{:S(2)}, u32[]{:S(2)}) collective-permute-start(f32[2,5409]{1,0:T(2,128)S(1)} %pad_maximum_fusion.30), channel_id=1, source_target_pairs={{0,24},{8,16},{16,8},{24,0},{1,25},{9,17},{17,9},{25,1},{2,26},{10... | collective-permute-start | bytes 129824 | tf_op jit(solution)/shard_map/ppermute | solution.py:346
  37.0 31.2 %collective-permute-start.7 = (bf16[256,1024]{1,0:T(8,128)(2,1)}, bf16[256,1024]{1,0:T(8,128)(2,1)S(1)}, u32[]{:S(2)}, u32[]{:S(2)}) collective-permute-start(bf16[256,1024]{1,0:T(8,128)(2,1)} %pad_maximum_fusion.10), channel_id=1, source_target_pairs={{0,8},{8,0},{16,24},{24,16},{1,9},{9,1},{17,25},{25,17},{2,10},{10... | collective-permute-start | bytes 1572872 | tf_op jit(solution)/shard_map/ppermute | solution.py:346
  68.2 30.4 %collective-permute-start.4 = (bf16[256,2048]{1,0:T(8,128)(2,1)S(1)}, bf16[256,2048]{1,0:T(8,128)(2,1)S(1)}, u32[]{:S(2)}, u32[]{:S(2)}) collective-permute-start(bf16[256,2048]{1,0:T(8,128)(2,1)S(1)} %copy-done.2), channel_id=1, source_target_pairs={{0,8},{8,0},{16,24},{24,16},{1,9},{9,1},{17,25},{25,17},{2,10},{10... | collective-permute-start | bytes 3145736 | tf_op jit(solution)/shard_map/ppermute | solution.py:346
  89.3 63.6 %collective-permute-start.11 = (bf16[256,1024]{1,0:T(8,128)(2,1)}, bf16[256,1024]{1,0:T(8,128)(2,1)}, u32[]{:S(2)}, u32[]{:S(2)}) collective-permute-start(bf16[256,1024]{1,0:T(8,128)(2,1)} %pad_maximum_fusion.14), channel_id=1, source_target_pairs={{0,8},{8,0},{16,24},{24,16},{1,9},{9,1},{17,25},{25,17},{2,10},{10... | collective-permute-start | bytes 1572872 | tf_op jit(solution)/shard_map/ppermute | solution.py:346
  102.1 53.2 %collective-permute-start.13 = (bf16[256,1024]{1,0:T(8,128)(2,1)}, bf16[256,1024]{1,0:T(8,128)(2,1)}, u32[]{:S(2)}, u32[]{:S(2)}) collective-permute-start(bf16[256,1024]{1,0:T(8,128)(2,1)} %pad_maximum_fusion.15), channel_id=1, source_target_pairs={{0,16},{8,24},{16,0},{24,8},{1,17},{9,25},{17,1},{25,9},{2,18},{10... | collective-permute-start | bytes 1572872 | tf_op jit(solution)/shard_map/ppermute | solution.py:346
  103.6 44.1 %collective-permute-start.29 = (bf16[64,2816]{1,0:T(8,128)(2,1)}, bf16[64,2816]{1,0:T(8,128)(2,1)}, u32[]{:S(2)}, u32[]{:S(2)}) collective-permute-start(bf16[64,2816]{1,0:T(8,128)(2,1)} %pad_maximum_fusion.21), channel_id=1, source_target_pairs={{0,24},{8,16},{16,8},{24,0},{1,25},{9,17},{17,9},{25,1},{2,26},{10... | collective-permute-start | bytes 1081352 | tf_op jit(solution)/shard_map/ppermute | solution.py:346
  105.1 47.0 %collective-permute-start.28 = (bf16[64,2816]{1,0:T(8,128)(2,1)}, bf16[64,2816]{1,0:T(8,128)(2,1)}, u32[]{:S(2)}, u32[]{:S(2)}) collective-permute-start(bf16[64,2816]{1,0:T(8,128)(2,1)} %pad_maximum_fusion.20), channel_id=1, source_target_pairs={{0,16},{8,24},{16,0},{24,8},{1,17},{9,25},{17,1},{25,9},{2,18},{10... | collective-permute-start | bytes 1081352 | tf_op jit(solution)/shard_map/ppermute | solution.py:346
  169.4 47.8 %collective-permute-start.35 = (bf16[256,2048]{1,0:T(8,128)(2,1)}, bf16[256,2048]{1,0:T(8,128)(2,1)}, u32[]{:S(2)}, u32[]{:S(2)}) collective-permute-start(bf16[256,2048]{1,0:T(8,128)(2,1)} %param.33), channel_id=1, source_target_pairs={{0,24},{8,16},{16,8},{24,0},{1,25},{9,17},{17,9},{25,1},{2,26},{10... | collective-permute-start | bytes 3145736 | tf_op jit(solution)/shard_map/ppermute | solution.py:346
  170.9 46.8 %collective-permute-start.34 = (bf16[256,2048]{1,0:T(8,128)(2,1)}, bf16[256,2048]{1,0:T(8,128)(2,1)}, u32[]{:S(2)}, u32[]{:S(2)}) collective-permute-start(bf16[256,2048]{1,0:T(8,128)(2,1)} %param.33), channel_id=1, source_target_pairs={{0,16},{8,24},{16,0},{24,8},{1,17},{9,25},{17,1},{25,9},{2,18},{10... | collective-permute-start | bytes 3145736 | tf_op jit(solution)/shard_map/ppermute | solution.py:346
  171.4 46.5 %collective-permute-start.33 = (bf16[256,2048]{1,0:T(8,128)(2,1)}, bf16[256,2048]{1,0:T(8,128)(2,1)}, u32[]{:S(2)}, u32[]{:S(2)}) collective-permute-start(bf16[256,2048]{1,0:T(8,128)(2,1)} %param.33), channel_id=1, source_target_pairs={{0,8},{8,0},{16,24},{24,16},{1,9},{9,1},{17,25},{25,17},{2,10},{10... | collective-permute-start | bytes 3145736 | tf_op jit(solution)/shard_map/ppermute | solution.py:346
  191.1 58.4 %collective-permute-start.40 = (bf16[4,64,2816]{2,1,0:T(8,128)(2,1)}, bf16[4,64,2816]{2,1,0:T(8,128)(2,1)}, u32[]{:S(2)}, u32[]{:S(2)}) collective-permute-start(bf16[4,64,2816]{2,1,0:T(8,128)(2,1)} %pad_maximum_fusion.6.refs_0_), channel_id=1, source_target_pairs={{0,1},{1,0},{2,3},{3,2},{4,5},{5,4},{6,7},{7,6},{8,9},{9,8},{10,11... | collective-permute-start | bytes 4325384 | tf_op jit(solution)/shard_map/ppermute | solution.py:346
  194.2 62.6 %collective-permute-start.42 = (bf16[4,64,2816]{2,1,0:T(8,128)(2,1)}, bf16[4,64,2816]{2,1,0:T(8,128)(2,1)}, u32[]{:S(2)}, u32[]{:S(2)}) collective-permute-start(bf16[4,64,2816]{2,1,0:T(8,128)(2,1)} %pad_maximum_fusion.6.refs_0_), channel_id=1, source_target_pairs={{0,2},{1,3},{2,0},{3,1},{4,6},{5,7},{6,4},{7,5},{8,10},{9,11},{10,... | collective-permute-start | bytes 4325384 | tf_op jit(solution)/shard_map/ppermute | solution.py:346
  217.8 75.4 %collective-permute-start.39 = (bf16[4,64,2816]{2,1,0:T(8,128)(2,1)}, bf16[4,64,2816]{2,1,0:T(8,128)(2,1)}, u32[]{:S(2)}, u32[]{:S(2)}) collective-permute-start(bf16[4,64,2816]{2,1,0:T(8,128)(2,1)} %pad_maximum_fusion.6.refs_0_), channel_id=1, source_target_pairs={{0,4},{4,0},{1,5},{5,1},{2,6},{6,2},{3,7},{7,3},{8,12},{12,8},{9,1... | collective-permute-start | bytes 4325384 | tf_op jit(solution)/shard_map/ppermute | solution.py:346
  217.8 52.4 %collective-permute-start.31 = (bf16[256,2048]{1,0:T(8,128)(2,1)}, bf16[256,2048]{1,0:T(8,128)(2,1)}, u32[]{:S(2)}, u32[]{:S(2)}) collective-permute-start(bf16[256,2048]{1,0:T(8,128)(2,1)} %get-tuple-element.256), channel_id=1, source_target_pairs={{0,16},{8,24},{16,0},{24,8},{1,17},{9,25},{17,1},{25,9},{2,18},{10... | collective-permute-start | bytes 3145736 | tf_op jit(solution)/shard_map/ppermute | solution.py:346
  240.2 47.3 %collective-permute-start.32 = (bf16[256,2048]{1,0:T(8,128)(2,1)S(1)}, bf16[256,2048]{1,0:T(8,128)(2,1)}, u32[]{:S(2)}, u32[]{:S(2)}) collective-permute-start(bf16[256,2048]{1,0:T(8,128)(2,1)S(1)} %get-tuple-element.255), channel_id=1, source_target_pairs={{0,24},{8,16},{16,8},{24,0},{1,25},{9,17},{17,9},{25,1},{2,26},{10... | collective-permute-start | bytes 3145736 | tf_op jit(solution)/shard_map/ppermute | solution.py:346
  249.5 44.1 %collective-permute-start.41 = (bf16[4,64,2816]{2,1,0:T(8,128)(2,1)}, bf16[4,64,2816]{2,1,0:T(8,128)(2,1)}, u32[]{:S(2)}, u32[]{:S(2)}) collective-permute-start(bf16[4,64,2816]{2,1,0:T(8,128)(2,1)} %collective-permute-done.40.refs_2_), channel_id=1, source_target_pairs={{0,4},{4,0},{1,5},{5,1},{2,6},{6,2},{3,7},{7,3},{8,12},{12,8},{9,1... | collective-permute-start | bytes 4325384 | tf_op jit(solution)/shard_map/ppermute | solution.py:346
  256.8 30.8 %collective-permute-start.44 = (bf16[4,64,2816]{2,1,0:T(8,128)(2,1)}, bf16[4,64,2816]{2,1,0:T(8,128)(2,1)}, u32[]{:S(2)}, u32[]{:S(2)}) collective-permute-start(bf16[4,64,2816]{2,1,0:T(8,128)(2,1)} %collective-permute-done.42.refs_4_), channel_id=1, source_target_pairs={{0,1},{1,0},{2,3},{3,2},{4,5},{5,4},{6,7},{7,6},{8,9},{9,8},{10,11... | collective-permute-start | bytes 4325384 | tf_op jit(solution)/shard_map/ppermute | solution.py:346
  293.2 47.6 %collective-permute-start.37 = (bf16[256,2048]{1,0:T(8,128)(2,1)S(1)}, bf16[256,2048]{1,0:T(8,128)(2,1)}, u32[]{:S(2)}, u32[]{:S(2)}) collective-permute-start(bf16[256,2048]{1,0:T(8,128)(2,1)S(1)} %multiply_convert_fusion.5), channel_id=1, source_target_pairs={{0,16},{8,24},{16,0},{24,8},{1,17},{9,25},{17,1},{25,9},{2,18},{10... | collective-permute-start | bytes 3145736 | tf_op jit(solution)/shard_map/ppermute | solution.py:346
  293.6 47.1 %collective-permute-start.36 = (bf16[256,2048]{1,0:T(8,128)(2,1)S(1)}, bf16[256,2048]{1,0:T(8,128)(2,1)}, u32[]{:S(2)}, u32[]{:S(2)}) collective-permute-start(bf16[256,2048]{1,0:T(8,128)(2,1)S(1)} %multiply_convert_fusion.5), channel_id=1, source_target_pairs={{0,8},{8,0},{16,24},{24,16},{1,9},{9,1},{17,25},{25,17},{2,10},{10... | collective-permute-start | bytes 3145736 | tf_op jit(solution)/shard_map/ppermute | solution.py:346
  408.0 271.9 %all-gather.8.cloned.1.call-start = ((), (), s32[]{:S(2)}) async-start(), calls=%async_computation.5 | async-start | bytes 7208960 | tf_op jit(solution)/shard_map/all_gather | solution.py:719
  420.1 47.3 %collective-permute-start.48 = (bf16[256,2048]{1,0:T(8,128)(2,1)S(1)}, bf16[256,2048]{1,0:T(8,128)(2,1)S(1)}, u32[]{:S(2)}, u32[]{:S(2)}) collective-permute-start(bf16[256,2048]{1,0:T(8,128)(2,1)S(1)} %get-tuple-element.245), channel_id=1, source_target_pairs={{0,16},{8,24},{16,0},{24,8},{1,17},{9,25},{17,1},{25,9},{2,18},{10... | collective-permute-start | bytes 3145736 | tf_op jit(solution)/shard_map/ppermute | solution.py:346
  421.5 45.9 %collective-permute-start.49 = (bf16[256,2048]{1,0:T(8,128)(2,1)S(1)}, bf16[256,2048]{1,0:T(8,128)(2,1)S(1)}, u32[]{:S(2)}, u32[]{:S(2)}) collective-permute-start(bf16[256,2048]{1,0:T(8,128)(2,1)S(1)} %get-tuple-element.244), channel_id=1, source_target_pairs={{0,24},{8,16},{16,8},{24,0},{1,25},{9,17},{17,9},{25,1},{2,26},{10... | collective-permute-start | bytes 3145736 | tf_op jit(solution)/shard_map/ppermute | solution.py:346
  473.7 46.3 %collective-permute-start.52 = (bf16[256,2048]{1,0:T(8,128)(2,1)S(1)}, bf16[256,2048]{1,0:T(8,128)(2,1)S(1)}, u32[]{:S(2)}, u32[]{:S(2)}) collective-permute-start(bf16[256,2048]{1,0:T(8,128)(2,1)S(1)} %get-tuple-element.115), channel_id=1, source_target_pairs={{0,16},{8,24},{16,0},{24,8},{1,17},{9,25},{17,1},{25,9},{2,18},{10... | collective-permute-start | bytes 3145736 | tf_op jit(solution)/shard_map/ppermute | solution.py:346
  474.5 46.5 %collective-permute-start.53 = (bf16[256,2048]{1,0:T(8,128)(2,1)S(1)}, bf16[256,2048]{1,0:T(8,128)(2,1)}, u32[]{:S(2)}, u32[]{:S(2)}) collective-permute-start(bf16[256,2048]{1,0:T(8,128)(2,1)S(1)} %get-tuple-element.115), channel_id=1, source_target_pairs={{0,24},{8,16},{16,8},{24,0},{1,25},{9,17},{17,9},{25,1},{2,26},{10... | collective-permute-start | bytes 3145736 | tf_op jit(solution)/shard_map/ppermute | solution.py:346
  550.6 408.8 %reduce-scatter.7.cloned.1.call-start = ((), (), s32[]{:S(2)}) async-start(), calls=%async_computation.6 | async-start | bytes 5242880
  577.9 54.6 %collective-permute-start.57 = (bf16[4,64,512]{2,1,0:T(8,128)(2,1)S(1)}, bf16[4,64,512]{2,1,0:T(8,128)(2,1)S(1)}, u32[]{:S(2)}, u32[]{:S(2)}) collective-permute-start(bf16[4,64,512]{2,1,0:T(8,128)(2,1)S(1)} %get-tuple-element.274), channel_id=1, source_target_pairs={{1,0},{5,4},{9,8},{13,12},{17,16},{21,20},{25,24},{29,28}} | collective-permute-start | bytes 786440 | tf_op jit(solution)/shard_map/ppermute | solution.py:465
  579.3 78.9 %collective-permute-start.60 = (bf16[4,64,512]{2,1,0:T(8,128)(2,1)S(1)}, bf16[4,64,512]{2,1,0:T(8,128)(2,1)S(1)}, u32[]{:S(2)}, u32[]{:S(2)}) collective-permute-start(bf16[4,64,512]{2,1,0:T(8,128)(2,1)S(1)} %add_convert_fusion.5), channel_id=1, source_target_pairs={{1,0},{5,4},{9,8},{13,12},{17,16},{21,20},{25,24},{29,28}} | collective-permute-start | bytes 786440 | tf_op jit(solution)/shard_map/ppermute | solution.py:465
  681.4 31.0 %collective-permute-start.63 = (bf16[352,2048]{1,0:T(8,128)(2,1)S(1)}, bf16[352,2048]{1,0:T(8,128)(2,1)S(1)}, u32[]{:S(2)}, u32[]{:S(2)}) collective-permute-start(bf16[352,2048]{1,0:T(8,128)(2,1)S(1)} %slice.196), channel_id=1, source_target_pairs={{0,1},{3,2},{4,5},{7,6},{8,9},{11,10},{12,13},{15,14},{16,17},{19,... | collective-permute-start | bytes 4325384 | tf_op jit(solution)/shard_map/ppermute | solution.py:547
  688.9 87.0 %collective-permute-start.67 = (bf16[1024,1024]{1,0:T(8,128)(2,1)}, bf16[1024,1024]{1,0:T(8,128)(2,1)}, u32[]{:S(2)}, u32[]{:S(2)}) collective-permute-start(bf16[1024,1024]{1,0:T(8,128)(2,1)} %convolution_convert_fusion.6), channel_id=1, source_target_pairs={{0,4},{4,0},{1,5},{5,1},{2,6},{6,2},{3,7},{7,3},{8,12},{12,8},{9,1... | collective-permute-start | bytes 6291464 | tf_op jit(solution)/shard_map/ppermute | solution.py:346
  714.2 33.4 %collective-permute-start.72 = (bf16[352,2048]{1,0:T(8,128)(2,1)}, bf16[352,2048]{1,0:T(8,128)(2,1)}, u32[]{:S(2)}, u32[]{:S(2)}) collective-permute-start(bf16[352,2048]{1,0:T(8,128)(2,1)} %get-tuple-element.142), channel_id=1, source_target_pairs={{0,1},{3,2},{4,5},{7,6},{8,9},{11,10},{12,13},{15,14},{16,17},{19,... | collective-permute-start | bytes 4325384 | tf_op jit(solution)/shard_map/ppermute | solution.py:547
  719.8 46.9 %collective-permute-start.78 = (bf16[352,2048]{1,0:T(8,128)(2,1)}, bf16[352,2048]{1,0:T(8,128)(2,1)}, u32[]{:S(2)}, u32[]{:S(2)}) collective-permute-start(bf16[352,2048]{1,0:T(8,128)(2,1)} %get-tuple-element.148), channel_id=1, source_target_pairs={{1,2},{2,1},{5,6},{6,5},{9,10},{10,9},{13,14},{14,13},{17,18},{18,... | collective-permute-start | bytes 4325384 | tf_op jit(solution)/shard_map/ppermute | solution.py:556
  737.6 40.2 %collective-permute-start.64 = (bf16[256,2048]{1,0:T(8,128)(2,1)}, bf16[256,2048]{1,0:T(8,128)(2,1)}, u32[]{:S(2)}, u32[]{:S(2)}) collective-permute-start(bf16[256,2048]{1,0:T(8,128)(2,1)} %get-tuple-element.231), channel_id=1, source_target_pairs={{0,8},{8,0},{16,24},{24,16},{1,9},{9,1},{17,25},{25,17},{2,10},{10... | collective-permute-start | bytes 3145736 | tf_op jit(solution)/shard_map/ppermute | solution.py:346
  743.6 50.0 %collective-permute-start.65 = (bf16[256,2048]{1,0:T(8,128)(2,1)}, bf16[256,2048]{1,0:T(8,128)(2,1)}, u32[]{:S(2)}, u32[]{:S(2)}) collective-permute-start(bf16[256,2048]{1,0:T(8,128)(2,1)} %get-tuple-element.230), channel_id=1, source_target_pairs={{0,16},{8,24},{16,0},{24,8},{1,17},{9,25},{17,1},{25,9},{2,18},{10... | collective-permute-start | bytes 3145736 | tf_op jit(solution)/shard_map/ppermute | solution.py:346
  747.7 58.7 %collective-permute-start.66 = (bf16[256,2048]{1,0:T(8,128)(2,1)}, bf16[256,2048]{1,0:T(8,128)(2,1)}, u32[]{:S(2)}, u32[]{:S(2)}) collective-permute-start(bf16[256,2048]{1,0:T(8,128)(2,1)} %get-tuple-element.229), channel_id=1, source_target_pairs={{0,24},{8,16},{16,8},{24,0},{1,25},{9,17},{17,9},{25,1},{2,26},{10... | collective-permute-start | bytes 3145736 | tf_op jit(solution)/shard_map/ppermute | solution.py:346
  766.7 43.1 %collective-permute-start.73 = (bf16[2,256,1024]{2,1,0:T(8,128)(2,1)}, bf16[2,256,1024]{2,1,0:T(8,128)(2,1)}, u32[]{:S(2)}, u32[]{:S(2)}) collective-permute-start(bf16[2,256,1024]{2,1,0:T(8,128)(2,1)} %get-tuple-element.143), channel_id=1, source_target_pairs={{0,1},{3,2},{4,5},{7,6},{8,9},{11,10},{12,13},{15,14},{16,17},{19,... | collective-permute-start | bytes 3145736 | tf_op jit(solution)/shard_map/ppermute | solution.py:547
  775.8 41.3 %collective-permute-start.79 = (bf16[352,2048]{1,0:T(8,128)(2,1)}, bf16[352,2048]{1,0:T(8,128)(2,1)}, u32[]{:S(2)}, u32[]{:S(2)}) collective-permute-start(bf16[352,2048]{1,0:T(8,128)(2,1)} %add.753), channel_id=1, source_target_pairs={{1,2},{2,1},{5,6},{6,5},{9,10},{10,9},{13,14},{14,13},{17,18},{18,... | collective-permute-start | bytes 4325384 | tf_op jit(solution)/shard_map/ppermute | solution.py:556
  777.8 42.4 %collective-permute-start.85 = (bf16[352,2048]{1,0:T(8,128)(2,1)}, bf16[352,2048]{1,0:T(8,128)(2,1)}, u32[]{:S(2)}, u32[]{:S(2)}) collective-permute-start(bf16[352,2048]{1,0:T(8,128)(2,1)} %add.760), channel_id=1, source_target_pairs={{1,0},{2,3},{5,4},{6,7},{9,8},{10,11},{13,12},{14,15},{17,16},{18,... | collective-permute-start | bytes 4325384 | tf_op jit(solution)/shard_map/ppermute | solution.py:565
  820.2 31.6 %collective-permute-start.86 = (bf16[352,2048]{1,0:T(8,128)(2,1)S(1)}, bf16[352,2048]{1,0:T(8,128)(2,1)S(1)}, u32[]{:S(2)}, u32[]{:S(2)}) collective-permute-start(bf16[352,2048]{1,0:T(8,128)(2,1)S(1)} %add.759), channel_id=1, source_target_pairs={{1,0},{2,3},{5,4},{6,7},{9,8},{10,11},{13,12},{14,15},{17,16},{18,... | collective-permute-start | bytes 4325384 | tf_op jit(solution)/shard_map/ppermute | solution.py:565
  836.4 36.6 %collective-permute-start.81 = (bf16[2,256,1024]{2,1,0:T(8,128)(2,1)}, bf16[2,256,1024]{2,1,0:T(8,128)(2,1)}, u32[]{:S(2)}, u32[]{:S(2)}) collective-permute-start(bf16[2,256,1024]{2,1,0:T(8,128)(2,1)} %add.751), channel_id=1, source_target_pairs={{1,2},{2,1},{5,6},{6,5},{9,10},{10,9},{13,14},{14,13},{17,18},{18,... | collective-permute-start | bytes 3145736 | tf_op jit(solution)/shard_map/ppermute | solution.py:556
  854.1 33.4 %collective-permute-start.76 = (bf16[2,256,1024]{2,1,0:T(8,128)(2,1)}, bf16[2,256,1024]{2,1,0:T(8,128)(2,1)}, u32[]{:S(2)}, u32[]{:S(2)}) collective-permute-start(bf16[2,256,1024]{2,1,0:T(8,128)(2,1)} %get-tuple-element.146), channel_id=1, source_target_pairs={{0,1},{3,2},{4,5},{7,6},{8,9},{11,10},{12,13},{15,14},{16,17},{19,... | collective-permute-start | bytes 3145736 | tf_op jit(solution)/shard_map/ppermute | solution.py:547
  893.4 40.4 %collective-permute-start.94 = (bf16[256,1024]{1,0:T(8,128)(2,1)S(1)}, bf16[256,1024]{1,0:T(8,128)(2,1)S(1)}, u32[]{:S(2)}, u32[]{:S(2)}) collective-permute-start(bf16[256,1024]{1,0:T(8,128)(2,1)S(1)} %get-tuple-element.289), channel_id=1, source_target_pairs={{0,24},{8,16},{16,8},{24,0},{1,25},{9,17},{17,9},{25,1},{2,26},{10... | collective-permute-start | bytes 1572872 | tf_op jit(solution)/shard_map/ppermute | solution.py:346
  893.8 39.9 %collective-permute-start.92 = (bf16[256,1024]{1,0:T(8,128)(2,1)S(1)}, bf16[256,1024]{1,0:T(8,128)(2,1)S(1)}, u32[]{:S(2)}, u32[]{:S(2)}) collective-permute-start(bf16[256,1024]{1,0:T(8,128)(2,1)S(1)} %get-tuple-element.288), channel_id=1, source_target_pairs={{0,8},{8,0},{16,24},{24,16},{1,9},{9,1},{17,25},{25,17},{2,10},{10... | collective-permute-start | bytes 1572872 | tf_op jit(solution)/shard_map/ppermute | solution.py:346
  (141 other events, 2233.0 us)
Sparse Core Ops, SparseCore 0:
  9.5 13.2 all-gather.3
  24.4 17.1 all-gather.5
  408.1 99.6 reduce-scatter.4
  550.7 119.9 all-gather.7
  755.1 76.1 reduce-scatter.6

commit v10 on v9

--- a/solution.py
+++ b/solution.py
@@ -798,7 +798,7 @@
         summed.append(outward(across(inward(chunk, line), line), line))
     near, far, *wide, tail = summed
     down_grad = jnp.concatenate([near, far])
-    gate_grad, up_grad = assemble(gu_whole[None], order, 2)
+    gate_grad, up_grad = assemble(after(gu_whole, wide[2])[None], order, 2)
     query_grad, swish_grad = spread_line(wide[0], wide[1], here)
     key_grad, value_grad = spread_line(wide[2], wide[3], here)
     out_grad = tail[:shard].astype(F32)

time: 999 us -> 999 us (level)
  transfers between devices with their start and end apart: 103 -> 103, of which waited for: 32 -> 30; matrix products, arithmetic and copies ran while one was open for 28% -> 28% of each run, Pallas kernels for 9% -> 9%
where the time goes in v10:
time: 999 us; the launch traced here: 992 us
  waiting for transfers between devices  403 us (40%)
  matrix products  175 us (18%)
  starting transfers between devices  134 us (13%)
  other arithmetic  108 us (11%)
  Pallas kernels  92.1 us (9%)
  local copies, waits for them, and re-layouts  63.6 us (6%)
  between operations  16.6 us (2%)
    ppermute x64, waiting for transfers between devices, swap(): return lax.ppermute(value, axis, [(i, i ^ step) for i in range(count)])  243 us
    ppermute x12, waiting for transfers between devices, chain(): total = total + lax.ppermute(sent, 'seq', [pair]).astype(F32)  76 us
    dot_general x11, matrix products, mm_tn(): lax.dot_general(a, b, (((0,), (0,)), ((), ())), preferred_element_type=F32)  67 us
    ppermute x64, starting transfers between devices, swap(): return lax.ppermute(value, axis, [(i, i ^ step) for i in range(count)])  62.2 us
    dot_general x6, matrix products, mm_nt(): lax.dot_general(a, b, (((1,), (1,)), ((), ())), preferred_element_type=F32)  57 us
    dot_general x6, matrix products, mm(): lax.dot_general(a, b, (((1,), (0,)), ((), ())), preferred_element_type=F32)  49.4 us
    pallas_call x4, Pallas kernels, run(): pl.pallas_call(kernel, grid=(args[0].shape[0],), in_specs=specs, out_spec...  49.2 us
    ppermute x7, waiting for transfers between devices, inward(): last[i] = lax.ppermute(value, 'seq', line_pairs(i))  43.4 us
  transfers between devices with their start and end apart: 103, of which 30 were waited for; matrix products, arithmetic and copies ran while one was open for 28% of the time, Pallas kernels for 9%

profile of v10, /device:TPU:0, one launch (start us, length us, event | category | flops | bytes accessed | tf_op | source)
XLA Modules:
  0.0 992.1 jit_solution(5459783247476608614)
XLA Ops:
  27.4 9.6 collective-permute-done.1
  38.5 21.2 %collective-permute-done.2 = f32[2,5409]{1,0:T(2,128)S(1)} collective-permute-done((f32[2,5409]{1,0:T(2,128)S(1)}, f32[2,5409]{1,0:T(2,128)S(1)}, u32[]{:S(2)}, u32[]{:S(2)}) %collective-permute-start.2) | collective-permute-done | bytes 43304 | tf_op jit(solution)/shard_map/ppermute | solution.py:346
  68.7 16.4 %collective-permute-done.8 = bf16[256,1024]{1,0:T(8,128)(2,1)} collective-permute-done((bf16[256,1024]{1,0:T(8,128)(2,1)}, bf16[256,1024]{1,0:T(8,128)(2,1)}, u32[]{:S(2)}, u32[]{:S(2)}) %collective-permute-start.8) | collective-permute-done | bytes 524320 | tf_op jit(solution)/shard_map/ppermute | solution.py:346
  106.6 5.6 shard_map.289
  112.2 6.8 fusion.2
  119.0 5.7 convolution_convert_fusion.8
  155.3 5.7 collective-permute-done.15
  173.7 6.0 shard_map.288
  181.2 8.6 fusion.84
  194.8 15.0 %shard_map.291 = (bf16[4,256,512]{2,1,0:T(8,128)(2,1)}, f32[4,256,512]{2,1,0:T(8,128)}, f32[4,256,64]{2,1,0:T(8,128)}, bf16[4,256,256]{2,1,0:T(8,128)(2,1)}) custom-call(f32[4,256,1024]{2,1,0:T(8,128)} %bitcast.220, bf16[4,256,1024]{2,1,0:T(8,128)(2,1)} %bitcast.223, f32[4,256,128]{2,1,0:T(8,128)} %bitcast.199, f32[4,64,1024]{2,1,0:T(8,128)} %pad_maximum_fusion.8.init_ref, ...), custom_call_target="tpu_custom_call" | custom-call | flops 12000000000 | bytes 16000000 | tf_op jit(solution)/shard_map/pallas_call | solution.py:258
  219.5 20.8 %collective-permute-done.30 = bf16[256,2048]{1,0:T(8,128)(2,1)S(1)} collective-permute-done((bf16[256,2048]{1,0:T(8,128)(2,1)S(1)}, bf16[256,2048]{1,0:T(8,128)(2,1)S(1)}, u32[]{:S(2)}, u32[]{:S(2)}) %collective-permute-start.30) | collective-permute-done | bytes 1048608 | tf_op jit(solution)/shard_map/ppermute | solution.py:346
  242.2 7.4 collective-permute-done.40.refs_2_
  249.5 7.2 collective-permute-done.42.refs_4_
  256.8 13.4 %fusion.68 = f32[1024,1408]{1,0:T(8,128)} fusion(bf16[1408,2048]{1,0:T(8,128)(2,1)} %all-gather.6.cloned.1.call-done, bf16[256,2048]{1,0:T(8,128)(2,1)} %collective-permute-done.35, bf16[256,2048]{1,0:T(8,128)(2,1)} %collective-permute-done.34, bf16[256,2048]{1,0:T(8,128)(2,1)} %collective-permute-done.33, bf16[256,2048]{1,0:T(8,128)(2,1)} %param.33, ...), kind=kOutput, calls=%fused_computation.246 | convolution fusion | flops 5926551552 | bytes 15732736 | tf_op jit(solution)/shard_map/dot_general | solution.py:23
  270.3 17.2 %collective-permute-done.44.refs_6_ = bf16[4,64,2816]{2,1,0:T(8,128)(2,1)} collective-permute-done((bf16[4,64,2816]{2,1,0:T(8,128)(2,1)}, bf16[4,64,2816]{2,1,0:T(8,128)(2,1)}, u32[]{:S(2)}, u32[]{:S(2)}) %collective-permute-start.44) | collective-permute-done | bytes 1441824 | tf_op jit(solution)/shard_map/ppermute | solution.py:346
  295.8 13.7 %shard_map.292 = bf16[2048,2816]{1,0:T(8,128)(2,1)} custom-call(s32[32]{0:T(128)} %stack.252.spot_ref, bf16[4,64,2816]{2,1,0:T(8,128)(2,1)} %pad_maximum_fusion.6.refs_0_, bf16[4,64,2816]{2,1,0:T(8,128)(2,1)} %collective-permute-done.39.refs_1_, bf16[4,64,2816]{2,1,0:T(8,128)(2,1)} %collective-permute-done.40.refs_2_, ...), custom_call_target="tpu_custom_call" | custom-call | bytes 23068672 | tf_op jit(solution)/shard_map/pallas_call | solution.py:382
  309.5 9.3 collective-permute-done.38
  318.7 22.0 %collective-permute-done.37 = bf16[256,2048]{1,0:T(8,128)(2,1)} collective-permute-done((bf16[256,2048]{1,0:T(8,128)(2,1)S(1)}, bf16[256,2048]{1,0:T(8,128)(2,1)}, u32[]{:S(2)}, u32[]{:S(2)}) %collective-permute-start.37) | collective-permute-done | bytes 1048608 | tf_op jit(solution)/shard_map/ppermute | solution.py:346
  340.7 21.2 %fusion.67 = f32[1024,2816]{1,0:T(8,128)} fusion(bf16[2048,2816]{1,0:T(8,128)(2,1)} %shard_map.292, bf16[256,2048]{1,0:T(8,128)(2,1)} %collective-permute-done.38, bf16[256,2048]{1,0:T(8,128)(2,1)} %collective-permute-done.37, bf16[256,2048]{1,0:T(8,128)(2,1)} %collective-permute-done.36, bf16[256,2048]{1,0:T(8,128)(2,1)S(1)} %multiply_convert_fusion.5), kind=kOutput, calls=%fused_computation.245 | convolution fusion | flops 11827937280 | bytes 27262976 | tf_op jit(solution)/shard_map/dot_general | solution.py:19
  362.0 7.1 multiply_convert_fusion.2
  371.8 8.9 convolution_convert_fusion
  381.2 16.3 %convolution_convert_fusion.1 = bf16[1024,2048]{1,0:T(8,128)(2,1)} fusion(bf16[1024,2816]{1,0:T(8,128)(2,1)S(1)} %pad_maximum_fusion, bf16[2048,2816]{1,0:T(8,128)(2,1)} %shard_map.292), kind=kOutput, calls=%fused_computation.22 | convolution fusion | flops 11813257216 | bytes 21495808 | tf_op jit(solution)/shard_map/dot_general | solution.py:23
  397.5 10.4 %add_convert_fusion = bf16[1024,2816]{1,0:T(8,128)(2,1)} fusion(bf16[1024,2816]{1,0:T(8,128)(2,1)} %collective-permute-done.46, bf16[1024,2816]{1,0:T(8,128)(2,1)S(1)} %pad_maximum_fusion, bf16[1024,256]{1,0:T(8,128)(2,1)S(1)} %get-tuple-element.253, bf16[1024,256]{1,0:T(8,128)(2,1)S(1)} %get-tuple-element.254, ...), kind=kOutput, calls=%fused_computation.1 | convolution fusion | flops 5922619392 | bytes 19398656 | tf_op jit(solution)/shard_map/dot_general | solution.py:27
  408.4 8.0 convolution_convert_fusion.4
  422.9 8.4 add_convert_fusion.2
  431.3 14.1 %collective-permute-done.47 = bf16[256,2048]{1,0:T(8,128)(2,1)S(1)} collective-permute-done((bf16[256,2048]{1,0:T(8,128)(2,1)S(1)}, bf16[256,2048]{1,0:T(8,128)(2,1)S(1)}, u32[]{:S(2)}, u32[]{:S(2)}) %collective-permute-start.47) | collective-permute-done | bytes 1048608 | tf_op jit(solution)/shard_map/ppermute | solution.py:346
  445.5 21.9 %collective-permute-done.48 = bf16[256,2048]{1,0:T(8,128)(2,1)S(1)} collective-permute-done((bf16[256,2048]{1,0:T(8,128)(2,1)S(1)}, bf16[256,2048]{1,0:T(8,128)(2,1)S(1)}, u32[]{:S(2)}, u32[]{:S(2)}) %collective-permute-start.48) | collective-permute-done | bytes 1048608 | tf_op jit(solution)/shard_map/ppermute | solution.py:346
  475.8 8.5 convolution_convert_fusion.2
  484.3 14.1 %collective-permute-done.51 = bf16[256,2048]{1,0:T(8,128)(2,1)S(1)} collective-permute-done((bf16[256,2048]{1,0:T(8,128)(2,1)S(1)}, bf16[256,2048]{1,0:T(8,128)(2,1)S(1)}, u32[]{:S(2)}, u32[]{:S(2)}) %collective-permute-start.51) | collective-permute-done | bytes 1048608 | tf_op jit(solution)/shard_map/ppermute | solution.py:346
  498.3 21.7 %collective-permute-done.52 = bf16[256,2048]{1,0:T(8,128)(2,1)S(1)} collective-permute-done((bf16[256,2048]{1,0:T(8,128)(2,1)S(1)}, bf16[256,2048]{1,0:T(8,128)(2,1)S(1)}, u32[]{:S(2)}, u32[]{:S(2)}) %collective-permute-start.52) | collective-permute-done | bytes 1048608 | tf_op jit(solution)/shard_map/ppermute | solution.py:346
  529.7 19.7 %shard_map.293 = (bf16[4,256,1024]{2,1,0:T(8,128)(2,1)}, f32[4,256,1024]{2,1,0:T(8,128)}, f32[4,256,128]{2,1,0:T(8,128)}, f32[4,64,1024]{2,1,0:T(8,128)}, f32[8,512]{1,0:T(8,128)}) custom-call(f32[4,256,1024]{2,1,0:T(8,128)} %bitcast.221, bf16[4,256,1024]{2,1,0:T(8,128)(2,1)} %bitcast.224, f32[4,256,128]{2,1,0:T(8,128)} %bitcast.200, ...), custom_call_target="tpu_custom_call" | custom-call | flops 24000000000 | bytes 20000000 | tf_op jit(solution)/shard_map/pallas_call | solution.py:258
  586.4 46.1 %collective-permute-done.57 = bf16[4,64,512]{2,1,0:T(8,128)(2,1)S(1)} collective-permute-done((bf16[4,64,512]{2,1,0:T(8,128)(2,1)S(1)}, bf16[4,64,512]{2,1,0:T(8,128)(2,1)S(1)}, u32[]{:S(2)}, u32[]{:S(2)}) %collective-permute-start.57) | collective-permute-done | bytes 262176 | tf_op jit(solution)/shard_map/ppermute | solution.py:465
  633.6 24.6 %collective-permute-done.60 = bf16[4,64,512]{2,1,0:T(8,128)(2,1)S(1)} collective-permute-done((bf16[4,64,512]{2,1,0:T(8,128)(2,1)S(1)}, bf16[4,64,512]{2,1,0:T(8,128)(2,1)S(1)}, u32[]{:S(2)}, u32[]{:S(2)}) %collective-permute-start.60) | collective-permute-done | bytes 262176 | tf_op jit(solution)/shard_map/ppermute | solution.py:465
  659.4 9.1 shard_map.294
  683.0 5.9 convolution_convert_fusion.6
  688.9 6.8 fusion.87
  695.7 16.7 %collective-permute-done.63 = bf16[352,2048]{1,0:T(8,128)(2,1)S(1)} collective-permute-done((bf16[352,2048]{1,0:T(8,128)(2,1)S(1)}, bf16[352,2048]{1,0:T(8,128)(2,1)S(1)}, u32[]{:S(2)}, u32[]{:S(2)}) %collective-permute-start.63) | collective-permute-done | bytes 1441824 | tf_op jit(solution)/shard_map/ppermute | solution.py:547
  714.2 5.5 collective-permute-start.72
  721.7 12.2 %add_convert_fusion.1 = bf16[1024,2048]{1,0:T(8,128)(2,1)} fusion(f32[1024,2048]{1,0:T(8,128)S(1)} %bitcast.179, f32[1024,2048]{1,0:T(8,128)} %fusion.87, bf16[1024,1024]{1,0:T(8,128)(2,1)} %bitcast.226, bf16[2048,1024]{1,0:T(8,128)(2,1)} %shard_map.288), kind=kOutput, calls=%fused_computation.7 | convolution fusion | flops 4301258752 | bytes 27262976 | tf_op jit(solution)/shard_map/dot_general | solution.py:23
  776.1 17.5 %collective-permute-done.65 = bf16[256,2048]{1,0:T(8,128)(2,1)} collective-permute-done((bf16[256,2048]{1,0:T(8,128)(2,1)}, bf16[256,2048]{1,0:T(8,128)(2,1)}, u32[]{:S(2)}, u32[]{:S(2)}) %collective-permute-start.65) | collective-permute-done | bytes 1048608 | tf_op jit(solution)/shard_map/ppermute | solution.py:346
  793.6 12.6 %collective-permute-done.66 = bf16[256,2048]{1,0:T(8,128)(2,1)} collective-permute-done((bf16[256,2048]{1,0:T(8,128)(2,1)}, bf16[256,2048]{1,0:T(8,128)(2,1)}, u32[]{:S(2)}, u32[]{:S(2)}) %collective-permute-start.66) | collective-permute-done | bytes 1048608 | tf_op jit(solution)/shard_map/ppermute | solution.py:346
  839.1 12.6 %collective-permute-done.86 = bf16[352,2048]{1,0:T(8,128)(2,1)S(1)} collective-permute-done((bf16[352,2048]{1,0:T(8,128)(2,1)S(1)}, bf16[352,2048]{1,0:T(8,128)(2,1)S(1)}, u32[]{:S(2)}, u32[]{:S(2)}) %collective-permute-start.86) | collective-permute-done | bytes 1441824 | tf_op jit(solution)/shard_map/ppermute | solution.py:565
  854.1 10.5 %collective-permute-start.76 = (bf16[2,256,1024]{2,1,0:T(8,128)(2,1)}, bf16[2,256,1024]{2,1,0:T(8,128)(2,1)}, u32[]{:S(2)}, u32[]{:S(2)}) collective-permute-start(bf16[2,256,1024]{2,1,0:T(8,128)(2,1)} %get-tuple-element.147), channel_id=1, source_target_pairs={{0,1},{3,2},{4,5},{7,6},{8,9},{11,10},{12,13},{15,14},{16,17},{19,... | collective-permute-start | bytes 3145736 | tf_op jit(solution)/shard_map/ppermute | solution.py:547
  878.1 9.0 collective-permute-done.76
  903.9 10.4 %collective-permute-done.77 = bf16[264,2048]{1,0:T(8,128)(2,1)S(1)} collective-permute-done((bf16[264,2048]{1,0:T(8,128)(2,1)S(1)}, bf16[264,2048]{1,0:T(8,128)(2,1)S(1)}, u32[]{:S(2)}, u32[]{:S(2)}) %collective-permute-start.77) | collective-permute-done | bytes 1081376 | tf_op jit(solution)/shard_map/ppermute | solution.py:547
  917.2 11.4 %collective-permute-done.89 = bf16[2,256,1024]{2,1,0:T(8,128)(2,1)S(1)} collective-permute-done((bf16[2,256,1024]{2,1,0:T(8,128)(2,1)S(1)}, bf16[2,256,1024]{2,1,0:T(8,128)(2,1)S(1)}, u32[]{:S(2)}, u32[]{:S(2)}) %collective-permute-start.89) | collective-permute-done | bytes 1048608 | tf_op jit(solution)/shard_map/ppermute | solution.py:565
  943.9 10.3 %collective-permute-done.90 = bf16[2,256,1024]{2,1,0:T(8,128)(2,1)} collective-permute-done((bf16[2,256,1024]{2,1,0:T(8,128)(2,1)S(1)}, bf16[2,256,1024]{2,1,0:T(8,128)(2,1)}, u32[]{:S(2)}, u32[]{:S(2)}) %collective-permute-start.90) | collective-permute-done | bytes 1048608 | tf_op jit(solution)/shard_map/ppermute | solution.py:565
  961.7 8.0 shard_map.297
  (548 shorter events, 354.6 us)
Async XLA Ops:
  7.2 202.6 %all-gather.4.cloned.1.call-start = ((), (), s32[]{:S(2)}) async-start(), calls=%async_computation.2 | async-start | bytes 3145728 | tf_op jit(solution)/shard_map/all_gather | solution.py:638
  7.9 248.9 %all-gather.6.cloned.1.call-start = ((), (), s32[]{:S(2)}) async-start(), calls=%async_computation.3 | async-start | bytes 8650752 | tf_op jit(solution)/shard_map/all_gather | solution.py:639
  8.0 90.2 %collective-permute-start.6 = (bf16[256,2048]{1,0:T(8,128)(2,1)}, bf16[256,2048]{1,0:T(8,128)(2,1)S(1)}, u32[]{:S(2)}, u32[]{:S(2)}) collective-permute-start(bf16[256,2048]{1,0:T(8,128)(2,1)} %param.17), channel_id=1, source_target_pairs={{0,24},{8,16},{16,8},{24,0},{1,25},{9,17},{17,9},{25,1},{2,26},{10... | collective-permute-start | bytes 3145736 | tf_op jit(solution)/shard_map/ppermute | solution.py:346
  12.0 86.4 %collective-permute-start.5 = (bf16[256,2048]{1,0:T(8,128)(2,1)}, bf16[256,2048]{1,0:T(8,128)(2,1)}, u32[]{:S(2)}, u32[]{:S(2)}) collective-permute-start(bf16[256,2048]{1,0:T(8,128)(2,1)} %param.17), channel_id=1, source_target_pairs={{0,16},{8,24},{16,0},{24,8},{1,17},{9,25},{17,1},{25,9},{2,18},{10... | collective-permute-start | bytes 3145736 | tf_op jit(solution)/shard_map/ppermute | solution.py:346
  17.7 503.3 %reduce-scatter.5.cloned.1.call-start = ((), (), s32[]{:S(2)}) async-start(), calls=%async_computation.4 | async-start | bytes 7208960 | tf_op jit(solution)/shard_map/reduce_scatter | solution.py:686
  23.4 36.3 %collective-permute-start.2 = (f32[2,5409]{1,0:T(2,128)S(1)}, f32[2,5409]{1,0:T(2,128)S(1)}, u32[]{:S(2)}, u32[]{:S(2)}) collective-permute-start(f32[2,5409]{1,0:T(2,128)S(1)} %pad_maximum_fusion.30), channel_id=1, source_target_pairs={{0,16},{8,24},{16,0},{24,8},{1,17},{9,25},{17,1},{25,9},{2,18},{10... | collective-permute-start | bytes 129824 | tf_op jit(solution)/shard_map/ppermute | solution.py:346
  25.3 36.1 %collective-permute-start.3 = (f32[2,5409]{1,0:T(2,128)S(1)}, f32[2,5409]{1,0:T(2,128)S(1)}, u32[]{:S(2)}, u32[]{:S(2)}) collective-permute-start(f32[2,5409]{1,0:T(2,128)S(1)} %pad_maximum_fusion.30), channel_id=1, source_target_pairs={{0,24},{8,16},{16,8},{24,0},{1,25},{9,17},{17,9},{25,1},{2,26},{10... | collective-permute-start | bytes 129824 | tf_op jit(solution)/shard_map/ppermute | solution.py:346
  37.0 31.2 %collective-permute-start.7 = (bf16[256,1024]{1,0:T(8,128)(2,1)}, bf16[256,1024]{1,0:T(8,128)(2,1)S(1)}, u32[]{:S(2)}, u32[]{:S(2)}) collective-permute-start(bf16[256,1024]{1,0:T(8,128)(2,1)} %pad_maximum_fusion.10), channel_id=1, source_target_pairs={{0,8},{8,0},{16,24},{24,16},{1,9},{9,1},{17,25},{25,17},{2,10},{10... | collective-permute-start | bytes 1572872 | tf_op jit(solution)/shard_map/ppermute | solution.py:346
  68.2 30.4 %collective-permute-start.4 = (bf16[256,2048]{1,0:T(8,128)(2,1)S(1)}, bf16[256,2048]{1,0:T(8,128)(2,1)S(1)}, u32[]{:S(2)}, u32[]{:S(2)}) collective-permute-start(bf16[256,2048]{1,0:T(8,128)(2,1)S(1)} %copy-done.2), channel_id=1, source_target_pairs={{0,8},{8,0},{16,24},{24,16},{1,9},{9,1},{17,25},{25,17},{2,10},{10... | collective-permute-start | bytes 3145736 | tf_op jit(solution)/shard_map/ppermute | solution.py:346
  89.3 63.6 %collective-permute-start.11 = (bf16[256,1024]{1,0:T(8,128)(2,1)}, bf16[256,1024]{1,0:T(8,128)(2,1)}, u32[]{:S(2)}, u32[]{:S(2)}) collective-permute-start(bf16[256,1024]{1,0:T(8,128)(2,1)} %pad_maximum_fusion.14), channel_id=1, source_target_pairs={{0,8},{8,0},{16,24},{24,16},{1,9},{9,1},{17,25},{25,17},{2,10},{10... | collective-permute-start | bytes 1572872 | tf_op jit(solution)/shard_map/ppermute | solution.py:346
  102.1 53.2 %collective-permute-start.13 = (bf16[256,1024]{1,0:T(8,128)(2,1)}, bf16[256,1024]{1,0:T(8,128)(2,1)}, u32[]{:S(2)}, u32[]{:S(2)}) collective-permute-start(bf16[256,1024]{1,0:T(8,128)(2,1)} %pad_maximum_fusion.15), channel_id=1, source_target_pairs={{0,16},{8,24},{16,0},{24,8},{1,17},{9,25},{17,1},{25,9},{2,18},{10... | collective-permute-start | bytes 1572872 | tf_op jit(solution)/shard_map/ppermute | solution.py:346
  103.6 44.1 %collective-permute-start.29 = (bf16[64,2816]{1,0:T(8,128)(2,1)}, bf16[64,2816]{1,0:T(8,128)(2,1)}, u32[]{:S(2)}, u32[]{:S(2)}) collective-permute-start(bf16[64,2816]{1,0:T(8,128)(2,1)} %pad_maximum_fusion.21), channel_id=1, source_target_pairs={{0,24},{8,16},{16,8},{24,0},{1,25},{9,17},{17,9},{25,1},{2,26},{10... | collective-permute-start | bytes 1081352 | tf_op jit(solution)/shard_map/ppermute | solution.py:346
  105.1 47.0 %collective-permute-start.28 = (bf16[64,2816]{1,0:T(8,128)(2,1)}, bf16[64,2816]{1,0:T(8,128)(2,1)}, u32[]{:S(2)}, u32[]{:S(2)}) collective-permute-start(bf16[64,2816]{1,0:T(8,128)(2,1)} %pad_maximum_fusion.20), channel_id=1, source_target_pairs={{0,16},{8,24},{16,0},{24,8},{1,17},{9,25},{17,1},{25,9},{2,18},{10... | collective-permute-start | bytes 1081352 | tf_op jit(solution)/shard_map/ppermute | solution.py:346
  169.4 47.8 %collective-permute-start.35 = (bf16[256,2048]{1,0:T(8,128)(2,1)}, bf16[256,2048]{1,0:T(8,128)(2,1)}, u32[]{:S(2)}, u32[]{:S(2)}) collective-permute-start(bf16[256,2048]{1,0:T(8,128)(2,1)} %param.33), channel_id=1, source_target_pairs={{0,24},{8,16},{16,8},{24,0},{1,25},{9,17},{17,9},{25,1},{2,26},{10... | collective-permute-start | bytes 3145736 | tf_op jit(solution)/shard_map/ppermute | solution.py:346
  170.9 46.8 %collective-permute-start.34 = (bf16[256,2048]{1,0:T(8,128)(2,1)}, bf16[256,2048]{1,0:T(8,128)(2,1)}, u32[]{:S(2)}, u32[]{:S(2)}) collective-permute-start(bf16[256,2048]{1,0:T(8,128)(2,1)} %param.33), channel_id=1, source_target_pairs={{0,16},{8,24},{16,0},{24,8},{1,17},{9,25},{17,1},{25,9},{2,18},{10... | collective-permute-start | bytes 3145736 | tf_op jit(solution)/shard_map/ppermute | solution.py:346
  171.4 46.5 %collective-permute-start.33 = (bf16[256,2048]{1,0:T(8,128)(2,1)}, bf16[256,2048]{1,0:T(8,128)(2,1)}, u32[]{:S(2)}, u32[]{:S(2)}) collective-permute-start(bf16[256,2048]{1,0:T(8,128)(2,1)} %param.33), channel_id=1, source_target_pairs={{0,8},{8,0},{16,24},{24,16},{1,9},{9,1},{17,25},{25,17},{2,10},{10... | collective-permute-start | bytes 3145736 | tf_op jit(solution)/shard_map/ppermute | solution.py:346
  191.1 58.4 %collective-permute-start.40 = (bf16[4,64,2816]{2,1,0:T(8,128)(2,1)}, bf16[4,64,2816]{2,1,0:T(8,128)(2,1)}, u32[]{:S(2)}, u32[]{:S(2)}) collective-permute-start(bf16[4,64,2816]{2,1,0:T(8,128)(2,1)} %pad_maximum_fusion.6.refs_0_), channel_id=1, source_target_pairs={{0,1},{1,0},{2,3},{3,2},{4,5},{5,4},{6,7},{7,6},{8,9},{9,8},{10,11... | collective-permute-start | bytes 4325384 | tf_op jit(solution)/shard_map/ppermute | solution.py:346
  194.2 62.6 %collective-permute-start.42 = (bf16[4,64,2816]{2,1,0:T(8,128)(2,1)}, bf16[4,64,2816]{2,1,0:T(8,128)(2,1)}, u32[]{:S(2)}, u32[]{:S(2)}) collective-permute-start(bf16[4,64,2816]{2,1,0:T(8,128)(2,1)} %pad_maximum_fusion.6.refs_0_), channel_id=1, source_target_pairs={{0,2},{1,3},{2,0},{3,1},{4,6},{5,7},{6,4},{7,5},{8,10},{9,11},{10,... | collective-permute-start | bytes 4325384 | tf_op jit(solution)/shard_map/ppermute | solution.py:346
  217.8 75.4 %collective-permute-start.39 = (bf16[4,64,2816]{2,1,0:T(8,128)(2,1)}, bf16[4,64,2816]{2,1,0:T(8,128)(2,1)}, u32[]{:S(2)}, u32[]{:S(2)}) collective-permute-start(bf16[4,64,2816]{2,1,0:T(8,128)(2,1)} %pad_maximum_fusion.6.refs_0_), channel_id=1, source_target_pairs={{0,4},{4,0},{1,5},{5,1},{2,6},{6,2},{3,7},{7,3},{8,12},{12,8},{9,1... | collective-permute-start | bytes 4325384 | tf_op jit(solution)/shard_map/ppermute | solution.py:346
  217.8 52.4 %collective-permute-start.31 = (bf16[256,2048]{1,0:T(8,128)(2,1)}, bf16[256,2048]{1,0:T(8,128)(2,1)}, u32[]{:S(2)}, u32[]{:S(2)}) collective-permute-start(bf16[256,2048]{1,0:T(8,128)(2,1)} %get-tuple-element.258), channel_id=1, source_target_pairs={{0,16},{8,24},{16,0},{24,8},{1,17},{9,25},{17,1},{25,9},{2,18},{10... | collective-permute-start | bytes 3145736 | tf_op jit(solution)/shard_map/ppermute | solution.py:346
  240.2 47.3 %collective-permute-start.32 = (bf16[256,2048]{1,0:T(8,128)(2,1)S(1)}, bf16[256,2048]{1,0:T(8,128)(2,1)}, u32[]{:S(2)}, u32[]{:S(2)}) collective-permute-start(bf16[256,2048]{1,0:T(8,128)(2,1)S(1)} %get-tuple-element.257), channel_id=1, source_target_pairs={{0,24},{8,16},{16,8},{24,0},{1,25},{9,17},{17,9},{25,1},{2,26},{10... | collective-permute-start | bytes 3145736 | tf_op jit(solution)/shard_map/ppermute | solution.py:346
  249.5 44.1 %collective-permute-start.41 = (bf16[4,64,2816]{2,1,0:T(8,128)(2,1)}, bf16[4,64,2816]{2,1,0:T(8,128)(2,1)}, u32[]{:S(2)}, u32[]{:S(2)}) collective-permute-start(bf16[4,64,2816]{2,1,0:T(8,128)(2,1)} %collective-permute-done.40.refs_2_), channel_id=1, source_target_pairs={{0,4},{4,0},{1,5},{5,1},{2,6},{6,2},{3,7},{7,3},{8,12},{12,8},{9,1... | collective-permute-start | bytes 4325384 | tf_op jit(solution)/shard_map/ppermute | solution.py:346
  256.8 30.8 %collective-permute-start.44 = (bf16[4,64,2816]{2,1,0:T(8,128)(2,1)}, bf16[4,64,2816]{2,1,0:T(8,128)(2,1)}, u32[]{:S(2)}, u32[]{:S(2)}) collective-permute-start(bf16[4,64,2816]{2,1,0:T(8,128)(2,1)} %collective-permute-done.42.refs_4_), channel_id=1, source_target_pairs={{0,1},{1,0},{2,3},{3,2},{4,5},{5,4},{6,7},{7,6},{8,9},{9,8},{10,11... | collective-permute-start | bytes 4325384 | tf_op jit(solution)/shard_map/ppermute | solution.py:346
  293.2 47.6 %collective-permute-start.37 = (bf16[256,2048]{1,0:T(8,128)(2,1)S(1)}, bf16[256,2048]{1,0:T(8,128)(2,1)}, u32[]{:S(2)}, u32[]{:S(2)}) collective-permute-start(bf16[256,2048]{1,0:T(8,128)(2,1)S(1)} %multiply_convert_fusion.5), channel_id=1, source_target_pairs={{0,16},{8,24},{16,0},{24,8},{1,17},{9,25},{17,1},{25,9},{2,18},{10... | collective-permute-start | bytes 3145736 | tf_op jit(solution)/shard_map/ppermute | solution.py:346
  293.6 47.1 %collective-permute-start.36 = (bf16[256,2048]{1,0:T(8,128)(2,1)S(1)}, bf16[256,2048]{1,0:T(8,128)(2,1)}, u32[]{:S(2)}, u32[]{:S(2)}) collective-permute-start(bf16[256,2048]{1,0:T(8,128)(2,1)S(1)} %multiply_convert_fusion.5), channel_id=1, source_target_pairs={{0,8},{8,0},{16,24},{24,16},{1,9},{9,1},{17,25},{25,17},{2,10},{10... | collective-permute-start | bytes 3145736 | tf_op jit(solution)/shard_map/ppermute | solution.py:346
  408.0 271.9 %all-gather.8.cloned.1.call-start = ((), (), s32[]{:S(2)}) async-start(), calls=%async_computation.5 | async-start | bytes 7208960 | tf_op jit(solution)/shard_map/all_gather | solution.py:719
  420.1 47.3 %collective-permute-start.48 = (bf16[256,2048]{1,0:T(8,128)(2,1)S(1)}, bf16[256,2048]{1,0:T(8,128)(2,1)S(1)}, u32[]{:S(2)}, u32[]{:S(2)}) collective-permute-start(bf16[256,2048]{1,0:T(8,128)(2,1)S(1)} %get-tuple-element.247), channel_id=1, source_target_pairs={{0,16},{8,24},{16,0},{24,8},{1,17},{9,25},{17,1},{25,9},{2,18},{10... | collective-permute-start | bytes 3145736 | tf_op jit(solution)/shard_map/ppermute | solution.py:346
  421.5 45.9 %collective-permute-start.49 = (bf16[256,2048]{1,0:T(8,128)(2,1)S(1)}, bf16[256,2048]{1,0:T(8,128)(2,1)S(1)}, u32[]{:S(2)}, u32[]{:S(2)}) collective-permute-start(bf16[256,2048]{1,0:T(8,128)(2,1)S(1)} %get-tuple-element.246), channel_id=1, source_target_pairs={{0,24},{8,16},{16,8},{24,0},{1,25},{9,17},{17,9},{25,1},{2,26},{10... | collective-permute-start | bytes 3145736 | tf_op jit(solution)/shard_map/ppermute | solution.py:346
  473.7 46.3 %collective-permute-start.52 = (bf16[256,2048]{1,0:T(8,128)(2,1)S(1)}, bf16[256,2048]{1,0:T(8,128)(2,1)S(1)}, u32[]{:S(2)}, u32[]{:S(2)}) collective-permute-start(bf16[256,2048]{1,0:T(8,128)(2,1)S(1)} %get-tuple-element.116), channel_id=1, source_target_pairs={{0,16},{8,24},{16,0},{24,8},{1,17},{9,25},{17,1},{25,9},{2,18},{10... | collective-permute-start | bytes 3145736 | tf_op jit(solution)/shard_map/ppermute | solution.py:346
  474.5 46.5 %collective-permute-start.53 = (bf16[256,2048]{1,0:T(8,128)(2,1)S(1)}, bf16[256,2048]{1,0:T(8,128)(2,1)}, u32[]{:S(2)}, u32[]{:S(2)}) collective-permute-start(bf16[256,2048]{1,0:T(8,128)(2,1)S(1)} %get-tuple-element.116), channel_id=1, source_target_pairs={{0,24},{8,16},{16,8},{24,0},{1,25},{9,17},{17,9},{25,1},{2,26},{10... | collective-permute-start | bytes 3145736 | tf_op jit(solution)/shard_map/ppermute | solution.py:346
  550.6 408.5 %reduce-scatter.7.cloned.1.call-start = ((), (), s32[]{:S(2)}) async-start(), calls=%async_computation.6 | async-start | bytes 5242880
  577.9 54.6 %collective-permute-start.57 = (bf16[4,64,512]{2,1,0:T(8,128)(2,1)S(1)}, bf16[4,64,512]{2,1,0:T(8,128)(2,1)S(1)}, u32[]{:S(2)}, u32[]{:S(2)}) collective-permute-start(bf16[4,64,512]{2,1,0:T(8,128)(2,1)S(1)} %get-tuple-element.276), channel_id=1, source_target_pairs={{1,0},{5,4},{9,8},{13,12},{17,16},{21,20},{25,24},{29,28}} | collective-permute-start | bytes 786440 | tf_op jit(solution)/shard_map/ppermute | solution.py:465
  579.3 78.9 %collective-permute-start.60 = (bf16[4,64,512]{2,1,0:T(8,128)(2,1)S(1)}, bf16[4,64,512]{2,1,0:T(8,128)(2,1)S(1)}, u32[]{:S(2)}, u32[]{:S(2)}) collective-permute-start(bf16[4,64,512]{2,1,0:T(8,128)(2,1)S(1)} %add_convert_fusion.5), channel_id=1, source_target_pairs={{1,0},{5,4},{9,8},{13,12},{17,16},{21,20},{25,24},{29,28}} | collective-permute-start | bytes 786440 | tf_op jit(solution)/shard_map/ppermute | solution.py:465
  681.4 31.0 %collective-permute-start.63 = (bf16[352,2048]{1,0:T(8,128)(2,1)S(1)}, bf16[352,2048]{1,0:T(8,128)(2,1)S(1)}, u32[]{:S(2)}, u32[]{:S(2)}) collective-permute-start(bf16[352,2048]{1,0:T(8,128)(2,1)S(1)} %slice.196), channel_id=1, source_target_pairs={{0,1},{3,2},{4,5},{7,6},{8,9},{11,10},{12,13},{15,14},{16,17},{19,... | collective-permute-start | bytes 4325384 | tf_op jit(solution)/shard_map/ppermute | solution.py:547
  688.9 78.7 %collective-permute-start.67 = (bf16[1024,1024]{1,0:T(8,128)(2,1)}, bf16[1024,1024]{1,0:T(8,128)(2,1)}, u32[]{:S(2)}, u32[]{:S(2)}) collective-permute-start(bf16[1024,1024]{1,0:T(8,128)(2,1)} %convolution_convert_fusion.6), channel_id=1, source_target_pairs={{0,4},{4,0},{1,5},{5,1},{2,6},{6,2},{3,7},{7,3},{8,12},{12,8},{9,1... | collective-permute-start | bytes 6291464 | tf_op jit(solution)/shard_map/ppermute | solution.py:346
  714.2 33.4 %collective-permute-start.72 = (bf16[352,2048]{1,0:T(8,128)(2,1)}, bf16[352,2048]{1,0:T(8,128)(2,1)}, u32[]{:S(2)}, u32[]{:S(2)}) collective-permute-start(bf16[352,2048]{1,0:T(8,128)(2,1)} %get-tuple-element.143), channel_id=1, source_target_pairs={{0,1},{3,2},{4,5},{7,6},{8,9},{11,10},{12,13},{15,14},{16,17},{19,... | collective-permute-start | bytes 4325384 | tf_op jit(solution)/shard_map/ppermute | solution.py:547
  719.8 38.9 %collective-permute-start.78 = (bf16[352,2048]{1,0:T(8,128)(2,1)}, bf16[352,2048]{1,0:T(8,128)(2,1)}, u32[]{:S(2)}, u32[]{:S(2)}) collective-permute-start(bf16[352,2048]{1,0:T(8,128)(2,1)} %get-tuple-element.149), channel_id=1, source_target_pairs={{1,2},{2,1},{5,6},{6,5},{9,10},{10,9},{13,14},{14,13},{17,18},{18,... | collective-permute-start | bytes 4325384 | tf_op jit(solution)/shard_map/ppermute | solution.py:556
  737.5 32.0 %collective-permute-start.64 = (bf16[256,2048]{1,0:T(8,128)(2,1)}, bf16[256,2048]{1,0:T(8,128)(2,1)}, u32[]{:S(2)}, u32[]{:S(2)}) collective-permute-start(bf16[256,2048]{1,0:T(8,128)(2,1)} %get-tuple-element.233), channel_id=1, source_target_pairs={{0,8},{8,0},{16,24},{24,16},{1,9},{9,1},{17,25},{25,17},{2,10},{10... | collective-permute-start | bytes 3145736 | tf_op jit(solution)/shard_map/ppermute | solution.py:346
  743.6 50.0 %collective-permute-start.65 = (bf16[256,2048]{1,0:T(8,128)(2,1)}, bf16[256,2048]{1,0:T(8,128)(2,1)}, u32[]{:S(2)}, u32[]{:S(2)}) collective-permute-start(bf16[256,2048]{1,0:T(8,128)(2,1)} %get-tuple-element.232), channel_id=1, source_target_pairs={{0,16},{8,24},{16,0},{24,8},{1,17},{9,25},{17,1},{25,9},{2,18},{10... | collective-permute-start | bytes 3145736 | tf_op jit(solution)/shard_map/ppermute | solution.py:346
  747.7 58.5 %collective-permute-start.66 = (bf16[256,2048]{1,0:T(8,128)(2,1)}, bf16[256,2048]{1,0:T(8,128)(2,1)}, u32[]{:S(2)}, u32[]{:S(2)}) collective-permute-start(bf16[256,2048]{1,0:T(8,128)(2,1)} %get-tuple-element.231), channel_id=1, source_target_pairs={{0,24},{8,16},{16,8},{24,0},{1,25},{9,17},{17,9},{25,1},{2,26},{10... | collective-permute-start | bytes 3145736 | tf_op jit(solution)/shard_map/ppermute | solution.py:346
  758.7 51.0 %collective-permute-start.73 = (bf16[2,256,1024]{2,1,0:T(8,128)(2,1)}, bf16[2,256,1024]{2,1,0:T(8,128)(2,1)}, u32[]{:S(2)}, u32[]{:S(2)}) collective-permute-start(bf16[2,256,1024]{2,1,0:T(8,128)(2,1)} %get-tuple-element.144), channel_id=1, source_target_pairs={{0,1},{3,2},{4,5},{7,6},{8,9},{11,10},{12,13},{15,14},{16,17},{19,... | collective-permute-start | bytes 3145736 | tf_op jit(solution)/shard_map/ppermute | solution.py:547
  767.6 49.6 %collective-permute-start.79 = (bf16[352,2048]{1,0:T(8,128)(2,1)}, bf16[352,2048]{1,0:T(8,128)(2,1)}, u32[]{:S(2)}, u32[]{:S(2)}) collective-permute-start(bf16[352,2048]{1,0:T(8,128)(2,1)} %add.753), channel_id=1, source_target_pairs={{1,2},{2,1},{5,6},{6,5},{9,10},{10,9},{13,14},{14,13},{17,18},{18,... | collective-permute-start | bytes 4325384 | tf_op jit(solution)/shard_map/ppermute | solution.py:556
  769.5 50.7 %collective-permute-start.85 = (bf16[352,2048]{1,0:T(8,128)(2,1)}, bf16[352,2048]{1,0:T(8,128)(2,1)}, u32[]{:S(2)}, u32[]{:S(2)}) collective-permute-start(bf16[352,2048]{1,0:T(8,128)(2,1)} %add.760), channel_id=1, source_target_pairs={{1,0},{2,3},{5,4},{6,7},{9,8},{10,11},{13,12},{14,15},{17,16},{18,... | collective-permute-start | bytes 4325384 | tf_op jit(solution)/shard_map/ppermute | solution.py:565
  820.1 31.6 %collective-permute-start.86 = (bf16[352,2048]{1,0:T(8,128)(2,1)S(1)}, bf16[352,2048]{1,0:T(8,128)(2,1)S(1)}, u32[]{:S(2)}, u32[]{:S(2)}) collective-permute-start(bf16[352,2048]{1,0:T(8,128)(2,1)S(1)} %add.759), channel_id=1, source_target_pairs={{1,0},{2,3},{5,4},{6,7},{9,8},{10,11},{13,12},{14,15},{17,16},{18,... | collective-permute-start | bytes 4325384 | tf_op jit(solution)/shard_map/ppermute | solution.py:565
  836.0 36.5 %collective-permute-start.81 = (bf16[2,256,1024]{2,1,0:T(8,128)(2,1)}, bf16[2,256,1024]{2,1,0:T(8,128)(2,1)}, u32[]{:S(2)}, u32[]{:S(2)}) collective-permute-start(bf16[2,256,1024]{2,1,0:T(8,128)(2,1)} %add.751), channel_id=1, source_target_pairs={{1,2},{2,1},{5,6},{6,5},{9,10},{10,9},{13,14},{14,13},{17,18},{18,... | collective-permute-start | bytes 3145736 | tf_op jit(solution)/shard_map/ppermute | solution.py:556
  854.1 32.9 %collective-permute-start.76 = (bf16[2,256,1024]{2,1,0:T(8,128)(2,1)}, bf16[2,256,1024]{2,1,0:T(8,128)(2,1)}, u32[]{:S(2)}, u32[]{:S(2)}) collective-permute-start(bf16[2,256,1024]{2,1,0:T(8,128)(2,1)} %get-tuple-element.147), channel_id=1, source_target_pairs={{0,1},{3,2},{4,5},{7,6},{8,9},{11,10},{12,13},{15,14},{16,17},{19,... | collective-permute-start | bytes 3145736 | tf_op jit(solution)/shard_map/ppermute | solution.py:547
  892.9 40.4 %collective-permute-start.94 = (bf16[256,1024]{1,0:T(8,128)(2,1)S(1)}, bf16[256,1024]{1,0:T(8,128)(2,1)S(1)}, u32[]{:S(2)}, u32[]{:S(2)}) collective-permute-start(bf16[256,1024]{1,0:T(8,128)(2,1)S(1)} %get-tuple-element.291), channel_id=1, source_target_pairs={{0,24},{8,16},{16,8},{24,0},{1,25},{9,17},{17,9},{25,1},{2,26},{10... | collective-permute-start | bytes 1572872 | tf_op jit(solution)/shard_map/ppermute | solution.py:346
  893.6 39.7 %collective-permute-start.92 = (bf16[256,1024]{1,0:T(8,128)(2,1)S(1)}, bf16[256,1024]{1,0:T(8,128)(2,1)S(1)}, u32[]{:S(2)}, u32[]{:S(2)}) collective-permute-start(bf16[256,1024]{1,0:T(8,128)(2,1)S(1)} %get-tuple-element.290), channel_id=1, source_target_pairs={{0,8},{8,0},{16,24},{24,16},{1,9},{9,1},{17,25},{25,17},{2,10},{10... | collective-permute-start | bytes 1572872 | tf_op jit(solution)/shard_map/ppermute | solution.py:346
  (141 other events, 2257.3 us)
Sparse Core Ops, SparseCore 0:
  9.5 13.2 all-gather.3
  24.4 17.1 all-gather.5
  408.1 99.6 reduce-scatter.4
  550.7 119.9 all-gather.7
  755.1 76.0 reduce-scatter.6
